TPU v7x, 256 devices: a whole 4x4x8 slice. The times are simulated.
256 devices in a mesh: ang: 32 (over z_lo, x, core), strip: 8 (over z_hi, y).
Axes of the slice: x: 4, y: 4, z: 8 (z_hi: 2, z_lo: 4; z = z_hi * 4 + z_lo), core: 2. Of those that a mesh axis runs over, the one named last changes fastest.
Arguments:
- measured: float32 [32, 64, 128, 128], P('ang', 'strip'), may hold values from 0.05 to 4
- positions: int32 [32, 64], P('ang', 'strip'), may hold values from 0 to 384
- probe_field: float32 [2, 128, 128], replicated, may hold values from -6 to 6
- object_field: float32 [32, 512, 2, 128], P('ang', 'strip'), may hold values from -6 to 6
- dual_field: float32 [32, 512, 2, 128], P('ang', 'strip'), may hold values from -6 to 6
- volume: float32 [65536, 2, 128], P(('ang', 'strip')), may hold values from -6 to 6
- radon_tiles: bfloat16 [256, 32, 2, 32, 256], P(('ang', 'strip')), may hold values from -0.0625 to 0.0625
- tile_range: int32 [32, 32, 8, 1], P('ang', None, 'strip'), may hold values from 0 to 14
Outputs:
- object_next: float32 [32, 512, 2, 128], P('ang', 'strip')
- dual_next: float32 [32, 512, 2, 128], P('ang', 'strip')
- volume_next: float32 [65536, 2, 128], P(('ang', 'strip'))
Inputs may be any that keep to these rules, and one draw needn't show every extreme that they name: `positions`: a frame covers 128 detector columns from its position. A pixel tile meets ray tiles tile_range to tile_range + 1 at that angle.
All inputs are finite; a program needn't handle non-finite values.
Results may differ from a plain program's by a relative error of at most 0.0027.
Values may be sent and summed in bfloat16 or wider, within the bound.
No kernel may reach another device: no remote copies, remote signals or barrier semaphores. Data moves between devices by JAX's collectives and lax.ppermute only.
A program may use at most 64 MiB of HBM per device.

v0:
```python
import math

import jax
import jax.numpy as jnp
from jax import lax
from jax.sharding import PartitionSpec as P

PROBE = 128
NZ = 128
NDET = 512
RAYS = 32
TILE = 256
HITS = 2
PT_DEV = 1
NR = 16


penalty = 1.0
object_step = 0.1
volume_step = 1.0
precise = lax.Precision.HIGHEST


def joined_along(pieces, dim):
    lengths = list(pieces.shape[1:])
    lengths[dim] *= pieces.shape[0]
    return jnp.moveaxis(pieces, 0, dim).reshape(lengths)


def sent_to_all(array, axis):
    copies = jnp.broadcast_to(array, (lax.axis_size(axis), *array.shape))
    return lax.all_to_all(copies, axis, split_axis=0, concat_axis=0, tiled=True)


def gathered_copies(array, axis, dim):
    return joined_along(sent_to_all(array, axis), dim)


def in_blocks(array, dim, count):
    lengths = array.shape
    pieces = array.reshape(*lengths[:dim], count, lengths[dim] // count, *lengths[dim + 1 :])
    return jnp.moveaxis(pieces, dim, 0)


def sent_and_summed(array, axis, dim):
    count = lax.axis_size(axis)
    pieces = lax.all_to_all(in_blocks(array, dim, count), axis, 0, 0, tiled=True)
    return jnp.sum(pieces, axis=0)


def dft_tables(length):
    indices = jnp.arange(length, dtype=jnp.int32)
    phases = indices[:, None] * indices[None, :] % length
    angles = phases.astype(jnp.float32) * (2.0 * math.pi / length)
    scaling = 1.0 / math.sqrt(length)
    return (jnp.cos(angles) * scaling, jnp.sin(angles) * scaling)


def transform(real_part, imag_part, cosine_table, sine_table, handed):
    left_re = jnp.einsum(
        "kc,fcr->fkr", cosine_table, real_part, precision=precise
    ) + handed * jnp.einsum("kc,fcr->fkr", sine_table, imag_part, precision=precise)
    left_im = jnp.einsum(
        "kc,fcr->fkr", cosine_table, imag_part, precision=precise
    ) - handed * jnp.einsum("kc,fcr->fkr", sine_table, real_part, precision=precise)
    out_re = jnp.einsum(
        "fkr,rl->fkl", left_re, cosine_table, precision=precise
    ) + handed * jnp.einsum("fkr,rl->fkl", left_im, sine_table, precision=precise)
    out_im = jnp.einsum(
        "fkr,rl->fkl", left_im, cosine_table, precision=precise
    ) - handed * jnp.einsum("fkr,rl->fkl", left_re, sine_table, precision=precise)
    return (out_re, out_im)


def intersection_gradient(intensity, starts, field, probe_field, cosine_table, sine_table):
    window = probe_field.shape[1]

    def cutout(start):
        return lax.dynamic_slice_in_dim(field, start, window, 0)

    patches = jax.vmap(cutout)(starts)
    object_re = patches[:, :, 0, :]
    object_im = patches[:, :, 1, :]
    probe_re = probe_field[0]
    probe_im = probe_field[1]
    wave_re = probe_re * object_re - probe_im * object_im
    wave_im = probe_re * object_im + probe_im * object_re
    far_re, far_im = transform(wave_re, wave_im, cosine_table, sine_table, 1.0)
    modulus = jnp.sqrt(far_re * far_re + far_im * far_im)
    shrink = 1.0 - jnp.sqrt(intensity) / jnp.maximum(modulus, 1.0)
    back_re, back_im = transform(far_re * shrink, far_im * shrink, cosine_table, sine_table, -1.0)
    grad_re = probe_re * back_re + probe_im * back_im
    grad_im = probe_re * back_im - probe_im * back_re
    frame_grads = jnp.stack([grad_re, grad_im], axis=2)

    def deposit(index, total):
        piece = lax.dynamic_slice_in_dim(total, starts[index], window, 0)
        return lax.dynamic_update_slice_in_dim(total, piece + frame_grads[index], starts[index], 0)

    return lax.fori_loop(0, starts.shape[0], deposit, jnp.zeros(field.shape, jnp.float32))


def body(
    measured, positions, probe_field, object_field, dual_field, volume, radon_tiles, tile_range
):
    angles = lax.axis_size("ang")
    range_ids = jnp.arange(NR, dtype=jnp.int32)
    hit_offsets = jnp.arange(HITS, dtype=jnp.int32)
    targets_flat = (tile_range.reshape(angles * PT_DEV, 1) + hit_offsets[None, :]).reshape(
        angles * PT_DEV * HITS
    )
    cosine_table, sine_table = dft_tables(PROBE)
    gathered = gathered_copies(object_field, "strip", 1)
    full_grad = intersection_gradient(
        measured[0], positions[0], gathered[0], probe_field, cosine_table, sine_table
    )
    intersection = sent_and_summed(full_grad[None], "strip", 1)
    volume_half = volume.astype(jnp.bfloat16).reshape(PT_DEV, TILE, 2 * NZ)
    partials = jnp.einsum(
        "pahrt,ptc->aphrc", radon_tiles, volume_half, preferred_element_type=jnp.float32
    )
    received = lax.all_to_all(partials, "ang", split_axis=0, concat_axis=0, tiled=True)
    selector = (range_ids[:, None] == targets_flat[None, :]).astype(jnp.float32)
    dense_rows = jnp.dot(
        selector, received.reshape(angles * PT_DEV * HITS, RAYS * 2 * NZ), precision=precise
    )
    projection = sent_and_summed(dense_rows.reshape(1, NDET, 2, NZ), "strip", 1)
    object_next = object_field - object_step * (
        intersection + dual_field + penalty * (object_field - projection)
    )
    dual_next = dual_field + penalty * (object_next - projection)
    residual = (penalty * (projection - object_next) - dual_field).astype(jnp.bfloat16)
    gathered_rows = gathered_copies(residual, "strip", 1)
    pick_table = (targets_flat[:, None] == range_ids[None, :]).astype(jnp.bfloat16)
    picked = jnp.dot(
        pick_table, gathered_rows.reshape(NR, RAYS * 2 * NZ), preferred_element_type=jnp.float32
    ).astype(jnp.bfloat16)
    picked = picked.reshape(angles, PT_DEV, HITS, RAYS, 2 * NZ)
    returned = lax.all_to_all(picked, "ang", split_axis=0, concat_axis=0, tiled=True)
    gradient = jnp.einsum(
        "pahrt,aphrc->ptc", radon_tiles, returned, preferred_element_type=jnp.float32
    )
    volume_next = volume - volume_step * gradient.reshape(volume.shape)
    return (object_next, dual_next, volume_next)


def solution(mesh):
    return jax.shard_map(
        body,
        mesh=mesh,
        in_specs=(
            P("ang", "strip", None, None),
            P("ang", "strip"),
            P(),
            P("ang", "strip", None, None),
            P("ang", "strip", None, None),
            P(("ang", "strip"), None, None),
            P(("ang", "strip"), None, None, None, None),
            P("ang", None, "strip", None),
        ),
        out_specs=(
            P("ang", "strip", None, None),
            P("ang", "strip", None, None),
            P(("ang", "strip"), None, None),
        ),
        check_vma=False,
    )
```

profile of v0, /device:TPU:1, one launch (start us, length us, event | category | flops | bytes accessed | tf_op | source)
XLA Modules:
  0.0 203.0 jit_solution(5320532255179098033)
XLA Ops:
  0.7 1.9 broadcast_in_dim.7
  2.5 11.6 %all-to-all-start = ((f32[8,1,64,2,128]{4,3,2,1,0:T(2,128)}), f32[8,1,64,2,128]{4,3,2,1,0:T(2,128)S(1)}, u32[]{:S(2)}, u32[]{:S(2)}) async-start(f32[8,1,64,2,128]{4,3,2,1,0:T(2,128)} %broadcast_in_dim.7), calls=%async_computation | async-start | bytes 1048576 | tf_op jit(solution)/shard_map/all_to_all | solution.py:32
  15.4 1.8 convolution_bitcast_fusion
  17.2 8.6 %all-to-all-done = f32[8,1,64,2,128]{4,3,2,1,0:T(2,128)S(1)} async-done(((f32[8,1,64,2,128]{4,3,2,1,0:T(2,128)}), f32[8,1,64,2,128]{4,3,2,1,0:T(2,128)S(1)}, u32[]{:S(2)}, u32[]{:S(2)}) %all-to-all-start) | async-done | bytes 524320 | tf_op jit(solution)/shard_map/all_to_all | solution.py:32
  26.5 13.6 %all-to-all-start.2 = ((f32[32,1,2,32,256]{4,3,2,1,0:T(8,128)}), f32[32,1,2,32,256]{4,3,2,1,0:T(8,128)S(1)}, u32[]{:S(2)}, u32[]{:S(2)}) async-start(f32[32,1,2,32,256]{4,3,2,1,0:T(8,128)} %convolution_bitcast_fusion), calls=%async_computation.2 | async-start | bytes 4194304 | tf_op jit(solution)/shard_map/all_to_all | solution.py:122
  40.2 3.6 %gather_fusion = f32[8,128,2,128]{3,2,1,0:T(2,128)} fusion(f32[512,2,128]{2,1,0:T(2,128)} %bitcast.182, s32[8]{0:T(128)S(1)} %fusion.61), kind=kCustom, calls=%fused_computation | custom fusion | bytes 2097248 | tf_op jit(solution)/shard_map/vmap()/gather | solution.py:79
  43.8 2.6 %fusion.143 = (f32[8,128,1,128]{3,2,1,0:T(1,128)S(1)}, f32[8,128,1,128]{3,2,1,0:T(1,128)S(1)}) fusion(f32[8,128,2,128]{3,2,1,0:T(2,128)} %gather_fusion), kind=kLoop, calls=%fused_computation.177 | loop fusion | bytes 2097152 | tf_op jit(solution)/shard_map/slice | solution.py:82
  46.4 1.2 fusion.19
  47.6 1.2 fusion.20
  48.8 1.2 fusion.9
  51.2 1.2 fusion.8
  54.7 1.5 fusion.16
  67.3 41.2 %while.13 = (s32[]{:T(128)}, f32[512,2,128]{2,1,0:T(2,128)}, s32[8]{0:T(128)S(1)}, f32[8,128,2,128]{3,1,0,2:T(8,128)}, s32[]{:T(128)}, /*index=5*/s32[]{:T(128)}, s32[]{:T(128)}) while((s32[]{:T(128)}, f32[512,2,128]{2,1,0:T(2,128)}, s32[8]{0:T(128)S(1)}, f32[8,128,2,128]{3,1,0,2:T(8,128)}, s32[]{:T(128)}, /*index=5*/s32[]{:T(128)}, ...), condition=%wide.region_1.2_spmd, body=%wide.region_0.1_spmd.sunk | while | flops 32773 | bytes 655499 | solution.py:100
  70.8 1.7 fusion.162
  75.9 1.7 fusion.162
  81.1 1.7 fusion.162
  86.2 1.7 fusion.162
  91.4 1.7 fusion.162
  96.5 1.7 fusion.162
  101.7 1.7 fusion.162
  106.8 1.7 fusion.162
  108.5 4.4 %all-to-all-start.1 = ((f32[8,1,64,2,128]{4,3,2,1,0:T(2,128)}), f32[8,1,64,2,128]{4,3,2,1,0:T(2,128)}, u32[]{:S(2)}, u32[]{:S(2)}) async-start(f32[8,1,64,2,128]{4,3,2,1,0:T(2,128)} %bitcast.181), calls=%async_computation.1 | async-start | bytes 1048576 | tf_op jit(solution)/shard_map/all_to_all | solution.py:47
  113.1 1.2 copy.101
  115.1 1.2 transpose_reshape_reshape.3
  116.3 9.0 %all-to-all-done.1 = f32[8,1,64,2,128]{4,3,2,1,0:T(2,128)} async-done(((f32[8,1,64,2,128]{4,3,2,1,0:T(2,128)}), f32[8,1,64,2,128]{4,3,2,1,0:T(2,128)}, u32[]{:S(2)}, u32[]{:S(2)}) %all-to-all-start.1) | async-done | bytes 524320 | tf_op jit(solution)/shard_map/all_to_all | solution.py:47
  125.3 4.3 %all-to-all-start.3 = ((f32[8,1,64,2,128]{4,3,2,1,0:T(2,128)}), f32[8,1,64,2,128]{4,3,2,1,0:T(2,128)S(1)}, u32[]{:S(2)}, u32[]{:S(2)}) async-start(f32[8,1,64,2,128]{4,3,2,1,0:T(2,128)} %bitcast.28), calls=%async_computation.3 | async-start | bytes 1048576 | tf_op jit(solution)/shard_map/all_to_all | solution.py:47
  129.6 1.2 reduce_sum.22
  130.8 10.3 %all-to-all-done.3 = f32[8,1,64,2,128]{4,3,2,1,0:T(2,128)S(1)} async-done(((f32[8,1,64,2,128]{4,3,2,1,0:T(2,128)}), f32[8,1,64,2,128]{4,3,2,1,0:T(2,128)S(1)}, u32[]{:S(2)}, u32[]{:S(2)}) %all-to-all-start.3) | async-done | bytes 524320 | tf_op jit(solution)/shard_map/all_to_all | solution.py:47
  141.6 15.2 %all_to_all.30 = bf16[8,1,64,2,128]{4,3,2,1,0:T(2,128)(2,1)S(1)} all-to-all(bf16[8,1,64,2,128]{4,3,2,1,0:T(2,128)(2,1)S(1)} %broadcast_in_dim.8), channel_id=1, replica_groups=mesh['ang'=32,'strip'=8] {'strip'}, dimensions={0} | all-to-all | bytes 524288 | tf_op jit(solution)/shard_map/all_to_all | solution.py:32
  157.5 1.3 copy.102
  158.7 16.4 %all-to-all-start.5 = ((bf16[32,1,2,32,256]{4,3,2,1,0:T(8,128)(2,1)}), bf16[32,1,2,32,256]{4,3,2,1,0:T(8,128)(2,1)S(1)}, u32[]{:S(2)}, u32[]{:S(2)}) async-start(bf16[32,1,2,32,256]{4,3,2,1,0:T(8,128)(2,1)} %bitcast.31), calls=%async_computation.5 | async-start | bytes 2097152 | tf_op jit(solution)/shard_map/all_to_all | solution.py:139
  176.0 25.7 %all-to-all-done.5 = bf16[32,1,2,32,256]{4,3,2,1,0:T(8,128)(2,1)S(1)} async-done(((bf16[32,1,2,32,256]{4,3,2,1,0:T(8,128)(2,1)}), bf16[32,1,2,32,256]{4,3,2,1,0:T(8,128)(2,1)S(1)}, u32[]{:S(2)}, u32[]{:S(2)}) %all-to-all-start.5) | async-done | bytes 1048608 | tf_op jit(solution)/shard_map/all_to_all | solution.py:139
  (66 shorter events, 32.6 us)
Async XLA Ops:
  0.6 14.7 %copy-start = (bf16[1,32,2,32,256]{4,3,2,1,0:T(8,128)(2,1)S(1)}, bf16[1,32,2,32,256]{4,3,2,1,0:T(8,128)(2,1)}, u32[]{:S(2)}) copy-start(bf16[1,32,2,32,256]{4,3,2,1,0:T(8,128)(2,1)} %param.16) | copy-start | bytes 3145732
  0.6 14.7 %copy-start.9 = (s32[1,8]{1,0:T(1,128)S(1)}, s32[1,8]{1,0:T(1,128)}, u32[]{:S(2)}) copy-start(s32[1,8]{1,0:T(1,128)} %param.11) | copy-start | bytes 100
  0.7 14.7 %copy-start.6 = (f32[2,128,128]{2,1,0:T(8,128)S(1)}, f32[2,128,128]{2,1,0:T(8,128)}, u32[]{:S(2)}) copy-start(f32[2,128,128]{2,1,0:T(8,128)} %param.12) | copy-start | bytes 393220
  2.5 23.2 %all-to-all-start = ((f32[8,1,64,2,128]{4,3,2,1,0:T(2,128)}), f32[8,1,64,2,128]{4,3,2,1,0:T(2,128)S(1)}, u32[]{:S(2)}, u32[]{:S(2)}) async-start(f32[8,1,64,2,128]{4,3,2,1,0:T(2,128)} %broadcast_in_dim.7), calls=%async_computation | async-start | bytes 1048576 | tf_op jit(solution)/shard_map/all_to_all | solution.py:32
  25.8 0.8 copy-start.1
  26.5 82.0 %all-to-all-start.2 = ((f32[32,1,2,32,256]{4,3,2,1,0:T(8,128)}), f32[32,1,2,32,256]{4,3,2,1,0:T(8,128)S(1)}, u32[]{:S(2)}, u32[]{:S(2)}) async-start(f32[32,1,2,32,256]{4,3,2,1,0:T(8,128)} %convolution_bitcast_fusion), calls=%async_computation.2 | async-start | bytes 4194304 | tf_op jit(solution)/shard_map/all_to_all | solution.py:122
  51.1 3.5 %copy-start.8 = (f32[1,8,128,128]{3,2,1,0:T(8,128)S(1)}, f32[1,8,128,128]{3,2,1,0:T(8,128)}, u32[]{:S(2)}) copy-start(f32[1,8,128,128]{3,2,1,0:T(8,128)} %param.10) | copy-start | bytes 1572868
  67.3 45.6 %copy-start.7 = (s32[1,32,1,1]{1,3,2,0:T(1,128)S(1)}, s32[1,32,1,1]{1,3,2,0:T(1,128)}, u32[]{:S(2)}) copy-start(s32[1,32,1,1]{1,3,2,0:T(1,128)} %param.17) | copy-start | bytes 388
  108.5 16.8 %all-to-all-start.1 = ((f32[8,1,64,2,128]{4,3,2,1,0:T(2,128)}), f32[8,1,64,2,128]{4,3,2,1,0:T(2,128)}, u32[]{:S(2)}, u32[]{:S(2)}) async-start(f32[8,1,64,2,128]{4,3,2,1,0:T(2,128)} %bitcast.181), calls=%async_computation.1 | async-start | bytes 1048576 | tf_op jit(solution)/shard_map/all_to_all | solution.py:47
  115.1 26.3 %copy-start.3 = (f32[1,64,2,128]{3,2,1,0:T(2,128)S(1)}, f32[1,64,2,128]{3,2,1,0:T(2,128)}, u32[]{:S(2)}) copy-start(f32[1,64,2,128]{3,2,1,0:T(2,128)} %param.13) | copy-start | bytes 196612
  115.1 26.3 %copy-start.4 = (f32[1,64,2,128]{3,2,1,0:T(2,128)S(1)}, f32[1,64,2,128]{3,2,1,0:T(2,128)}, u32[]{:S(2)}) copy-start(f32[1,64,2,128]{3,2,1,0:T(2,128)} %param.14) | copy-start | bytes 196612
  125.3 15.8 %all-to-all-start.3 = ((f32[8,1,64,2,128]{4,3,2,1,0:T(2,128)}), f32[8,1,64,2,128]{4,3,2,1,0:T(2,128)S(1)}, u32[]{:S(2)}, u32[]{:S(2)}) async-start(f32[8,1,64,2,128]{4,3,2,1,0:T(2,128)} %bitcast.28), calls=%async_computation.3 | async-start | bytes 1048576 | tf_op jit(solution)/shard_map/all_to_all | solution.py:47
  141.5 33.8 %copy-start.5 = (f32[1,64,2,128]{3,2,1,0:T(2,128)}, f32[1,64,2,128]{3,2,1,0:T(2,128)S(1)}, u32[]{:S(2)}) copy-start(f32[1,64,2,128]{3,2,1,0:T(2,128)S(1)} %get-tuple-element.113) | copy-start | bytes 196612
  157.4 17.7 %copy-start.2 = (f32[256,2,128]{2,1,0:T(2,128)S(1)}, f32[256,2,128]{2,1,0:T(2,128)}, u32[]{:S(2)}) copy-start(f32[256,2,128]{2,1,0:T(2,128)} %param.15) | copy-start | bytes 786436
  158.7 43.0 %all-to-all-start.5 = ((bf16[32,1,2,32,256]{4,3,2,1,0:T(8,128)(2,1)}), bf16[32,1,2,32,256]{4,3,2,1,0:T(8,128)(2,1)S(1)}, u32[]{:S(2)}, u32[]{:S(2)}) async-start(bf16[32,1,2,32,256]{4,3,2,1,0:T(8,128)(2,1)} %bitcast.31), calls=%async_computation.5 | async-start | bytes 2097152 | tf_op jit(solution)/shard_map/all_to_all | solution.py:139
where the time goes:
time: 204 us; the launch traced here: 203 us
  waiting for transfers between devices  53.6 us (26%)
  starting transfers between devices  50.3 us (25%)
  local copies, waits for them, and re-layouts  27.1 us (13%)
  matrix products  22.3 us (11%)
  other arithmetic  18 us (9%)
  loops' own time  15.6 us (8%)
  blocking collectives  15.2 us (7%)
    all_to_all x1, waiting for transfers between devices, body(): lax.all_to_all(picked, 'ang', split_axis=0, concat_axis=0, tiled=True)  25.7 us
    all_to_all x2, waiting for transfers between devices, sent_and_summed(): lax.all_to_all(in_blocks(array, dim, count), axis, 0, 0, tiled=True)  19.3 us
    all_to_all x1, starting transfers between devices, body(): lax.all_to_all(picked, 'ang', split_axis=0, concat_axis=0, tiled=True)  16.4 us
    another operation x1, loops' own time, intersection_gradient(): lax.fori_loop(0, starts.shape[0], deposit, jnp.zeros(field.shape, jnp.flo...  15.6 us
    all_to_all x1, blocking collectives, sent_to_all(): return lax.all_to_all(copies, axis, split_axis=0, concat_axis=0, tiled=True)  15.2 us
    all_to_all x1, starting transfers between devices, body(): lax.all_to_all(partials, 'ang', split_axis=0, concat_axis=0, tiled=True)  13.6 us
    dynamic_update_slice x8, other arithmetic, deposit(): lax.dynamic_update_slice_in_dim(total, piece + frame_grads[index], starts...  13.6 us
    all_to_all x1, starting transfers between devices, sent_to_all(): return lax.all_to_all(copies, axis, split_axis=0, concat_axis=0, tiled=True)  11.6 us
  transfers between devices with their start and end apart: 5, of which 4 were waited for; matrix products, arithmetic and copies ran while one was open for 30% of the time, Pallas kernels for 0%

commit v1 on v0

v1 whole, which is shorter than its diff:
```python
import math

import jax
import jax.numpy as jnp
import numpy as np
from jax import lax
from jax.experimental import pallas as pl
from jax.experimental.pallas import tpu as pltpu
from jax.sharding import Mesh
from jax.sharding import PartitionSpec as P

PROBE = 128
NZ = 128
NDET = 512
RAYS = 32
TILE = 256
HITS = 2
NR = 16

ZL, X, C, ZH, Y = 4, 4, 2, 2, 4
XC = X * C
CROSS = ("x", "c", "y")
ALONG = ("zh", "zl")
NEAR = XC * Y
DEEP = ZH * ZL
QR = RAYS // Y
FR_DEV = 8

penalty = 1.0
object_step = 0.1
volume_step = 1.0
f32 = jnp.float32
bf16 = jnp.bfloat16

VM = pl.BlockSpec(memory_space=pltpu.VMEM)
SM = pl.BlockSpec(memory_space=pltpu.SMEM)


def call(kernel, outs, n_smem, n_vmem, scratch=(), flops=0, moved=1 << 20, limit=48 << 20):
    many = isinstance(outs, tuple)
    return pl.pallas_call(
        kernel,
        out_shape=outs,
        in_specs=[SM] * n_smem + [VM] * n_vmem,
        out_specs=tuple(VM for _ in outs) if many else VM,
        scratch_shapes=list(scratch),
        compiler_params=pltpu.CompilerParams(vmem_limit_bytes=limit),
        cost_estimate=pl.CostEstimate(flops=flops, bytes_accessed=moved, transcendentals=0),
        name=kernel.__name__,
    )


def shape(*dims, dtype=f32):
    return jax.ShapeDtypeStruct(dims, dtype)


def dft_blocks():
    k = np.arange(PROBE)
    angles = (k[:, None] * k[None, :] % PROBE) * (2.0 * math.pi / PROBE)
    cosine = np.cos(angles) / math.sqrt(PROBE)
    sine = np.sin(angles) / math.sqrt(PROBE)
    left = np.block([[cosine, sine], [-sine, cosine]]).astype(np.float32)
    high = left.astype(jnp.bfloat16)
    low = (left - high.astype(np.float32)).astype(jnp.bfloat16)
    return jnp.asarray(high), jnp.asarray(low), jnp.asarray(high.T.copy()), jnp.asarray(low.T.copy())


def ray_sums(radon_ref, volume_ref, out_ref):
    volume_half = jnp.concatenate(
        [volume_ref[pl.ds(0, TILE, stride=2), :], volume_ref[pl.ds(1, TILE, stride=2), :]], axis=1
    ).astype(bf16)
    for zl in range(ZL):
        for xc in range(XC):
            rows = radon_ref[zl * XC + xc].reshape(HITS * RAYS, TILE)
            sums = jnp.dot(rows, volume_half, preferred_element_type=f32)
            for y in range(Y):
                low = sums[y * QR : (y + 1) * QR]
                high = sums[RAYS + y * QR : RAYS + (y + 1) * QR]
                out_ref[xc * Y + y, zl] = jnp.concatenate([low, high], axis=0).astype(bf16)


def add_tiles(target_ref, sums_ref, out_ref, total):
    total[...] = jnp.zeros(total.shape, f32)

    def step(source, carry):
        for zl in range(ZL):
            row = pl.multiple_of(target_ref[zl, source] * QR, QR)
            total[zl, pl.ds(row, HITS * QR), :] += sums_ref[source, zl].astype(f32)
        return carry

    lax.fori_loop(0, NEAR, step, 0, unroll=4)
    for zh in range(ZH):
        for zl in range(ZL):
            out_ref[zh * ZL + zl] = total[zl, :, zh * NZ : (zh + 1) * NZ].astype(bf16)


def residual_part(sums_ref, inter_ref, drift_ref, residual_ref, keep_ref):
    projection = sums_ref[0].astype(f32)
    for source in range(1, DEEP):
        projection = projection + sums_ref[source].astype(f32)
    inter = inter_ref[...]
    gap = projection - drift_ref[...]
    residual_ref[...] = (gap + object_step * (inter - gap)).astype(bf16)
    keep_ref[0] = projection
    keep_ref[1] = inter


def pick_tiles(target_ref, residual_ref, out_ref, rows_ref):
    for zl in range(ZL):
        rows_ref[zl] = jnp.concatenate(
            [residual_ref[zl].astype(f32), residual_ref[ZL + zl].astype(f32)], axis=1
        )

    def step(dest, carry):
        for zl in range(ZL):
            row = pl.multiple_of(target_ref[zl, dest] * QR, QR)
            out_ref[dest, zl] = rows_ref[zl, pl.ds(row, HITS * QR), :].astype(bf16)
        return carry

    lax.fori_loop(0, NEAR, step, 0, unroll=4)


def back_project(radon_ref, picked_ref, volume_ref, out_ref):
    gradient = jnp.dot(
        radon_ref[...],
        picked_ref[...].reshape(NEAR * ZL * HITS * QR, 2 * NZ),
        preferred_element_type=f32,
    )
    for part in range(2):
        rows = pl.ds(part, TILE, stride=2)
        out_ref[rows, :] = volume_ref[rows, :] - volume_step * gradient[:, part * NZ : (part + 1) * NZ]


def updates(place_ref, kept_ref, object_ref, dual_ref, object_out, dual_out):
    zh = place_ref[0]
    y = place_ref[1]
    for other in range(ZH):
        part = lax.rem(zh + other, ZH)
        for back in range(Y):
            source = lax.rem(y + Y - back, Y)
            for tile in range(2):
                rows = pl.ds((tile * RAYS + source * QR) * 2 + part, QR, stride=2)
                projection = kept_ref[other, back, 0, tile * QR : (tile + 1) * QR, :]
                inter = kept_ref[other, back, 1, tile * QR : (tile + 1) * QR, :]
                field = object_ref[rows, :]
                dual = dual_ref[rows, :]
                object_next = field - object_step * (inter + dual + penalty * (field - projection))
                object_out[rows, :] = object_next
                dual_out[rows, :] = dual + penalty * (object_next - projection)


def split(value):
    high = value.astype(bf16)
    return high, (value - high.astype(f32)).astype(bf16)


def from_left(high_table, low_table, value):
    high, low = split(value)
    return (
        jnp.dot(high_table, high, preferred_element_type=f32)
        + jnp.dot(high_table, low, preferred_element_type=f32)
        + jnp.dot(low_table, high, preferred_element_type=f32)
    )


def from_right(value, high_table, low_table):
    high, low = split(value)
    return (
        jnp.dot(high, high_table, preferred_element_type=f32)
        + jnp.dot(low, high_table, preferred_element_type=f32)
        + jnp.dot(high, low_table, preferred_element_type=f32)
    )


def frame_gradients(
    place_ref, starts_ref, field_ref, probe_ref, measured_ref, ah_ref, al_ref, bh_ref, bl_ref,
    own_ref, sent_ref, field_re, field_im, total_re, total_im, staged,
):
    zh = place_ref[0]
    y = place_ref[1]
    for back in range(Y):
        for other in range(ZH):
            owner = lax.rem(zh + other, ZH) * Y + lax.rem(y + Y - back, Y)
            rows = pl.ds(pl.multiple_of(owner * 64, 64), 64)
            staged[...] = field_ref[back, other]
            field_re[rows, :] = staged[pl.ds(0, 64, stride=2), :]
            field_im[rows, :] = staged[pl.ds(1, 64, stride=2), :]
    total_re[...] = jnp.zeros(total_re.shape, f32)
    total_im[...] = jnp.zeros(total_im.shape, f32)
    probe_re = probe_ref[0]
    probe_im = probe_ref[1]
    ah, al, bh, bl = ah_ref[...], al_ref[...], bh_ref[...], bl_ref[...]
    for pair in range(FR_DEV // 2):
        waves = []
        for frame in (2 * pair, 2 * pair + 1):
            rows = pl.ds(starts_ref[0, frame], PROBE)
            object_re = field_re[rows, :]
            object_im = field_im[rows, :]
            waves.append(
                jnp.concatenate(
                    [
                        probe_re * object_re - probe_im * object_im,
                        probe_re * object_im + probe_im * object_re,
                    ],
                    axis=0,
                )
            )
        lefts = from_left(ah, al, jnp.concatenate(waves, axis=1))
        sides = jnp.concatenate(
            [
                jnp.concatenate([lefts[:PROBE, i * NZ : (i + 1) * NZ], lefts[PROBE:, i * NZ : (i + 1) * NZ]], axis=1)
                for i in range(2)
            ],
            axis=0,
        )
        far = from_right(sides, bh, bl)
        far_re = far[:, :NZ]
        far_im = far[:, NZ:]
        modulus = jnp.sqrt(far_re * far_re + far_im * far_im)
        intensity = measured_ref[2 * pair : 2 * pair + 2].reshape(2 * PROBE, NZ)
        shrink = 1.0 - jnp.sqrt(intensity) / jnp.maximum(modulus, 1.0)
        diff = jnp.concatenate([far_re * shrink, far_im * shrink], axis=1)
        half = from_right(diff, ah, al)
        stacked = jnp.concatenate(
            [
                jnp.concatenate([half[i * PROBE : (i + 1) * PROBE, :NZ], half[i * PROBE : (i + 1) * PROBE, NZ:]], axis=0)
                for i in range(2)
            ],
            axis=1,
        )
        backs = from_left(bh, bl, stacked)
        for i in range(2):
            back_re = backs[:PROBE, i * NZ : (i + 1) * NZ]
            back_im = backs[PROBE:, i * NZ : (i + 1) * NZ]
            rows = pl.ds(starts_ref[0, 2 * pair + i], PROBE)
            total_re[rows, :] += probe_re * back_re + probe_im * back_im
            total_im[rows, :] += probe_re * back_im - probe_im * back_re
    for ahead in range(Y):
        owner = lax.rem(y + ahead, Y)
        for tile in range(0, NR, 2):
            low = pl.ds(pl.multiple_of(tile * RAYS + owner * QR, QR), QR)
            high = pl.ds(pl.multiple_of((tile + 1) * RAYS + owner * QR, QR), QR)
            rows = slice(tile * QR, (tile + 2) * QR)
            for part, total in enumerate((total_re, total_im)):
                piece = jnp.concatenate([total[low, :], total[high, :]], axis=0)
                if ahead == 0:
                    own_ref[part, rows, :] = piece
                else:
                    sent_ref[ahead - 1, part, rows, :] = piece.astype(bf16)


def shifted(value, axis, length, step):
    return lax.ppermute(value, axis, [(i, (i + step) % length) for i in range(length)])


def across(value):
    return shifted(value, "zh", ZH, 1)


def round_y(pieces):
    return [pieces[0]] + [shifted(pieces[k], "y", Y, k) for k in range(1, Y)]


def body(measured, positions, probe_field, object_field, dual_field, volume, radon_tiles, tile_range):
    zh = lax.axis_index("zh")
    zl = lax.axis_index("zl")
    y = lax.axis_index("y")
    place = jnp.stack([zh, y]).astype(jnp.int32)
    order = (y + jnp.arange(Y)) % Y
    back_order = (y - jnp.arange(Y)) % Y
    ah, al, bh, bl = dft_blocks()
    radon = radon_tiles.reshape(ZL * XC, HITS, RAYS, TILE)
    volume_rows = volume.reshape(2 * TILE, NZ)
    object_rows = object_field.reshape(128, NZ)
    dual_rows = dual_field.reshape(128, NZ)

    with jax.named_scope("ray_sums"):
        sums = call(ray_sums, shape(NEAR, ZL, HITS * QR, 2 * NZ, dtype=bf16), 0, 2, flops=2 * 2048 * 256 * 256)(
            radon, volume_rows
        )
        near_sums = lax.all_to_all(sums, CROSS, 0, 0, tiled=True)

    with jax.named_scope("fields"):
        pair = jnp.stack([object_rows, across(object_rows)])
        fields = jnp.stack(round_y([pair] * Y))

    with jax.named_scope("targets"):
        own_targets = tile_range.reshape(ZL, XC)
        ahead = [lax.dynamic_index_in_dim(own_targets, (zl + k) % ZL, 0, keepdims=False) for k in range(ZL)]
        rounds = [ahead[0]] + [shifted(ahead[k], "zl", ZL, k) for k in range(1, ZL)]
        targets = jnp.stack(rounds)
        targets = jnp.stack(round_y([targets] * Y))
        targets = jnp.take(jnp.take(targets, back_order, axis=0), (zl - jnp.arange(ZL)) % ZL, axis=1)
        targets = targets.transpose(1, 2, 0).reshape(ZL, NEAR)

    with jax.named_scope("drift"):
        drift = (object_field + dual_field).reshape(2, Y, QR, 2, NZ)
        drift = jnp.take(drift.transpose(1, 3, 0, 2, 4).reshape(Y, 2, 2 * QR, NZ), order, axis=0)
        drift = jnp.stack(round_y([drift[k] for k in range(Y)]))
        mine = lax.dynamic_index_in_dim(drift, zh, 1, keepdims=False)
        theirs = across(lax.dynamic_index_in_dim(drift, 1 - zh, 1, keepdims=False))
        both = jnp.where(zh == 0, jnp.stack([mine, theirs]), jnp.stack([theirs, mine]))
        drift_part = jnp.take(both, back_order, axis=1).reshape(128, NZ)

    with jax.named_scope("frames"):
        inter_own, inter_others = call(
            frame_gradients,
            (shape(2, 128, NZ), shape(Y - 1, 2, 128, NZ, dtype=bf16)),
            2,
            7,
            scratch=[pltpu.VMEM((NDET, NZ), f32)] * 4 + [pltpu.VMEM((128, NZ), f32)],
            flops=1_600_000_000,
        )(place, positions, fields, probe_field, measured[0], ah, al, bh, bl)
        arrived = round_y([inter_own] + [inter_others[k] for k in range(Y - 1)])
        inter_sum = sum(piece.astype(f32) for piece in arrived)
        inter_mine = lax.dynamic_index_in_dim(inter_sum, zh, 0, keepdims=False)
        inter_sent = lax.dynamic_index_in_dim(inter_sum, 1 - zh, 0, keepdims=False)
        inter = inter_mine + across(inter_sent)

    with jax.named_scope("near_sum"):
        dense = call(
            add_tiles,
            shape(DEEP, 128, NZ, dtype=bf16),
            1,
            1,
            scratch=[pltpu.VMEM((ZL, 128, 2 * NZ), f32)],
            flops=1_000_000,
        )(targets, near_sums)
        far_sums = lax.all_to_all(dense, ALONG, 0, 0, tiled=True)

    with jax.named_scope("residual"):
        residual, kept = call(
            residual_part, (shape(128, NZ, dtype=bf16), shape(2, 128, NZ)), 0, 3, flops=1_000_000
        )(far_sums, inter, drift_part)
        copies = jnp.broadcast_to(residual, (DEEP, 128, NZ))
        residuals = lax.all_to_all(copies, ALONG, 0, 0, tiled=True)

    with jax.named_scope("pick"):
        picked = call(
            pick_tiles,
            shape(NEAR, ZL, HITS * QR, 2 * NZ, dtype=bf16),
            1,
            1,
            scratch=[pltpu.VMEM((ZL, 128, 2 * NZ), f32)],
            flops=1_000_000,
        )(targets, residuals)
        returned = lax.all_to_all(picked, CROSS, 0, 0, tiled=True)

    with jax.named_scope("updates"):
        kept = jnp.take(kept.reshape(2, ZH, Y, 2 * QR, NZ).transpose(2, 1, 0, 3, 4), order, axis=0)
        kept = jnp.stack(round_y([kept[k] for k in range(Y)]))
        mine = lax.dynamic_index_in_dim(kept, zh, 1, keepdims=False)
        theirs = across(lax.dynamic_index_in_dim(kept, 1 - zh, 1, keepdims=False))
        object_next, dual_next = call(updates, (shape(128, NZ), shape(128, NZ)), 1, 3, flops=1_000_000)(
            place, jnp.stack([mine, theirs]), object_rows, dual_rows
        )

    with jax.named_scope("back_project"):
        ordered = radon.reshape(ZL, XC, HITS, Y, QR, TILE).transpose(5, 1, 3, 0, 2, 4).reshape(TILE, -1)
        volume_next = call(back_project, shape(2 * TILE, NZ), 0, 3, flops=2 * 2048 * 256 * 256)(
            ordered, returned, volume_rows
        )
    return (
        object_next.reshape(object_field.shape),
        dual_next.reshape(dual_field.shape),
        volume_next.reshape(volume.shape),
    )


def solution(mesh):
    fine = Mesh(mesh.devices.reshape(ZL, X, C, ZH, Y), ("zl", "x", "c", "zh", "y"))
    ang = ("zl", "x", "c")
    strip = ("zh", "y")
    return jax.shard_map(
        body,
        mesh=fine,
        in_specs=(
            P(ang, strip, None, None),
            P(ang, strip),
            P(),
            P(ang, strip, None, None),
            P(ang, strip, None, None),
            P(ang + strip, None, None),
            P(ang + strip, None, None, None, None),
            P(ang, None, strip, None),
        ),
        out_specs=(
            P(ang, strip, None, None),
            P(ang, strip, None, None),
            P(ang + strip, None, None),
        ),
        check_vma=False,
    )
```

time: 204 us -> 145 us (0.71)
  the two profiles are of different devices: /device:TPU:1 before, /device:TPU:2 now
where the time goes in v1:
time: 145 us; the launch traced here: 144 us
  starting transfers between devices  63.4 us (44%)
  waiting for transfers between devices  42.3 us (29%)
  blocking collectives  14.8 us (10%)
  Pallas kernels  12.7 us (9%)
  local copies, waits for them, and re-layouts  7.71 us (5%)
  other arithmetic  2.23 us (2%)
    ppermute x22, starting transfers between devices, shifted(): lax.ppermute(value, axis, [(i, (i + step) % length) for i in range(length)])  44.2 us
    ppermute x22, waiting for transfers between devices, shifted(): lax.ppermute(value, axis, [(i, (i + step) % length) for i in range(length)])  42.3 us
    all_to_all x1, blocking collectives, body(): residuals = lax.all_to_all(copies, ALONG, 0, 0, tiled=True)  14.8 us
    all_to_all x1, starting transfers between devices, body(): near_sums = lax.all_to_all(sums, CROSS, 0, 0, tiled=True)  7.33 us
    all_to_all x1, starting transfers between devices, body(): returned = lax.all_to_all(picked, CROSS, 0, 0, tiled=True)  7.06 us
    all_to_all x1, starting transfers between devices, body(): far_sums = lax.all_to_all(dense, ALONG, 0, 0, tiled=True)  4.8 us
    pallas_call x1, Pallas kernels, body(): call(frame_gradients, (shape(2, 128, NZ), shape(Y - 1, 2, 128, NZ, dtype=...  4.64 us
    unnamed x27, local copies, waits for them, and re-layouts  2.92 us
  transfers between devices with their start and end apart: 25, of which 9 were waited for; matrix products, arithmetic and copies ran while one was open for 4% of the time, Pallas kernels for 5%

profile of v1, /device:TPU:2, one launch (start us, length us, event | category | flops | bytes accessed | tf_op | source)
XLA Modules:
  0.0 144.3 jit_solution(5899751765524930213)
XLA Ops:
  2.1 4.7 %collective-permute-start.2 = (s32[8]{0:T(128)S(1)}, s32[8]{0:T(128)S(1)}, u32[]{:S(2)}, u32[]{:S(2)}) collective-permute-start(s32[8]{0:T(128)S(1)} %get-tuple-element.35), channel_id=1, source_target_pairs={{0,192},{64,0},{128,64},{192,128},{1,193},{65,1},{129,65},{193,129... | collective-permute-start | bytes 104 | tf_op jit(solution)/shard_map/targets/ppermute | solution.py:253
  8.2 3.1 %collective-permute-start.16 = (f32[2,16,128]{2,1,0:T(8,128)S(1)}, f32[2,16,128]{2,1,0:T(8,128)S(1)}, u32[]{:S(2)}, u32[]{:S(2)}) collective-permute-start(f32[2,16,128]{2,1,0:T(8,128)S(1)} %get-tuple-element.29), channel_id=1, source_target_pairs={{0,3},{1,0},{2,1},{3,2},{4,7},{5,4},{6,5},{7,6},{8,11},{9,8},{10,9... | collective-permute-start | bytes 49160 | tf_op jit(solution)/shard_map/drift/ppermute | solution.py:253
  11.9 1.2 copy-done
  13.1 1.8 %ray_sums.1 = bf16[32,4,16,256]{3,2,1,0:T(8,128)(2,1)} custom-call(bf16[32,2,32,256]{3,2,1,0:T(8,128)(2,1)S(1)} %bitcast.95, f32[512,128]{1,0:T(8,128)S(1)} %bitcast.97), custom_call_target="tpu_custom_call" | custom-call | flops 268435456 | bytes 1048576 | tf_op jit(solution)/shard_map/ray_sums/ray_sums/pallas_call | solution.py:278
  15.0 7.3 %all-to-all-start = ((bf16[32,4,16,256]{3,2,1,0:T(8,128)(2,1)}), bf16[32,4,16,256]{3,2,1,0:T(8,128)(2,1)S(1)}, u32[]{:S(2)}, u32[]{:S(2)}) async-start(bf16[32,4,16,256]{3,2,1,0:T(8,128)(2,1)} %ray_sums.1), calls=%async_computation | async-start | bytes 2097152 | tf_op jit(solution)/shard_map/ray_sums/all_to_all | solution.py:281
  22.6 1.5 %collective-permute-start.14 = (f32[2,16,128]{2,1,0:T(8,128)S(1)}, f32[2,16,128]{2,1,0:T(8,128)S(1)}, u32[]{:S(2)}, u32[]{:S(2)}) collective-permute-start(f32[2,16,128]{2,1,0:T(8,128)S(1)} %get-tuple-element.31), channel_id=1, source_target_pairs={{0,1},{1,2},{2,3},{3,0},{4,5},{5,6},{6,7},{7,4},{8,9},{9,10},{10,1... | collective-permute-start | bytes 49160 | tf_op jit(solution)/shard_map/drift/ppermute | solution.py:253
  24.1 2.8 %collective-permute-start.4 = (s32[4,8]{1,0:T(4,128)S(1)}, s32[4,8]{1,0:T(4,128)S(1)}, u32[]{:S(2)}, u32[]{:S(2)}) collective-permute-start(s32[4,8]{1,0:T(4,128)S(1)} %get-tuple-element.33), channel_id=1, source_target_pairs={{0,2},{1,3},{2,0},{3,1},{4,6},{5,7},{6,4},{7,5},{8,10},{9,11},{10,... | collective-permute-start | bytes 392 | tf_op jit(solution)/shard_map/targets/ppermute | solution.py:253
  26.9 11.2 %collective-permute-done.4 = s32[4,8]{1,0:T(4,128)S(1)} collective-permute-done((s32[4,8]{1,0:T(4,128)S(1)}, s32[4,8]{1,0:T(4,128)S(1)}, u32[]{:S(2)}, u32[]{:S(2)}) %collective-permute-start.4) | collective-permute-done | bytes 160 | tf_op jit(solution)/shard_map/targets/ppermute | solution.py:253
  38.8 5.4 %collective-permute-start.6 = (f32[128,128]{1,0:T(8,128)S(1)}, f32[128,128]{1,0:T(8,128)S(1)}, u32[]{:S(2)}, u32[]{:S(2)}) collective-permute-start(f32[128,128]{1,0:T(8,128)S(1)} %bitcast.99), channel_id=1, source_target_pairs={{0,4},{4,0},{1,5},{5,1},{2,6},{6,2},{3,7},{7,3},{8,12},{12,8},{9,1... | collective-permute-start | bytes 196616 | tf_op jit(solution)/shard_map/fields/ppermute | solution.py:253
  45.7 1.4 collective-permute-done.6
  47.1 1.6 %collective-permute-start.8 = (f32[2,128,128]{2,1,0:T(8,128)S(1)}, f32[2,128,128]{2,1,0:T(8,128)S(1)}, u32[]{:S(2)}, u32[]{:S(2)}) collective-permute-start(f32[2,128,128]{2,1,0:T(8,128)S(1)} %get-tuple-element.25), channel_id=1, source_target_pairs={{0,2},{1,3},{2,0},{3,1},{4,6},{5,7},{6,4},{7,5},{8,10},{9,11},{10,... | collective-permute-start | bytes 393224 | tf_op jit(solution)/shard_map/fields/ppermute | solution.py:253
  48.7 3.2 %collective-permute-start.9 = (f32[2,128,128]{2,1,0:T(8,128)S(1)}, f32[2,128,128]{2,1,0:T(8,128)S(1)}, u32[]{:S(2)}, u32[]{:S(2)}) collective-permute-start(f32[2,128,128]{2,1,0:T(8,128)S(1)} %get-tuple-element.25), channel_id=1, source_target_pairs={{0,3},{1,0},{2,1},{3,2},{4,7},{5,4},{6,5},{7,6},{8,11},{9,8},{10,9... | collective-permute-start | bytes 393224 | tf_op jit(solution)/shard_map/fields/ppermute | solution.py:253
  52.0 5.7 %collective-permute-start.17 = (f32[4,16,128]{2,1,0:T(8,128)S(1)}, f32[4,16,128]{2,1,0:T(8,128)S(1)}, u32[]{:S(2)}, u32[]{:S(2)}) collective-permute-start(f32[4,16,128]{2,1,0:T(8,128)S(1)} %get-tuple-element.27), channel_id=1, source_target_pairs={{0,4},{4,0},{1,5},{5,1},{2,6},{6,2},{3,7},{7,3},{8,12},{12,8},{9,1... | collective-permute-start | bytes 98312 | tf_op jit(solution)/shard_map/drift/ppermute | solution.py:253
  57.8 0.9 copy-done.5
  58.8 4.6 %frame_gradients.1 = (f32[2,128,128]{2,1,0:T(8,128)S(1)}, bf16[3,2,128,128]{3,2,1,0:T(8,128)(2,1)S(1)}) custom-call(s32[2]{0:T(128)S(1)} %pad_add_fusion.2.place_ref, s32[1,8]{1,0:T(1,128)S(1)} %copy-done.7, f32[4,2,128,128]{3,2,1,0:T(8,128)S(1)} %pad_maximum_fusion.field_ref, f32[2,128,128]{2,1,0:T(8,128)S(1)} %copy-done.6, f32[8,128,128]{2,1,0:T(8,128)S(1)} %bitcast.104, ...), custom_call_target="tpu_custom_call" | custom-call | flops 1600000000 | bytes 1048576 | tf_op jit(solution)/shard_map/frames/frame_gradients/pallas_call | solution.py:306
  63.6 3.2 %collective-permute-start.12 = (bf16[2,128,128]{2,1,0:T(8,128)(2,1)S(1)}, bf16[2,128,128]{2,1,0:T(8,128)(2,1)S(1)}, u32[]{:S(2)}, u32[]{:S(2)}) collective-permute-start(bf16[2,128,128]{2,1,0:T(8,128)(2,1)S(1)} %get-tuple-element.16), channel_id=1, source_target_pairs={{0,3},{1,0},{2,1},{3,2},{4,7},{5,4},{6,5},{7,6},{8,11},{9,8},{10,9... | collective-permute-start | bytes 196616 | tf_op jit(solution)/shard_map/frames/ppermute | solution.py:253
  67.4 1.8 %collective-permute-done.10 = bf16[2,128,128]{2,1,0:T(8,128)(2,1)S(1)} collective-permute-done((bf16[2,128,128]{2,1,0:T(8,128)(2,1)S(1)}, bf16[2,128,128]{2,1,0:T(8,128)(2,1)S(1)}, u32[]{:S(2)}, u32[]{:S(2)}) %collective-permute-start.10) | collective-permute-done | bytes 65568 | tf_op jit(solution)/shard_map/frames/ppermute | solution.py:253
  69.2 3.4 %collective-permute-done.11 = bf16[2,128,128]{2,1,0:T(8,128)(2,1)S(1)} collective-permute-done((bf16[2,128,128]{2,1,0:T(8,128)(2,1)S(1)}, bf16[2,128,128]{2,1,0:T(8,128)(2,1)S(1)}, u32[]{:S(2)}, u32[]{:S(2)}) %collective-permute-start.11) | collective-permute-done | bytes 65568 | tf_op jit(solution)/shard_map/frames/ppermute | solution.py:253
  72.6 2.0 %add_tiles.1 = bf16[8,128,128]{2,1,0:T(8,128)(2,1)} custom-call(s32[4,32]{1,0:T(4,128)S(1)} %reshape.213.target_ref, bf16[32,4,16,256]{3,2,1,0:T(8,128)(2,1)S(1)} %all-to-all-done.sums_ref), custom_call_target="tpu_custom_call" | custom-call | flops 1000000 | bytes 1048576 | tf_op jit(solution)/shard_map/near_sum/add_tiles/pallas_call | solution.py:321
  74.6 4.8 %all-to-all-start.1 = ((bf16[8,128,128]{2,1,0:T(8,128)(2,1)}), bf16[8,128,128]{2,1,0:T(8,128)(2,1)S(1)}, u32[]{:S(2)}, u32[]{:S(2)}) async-start(bf16[8,128,128]{2,1,0:T(8,128)(2,1)} %add_tiles.1), calls=%async_computation.1 | async-start | bytes 524288 | tf_op jit(solution)/shard_map/near_sum/all_to_all | solution.py:329
  79.4 6.0 %collective-permute-start.13 = (f32[128,128]{1,0:T(8,128)S(1)}, f32[128,128]{1,0:T(8,128)S(1)}, u32[]{:S(2)}, u32[]{:S(2)}) collective-permute-start(f32[128,128]{1,0:T(8,128)S(1)} %dynamic-slice_bitcast_fusion.2), channel_id=1, source_target_pairs={{0,4},{4,0},{1,5},{5,1},{2,6},{6,2},{3,7},{7,3},{8,12},{12,8},{9,1... | collective-permute-start | bytes 196616 | tf_op jit(solution)/shard_map/frames/ppermute | solution.py:253
  85.5 5.8 %collective-permute-done.13 = f32[128,128]{1,0:T(8,128)S(1)} collective-permute-done((f32[128,128]{1,0:T(8,128)S(1)}, f32[128,128]{1,0:T(8,128)S(1)}, u32[]{:S(2)}, u32[]{:S(2)}) %collective-permute-start.13) | collective-permute-done | bytes 65568 | tf_op jit(solution)/shard_map/frames/ppermute | solution.py:253
  91.4 14.8 %all_to_all.20.residual_ref = bf16[8,128,128]{2,1,0:T(8,128)(2,1)S(1)} all-to-all(bf16[8,128,128]{2,1,0:T(8,128)(2,1)S(1)} %broadcast_in_dim.66), channel_id=1, replica_groups=mesh['zl'=4,'x'=4,'c'=2,'zh'=2,'y'=4] {'zh','zl'}, dimensions={0} | all-to-all | bytes 524288 | tf_op jit(solution)/shard_map/residual/all_to_all | solution.py:336
  106.2 1.9 %pick_tiles.1 = bf16[32,4,16,256]{3,2,1,0:T(8,128)(2,1)} custom-call(s32[4,32]{1,0:T(4,128)S(1)} %reshape.213.target_ref, bf16[8,128,128]{2,1,0:T(8,128)(2,1)S(1)} %all_to_all.20.residual_ref), custom_call_target="tpu_custom_call" | custom-call | flops 1000000 | bytes 1048576 | tf_op jit(solution)/shard_map/pick/pick_tiles/pallas_call | solution.py:339
  108.1 7.1 %all-to-all-start.3 = ((bf16[32,4,16,256]{3,2,1,0:T(8,128)(2,1)}), bf16[32,4,16,256]{3,2,1,0:T(8,128)(2,1)S(1)}, u32[]{:S(2)}, u32[]{:S(2)}) async-start(bf16[32,4,16,256]{3,2,1,0:T(8,128)(2,1)} %pick_tiles.1), calls=%async_computation.3 | async-start | bytes 2097152 | tf_op jit(solution)/shard_map/pick/all_to_all | solution.py:347
  115.9 2.8 %collective-permute-start.20 = (f32[2,2,16,128]{3,2,1,0:T(8,128)S(1)}, f32[2,2,16,128]{3,2,1,0:T(8,128)S(1)}, u32[]{:S(2)}, u32[]{:S(2)}) collective-permute-start(f32[2,2,16,128]{3,2,1,0:T(8,128)S(1)} %get-tuple-element.21), channel_id=1, source_target_pairs={{0,3},{1,0},{2,1},{3,2},{4,7},{5,4},{6,5},{7,6},{8,11},{9,8},{10,9... | collective-permute-start | bytes 98312 | tf_op jit(solution)/shard_map/updates/ppermute | solution.py:253
  120.3 9.7 %collective-permute-done.20 = f32[2,2,16,128]{3,2,1,0:T(8,128)S(1)} collective-permute-done((f32[2,2,16,128]{3,2,1,0:T(8,128)S(1)}, f32[2,2,16,128]{3,2,1,0:T(8,128)S(1)}, u32[]{:S(2)}, u32[]{:S(2)}) %collective-permute-start.20) | collective-permute-done | bytes 32800 | tf_op jit(solution)/shard_map/updates/ppermute | solution.py:253
  130.0 1.4 collective-permute-done.19
  133.9 7.1 %collective-permute-done.21 = f32[4,2,16,128]{3,2,1,0:T(8,128)} collective-permute-done((f32[4,2,16,128]{3,2,1,0:T(8,128)}, f32[4,2,16,128]{3,2,1,0:T(8,128)}, u32[]{:S(2)}, u32[]{:S(2)}) %collective-permute-start.21) | collective-permute-done | bytes 65568 | tf_op jit(solution)/shard_map/updates/ppermute | solution.py:253
  141.0 0.9 pad_maximum_fusion.3.kept_ref
  141.9 1.2 updates.1
  143.2 1.1 back_project.1
  (102 shorter events, 11.8 us)
Async XLA Ops:
  0.7 6.8 %copy-start.3 = (f32[1,64,2,128]{3,2,1,0:T(2,128)S(1)}, f32[1,64,2,128]{3,2,1,0:T(2,128)}, u32[]{:S(2)}) copy-start(f32[1,64,2,128]{3,2,1,0:T(2,128)} %param.15) | copy-start | bytes 196612
  0.7 6.8 %copy-start.4 = (f32[1,64,2,128]{3,2,1,0:T(2,128)S(1)}, f32[1,64,2,128]{3,2,1,0:T(2,128)}, u32[]{:S(2)}) copy-start(f32[1,64,2,128]{3,2,1,0:T(2,128)} %param.16) | copy-start | bytes 196612
  2.1 20.6 %collective-permute-start.2 = (s32[8]{0:T(128)S(1)}, s32[8]{0:T(128)S(1)}, u32[]{:S(2)}, u32[]{:S(2)}) collective-permute-start(s32[8]{0:T(128)S(1)} %get-tuple-element.35), channel_id=1, source_target_pairs={{0,192},{64,0},{128,64},{192,128},{1,193},{65,1},{129,65},{193,129... | collective-permute-start | bytes 104 | tf_op jit(solution)/shard_map/targets/ppermute | solution.py:253
  6.8 17.4 %collective-permute-start.1 = (s32[8]{0:T(128)S(1)}, s32[8]{0:T(128)S(1)}, u32[]{:S(2)}, u32[]{:S(2)}) collective-permute-start(s32[8]{0:T(128)S(1)} %get-tuple-element.36), channel_id=1, source_target_pairs={{0,128},{64,192},{128,0},{192,64},{1,129},{65,193},{129,1},{193,65... | collective-permute-start | bytes 104 | tf_op jit(solution)/shard_map/targets/ppermute | solution.py:253
  6.8 17.4 %collective-permute-start = (s32[8]{0:T(128)S(1)}, s32[8]{0:T(128)S(1)}, u32[]{:S(2)}, u32[]{:S(2)}) collective-permute-start(s32[8]{0:T(128)S(1)} %get-tuple-element.37), channel_id=1, source_target_pairs={{0,64},{64,128},{128,192},{192,0},{1,65},{65,129},{129,193},{193,1... | collective-permute-start | bytes 104 | tf_op jit(solution)/shard_map/targets/ppermute | solution.py:253
  7.5 4.4 %copy-start.2 = (f32[256,2,128]{2,1,0:T(2,128)S(1)}, f32[256,2,128]{2,1,0:T(2,128)}, u32[]{:S(2)}) copy-start(f32[256,2,128]{2,1,0:T(2,128)} %param.17) | copy-start | bytes 786436
  8.2 40.5 %collective-permute-start.16 = (f32[2,16,128]{2,1,0:T(8,128)S(1)}, f32[2,16,128]{2,1,0:T(8,128)S(1)}, u32[]{:S(2)}, u32[]{:S(2)}) collective-permute-start(f32[2,16,128]{2,1,0:T(8,128)S(1)} %get-tuple-element.29), channel_id=1, source_target_pairs={{0,3},{1,0},{2,1},{3,2},{4,7},{5,4},{6,5},{7,6},{8,11},{9,8},{10,9... | collective-permute-start | bytes 49160 | tf_op jit(solution)/shard_map/drift/ppermute | solution.py:253
  11.3 40.6 %collective-permute-start.15 = (f32[2,16,128]{2,1,0:T(8,128)S(1)}, f32[2,16,128]{2,1,0:T(8,128)S(1)}, u32[]{:S(2)}, u32[]{:S(2)}) collective-permute-start(f32[2,16,128]{2,1,0:T(8,128)S(1)} %get-tuple-element.30), channel_id=1, source_target_pairs={{0,2},{1,3},{2,0},{3,1},{4,6},{5,7},{6,4},{7,5},{8,10},{9,11},{10,... | collective-permute-start | bytes 49160 | tf_op jit(solution)/shard_map/drift/ppermute | solution.py:253
  11.9 1.2 copy-start
  15.0 57.6 %all-to-all-start = ((bf16[32,4,16,256]{3,2,1,0:T(8,128)(2,1)}), bf16[32,4,16,256]{3,2,1,0:T(8,128)(2,1)S(1)}, u32[]{:S(2)}, u32[]{:S(2)}) async-start(bf16[32,4,16,256]{3,2,1,0:T(8,128)(2,1)} %ray_sums.1), calls=%async_computation | async-start | bytes 2097152 | tf_op jit(solution)/shard_map/ray_sums/all_to_all | solution.py:281
  22.6 29.3 %collective-permute-start.14 = (f32[2,16,128]{2,1,0:T(8,128)S(1)}, f32[2,16,128]{2,1,0:T(8,128)S(1)}, u32[]{:S(2)}, u32[]{:S(2)}) collective-permute-start(f32[2,16,128]{2,1,0:T(8,128)S(1)} %get-tuple-element.31), channel_id=1, source_target_pairs={{0,1},{1,2},{2,3},{3,0},{4,5},{5,6},{6,7},{7,4},{8,9},{9,10},{10,1... | collective-permute-start | bytes 49160 | tf_op jit(solution)/shard_map/drift/ppermute | solution.py:253
  24.1 14.0 %collective-permute-start.4 = (s32[4,8]{1,0:T(4,128)S(1)}, s32[4,8]{1,0:T(4,128)S(1)}, u32[]{:S(2)}, u32[]{:S(2)}) collective-permute-start(s32[4,8]{1,0:T(4,128)S(1)} %get-tuple-element.33), channel_id=1, source_target_pairs={{0,2},{1,3},{2,0},{3,1},{4,6},{5,7},{6,4},{7,5},{8,10},{9,11},{10,... | collective-permute-start | bytes 392 | tf_op jit(solution)/shard_map/targets/ppermute | solution.py:253
  26.9 11.9 %collective-permute-start.3 = (s32[4,8]{1,0:T(4,128)S(1)}, s32[4,8]{1,0:T(4,128)S(1)}, u32[]{:S(2)}, u32[]{:S(2)}) collective-permute-start(s32[4,8]{1,0:T(4,128)S(1)} %get-tuple-element.33), channel_id=1, source_target_pairs={{0,1},{1,2},{2,3},{3,0},{4,5},{5,6},{6,7},{7,4},{8,9},{9,10},{10,1... | collective-permute-start | bytes 392 | tf_op jit(solution)/shard_map/targets/ppermute | solution.py:253
  38.1 6.1 %collective-permute-start.5 = (s32[4,8]{1,0:T(4,128)S(1)}, s32[4,8]{1,0:T(4,128)S(1)}, u32[]{:S(2)}, u32[]{:S(2)}) collective-permute-start(s32[4,8]{1,0:T(4,128)S(1)} %get-tuple-element.33), channel_id=1, source_target_pairs={{0,3},{1,0},{2,1},{3,2},{4,7},{5,4},{6,5},{7,6},{8,11},{9,8},{10,9... | collective-permute-start | bytes 392 | tf_op jit(solution)/shard_map/targets/ppermute | solution.py:253
  38.8 8.3 %collective-permute-start.6 = (f32[128,128]{1,0:T(8,128)S(1)}, f32[128,128]{1,0:T(8,128)S(1)}, u32[]{:S(2)}, u32[]{:S(2)}) collective-permute-start(f32[128,128]{1,0:T(8,128)S(1)} %bitcast.99), channel_id=1, source_target_pairs={{0,4},{4,0},{1,5},{5,1},{2,6},{6,2},{3,7},{7,3},{8,12},{12,8},{9,1... | collective-permute-start | bytes 196616 | tf_op jit(solution)/shard_map/fields/ppermute | solution.py:253
  47.1 10.5 %collective-permute-start.8 = (f32[2,128,128]{2,1,0:T(8,128)S(1)}, f32[2,128,128]{2,1,0:T(8,128)S(1)}, u32[]{:S(2)}, u32[]{:S(2)}) collective-permute-start(f32[2,128,128]{2,1,0:T(8,128)S(1)} %get-tuple-element.25), channel_id=1, source_target_pairs={{0,2},{1,3},{2,0},{3,1},{4,6},{5,7},{6,4},{7,5},{8,10},{9,11},{10,... | collective-permute-start | bytes 393224 | tf_op jit(solution)/shard_map/fields/ppermute | solution.py:253
  48.7 9.0 %collective-permute-start.7 = (f32[2,128,128]{2,1,0:T(8,128)S(1)}, f32[2,128,128]{2,1,0:T(8,128)S(1)}, u32[]{:S(2)}, u32[]{:S(2)}) collective-permute-start(f32[2,128,128]{2,1,0:T(8,128)S(1)} %get-tuple-element.25), channel_id=1, source_target_pairs={{0,1},{1,2},{2,3},{3,0},{4,5},{5,6},{6,7},{7,4},{8,9},{9,10},{10,1... | collective-permute-start | bytes 393224 | tf_op jit(solution)/shard_map/fields/ppermute | solution.py:253
  48.7 9.0 %collective-permute-start.9 = (f32[2,128,128]{2,1,0:T(8,128)S(1)}, f32[2,128,128]{2,1,0:T(8,128)S(1)}, u32[]{:S(2)}, u32[]{:S(2)}) collective-permute-start(f32[2,128,128]{2,1,0:T(8,128)S(1)} %get-tuple-element.25), channel_id=1, source_target_pairs={{0,3},{1,0},{2,1},{3,2},{4,7},{5,4},{6,5},{7,6},{8,11},{9,8},{10,9... | collective-permute-start | bytes 393224 | tf_op jit(solution)/shard_map/fields/ppermute | solution.py:253
  51.9 5.8 %copy-start.11 = (bf16[256,256]{1,0:T(8,128)(2,1)S(1)}, bf16[256,256]{1,0:T(8,128)(2,1)}, u32[]{:S(2)}) copy-start(bf16[256,256]{1,0:T(8,128)(2,1)} %constant.167.clone.ah_ref) | copy-start | bytes 393220
  52.0 14.9 %collective-permute-start.17 = (f32[4,16,128]{2,1,0:T(8,128)S(1)}, f32[4,16,128]{2,1,0:T(8,128)S(1)}, u32[]{:S(2)}, u32[]{:S(2)}) collective-permute-start(f32[4,16,128]{2,1,0:T(8,128)S(1)} %get-tuple-element.27), channel_id=1, source_target_pairs={{0,4},{4,0},{1,5},{5,1},{2,6},{6,2},{3,7},{7,3},{8,12},{12,8},{9,1... | collective-permute-start | bytes 98312 | tf_op jit(solution)/shard_map/drift/ppermute | solution.py:253
  57.7 1.1 copy-start.10
  63.5 5.7 %collective-permute-start.10 = (bf16[2,128,128]{2,1,0:T(8,128)(2,1)S(1)}, bf16[2,128,128]{2,1,0:T(8,128)(2,1)S(1)}, u32[]{:S(2)}, u32[]{:S(2)}) collective-permute-start(bf16[2,128,128]{2,1,0:T(8,128)(2,1)S(1)} %get-tuple-element.15), channel_id=1, source_target_pairs={{0,1},{1,2},{2,3},{3,0},{4,5},{5,6},{6,7},{7,4},{8,9},{9,10},{10,1... | collective-permute-start | bytes 196616 | tf_op jit(solution)/shard_map/frames/ppermute | solution.py:253
  63.6 5.6 %collective-permute-start.12 = (bf16[2,128,128]{2,1,0:T(8,128)(2,1)S(1)}, bf16[2,128,128]{2,1,0:T(8,128)(2,1)S(1)}, u32[]{:S(2)}, u32[]{:S(2)}) collective-permute-start(bf16[2,128,128]{2,1,0:T(8,128)(2,1)S(1)} %get-tuple-element.16), channel_id=1, source_target_pairs={{0,3},{1,0},{2,1},{3,2},{4,7},{5,4},{6,5},{7,6},{8,11},{9,8},{10,9... | collective-permute-start | bytes 196616 | tf_op jit(solution)/shard_map/frames/ppermute | solution.py:253
  66.8 5.8 %collective-permute-start.11 = (bf16[2,128,128]{2,1,0:T(8,128)(2,1)S(1)}, bf16[2,128,128]{2,1,0:T(8,128)(2,1)S(1)}, u32[]{:S(2)}, u32[]{:S(2)}) collective-permute-start(bf16[2,128,128]{2,1,0:T(8,128)(2,1)S(1)} %get-tuple-element.17), channel_id=1, source_target_pairs={{0,2},{1,3},{2,0},{3,1},{4,6},{5,7},{6,4},{7,5},{8,10},{9,11},{10,... | collective-permute-start | bytes 196616 | tf_op jit(solution)/shard_map/frames/ppermute | solution.py:253
  74.6 16.7 %all-to-all-start.1 = ((bf16[8,128,128]{2,1,0:T(8,128)(2,1)}), bf16[8,128,128]{2,1,0:T(8,128)(2,1)S(1)}, u32[]{:S(2)}, u32[]{:S(2)}) async-start(bf16[8,128,128]{2,1,0:T(8,128)(2,1)} %add_tiles.1), calls=%async_computation.1 | async-start | bytes 524288 | tf_op jit(solution)/shard_map/near_sum/all_to_all | solution.py:329
  79.4 11.9 %collective-permute-start.13 = (f32[128,128]{1,0:T(8,128)S(1)}, f32[128,128]{1,0:T(8,128)S(1)}, u32[]{:S(2)}, u32[]{:S(2)}) collective-permute-start(f32[128,128]{1,0:T(8,128)S(1)} %dynamic-slice_bitcast_fusion.2), channel_id=1, source_target_pairs={{0,4},{4,0},{1,5},{5,1},{2,6},{6,2},{3,7},{7,3},{8,12},{12,8},{9,1... | collective-permute-start | bytes 196616 | tf_op jit(solution)/shard_map/frames/ppermute | solution.py:253
  108.1 35.1 %all-to-all-start.3 = ((bf16[32,4,16,256]{3,2,1,0:T(8,128)(2,1)}), bf16[32,4,16,256]{3,2,1,0:T(8,128)(2,1)S(1)}, u32[]{:S(2)}, u32[]{:S(2)}) async-start(bf16[32,4,16,256]{3,2,1,0:T(8,128)(2,1)} %pick_tiles.1), calls=%async_computation.3 | async-start | bytes 2097152 | tf_op jit(solution)/shard_map/pick/all_to_all | solution.py:347
  115.2 18.0 %copy-start.1 = (bf16[1,32,2,32,256]{4,3,2,1,0:T(8,128)(2,1)S(1)}, bf16[1,32,2,32,256]{4,3,2,1,0:T(8,128)(2,1)}, u32[]{:S(2)}) copy-start(bf16[1,32,2,32,256]{4,3,2,1,0:T(8,128)(2,1)} %param.18) | copy-start | bytes 3145732
  115.9 14.1 %collective-permute-start.20 = (f32[2,2,16,128]{3,2,1,0:T(8,128)S(1)}, f32[2,2,16,128]{3,2,1,0:T(8,128)S(1)}, u32[]{:S(2)}, u32[]{:S(2)}) collective-permute-start(f32[2,2,16,128]{3,2,1,0:T(8,128)S(1)} %get-tuple-element.21), channel_id=1, source_target_pairs={{0,3},{1,0},{2,1},{3,2},{4,7},{5,4},{6,5},{7,6},{8,11},{9,8},{10,9... | collective-permute-start | bytes 98312 | tf_op jit(solution)/shard_map/updates/ppermute | solution.py:253
  118.6 12.8 %collective-permute-start.19 = (f32[2,2,16,128]{3,2,1,0:T(8,128)S(1)}, f32[2,2,16,128]{3,2,1,0:T(8,128)S(1)}, u32[]{:S(2)}, u32[]{:S(2)}) collective-permute-start(f32[2,2,16,128]{3,2,1,0:T(8,128)S(1)} %get-tuple-element.22), channel_id=1, source_target_pairs={{0,2},{1,3},{2,0},{3,1},{4,6},{5,7},{6,4},{7,5},{8,10},{9,11},{10,... | collective-permute-start | bytes 98312 | tf_op jit(solution)/shard_map/updates/ppermute | solution.py:253
  119.5 12.4 %collective-permute-start.18 = (f32[2,2,16,128]{3,2,1,0:T(8,128)S(1)}, f32[2,2,16,128]{3,2,1,0:T(8,128)S(1)}, u32[]{:S(2)}, u32[]{:S(2)}) collective-permute-start(f32[2,2,16,128]{3,2,1,0:T(8,128)S(1)} %get-tuple-element.23), channel_id=1, source_target_pairs={{0,1},{1,2},{2,3},{3,0},{4,5},{5,6},{6,7},{7,4},{8,9},{9,10},{10,1... | collective-permute-start | bytes 98312 | tf_op jit(solution)/shard_map/updates/ppermute | solution.py:253
  132.5 8.5 %collective-permute-start.21 = (f32[4,2,16,128]{3,2,1,0:T(8,128)}, f32[4,2,16,128]{3,2,1,0:T(8,128)}, u32[]{:S(2)}, u32[]{:S(2)}) collective-permute-start(f32[4,2,16,128]{3,2,1,0:T(8,128)} %get-tuple-element.19), channel_id=1, source_target_pairs={{0,4},{4,0},{1,5},{5,1},{2,6},{6,2},{3,7},{7,3},{8,12},{12,8},{9,1... | collective-permute-start | bytes 196616 | tf_op jit(solution)/shard_map/updates/ppermute | solution.py:253
  (6 other events, 6.0 us)

commit v2 on v1

--- a/solution.py
+++ b/solution.py
@@ -79,45 +79,71 @@
                 out_ref[xc * Y + y, zl] = jnp.concatenate([low, high], axis=0).astype(bf16)
 
 
-def add_tiles(target_ref, sums_ref, out_ref, total):
+def first_row(place_ref, target_ref, zl, y, xc):
+    back_zl = lax.rem(place_ref[2] + ZL - zl, ZL)
+    back_y = lax.rem(place_ref[1] + Y - y, Y)
+    return pl.multiple_of(target_ref[back_zl, back_y * XC + xc] * QR, QR)
+
+
+def add_tiles(place_ref, target_ref, sums_ref, out_ref, total):
     total[...] = jnp.zeros(total.shape, f32)
 
-    def step(source, carry):
-        for zl in range(ZL):
-            row = pl.multiple_of(target_ref[zl, source] * QR, QR)
-            total[zl, pl.ds(row, HITS * QR), :] += sums_ref[source, zl].astype(f32)
+    def step(xc, carry):
+        for y in range(Y):
+            for zl in range(ZL):
+                row = first_row(place_ref, target_ref, zl, y, xc)
+                total[zl, pl.ds(row, HITS * QR), :] += sums_ref[xc * Y + y, zl].astype(f32)
         return carry
 
-    lax.fori_loop(0, NEAR, step, 0, unroll=4)
+    lax.fori_loop(0, XC, step, 0)
     for zh in range(ZH):
         for zl in range(ZL):
             out_ref[zh * ZL + zl] = total[zl, :, zh * NZ : (zh + 1) * NZ].astype(bf16)
 
 
-def residual_part(sums_ref, inter_ref, drift_ref, residual_ref, keep_ref):
+def residual_part(
+    place_ref, sums_ref, inter_ref, mine_ref, theirs_ref, residual_ref, own_ref, one_ref, two_ref, three_ref, both
+):
+    zh = place_ref[0]
+    y = place_ref[1]
     projection = sums_ref[0].astype(f32)
     for source in range(1, DEEP):
         projection = projection + sums_ref[source].astype(f32)
     inter = inter_ref[...]
-    gap = projection - drift_ref[...]
+    both[0] = projection
+    both[1] = inter
+    first = zh == 0
+    drift = jnp.concatenate(
+        [
+            jnp.where(first, mine_ref[...], theirs_ref[...]),
+            jnp.where(first, theirs_ref[...], mine_ref[...]),
+        ],
+        axis=0,
+    )
+    gap = projection - drift
     residual_ref[...] = (gap + object_step * (inter - gap)).astype(bf16)
-    keep_ref[0] = projection
-    keep_ref[1] = inter
-
-
-def pick_tiles(target_ref, residual_ref, out_ref, rows_ref):
+    for ahead, ref in enumerate((own_ref, one_ref, two_ref, three_ref)):
+        for other in range(ZH):
+            owner = lax.rem(zh + other, ZH) * Y + lax.rem(y + ahead, Y)
+            rows = pl.ds(pl.multiple_of(owner * 2 * QR, 2 * QR), 2 * QR)
+            ref[other, 0] = both[0, rows, :]
+            ref[other, 1] = both[1, rows, :]
+
+
+def pick_tiles(place_ref, target_ref, residual_ref, out_ref, rows_ref):
     for zl in range(ZL):
         rows_ref[zl] = jnp.concatenate(
             [residual_ref[zl].astype(f32), residual_ref[ZL + zl].astype(f32)], axis=1
         )
 
-    def step(dest, carry):
-        for zl in range(ZL):
-            row = pl.multiple_of(target_ref[zl, dest] * QR, QR)
-            out_ref[dest, zl] = rows_ref[zl, pl.ds(row, HITS * QR), :].astype(bf16)
+    def step(xc, carry):
+        for y in range(Y):
+            for zl in range(ZL):
+                row = first_row(place_ref, target_ref, zl, y, xc)
+                out_ref[xc * Y + y, zl] = rows_ref[zl, pl.ds(row, HITS * QR), :].astype(bf16)
         return carry
 
-    lax.fori_loop(0, NEAR, step, 0, unroll=4)
+    lax.fori_loop(0, XC, step, 0)
 
 
 def back_project(radon_ref, picked_ref, volume_ref, out_ref):
@@ -131,17 +157,20 @@
         out_ref[rows, :] = volume_ref[rows, :] - volume_step * gradient[:, part * NZ : (part + 1) * NZ]
 
 
-def updates(place_ref, kept_ref, object_ref, dual_ref, object_out, dual_out):
+def updates(
+    place_ref, own_ref, one_ref, two_ref, three_ref, theirs_ref, object_ref, dual_ref, object_out, dual_out
+):
     zh = place_ref[0]
     y = place_ref[1]
-    for other in range(ZH):
-        part = lax.rem(zh + other, ZH)
-        for back in range(Y):
-            source = lax.rem(y + Y - back, Y)
+    for back, ref in enumerate((own_ref, one_ref, two_ref, three_ref)):
+        source = lax.rem(y + Y - back, Y)
+        for other in range(ZH):
+            part = lax.rem(zh + other, ZH)
             for tile in range(2):
+                piece = slice(tile * QR, (tile + 1) * QR)
+                projection = theirs_ref[back, 0, piece, :] if other else ref[0, 0, piece, :]
+                inter = theirs_ref[back, 1, piece, :] if other else ref[0, 1, piece, :]
                 rows = pl.ds((tile * RAYS + source * QR) * 2 + part, QR, stride=2)
-                projection = kept_ref[other, back, 0, tile * QR : (tile + 1) * QR, :]
-                inter = kept_ref[other, back, 1, tile * QR : (tile + 1) * QR, :]
                 field = object_ref[rows, :]
                 dual = dual_ref[rows, :]
                 object_next = field - object_step * (inter + dual + penalty * (field - projection))
@@ -172,19 +201,42 @@
     )
 
 
+FIELD_ROWS = 4 * 64
+DRIFT_ROWS = 4 * QR
+SENT_ROWS = FIELD_ROWS + DRIFT_ROWS + QR
+
+
+def pack(place_ref, object_ref, theirs_ref, dual_ref, target_ref, own_ref, one_ref, two_ref, three_ref, drift):
+    y = place_ref[1]
+    drift[...] = object_ref[...] + dual_ref[...]
+    for ahead, ref in enumerate((own_ref, one_ref, two_ref, three_ref)):
+        ref[0:128, :] = object_ref[...]
+        ref[128:256, :] = theirs_ref[...]
+        ref[FIELD_ROWS + DRIFT_ROWS :, :] = target_ref[...]
+        for part in range(2):
+            for tile in range(2):
+                start = (tile * RAYS + lax.rem(y + ahead, Y) * QR) * 2 + part
+                base = FIELD_ROWS + (part * 2 + tile) * QR
+                ref[base : base + QR, :] = drift[pl.ds(start, QR, stride=2), :]
+
+
 def frame_gradients(
-    place_ref, starts_ref, field_ref, probe_ref, measured_ref, ah_ref, al_ref, bh_ref, bl_ref,
-    own_ref, sent_ref, field_re, field_im, total_re, total_im, staged,
+    place_ref, starts_ref, own_field, one_field, two_field, three_field, probe_ref, measured_ref,
+    ah_ref, al_ref, bh_ref, bl_ref, own_ref, sent_one, sent_two, sent_three, mine_ref, theirs_ref,
+    field_re, field_im, total_re, total_im,
 ):
     zh = place_ref[0]
     y = place_ref[1]
-    for back in range(Y):
+    for back, field_ref in enumerate((own_field, one_field, two_field, three_field)):
+        source = lax.rem(y + Y - back, Y)
         for other in range(ZH):
-            owner = lax.rem(zh + other, ZH) * Y + lax.rem(y + Y - back, Y)
+            owner = lax.rem(zh + other, ZH) * Y + source
             rows = pl.ds(pl.multiple_of(owner * 64, 64), 64)
-            staged[...] = field_ref[back, other]
-            field_re[rows, :] = staged[pl.ds(0, 64, stride=2), :]
-            field_im[rows, :] = staged[pl.ds(1, 64, stride=2), :]
+            field_re[rows, :] = field_ref[pl.ds(other * 128, 64, stride=2), :]
+            field_im[rows, :] = field_ref[pl.ds(other * 128 + 1, 64, stride=2), :]
+        rows = pl.ds(pl.multiple_of(source * 2 * QR, 2 * QR), 2 * QR)
+        mine_ref[rows, :] = field_ref[pl.ds(pl.multiple_of(FIELD_ROWS + zh * 2 * QR, 2 * QR), 2 * QR), :]
+        theirs_ref[rows, :] = field_ref[pl.ds(pl.multiple_of(FIELD_ROWS + (1 - zh) * 2 * QR, 2 * QR), 2 * QR), :]
     total_re[...] = jnp.zeros(total_re.shape, f32)
     total_im[...] = jnp.zeros(total_im.shape, f32)
     probe_re = probe_ref[0]
@@ -246,7 +298,7 @@
                 if ahead == 0:
                     own_ref[part, rows, :] = piece
                 else:
-                    sent_ref[ahead - 1, part, rows, :] = piece.astype(bf16)
+                    (sent_one, sent_two, sent_three)[ahead - 1][part, rows, :] = piece.astype(bf16)
 
 
 def shifted(value, axis, length, step):
@@ -265,9 +317,7 @@
     zh = lax.axis_index("zh")
     zl = lax.axis_index("zl")
     y = lax.axis_index("y")
-    place = jnp.stack([zh, y]).astype(jnp.int32)
-    order = (y + jnp.arange(Y)) % Y
-    back_order = (y - jnp.arange(Y)) % Y
+    place = jnp.stack([zh, y, zl]).astype(jnp.int32)
     ah, al, bh, bl = dft_blocks()
     radon = radon_tiles.reshape(ZL * XC, HITS, RAYS, TILE)
     volume_rows = volume.reshape(2 * TILE, NZ)
@@ -281,57 +331,55 @@
         near_sums = lax.all_to_all(sums, CROSS, 0, 0, tiled=True)
 
     with jax.named_scope("fields"):
-        pair = jnp.stack([object_rows, across(object_rows)])
-        fields = jnp.stack(round_y([pair] * Y))
+        own_targets = jnp.zeros((QR, NZ), f32).at[0, : ZL * XC].set(tile_range.reshape(ZL * XC).astype(f32))
+        packed = call(
+            pack, (shape(SENT_ROWS, NZ),) * Y, 1, 4, scratch=[pltpu.VMEM((128, NZ), f32)], flops=1_000_000
+        )(place, object_rows, across(object_rows), dual_rows, own_targets)
+        fields = round_y(packed)
 
     with jax.named_scope("targets"):
-        own_targets = tile_range.reshape(ZL, XC)
-        ahead = [lax.dynamic_index_in_dim(own_targets, (zl + k) % ZL, 0, keepdims=False) for k in range(ZL)]
-        rounds = [ahead[0]] + [shifted(ahead[k], "zl", ZL, k) for k in range(1, ZL)]
-        targets = jnp.stack(rounds)
-        targets = jnp.stack(round_y([targets] * Y))
-        targets = jnp.take(jnp.take(targets, back_order, axis=0), (zl - jnp.arange(ZL)) % ZL, axis=1)
-        targets = targets.transpose(1, 2, 0).reshape(ZL, NEAR)
-
-    with jax.named_scope("drift"):
-        drift = (object_field + dual_field).reshape(2, Y, QR, 2, NZ)
-        drift = jnp.take(drift.transpose(1, 3, 0, 2, 4).reshape(Y, 2, 2 * QR, NZ), order, axis=0)
-        drift = jnp.stack(round_y([drift[k] for k in range(Y)]))
-        mine = lax.dynamic_index_in_dim(drift, zh, 1, keepdims=False)
-        theirs = across(lax.dynamic_index_in_dim(drift, 1 - zh, 1, keepdims=False))
-        both = jnp.where(zh == 0, jnp.stack([mine, theirs]), jnp.stack([theirs, mine]))
-        drift_part = jnp.take(both, back_order, axis=1).reshape(128, NZ)
+        tables = jnp.stack([field[FIELD_ROWS + DRIFT_ROWS, : ZL * XC] for field in fields])
+        tables = tables.reshape(Y, ZL, XC).astype(jnp.int32)
+        ahead = [lax.dynamic_index_in_dim(tables, (zl + k) % ZL, 1, keepdims=False) for k in range(ZL)]
+        targets = jnp.stack([ahead[0]] + [shifted(ahead[k], "zl", ZL, k) for k in range(1, ZL)])
+        targets = targets.reshape(ZL, Y * XC)
 
     with jax.named_scope("frames"):
-        inter_own, inter_others = call(
+        *inter_parts, drift_mine, drift_sent = call(
             frame_gradients,
-            (shape(2, 128, NZ), shape(Y - 1, 2, 128, NZ, dtype=bf16)),
+            (shape(2, 128, NZ),) + (shape(2, 128, NZ, dtype=bf16),) * 3 + (shape(64, NZ),) * 2,
             2,
-            7,
-            scratch=[pltpu.VMEM((NDET, NZ), f32)] * 4 + [pltpu.VMEM((128, NZ), f32)],
+            10,
+            scratch=[pltpu.VMEM((NDET, NZ), f32)] * 4,
             flops=1_600_000_000,
-        )(place, positions, fields, probe_field, measured[0], ah, al, bh, bl)
-        arrived = round_y([inter_own] + [inter_others[k] for k in range(Y - 1)])
-        inter_sum = sum(piece.astype(f32) for piece in arrived)
+        )(place, positions, *fields, probe_field, measured[0], ah, al, bh, bl)
+        inter_sum = sum(piece.astype(f32) for piece in round_y(inter_parts))
         inter_mine = lax.dynamic_index_in_dim(inter_sum, zh, 0, keepdims=False)
         inter_sent = lax.dynamic_index_in_dim(inter_sum, 1 - zh, 0, keepdims=False)
         inter = inter_mine + across(inter_sent)
+        drift_theirs = across(drift_sent)
 
     with jax.named_scope("near_sum"):
         dense = call(
             add_tiles,
             shape(DEEP, 128, NZ, dtype=bf16),
-            1,
+            2,
             1,
             scratch=[pltpu.VMEM((ZL, 128, 2 * NZ), f32)],
             flops=1_000_000,
-        )(targets, near_sums)
+        )(place, targets, near_sums)
         far_sums = lax.all_to_all(dense, ALONG, 0, 0, tiled=True)
 
     with jax.named_scope("residual"):
-        residual, kept = call(
-            residual_part, (shape(128, NZ, dtype=bf16), shape(2, 128, NZ)), 0, 3, flops=1_000_000
-        )(far_sums, inter, drift_part)
+        residual, *kept = call(
+            residual_part,
+            (shape(128, NZ, dtype=bf16),) + (shape(ZH, 2, 2 * QR, NZ),) * Y,
+            1,
+            4,
+            scratch=[pltpu.VMEM((2, 128, NZ), f32)],
+            flops=1_000_000,
+        )(place, far_sums, inter, drift_mine, drift_theirs)
+        kept = round_y(kept)
         copies = jnp.broadcast_to(residual, (DEEP, 128, NZ))
         residuals = lax.all_to_all(copies, ALONG, 0, 0, tiled=True)
 
@@ -339,20 +387,18 @@
         picked = call(
             pick_tiles,
             shape(NEAR, ZL, HITS * QR, 2 * NZ, dtype=bf16),
-            1,
+            2,
             1,
             scratch=[pltpu.VMEM((ZL, 128, 2 * NZ), f32)],
             flops=1_000_000,
-        )(targets, residuals)
+        )(place, targets, residuals)
+        picked, kept = lax.optimization_barrier((picked, kept))
         returned = lax.all_to_all(picked, CROSS, 0, 0, tiled=True)
 
     with jax.named_scope("updates"):
-        kept = jnp.take(kept.reshape(2, ZH, Y, 2 * QR, NZ).transpose(2, 1, 0, 3, 4), order, axis=0)
-        kept = jnp.stack(round_y([kept[k] for k in range(Y)]))
-        mine = lax.dynamic_index_in_dim(kept, zh, 1, keepdims=False)
-        theirs = across(lax.dynamic_index_in_dim(kept, 1 - zh, 1, keepdims=False))
-        object_next, dual_next = call(updates, (shape(128, NZ), shape(128, NZ)), 1, 3, flops=1_000_000)(
-            place, jnp.stack([mine, theirs]), object_rows, dual_rows
+        theirs = across(jnp.stack([piece[1] for piece in kept]))
+        object_next, dual_next = call(updates, (shape(128, NZ), shape(128, NZ)), 1, 7, flops=1_000_000)(
+            place, *kept, theirs, object_rows, dual_rows
         )
 
     with jax.named_scope("back_project"):

time: 145 us -> 116 us (0.80)
  the two profiles are of different devices: /device:TPU:2 before, /device:TPU:1 now
where the time goes in v2:
time: 116 us
  starting transfers between devices  57.5 us (50%)
  waiting for transfers between devices  34.4 us (30%)
  Pallas kernels  14.3 us (12%)
  local copies, waits for them, and re-layouts  8.34 us (7%)
    ppermute x16, starting transfers between devices, shifted(): lax.ppermute(value, axis, [(i, (i + step) % length) for i in range(length)])  29.2 us
    ppermute x16, waiting for transfers between devices, shifted(): lax.ppermute(value, axis, [(i, (i + step) % length) for i in range(length)])  22.9 us
    all_to_all x1, starting transfers between devices, body(): returned = lax.all_to_all(picked, CROSS, 0, 0, tiled=True)  9.3 us
    all_to_all x1, starting transfers between devices, body(): near_sums = lax.all_to_all(sums, CROSS, 0, 0, tiled=True)  8.74 us
    all_to_all x1, starting transfers between devices, body(): far_sums = lax.all_to_all(dense, ALONG, 0, 0, tiled=True)  6.8 us
    all_to_all x1, waiting for transfers between devices, body(): returned = lax.all_to_all(picked, CROSS, 0, 0, tiled=True)  5.85 us
    all_to_all x1, waiting for transfers between devices, body(): residuals = lax.all_to_all(copies, ALONG, 0, 0, tiled=True)  5.57 us
    pallas_call x1, Pallas kernels, body(): call(frame_gradients, (shape(2, 128, NZ),) + (shape(2, 128, NZ, dtype=bf1...  4.64 us
  transfers between devices with their start and end apart: 20, of which 8 were waited for; matrix products, arithmetic and copies ran while one was open for 3% of the time, Pallas kernels for 9%

profile of v2, /device:TPU:1, one launch (start us, length us, event | category | flops | bytes accessed | tf_op | source)
XLA Modules:
  0.0 115.6 jit_solution(9668006191343476440)
XLA Ops:
  0.6 1.2 %copy-done = bf16[1,32,2,32,256]{4,3,2,1,0:T(8,128)(2,1)S(1)} copy-done((bf16[1,32,2,32,256]{4,3,2,1,0:T(8,128)(2,1)S(1)}, bf16[1,32,2,32,256]{4,3,2,1,0:T(8,128)(2,1)}, u32[]{:S(2)}) %copy-start) | copy-done | bytes 1048600
  2.8 1.8 %ray_sums.1 = bf16[32,4,16,256]{3,2,1,0:T(8,128)(2,1)} custom-call(bf16[32,2,32,256]{3,2,1,0:T(8,128)(2,1)S(1)} %bitcast.24, f32[512,128]{1,0:T(8,128)S(1)} %bitcast.26), custom_call_target="tpu_custom_call" | custom-call | flops 268435456 | bytes 1048576 | tf_op jit(solution)/shard_map/ray_sums/ray_sums/pallas_call | solution.py:328
  4.7 8.7 %all-to-all-start = ((bf16[32,4,16,256]{3,2,1,0:T(8,128)(2,1)}), bf16[32,4,16,256]{3,2,1,0:T(8,128)(2,1)S(1)}, u32[]{:S(2)}, u32[]{:S(2)}) async-start(bf16[32,4,16,256]{3,2,1,0:T(8,128)(2,1)} %ray_sums.1), calls=%async_computation | async-start | bytes 2097152 | tf_op jit(solution)/shard_map/ray_sums/all_to_all | solution.py:331
  13.4 7.0 %collective-permute-start = (f32[128,128]{1,0:T(8,128)S(1)}, f32[128,128]{1,0:T(8,128)S(1)}, u32[]{:S(2)}, u32[]{:S(2)}) collective-permute-start(f32[128,128]{1,0:T(8,128)S(1)} %bitcast.28), channel_id=1, source_target_pairs={{0,4},{4,0},{1,5},{5,1},{2,6},{6,2},{3,7},{7,3},{8,12},{12,8},{9,1... | collective-permute-start | bytes 196616 | tf_op jit(solution)/shard_map/fields/ppermute | solution.py:305
  21.2 1.6 %collective-permute-done.theirs_ref = f32[128,128]{1,0:T(8,128)S(1)} collective-permute-done((f32[128,128]{1,0:T(8,128)S(1)}, f32[128,128]{1,0:T(8,128)S(1)}, u32[]{:S(2)}, u32[]{:S(2)}) %collective-permute-start) | collective-permute-done | bytes 65568 | tf_op jit(solution)/shard_map/fields/ppermute | solution.py:305
  23.3 1.3 %collective-permute-start.1 = (f32[296,128]{1,0:T(8,128)S(1)}, f32[296,128]{1,0:T(8,128)S(1)}, u32[]{:S(2)}, u32[]{:S(2)}) collective-permute-start(f32[296,128]{1,0:T(8,128)S(1)} %get-tuple-element.38), channel_id=1, source_target_pairs={{0,1},{1,2},{2,3},{3,0},{4,5},{5,6},{6,7},{7,4},{8,9},{9,10},{10,1... | collective-permute-start | bytes 454664 | tf_op jit(solution)/shard_map/fields/ppermute | solution.py:305
  24.7 2.4 %collective-permute-start.2 = (f32[296,128]{1,0:T(8,128)S(1)}, f32[296,128]{1,0:T(8,128)S(1)}, u32[]{:S(2)}, u32[]{:S(2)}) collective-permute-start(f32[296,128]{1,0:T(8,128)S(1)} %get-tuple-element.39), channel_id=1, source_target_pairs={{0,2},{1,3},{2,0},{3,1},{4,6},{5,7},{6,4},{7,5},{8,10},{9,11},{10,... | collective-permute-start | bytes 454664 | tf_op jit(solution)/shard_map/fields/ppermute | solution.py:305
  27.1 1.2 %collective-permute-start.3 = (f32[296,128]{1,0:T(8,128)S(1)}, f32[296,128]{1,0:T(8,128)S(1)}, u32[]{:S(2)}, u32[]{:S(2)}) collective-permute-start(f32[296,128]{1,0:T(8,128)S(1)} %get-tuple-element.40), channel_id=1, source_target_pairs={{0,3},{1,0},{2,1},{3,2},{4,7},{5,4},{6,5},{7,6},{8,11},{9,8},{10,9... | collective-permute-start | bytes 454664 | tf_op jit(solution)/shard_map/fields/ppermute | solution.py:305
  28.2 5.0 %collective-permute-done.1.one_field = f32[296,128]{1,0:T(8,128)S(1)} collective-permute-done((f32[296,128]{1,0:T(8,128)S(1)}, f32[296,128]{1,0:T(8,128)S(1)}, u32[]{:S(2)}, u32[]{:S(2)}) %collective-permute-start.1) | collective-permute-done | bytes 151584 | tf_op jit(solution)/shard_map/fields/ppermute | solution.py:305
  33.2 3.4 %collective-permute-done.2.two_field = f32[296,128]{1,0:T(8,128)S(1)} collective-permute-done((f32[296,128]{1,0:T(8,128)S(1)}, f32[296,128]{1,0:T(8,128)S(1)}, u32[]{:S(2)}, u32[]{:S(2)}) %collective-permute-start.2) | collective-permute-done | bytes 151584 | tf_op jit(solution)/shard_map/fields/ppermute | solution.py:305
  36.9 2.8 %collective-permute-start.6 = (s32[4,8]{1,0:T(4,128)S(1)}, s32[4,8]{1,0:T(4,128)S(1)}, u32[]{:S(2)}, u32[]{:S(2)}) collective-permute-start(s32[4,8]{1,0:T(4,128)S(1)} %bitcast.38), channel_id=1, source_target_pairs={{0,192},{64,0},{128,64},{192,128},{1,193},{65,1},{129,65},{193,129... | collective-permute-start | bytes 392 | tf_op jit(solution)/shard_map/targets/ppermute | solution.py:305
  39.7 1.4 %collective-permute-start.4 = (s32[4,8]{1,0:T(4,128)S(1)}, s32[4,8]{1,0:T(4,128)S(1)}, u32[]{:S(2)}, u32[]{:S(2)}) collective-permute-start(s32[4,8]{1,0:T(4,128)S(1)} %bitcast.36), channel_id=1, source_target_pairs={{0,64},{64,128},{128,192},{192,0},{1,65},{65,129},{129,193},{193,1... | collective-permute-start | bytes 392 | tf_op jit(solution)/shard_map/targets/ppermute | solution.py:305
  42.0 4.6 %frame_gradients.1 = (f32[2,128,128]{2,1,0:T(8,128)S(1)}, bf16[2,128,128]{2,1,0:T(8,128)(2,1)S(1)}, bf16[2,128,128]{2,1,0:T(8,128)(2,1)S(1)}, bf16[2,128,128]{2,...) custom-call(s32[3]{0:T(128)S(1)} %pad_add_fusion.1.place_ref, s32[1,8]{1,0:T(1,128)S(1)} %copy-done.12, ...), custom_call_target="tpu_custom_call" | custom-call | flops 1600000000 | bytes 1048576 | tf_op jit(solution)/shard_map/frames/frame_gradients/pallas_call | solution.py:348
  46.7 1.5 %collective-permute-start.8 = (bf16[2,128,128]{2,1,0:T(8,128)(2,1)S(1)}, bf16[2,128,128]{2,1,0:T(8,128)(2,1)S(1)}, u32[]{:S(2)}, u32[]{:S(2)}) collective-permute-start(bf16[2,128,128]{2,1,0:T(8,128)(2,1)S(1)} %get-tuple-element.43), channel_id=1, source_target_pairs={{0,2},{1,3},{2,0},{3,1},{4,6},{5,7},{6,4},{7,5},{8,10},{9,11},{10,... | collective-permute-start | bytes 196616 | tf_op jit(solution)/shard_map/frames/ppermute | solution.py:305
  48.2 1.4 %collective-permute-start.9 = (bf16[2,128,128]{2,1,0:T(8,128)(2,1)S(1)}, bf16[2,128,128]{2,1,0:T(8,128)(2,1)S(1)}, u32[]{:S(2)}, u32[]{:S(2)}) collective-permute-start(bf16[2,128,128]{2,1,0:T(8,128)(2,1)S(1)} %get-tuple-element.44), channel_id=1, source_target_pairs={{0,3},{1,0},{2,1},{3,2},{4,7},{5,4},{6,5},{7,6},{8,11},{9,8},{10,9... | collective-permute-start | bytes 196616 | tf_op jit(solution)/shard_map/frames/ppermute | solution.py:305
  49.8 2.1 %add_tiles.1 = bf16[8,128,128]{2,1,0:T(8,128)(2,1)} custom-call(s32[3]{0:T(128)S(1)} %pad_add_fusion.1.place_ref, s32[4,32]{1,0:T(4,128)S(1)} %pad_add_fusion.target_ref, bf16[32,4,16,256]{3,2,1,0:T(8,128)(2,1)S(1)} %all-to-all-done.sums_ref), custom_call_target="tpu_custom_call" | custom-call | flops 1000000 | bytes 1048576 | tf_op jit(solution)/shard_map/near_sum/add_tiles/pallas_call | solution.py:363
  51.9 6.8 %all-to-all-start.1 = ((bf16[8,128,128]{2,1,0:T(8,128)(2,1)}), bf16[8,128,128]{2,1,0:T(8,128)(2,1)S(1)}, u32[]{:S(2)}, u32[]{:S(2)}) async-start(bf16[8,128,128]{2,1,0:T(8,128)(2,1)} %add_tiles.1), calls=%async_computation.1 | async-start | bytes 524288 | tf_op jit(solution)/shard_map/near_sum/all_to_all | solution.py:371
  58.8 5.4 %collective-permute-start.10 = (f32[128,128]{1,0:T(8,128)S(1)}, f32[128,128]{1,0:T(8,128)S(1)}, u32[]{:S(2)}, u32[]{:S(2)}) collective-permute-start(f32[128,128]{1,0:T(8,128)S(1)} %dynamic-slice_bitcast_fusion), channel_id=1, source_target_pairs={{0,4},{4,0},{1,5},{5,1},{2,6},{6,2},{3,7},{7,3},{8,12},{12,8},{9,1... | collective-permute-start | bytes 196616 | tf_op jit(solution)/shard_map/frames/ppermute | solution.py:305
  64.6 6.7 %collective-permute-done.10 = f32[128,128]{1,0:T(8,128)S(1)} collective-permute-done((f32[128,128]{1,0:T(8,128)S(1)}, f32[128,128]{1,0:T(8,128)S(1)}, u32[]{:S(2)}, u32[]{:S(2)}) %collective-permute-start.10) | collective-permute-done | bytes 65568 | tf_op jit(solution)/shard_map/frames/ppermute | solution.py:305
  71.3 1.2 %collective-permute-done.11.theirs_ref = f32[64,128]{1,0:T(8,128)S(1)} collective-permute-done((f32[64,128]{1,0:T(8,128)S(1)}, f32[64,128]{1,0:T(8,128)S(1)}, u32[]{:S(2)}, u32[]{:S(2)}) %collective-permute-start.11) | collective-permute-done | bytes 32800 | tf_op jit(solution)/shard_map/frames/ppermute | solution.py:305
  73.8 3.4 %all-to-all-start.2 = ((bf16[8,128,128]{2,1,0:T(8,128)(2,1)}), bf16[8,128,128]{2,1,0:T(8,128)(2,1)S(1)}, u32[]{:S(2)}, u32[]{:S(2)}) async-start(bf16[8,128,128]{2,1,0:T(8,128)(2,1)} %broadcast_in_dim.4), calls=%async_computation.2 | async-start | bytes 524288 | tf_op jit(solution)/shard_map/residual/all_to_all | solution.py:384
  77.6 1.4 %collective-permute-start.13 = (f32[2,2,16,128]{3,2,1,0:T(8,128)S(1)}, f32[2,2,16,128]{3,2,1,0:T(8,128)S(1)}, u32[]{:S(2)}, u32[]{:S(2)}) collective-permute-start(f32[2,2,16,128]{3,2,1,0:T(8,128)S(1)} %get-tuple-element.50), channel_id=1, source_target_pairs={{0,2},{1,3},{2,0},{3,1},{4,6},{5,7},{6,4},{7,5},{8,10},{9,11},{10,... | collective-permute-start | bytes 98312 | tf_op jit(solution)/shard_map/residual/ppermute | solution.py:305
  79.0 2.0 %collective-permute-start.14 = (f32[2,2,16,128]{3,2,1,0:T(8,128)S(1)}, f32[2,2,16,128]{3,2,1,0:T(8,128)S(1)}, u32[]{:S(2)}, u32[]{:S(2)}) collective-permute-start(f32[2,2,16,128]{3,2,1,0:T(8,128)S(1)} %get-tuple-element.51), channel_id=1, source_target_pairs={{0,3},{1,0},{2,1},{3,2},{4,7},{5,4},{6,5},{7,6},{8,11},{9,8},{10,9... | collective-permute-start | bytes 98312 | tf_op jit(solution)/shard_map/residual/ppermute | solution.py:305
  81.0 5.6 %all-to-all-done.2.residual_ref = bf16[8,128,128]{2,1,0:T(8,128)(2,1)S(1)} async-done(((bf16[8,128,128]{2,1,0:T(8,128)(2,1)}), bf16[8,128,128]{2,1,0:T(8,128)(2,1)S(1)}, u32[]{:S(2)}, u32[]{:S(2)}) %all-to-all-start.2) | async-done | bytes 262176 | tf_op jit(solution)/shard_map/residual/all_to_all | solution.py:384
  86.6 2.2 %pick_tiles.1 = bf16[32,4,16,256]{3,2,1,0:T(8,128)(2,1)} custom-call(s32[3]{0:T(128)S(1)} %pad_add_fusion.1.place_ref, s32[4,32]{1,0:T(4,128)S(1)} %pad_add_fusion.target_ref, bf16[8,128,128]{2,1,0:T(8,128)(2,1)S(1)} %all-to-all-done.2.residual_ref), custom_call_target="tpu_custom_call" | custom-call | flops 1000000 | bytes 1048576 | tf_op jit(solution)/shard_map/pick/pick_tiles/pallas_call | solution.py:387
  88.8 9.3 %all-to-all-start.3 = ((bf16[32,4,16,256]{3,2,1,0:T(8,128)(2,1)}), bf16[32,4,16,256]{3,2,1,0:T(8,128)(2,1)S(1)}, u32[]{:S(2)}, u32[]{:S(2)}) async-start(bf16[32,4,16,256]{3,2,1,0:T(8,128)(2,1)} %pick_tiles.1), calls=%async_computation.3 | async-start | bytes 2097152 | tf_op jit(solution)/shard_map/pick/all_to_all | solution.py:396
  99.7 1.1 copy.17
  100.8 1.5 %copy.18.radon_ref = bf16[256,2048]{1,0:T(8,128)(2,1)S(1)} copy(bf16[256,2048]{0,1:T(8,128)(2,1)} %bitcast.34) | data formatting | bytes 2097152 | tf_op jit(solution)/shard_map/back_project/reshape | solution.py:405
  102.3 5.0 %collective-permute-done.15.theirs_ref = f32[4,2,16,128]{3,2,1,0:T(8,128)S(1)} collective-permute-done((f32[4,2,16,128]{3,2,1,0:T(8,128)S(1)}, f32[4,2,16,128]{3,2,1,0:T(8,128)S(1)}, u32[]{:S(2)}, u32[]{:S(2)}) %collective-permute-start.15) | collective-permute-done | bytes 65568 | tf_op jit(solution)/shard_map/updates/ppermute | solution.py:305
  107.3 1.2 %updates.1 = (f32[128,128]{1,0:T(8,128)}, f32[128,128]{1,0:T(8,128)}) custom-call(s32[3]{0:T(128)S(1)} %pad_add_fusion.1.place_ref, f32[2,2,16,128]{3,2,1,0:T(8,128)S(1)} %get-tuple-element.52.own_ref, f32[2,2,16,128]{3,2,1,0:T(8,128)S(1)} %copy-done.7, f32[2,2,16,128]{3,2,1,0:T(8,128)S(1)} %copy-done.9, ...), custom_call_target="tpu_custom_call" | custom-call | flops 1000000 | bytes 1048576 | tf_op jit(solution)/shard_map/updates/updates/pallas_call | solution.py:400
  108.6 5.9 %all-to-all-done.3.picked_ref = bf16[32,4,16,256]{3,2,1,0:T(8,128)(2,1)S(1)} async-done(((bf16[32,4,16,256]{3,2,1,0:T(8,128)(2,1)}), bf16[32,4,16,256]{3,2,1,0:T(8,128)(2,1)S(1)}, u32[]{:S(2)}, u32[]{:S(2)}) %all-to-all-start.3) | async-done | bytes 1048608 | tf_op jit(solution)/shard_map/pick/all_to_all | solution.py:396
  114.4 1.1 back_project.1
  (80 shorter events, 7.4 us)
Async XLA Ops:
  4.7 8.8 %copy-start.4 = (f32[1,64,2,128]{3,2,1,0:T(2,128)S(1)}, f32[1,64,2,128]{3,2,1,0:T(2,128)}, u32[]{:S(2)}) copy-start(f32[1,64,2,128]{3,2,1,0:T(2,128)} %param.17) | copy-start | bytes 196612
  4.7 18.1 %copy-start.5 = (f32[1,64,2,128]{3,2,1,0:T(2,128)S(1)}, f32[1,64,2,128]{3,2,1,0:T(2,128)}, u32[]{:S(2)}) copy-start(f32[1,64,2,128]{3,2,1,0:T(2,128)} %param.18) | copy-start | bytes 196612
  4.7 36.4 %copy-start.10 = (f32[1,8,128,128]{3,2,1,0:T(8,128)S(1)}, f32[1,8,128,128]{3,2,1,0:T(8,128)}, u32[]{:S(2)}) copy-start(f32[1,8,128,128]{3,2,1,0:T(8,128)} %param.14) | copy-start | bytes 1572868
  4.7 36.4 %copy-start.15 = (bf16[256,256]{1,0:T(8,128)(2,1)S(1)}, bf16[256,256]{1,0:T(8,128)(2,1)}, u32[]{:S(2)}) copy-start(bf16[256,256]{1,0:T(8,128)(2,1)} %constant.96.clone.al_ref) | copy-start | bytes 393220
  4.7 45.2 %all-to-all-start = ((bf16[32,4,16,256]{3,2,1,0:T(8,128)(2,1)}), bf16[32,4,16,256]{3,2,1,0:T(8,128)(2,1)S(1)}, u32[]{:S(2)}, u32[]{:S(2)}) async-start(bf16[32,4,16,256]{3,2,1,0:T(8,128)(2,1)} %ray_sums.1), calls=%async_computation | async-start | bytes 2097152 | tf_op jit(solution)/shard_map/ray_sums/all_to_all | solution.py:331
  13.4 9.3 %collective-permute-start = (f32[128,128]{1,0:T(8,128)S(1)}, f32[128,128]{1,0:T(8,128)S(1)}, u32[]{:S(2)}, u32[]{:S(2)}) collective-permute-start(f32[128,128]{1,0:T(8,128)S(1)} %bitcast.28), channel_id=1, source_target_pairs={{0,4},{4,0},{1,5},{5,1},{2,6},{6,2},{3,7},{7,3},{8,12},{12,8},{9,1... | collective-permute-start | bytes 196616 | tf_op jit(solution)/shard_map/fields/ppermute | solution.py:305
  21.1 20.0 %copy-start.14 = (bf16[256,256]{1,0:T(8,128)(2,1)S(1)}, bf16[256,256]{1,0:T(8,128)(2,1)}, u32[]{:S(2)}) copy-start(bf16[256,256]{1,0:T(8,128)(2,1)} %constant.97.clone.bh_ref) | copy-start | bytes 393220
  22.7 18.3 %copy-start.13 = (bf16[256,256]{1,0:T(8,128)(2,1)S(1)}, bf16[256,256]{1,0:T(8,128)(2,1)}, u32[]{:S(2)}) copy-start(bf16[256,256]{1,0:T(8,128)(2,1)} %constant.98.clone.bl_ref) | copy-start | bytes 393220
  23.3 17.7 %copy-start.11 = (f32[2,128,128]{2,1,0:T(8,128)S(1)}, f32[2,128,128]{2,1,0:T(8,128)}, u32[]{:S(2)}) copy-start(f32[2,128,128]{2,1,0:T(8,128)} %probe_ref.1) | copy-start | bytes 393220
  23.3 9.9 %collective-permute-start.1 = (f32[296,128]{1,0:T(8,128)S(1)}, f32[296,128]{1,0:T(8,128)S(1)}, u32[]{:S(2)}, u32[]{:S(2)}) collective-permute-start(f32[296,128]{1,0:T(8,128)S(1)} %get-tuple-element.38), channel_id=1, source_target_pairs={{0,1},{1,2},{2,3},{3,0},{4,5},{5,6},{6,7},{7,4},{8,9},{9,10},{10,1... | collective-permute-start | bytes 454664 | tf_op jit(solution)/shard_map/fields/ppermute | solution.py:305
  24.7 12.0 %collective-permute-start.2 = (f32[296,128]{1,0:T(8,128)S(1)}, f32[296,128]{1,0:T(8,128)S(1)}, u32[]{:S(2)}, u32[]{:S(2)}) collective-permute-start(f32[296,128]{1,0:T(8,128)S(1)} %get-tuple-element.39), channel_id=1, source_target_pairs={{0,2},{1,3},{2,0},{3,1},{4,6},{5,7},{6,4},{7,5},{8,10},{9,11},{10,... | collective-permute-start | bytes 454664 | tf_op jit(solution)/shard_map/fields/ppermute | solution.py:305
  27.1 9.6 %collective-permute-start.3 = (f32[296,128]{1,0:T(8,128)S(1)}, f32[296,128]{1,0:T(8,128)S(1)}, u32[]{:S(2)}, u32[]{:S(2)}) collective-permute-start(f32[296,128]{1,0:T(8,128)S(1)} %get-tuple-element.40), channel_id=1, source_target_pairs={{0,3},{1,0},{2,1},{3,2},{4,7},{5,4},{6,5},{7,6},{8,11},{9,8},{10,9... | collective-permute-start | bytes 454664 | tf_op jit(solution)/shard_map/fields/ppermute | solution.py:305
  36.9 11.3 %collective-permute-start.6 = (s32[4,8]{1,0:T(4,128)S(1)}, s32[4,8]{1,0:T(4,128)S(1)}, u32[]{:S(2)}, u32[]{:S(2)}) collective-permute-start(s32[4,8]{1,0:T(4,128)S(1)} %bitcast.38), channel_id=1, source_target_pairs={{0,192},{64,0},{128,64},{192,128},{1,193},{65,1},{129,65},{193,129... | collective-permute-start | bytes 392 | tf_op jit(solution)/shard_map/targets/ppermute | solution.py:305
  39.7 10.0 %collective-permute-start.5 = (s32[4,8]{1,0:T(4,128)S(1)}, s32[4,8]{1,0:T(4,128)S(1)}, u32[]{:S(2)}, u32[]{:S(2)}) collective-permute-start(s32[4,8]{1,0:T(4,128)S(1)} %bitcast.37), channel_id=1, source_target_pairs={{0,128},{64,192},{128,0},{192,64},{1,129},{65,193},{129,1},{193,65... | collective-permute-start | bytes 392 | tf_op jit(solution)/shard_map/targets/ppermute | solution.py:305
  39.7 10.0 %collective-permute-start.4 = (s32[4,8]{1,0:T(4,128)S(1)}, s32[4,8]{1,0:T(4,128)S(1)}, u32[]{:S(2)}, u32[]{:S(2)}) collective-permute-start(s32[4,8]{1,0:T(4,128)S(1)} %bitcast.36), channel_id=1, source_target_pairs={{0,64},{64,128},{128,192},{192,0},{1,65},{65,129},{129,193},{193,1... | collective-permute-start | bytes 392 | tf_op jit(solution)/shard_map/targets/ppermute | solution.py:305
  46.7 12.1 %collective-permute-start.7 = (bf16[2,128,128]{2,1,0:T(8,128)(2,1)S(1)}, bf16[2,128,128]{2,1,0:T(8,128)(2,1)S(1)}, u32[]{:S(2)}, u32[]{:S(2)}) collective-permute-start(bf16[2,128,128]{2,1,0:T(8,128)(2,1)S(1)} %get-tuple-element.42), channel_id=1, source_target_pairs={{0,1},{1,2},{2,3},{3,0},{4,5},{5,6},{6,7},{7,4},{8,9},{9,10},{10,1... | collective-permute-start | bytes 196616 | tf_op jit(solution)/shard_map/frames/ppermute | solution.py:305
  46.7 12.0 %collective-permute-start.8 = (bf16[2,128,128]{2,1,0:T(8,128)(2,1)S(1)}, bf16[2,128,128]{2,1,0:T(8,128)(2,1)S(1)}, u32[]{:S(2)}, u32[]{:S(2)}) collective-permute-start(bf16[2,128,128]{2,1,0:T(8,128)(2,1)S(1)} %get-tuple-element.43), channel_id=1, source_target_pairs={{0,2},{1,3},{2,0},{3,1},{4,6},{5,7},{6,4},{7,5},{8,10},{9,11},{10,... | collective-permute-start | bytes 196616 | tf_op jit(solution)/shard_map/frames/ppermute | solution.py:305
  48.2 10.5 %collective-permute-start.9 = (bf16[2,128,128]{2,1,0:T(8,128)(2,1)S(1)}, bf16[2,128,128]{2,1,0:T(8,128)(2,1)S(1)}, u32[]{:S(2)}, u32[]{:S(2)}) collective-permute-start(bf16[2,128,128]{2,1,0:T(8,128)(2,1)S(1)} %get-tuple-element.44), channel_id=1, source_target_pairs={{0,3},{1,0},{2,1},{3,2},{4,7},{5,4},{6,5},{7,6},{8,11},{9,8},{10,9... | collective-permute-start | bytes 196616 | tf_op jit(solution)/shard_map/frames/ppermute | solution.py:305
  51.9 20.6 %all-to-all-start.1 = ((bf16[8,128,128]{2,1,0:T(8,128)(2,1)}), bf16[8,128,128]{2,1,0:T(8,128)(2,1)S(1)}, u32[]{:S(2)}, u32[]{:S(2)}) async-start(bf16[8,128,128]{2,1,0:T(8,128)(2,1)} %add_tiles.1), calls=%async_computation.1 | async-start | bytes 524288 | tf_op jit(solution)/shard_map/near_sum/all_to_all | solution.py:371
  58.8 12.4 %collective-permute-start.10 = (f32[128,128]{1,0:T(8,128)S(1)}, f32[128,128]{1,0:T(8,128)S(1)}, u32[]{:S(2)}, u32[]{:S(2)}) collective-permute-start(f32[128,128]{1,0:T(8,128)S(1)} %dynamic-slice_bitcast_fusion), channel_id=1, source_target_pairs={{0,4},{4,0},{1,5},{5,1},{2,6},{6,2},{3,7},{7,3},{8,12},{12,8},{9,1... | collective-permute-start | bytes 196616 | tf_op jit(solution)/shard_map/frames/ppermute | solution.py:305
  64.3 8.2 %collective-permute-start.11 = (f32[64,128]{1,0:T(8,128)S(1)}, f32[64,128]{1,0:T(8,128)S(1)}, u32[]{:S(2)}, u32[]{:S(2)}) collective-permute-start(f32[64,128]{1,0:T(8,128)S(1)} %get-tuple-element.46), channel_id=1, source_target_pairs={{0,4},{4,0},{1,5},{5,1},{2,6},{6,2},{3,7},{7,3},{8,12},{12,8},{9,1... | collective-permute-start | bytes 98312 | tf_op jit(solution)/shard_map/frames/ppermute | solution.py:305
  73.8 12.8 %all-to-all-start.2 = ((bf16[8,128,128]{2,1,0:T(8,128)(2,1)}), bf16[8,128,128]{2,1,0:T(8,128)(2,1)S(1)}, u32[]{:S(2)}, u32[]{:S(2)}) async-start(bf16[8,128,128]{2,1,0:T(8,128)(2,1)} %broadcast_in_dim.4), calls=%async_computation.2 | async-start | bytes 524288 | tf_op jit(solution)/shard_map/residual/all_to_all | solution.py:384
  77.2 11.5 %collective-permute-start.12 = (f32[2,2,16,128]{3,2,1,0:T(8,128)S(1)}, f32[2,2,16,128]{3,2,1,0:T(8,128)S(1)}, u32[]{:S(2)}, u32[]{:S(2)}) collective-permute-start(f32[2,2,16,128]{3,2,1,0:T(8,128)S(1)} %get-tuple-element.49), channel_id=1, source_target_pairs={{0,1},{1,2},{2,3},{3,0},{4,5},{5,6},{6,7},{7,4},{8,9},{9,10},{10,1... | collective-permute-start | bytes 98312 | tf_op jit(solution)/shard_map/residual/ppermute | solution.py:305
  77.6 11.1 %collective-permute-start.13 = (f32[2,2,16,128]{3,2,1,0:T(8,128)S(1)}, f32[2,2,16,128]{3,2,1,0:T(8,128)S(1)}, u32[]{:S(2)}, u32[]{:S(2)}) collective-permute-start(f32[2,2,16,128]{3,2,1,0:T(8,128)S(1)} %get-tuple-element.50), channel_id=1, source_target_pairs={{0,2},{1,3},{2,0},{3,1},{4,6},{5,7},{6,4},{7,5},{8,10},{9,11},{10,... | collective-permute-start | bytes 98312 | tf_op jit(solution)/shard_map/residual/ppermute | solution.py:305
  79.0 9.7 %collective-permute-start.14 = (f32[2,2,16,128]{3,2,1,0:T(8,128)S(1)}, f32[2,2,16,128]{3,2,1,0:T(8,128)S(1)}, u32[]{:S(2)}, u32[]{:S(2)}) collective-permute-start(f32[2,2,16,128]{3,2,1,0:T(8,128)S(1)} %get-tuple-element.51), channel_id=1, source_target_pairs={{0,3},{1,0},{2,1},{3,2},{4,7},{5,4},{6,5},{7,6},{8,11},{9,8},{10,9... | collective-permute-start | bytes 98312 | tf_op jit(solution)/shard_map/residual/ppermute | solution.py:305
  88.8 9.4 %copy-start.6 = (f32[2,2,16,128]{3,2,1,0:T(8,128)}, f32[2,2,16,128]{3,2,1,0:T(8,128)S(1)}, u32[]{:S(2)}) copy-start(f32[2,2,16,128]{3,2,1,0:T(8,128)S(1)} %collective-permute-done.12.one_ref) | copy-start | bytes 98308
  88.8 9.4 %copy-start.8 = (f32[2,2,16,128]{3,2,1,0:T(8,128)}, f32[2,2,16,128]{3,2,1,0:T(8,128)S(1)}, u32[]{:S(2)}) copy-start(f32[2,2,16,128]{3,2,1,0:T(8,128)S(1)} %collective-permute-done.13.two_ref) | copy-start | bytes 98308
  88.8 10.9 %copy-start.1 = (bf16[1,32,2,32,256]{4,3,2,1,0:T(8,128)(2,1)S(1)}, bf16[1,32,2,32,256]{4,3,2,1,0:T(8,128)(2,1)}, u32[]{:S(2)}) copy-start(bf16[1,32,2,32,256]{4,3,2,1,0:T(8,128)(2,1)} %param.20) | copy-start | bytes 3145732
  88.8 25.6 %all-to-all-start.3 = ((bf16[32,4,16,256]{3,2,1,0:T(8,128)(2,1)}), bf16[32,4,16,256]{3,2,1,0:T(8,128)(2,1)S(1)}, u32[]{:S(2)}, u32[]{:S(2)}) async-start(bf16[32,4,16,256]{3,2,1,0:T(8,128)(2,1)} %pick_tiles.1), calls=%async_computation.3 | async-start | bytes 2097152 | tf_op jit(solution)/shard_map/pick/all_to_all | solution.py:396
  98.9 8.5 %collective-permute-start.15 = (f32[4,2,16,128]{3,2,1,0:T(8,128)S(1)}, f32[4,2,16,128]{3,2,1,0:T(8,128)S(1)}, u32[]{:S(2)}, u32[]{:S(2)}) collective-permute-start(f32[4,2,16,128]{3,2,1,0:T(8,128)S(1)} %pad_maximum_fusion), channel_id=1, source_target_pairs={{0,4},{4,0},{1,5},{5,1},{2,6},{6,2},{3,7},{7,3},{8,12},{12,8},{9,1... | collective-permute-start | bytes 196616 | tf_op jit(solution)/shard_map/updates/ppermute | solution.py:305
  100.8 6.5 %copy-start.9 = (f32[2,2,16,128]{3,2,1,0:T(8,128)S(1)}, f32[2,2,16,128]{3,2,1,0:T(8,128)}, u32[]{:S(2)}) copy-start(f32[2,2,16,128]{3,2,1,0:T(8,128)} %copy-done.8) | copy-start | bytes 98308
  102.3 12.1 %copy-start.3 = (f32[256,2,128]{2,1,0:T(2,128)S(1)}, f32[256,2,128]{2,1,0:T(2,128)}, u32[]{:S(2)}) copy-start(f32[256,2,128]{2,1,0:T(2,128)} %param.19) | copy-start | bytes 786436
  (8 other events, 13.1 us)

commit v3 on v2

--- a/solution.py
+++ b/solution.py
@@ -29,6 +29,8 @@
 penalty = 1.0
 object_step = 0.1
 volume_step = 1.0
+keep = 1.0 - object_step
+share = object_step / keep
 f32 = jnp.float32
 bf16 = jnp.bfloat16
 
@@ -79,39 +81,41 @@
                 out_ref[xc * Y + y, zl] = jnp.concatenate([low, high], axis=0).astype(bf16)
 
 
-def first_row(place_ref, target_ref, zl, y, xc):
-    back_zl = lax.rem(place_ref[2] + ZL - zl, ZL)
-    back_y = lax.rem(place_ref[1] + Y - y, Y)
-    return pl.multiple_of(target_ref[back_zl, back_y * XC + xc] * QR, QR)
-
-
-def add_tiles(place_ref, target_ref, sums_ref, out_ref, total):
+def first_rows(place_ref, target_ref):
+    back_y = [lax.rem(place_ref[1] + Y - y, Y) for y in range(Y)]
+    back_zl = [lax.rem(place_ref[2] + ZL - zl, ZL) * XC for zl in range(ZL)]
+
+    def row(zl, y, xc):
+        return pl.multiple_of(target_ref[back_y[y], back_zl[zl] + xc] * QR, QR)
+
+    return row
+
+
+def add_tiles(place_ref, target_ref, sums_ref, own_ref, one_ref, two_ref, three_ref, out_ref, inter_ref, total):
+    row = first_rows(place_ref, target_ref)
     total[...] = jnp.zeros(total.shape, f32)
-
-    def step(xc, carry):
+    for part in range(2):
+        inter = (own_ref[part] + one_ref[part].astype(f32)) + (two_ref[part].astype(f32) + three_ref[part].astype(f32))
+        inter_ref[part] = inter
+        total[place_ref[2], :, part * NZ : (part + 1) * NZ] = inter * share
+    for xc in range(XC):
         for y in range(Y):
             for zl in range(ZL):
-                row = first_row(place_ref, target_ref, zl, y, xc)
-                total[zl, pl.ds(row, HITS * QR), :] += sums_ref[xc * Y + y, zl].astype(f32)
-        return carry
-
-    lax.fori_loop(0, XC, step, 0)
+                total[zl, pl.ds(row(zl, y, xc), HITS * QR), :] += sums_ref[xc * Y + y, zl].astype(f32)
     for zh in range(ZH):
         for zl in range(ZL):
             out_ref[zh * ZL + zl] = total[zl, :, zh * NZ : (zh + 1) * NZ].astype(bf16)
 
 
 def residual_part(
-    place_ref, sums_ref, inter_ref, mine_ref, theirs_ref, residual_ref, own_ref, one_ref, two_ref, three_ref, both
+    place_ref, sums_ref, inter_ref, mine_ref, theirs_ref, residual_ref, own_ref, one_ref, two_ref, three_ref, joint
 ):
     zh = place_ref[0]
     y = place_ref[1]
-    projection = sums_ref[0].astype(f32)
+    total = sums_ref[0].astype(f32)
     for source in range(1, DEEP):
-        projection = projection + sums_ref[source].astype(f32)
-    inter = inter_ref[...]
-    both[0] = projection
-    both[1] = inter
+        total = total + sums_ref[source].astype(f32)
+    joint[...] = total
     first = zh == 0
     drift = jnp.concatenate(
         [
@@ -120,14 +124,16 @@
         ],
         axis=0,
     )
-    gap = projection - drift
-    residual_ref[...] = (gap + object_step * (inter - gap)).astype(bf16)
+    residual = (keep * (total - drift)).astype(bf16)
+    for copy in range(DEEP):
+        residual_ref[copy] = residual
     for ahead, ref in enumerate((own_ref, one_ref, two_ref, three_ref)):
         for other in range(ZH):
             owner = lax.rem(zh + other, ZH) * Y + lax.rem(y + ahead, Y)
             rows = pl.ds(pl.multiple_of(owner * 2 * QR, 2 * QR), 2 * QR)
-            ref[other, 0] = both[0, rows, :]
-            ref[other, 1] = both[1, rows, :]
+            ref[other, 0] = joint[rows, :]
+            for part in range(2):
+                ref[other, 1 + part] = inter_ref[part, rows, :]
 
 
 def pick_tiles(place_ref, target_ref, residual_ref, out_ref, rows_ref):
@@ -136,14 +142,11 @@
             [residual_ref[zl].astype(f32), residual_ref[ZL + zl].astype(f32)], axis=1
         )
 
-    def step(xc, carry):
+    row = first_rows(place_ref, target_ref)
+    for xc in range(XC):
         for y in range(Y):
             for zl in range(ZL):
-                row = first_row(place_ref, target_ref, zl, y, xc)
-                out_ref[xc * Y + y, zl] = rows_ref[zl, pl.ds(row, HITS * QR), :].astype(bf16)
-        return carry
-
-    lax.fori_loop(0, XC, step, 0)
+                out_ref[xc * Y + y, zl] = rows_ref[zl, pl.ds(row(zl, y, xc), HITS * QR), :].astype(bf16)
 
 
 def back_project(radon_ref, picked_ref, volume_ref, out_ref):
@@ -168,8 +171,9 @@
             part = lax.rem(zh + other, ZH)
             for tile in range(2):
                 piece = slice(tile * QR, (tile + 1) * QR)
-                projection = theirs_ref[back, 0, piece, :] if other else ref[0, 0, piece, :]
-                inter = theirs_ref[back, 1, piece, :] if other else ref[0, 1, piece, :]
+                inter = ref[0, 1 + part, piece, :] + theirs_ref[back, 1 + part, piece, :]
+                joint = theirs_ref[back, 0, piece, :] if other else ref[0, 0, piece, :]
+                projection = joint - share * inter
                 rows = pl.ds((tile * RAYS + source * QR) * 2 + part, QR, stride=2)
                 field = object_ref[rows, :]
                 dual = dual_ref[rows, :]
@@ -324,25 +328,33 @@
     object_rows = object_field.reshape(128, NZ)
     dual_rows = dual_field.reshape(128, NZ)
 
+    with jax.named_scope("targets"):
+        own_targets = tile_range.reshape(ZL, XC)
+        ahead = [lax.dynamic_index_in_dim(own_targets, (zl + k) % ZL, 0, keepdims=False) for k in range(ZL)]
+        targets = jnp.stack([ahead[0]] + [shifted(ahead[k], "zl", ZL, k) for k in range(1, ZL)])
+        target_rows = jnp.zeros((QR, NZ), f32).at[0, : ZL * XC].set(targets.reshape(ZL * XC).astype(f32))
+
+    with jax.named_scope("fields"):
+        object_theirs = across(object_rows)
+
     with jax.named_scope("ray_sums"):
+        radon_first, target_rows = lax.optimization_barrier((radon, target_rows))
         sums = call(ray_sums, shape(NEAR, ZL, HITS * QR, 2 * NZ, dtype=bf16), 0, 2, flops=2 * 2048 * 256 * 256)(
-            radon, volume_rows
-        )
-        near_sums = lax.all_to_all(sums, CROSS, 0, 0, tiled=True)
+            radon_first, volume_rows
+        )
 
     with jax.named_scope("fields"):
-        own_targets = jnp.zeros((QR, NZ), f32).at[0, : ZL * XC].set(tile_range.reshape(ZL * XC).astype(f32))
         packed = call(
             pack, (shape(SENT_ROWS, NZ),) * Y, 1, 4, scratch=[pltpu.VMEM((128, NZ), f32)], flops=1_000_000
-        )(place, object_rows, across(object_rows), dual_rows, own_targets)
+        )(place, object_rows, object_theirs, dual_rows, target_rows)
+        sums, packed = lax.optimization_barrier((sums, packed))
         fields = round_y(packed)
 
+    with jax.named_scope("ray_sums"):
+        near_sums = lax.all_to_all(sums, CROSS, 0, 0, tiled=True)
+
     with jax.named_scope("targets"):
-        tables = jnp.stack([field[FIELD_ROWS + DRIFT_ROWS, : ZL * XC] for field in fields])
-        tables = tables.reshape(Y, ZL, XC).astype(jnp.int32)
-        ahead = [lax.dynamic_index_in_dim(tables, (zl + k) % ZL, 1, keepdims=False) for k in range(ZL)]
-        targets = jnp.stack([ahead[0]] + [shifted(ahead[k], "zl", ZL, k) for k in range(1, ZL)])
-        targets = targets.reshape(ZL, Y * XC)
+        tables = jnp.stack([field[FIELD_ROWS + DRIFT_ROWS, : ZL * XC] for field in fields]).astype(jnp.int32)
 
     with jax.named_scope("frames"):
         *inter_parts, drift_mine, drift_sent = call(
@@ -353,34 +365,31 @@
             scratch=[pltpu.VMEM((NDET, NZ), f32)] * 4,
             flops=1_600_000_000,
         )(place, positions, *fields, probe_field, measured[0], ah, al, bh, bl)
-        inter_sum = sum(piece.astype(f32) for piece in round_y(inter_parts))
-        inter_mine = lax.dynamic_index_in_dim(inter_sum, zh, 0, keepdims=False)
-        inter_sent = lax.dynamic_index_in_dim(inter_sum, 1 - zh, 0, keepdims=False)
-        inter = inter_mine + across(inter_sent)
+        inter_parts = round_y(inter_parts)
         drift_theirs = across(drift_sent)
 
     with jax.named_scope("near_sum"):
-        dense = call(
+        dense, inter = call(
             add_tiles,
-            shape(DEEP, 128, NZ, dtype=bf16),
+            (shape(DEEP, 128, NZ, dtype=bf16), shape(2, 128, NZ)),
             2,
-            1,
+            5,
             scratch=[pltpu.VMEM((ZL, 128, 2 * NZ), f32)],
             flops=1_000_000,
-        )(place, targets, near_sums)
+        )(place, tables, near_sums, *inter_parts)
+        dense, drift_theirs = lax.optimization_barrier((dense, drift_theirs))
         far_sums = lax.all_to_all(dense, ALONG, 0, 0, tiled=True)
 
     with jax.named_scope("residual"):
-        residual, *kept = call(
+        copies, *kept = call(
             residual_part,
-            (shape(128, NZ, dtype=bf16),) + (shape(ZH, 2, 2 * QR, NZ),) * Y,
+            (shape(DEEP, 128, NZ, dtype=bf16),) + (shape(ZH, 3, 2 * QR, NZ),) * Y,
             1,
             4,
-            scratch=[pltpu.VMEM((2, 128, NZ), f32)],
+            scratch=[pltpu.VMEM((128, NZ), f32)],
             flops=1_000_000,
         )(place, far_sums, inter, drift_mine, drift_theirs)
         kept = round_y(kept)
-        copies = jnp.broadcast_to(residual, (DEEP, 128, NZ))
         residuals = lax.all_to_all(copies, ALONG, 0, 0, tiled=True)
 
     with jax.named_scope("pick"):
@@ -391,7 +400,7 @@
             1,
             scratch=[pltpu.VMEM((ZL, 128, 2 * NZ), f32)],
             flops=1_000_000,
-        )(place, targets, residuals)
+        )(place, tables, residuals)
         picked, kept = lax.optimization_barrier((picked, kept))
         returned = lax.all_to_all(picked, CROSS, 0, 0, tiled=True)
 

time: 116 us -> 123 us (1.060)
  blocking collectives: 0 us -> 13.1 us
  starting transfers between devices: 57.5 us -> 50 us
  waiting for transfers between devices: 34.4 us -> 36.7 us
  local copies, waits for them, and re-layouts: 8.34 us -> 6.43 us
    all_to_all x0 -> x1, blocking collectives: none -> 13.1 us  [body(): far_sums = lax.all_to_all(dense, ALONG, 0, 0, tiled=True)]
    all_to_all x1 -> x0, starting transfers between devices: 6.8 us -> none  [body(): far_sums = lax.all_to_all(dense, ALONG, 0, 0, tiled=True)]
    ppermute x16 -> x15, starting transfers between devices: 29.2 us -> 26.3 us  [shifted(): lax.ppermute(value, axis, [(i, (i + step) % length) for i in range(length)])]
    all_to_all x1, starting transfers between devices: 9.3 us -> 11.3 us  [body(): returned = lax.all_to_all(picked, CROSS, 0, 0, tiled=True)]
    ppermute x16 -> x15, waiting for transfers between devices: 22.9 us -> 24.7 us  [shifted(): lax.ppermute(value, axis, [(i, (i + step) % length) for i in range(length)])]
    unnamed x36 -> x37, local copies, waits for them, and re-layouts: 3.79 us -> 2.91 us
  transfers between devices with their start and end apart: 20 -> 18, of which waited for: 8 -> 8; matrix products, arithmetic and copies ran while one was open for 3% -> 2% of each run, Pallas kernels for 9% -> 9%
where the time goes in v3:
time: 123 us; the launch traced here: 122 us
  starting transfers between devices  50 us (41%)
  waiting for transfers between devices  36.7 us (30%)
  Pallas kernels  14 us (11%)
  blocking collectives  13.1 us (11%)
  local copies, waits for them, and re-layouts  6.43 us (5%)
    ppermute x15, starting transfers between devices, shifted(): lax.ppermute(value, axis, [(i, (i + step) % length) for i in range(length)])  26.3 us
    ppermute x15, waiting for transfers between devices, shifted(): lax.ppermute(value, axis, [(i, (i + step) % length) for i in range(length)])  24.7 us
    all_to_all x1, blocking collectives, body(): far_sums = lax.all_to_all(dense, ALONG, 0, 0, tiled=True)  13.1 us
    all_to_all x1, starting transfers between devices, body(): returned = lax.all_to_all(picked, CROSS, 0, 0, tiled=True)  11.3 us
    all_to_all x1, starting transfers between devices, body(): near_sums = lax.all_to_all(sums, CROSS, 0, 0, tiled=True)  9.02 us
    all_to_all x1, waiting for transfers between devices, body(): residuals = lax.all_to_all(copies, ALONG, 0, 0, tiled=True)  6.05 us
    all_to_all x1, waiting for transfers between devices, body(): returned = lax.all_to_all(picked, CROSS, 0, 0, tiled=True)  5.91 us
    pallas_call x1, Pallas kernels, body(): call(frame_gradients, (shape(2, 128, NZ),) + (shape(2, 128, NZ, dtype=bf1...  4.67 us
  transfers between devices with their start and end apart: 18, of which 8 were waited for; matrix products, arithmetic and copies ran while one was open for 2% of the time, Pallas kernels for 9%

profile of v3, /device:TPU:1, one launch (start us, length us, event | category | flops | bytes accessed | tf_op | source)
XLA Modules:
  0.0 122.1 jit_solution(3341746289918490787)
XLA Ops:
  2.1 5.3 %collective-permute-start.2 = (s32[8]{0:T(128)S(1)}, s32[8]{0:T(128)S(1)}, u32[]{:S(2)}, u32[]{:S(2)}) collective-permute-start(s32[8]{0:T(128)S(1)} %get-tuple-element.82), channel_id=1, source_target_pairs={{0,192},{64,0},{128,64},{192,128},{1,193},{65,1},{129,65},{193,129... | collective-permute-start | bytes 104 | tf_op jit(solution)/shard_map/targets/ppermute | solution.py:309
  7.8 4.8 %collective-permute-start.3 = (f32[128,128]{1,0:T(8,128)S(1)}, f32[128,128]{1,0:T(8,128)S(1)}, u32[]{:S(2)}, u32[]{:S(2)}) collective-permute-start(f32[128,128]{1,0:T(8,128)S(1)} %bitcast.29), channel_id=1, source_target_pairs={{0,4},{4,0},{1,5},{5,1},{2,6},{6,2},{3,7},{7,3},{8,12},{12,8},{9,1... | collective-permute-start | bytes 196616 | tf_op jit(solution)/shard_map/fields/ppermute | solution.py:309
  12.8 1.2 %copy-done = bf16[1,32,2,32,256]{4,3,2,1,0:T(8,128)(2,1)S(1)} copy-done((bf16[1,32,2,32,256]{4,3,2,1,0:T(8,128)(2,1)S(1)}, bf16[1,32,2,32,256]{4,3,2,1,0:T(8,128)(2,1)}, u32[]{:S(2)}) %copy-start) | copy-done | bytes 1048600
  14.0 0.9 copy-done.2
  15.0 1.9 %ray_sums.1 = bf16[32,4,16,256]{3,2,1,0:T(8,128)(2,1)} custom-call(bf16[32,2,32,256]{3,2,1,0:T(8,128)(2,1)S(1)} %bitcast.25, f32[512,128]{1,0:T(8,128)S(1)} %bitcast.27), custom_call_target="tpu_custom_call" | custom-call | flops 268435456 | bytes 1048576 | tf_op jit(solution)/shard_map/ray_sums/ray_sums/pallas_call | solution.py:342
  17.5 9.0 %all-to-all-start = ((bf16[32,4,16,256]{3,2,1,0:T(8,128)(2,1)}), bf16[32,4,16,256]{3,2,1,0:T(8,128)(2,1)S(1)}, u32[]{:S(2)}, u32[]{:S(2)}) async-start(bf16[32,4,16,256]{3,2,1,0:T(8,128)(2,1)} %ray_sums.1), calls=%async_computation | async-start | bytes 2097152 | tf_op jit(solution)/shard_map/ray_sums/all_to_all | solution.py:354
  26.5 1.5 %collective-permute-start.4 = (f32[296,128]{1,0:T(8,128)S(1)}, f32[296,128]{1,0:T(8,128)S(1)}, u32[]{:S(2)}, u32[]{:S(2)}) collective-permute-start(f32[296,128]{1,0:T(8,128)S(1)} %get-tuple-element.55), channel_id=1, source_target_pairs={{0,1},{1,2},{2,3},{3,0},{4,5},{5,6},{6,7},{7,4},{8,9},{9,10},{10,1... | collective-permute-start | bytes 454664 | tf_op jit(solution)/shard_map/fields/ppermute | solution.py:309
  28.0 2.4 %collective-permute-start.5 = (f32[296,128]{1,0:T(8,128)S(1)}, f32[296,128]{1,0:T(8,128)S(1)}, u32[]{:S(2)}, u32[]{:S(2)}) collective-permute-start(f32[296,128]{1,0:T(8,128)S(1)} %get-tuple-element.56), channel_id=1, source_target_pairs={{0,2},{1,3},{2,0},{3,1},{4,6},{5,7},{6,4},{7,5},{8,10},{9,11},{10,... | collective-permute-start | bytes 454664 | tf_op jit(solution)/shard_map/fields/ppermute | solution.py:309
  30.4 1.2 collective-permute-start.6
  31.6 12.9 %collective-permute-done.4.one_field = f32[296,128]{1,0:T(8,128)S(1)} collective-permute-done((f32[296,128]{1,0:T(8,128)S(1)}, f32[296,128]{1,0:T(8,128)S(1)}, u32[]{:S(2)}, u32[]{:S(2)}) %collective-permute-start.4) | collective-permute-done | bytes 151584 | tf_op jit(solution)/shard_map/fields/ppermute | solution.py:309
  44.5 3.5 %collective-permute-done.5.two_field = f32[296,128]{1,0:T(8,128)S(1)} collective-permute-done((f32[296,128]{1,0:T(8,128)S(1)}, f32[296,128]{1,0:T(8,128)S(1)}, u32[]{:S(2)}, u32[]{:S(2)}) %collective-permute-start.5) | collective-permute-done | bytes 151584 | tf_op jit(solution)/shard_map/fields/ppermute | solution.py:309
  48.1 4.7 %frame_gradients.1 = (f32[2,128,128]{2,1,0:T(8,128)S(1)}, bf16[2,128,128]{2,1,0:T(8,128)(2,1)S(1)}, bf16[2,128,128]{2,1,0:T(8,128)(2,1)S(1)}, bf16[2,128,128]{2,...) custom-call(s32[3]{0:T(128)S(1)} %pad_add_fusion.place_ref, s32[1,8]{1,0:T(1,128)S(1)} %copy-done.12, ...), custom_call_target="tpu_custom_call" | custom-call | flops 1600000000 | bytes 1048576 | tf_op jit(solution)/shard_map/frames/frame_gradients/pallas_call | solution.py:360
  52.8 4.0 %collective-permute-start.10 = (f32[64,128]{1,0:T(8,128)S(1)}, f32[64,128]{1,0:T(8,128)S(1)}, u32[]{:S(2)}, u32[]{:S(2)}) collective-permute-start(f32[64,128]{1,0:T(8,128)S(1)} %get-tuple-element.64), channel_id=1, source_target_pairs={{0,4},{4,0},{1,5},{5,1},{2,6},{6,2},{3,7},{7,3},{8,12},{12,8},{9,1... | collective-permute-start | bytes 98312 | tf_op jit(solution)/shard_map/frames/ppermute | solution.py:309
  56.8 1.4 %collective-permute-start.8 = (bf16[2,128,128]{2,1,0:T(8,128)(2,1)S(1)}, bf16[2,128,128]{2,1,0:T(8,128)(2,1)S(1)}, u32[]{:S(2)}, u32[]{:S(2)}) collective-permute-start(bf16[2,128,128]{2,1,0:T(8,128)(2,1)S(1)} %get-tuple-element.61), channel_id=1, source_target_pairs={{0,2},{1,3},{2,0},{3,1},{4,6},{5,7},{6,4},{7,5},{8,10},{9,11},{10,... | collective-permute-start | bytes 196616 | tf_op jit(solution)/shard_map/frames/ppermute | solution.py:309
  58.2 1.6 %collective-permute-start.9 = (bf16[2,128,128]{2,1,0:T(8,128)(2,1)S(1)}, bf16[2,128,128]{2,1,0:T(8,128)(2,1)S(1)}, u32[]{:S(2)}, u32[]{:S(2)}) collective-permute-start(bf16[2,128,128]{2,1,0:T(8,128)(2,1)S(1)} %get-tuple-element.62), channel_id=1, source_target_pairs={{0,3},{1,0},{2,1},{3,2},{4,7},{5,4},{6,5},{7,6},{8,11},{9,8},{10,9... | collective-permute-start | bytes 196616 | tf_op jit(solution)/shard_map/frames/ppermute | solution.py:309
  59.8 1.7 %collective-permute-done.7.one_ref = bf16[2,128,128]{2,1,0:T(8,128)(2,1)S(1)} collective-permute-done((bf16[2,128,128]{2,1,0:T(8,128)(2,1)S(1)}, bf16[2,128,128]{2,1,0:T(8,128)(2,1)S(1)}, u32[]{:S(2)}, u32[]{:S(2)}) %collective-permute-start.7) | collective-permute-done | bytes 65568 | tf_op jit(solution)/shard_map/frames/ppermute | solution.py:309
  61.8 0.9 collective-permute-done.9.three_ref
  62.7 1.3 %add_tiles.1 = (bf16[8,128,128]{2,1,0:T(8,128)(2,1)S(1)}, f32[2,128,128]{2,1,0:T(8,128)S(1)}) custom-call(s32[3]{0:T(128)S(1)} %pad_add_fusion.place_ref, s32[4,32]{1,0:T(4,128)S(1)} %maximum_convert_fusion.target_ref, bf16[32,4,16,256]{3,2,1,0:T(8,128)(2,1)S(1)} %all-to-all-done.sums_ref, f32[2,128,128]{2,1,0:T(8,128)S(1)} %get-tuple-element.59.own_ref, ...), custom_call_target="tpu_custom_call" | custom-call | flops 1000000 | bytes 1048576 | tf_op jit(solution)/shard_map/near_sum/add_tiles/pallas_call | solution.py:372
  64.1 13.1 %all_to_all.20.sums_ref = bf16[8,128,128]{2,1,0:T(8,128)(2,1)S(1)} all-to-all(bf16[8,128,128]{2,1,0:T(8,128)(2,1)S(1)} %get-tuple-element.65), channel_id=1, replica_groups=mesh['zl'=4,'x'=4,'c'=2,'zh'=2,'y'=4] {'zh','zl'}, dimensions={0} | all-to-all | bytes 524288 | tf_op jit(solution)/shard_map/near_sum/all_to_all | solution.py:381
  77.2 1.3 %residual_part.1 = (bf16[8,128,128]{2,1,0:T(8,128)(2,1)}, f32[2,3,16,128]{3,2,1,0:T(8,128)S(1)}, f32[2,3,16,128]{3,2,1,0:T(8,128)S(1)}, f32[2,3,16,128]{3,2,1,0:T(8,128)S(1)}, f32[2,3,16,128]{3,2,1,0:T(8,128)S(1)}) custom-call(s32[3]{0:T(128)S(1)} %pad_add_fusion.place_ref, bf16[8,128,128]{2,1,0:T(8,128)(2,1)S(1)} %all_to_all.20.sums_ref, ...), custom_call_target="tpu_custom_call" | custom-call | flops 1000000 | bytes 1048576 | tf_op jit(solution)/shard_map/residual/residual_part/pallas_call | solution.py:384
  78.5 3.4 %all-to-all-start.2 = ((bf16[8,128,128]{2,1,0:T(8,128)(2,1)}), bf16[8,128,128]{2,1,0:T(8,128)(2,1)S(1)}, u32[]{:S(2)}, u32[]{:S(2)}) async-start(bf16[8,128,128]{2,1,0:T(8,128)(2,1)} %get-tuple-element.69), calls=%async_computation.2 | async-start | bytes 524288 | tf_op jit(solution)/shard_map/residual/all_to_all | solution.py:393
  82.5 2.8 %collective-permute-start.12 = (f32[2,3,16,128]{3,2,1,0:T(8,128)S(1)}, f32[2,3,16,128]{3,2,1,0:T(8,128)S(1)}, u32[]{:S(2)}, u32[]{:S(2)}) collective-permute-start(f32[2,3,16,128]{3,2,1,0:T(8,128)S(1)} %get-tuple-element.72), channel_id=1, source_target_pairs={{0,2},{1,3},{2,0},{3,1},{4,6},{5,7},{6,4},{7,5},{8,10},{9,11},{10,... | collective-permute-start | bytes 147464 | tf_op jit(solution)/shard_map/residual/ppermute | solution.py:309
  85.3 6.0 %all-to-all-done.2.residual_ref = bf16[8,128,128]{2,1,0:T(8,128)(2,1)S(1)} async-done(((bf16[8,128,128]{2,1,0:T(8,128)(2,1)}), bf16[8,128,128]{2,1,0:T(8,128)(2,1)S(1)}, u32[]{:S(2)}, u32[]{:S(2)}) %all-to-all-start.2) | async-done | bytes 262176 | tf_op jit(solution)/shard_map/residual/all_to_all | solution.py:393
  91.3 1.9 %pick_tiles.1 = bf16[32,4,16,256]{3,2,1,0:T(8,128)(2,1)} custom-call(s32[3]{0:T(128)S(1)} %pad_add_fusion.place_ref, s32[4,32]{1,0:T(4,128)S(1)} %maximum_convert_fusion.target_ref, bf16[8,128,128]{2,1,0:T(8,128)(2,1)S(1)} %all-to-all-done.2.residual_ref), custom_call_target="tpu_custom_call" | custom-call | flops 1000000 | bytes 1048576 | tf_op jit(solution)/shard_map/pick/pick_tiles/pallas_call | solution.py:396
  93.3 11.3 %all-to-all-start.3 = ((bf16[32,4,16,256]{3,2,1,0:T(8,128)(2,1)}), bf16[32,4,16,256]{3,2,1,0:T(8,128)(2,1)S(1)}, u32[]{:S(2)}, u32[]{:S(2)}) async-start(bf16[32,4,16,256]{3,2,1,0:T(8,128)(2,1)} %pick_tiles.1), calls=%async_computation.3 | async-start | bytes 2097152 | tf_op jit(solution)/shard_map/pick/all_to_all | solution.py:405
  104.7 0.7 slice-done
  105.8 1.1 copy.17
  106.9 1.5 %copy.18.radon_ref = bf16[256,2048]{1,0:T(8,128)(2,1)S(1)} copy(bf16[256,2048]{0,1:T(8,128)(2,1)} %bitcast.35) | data formatting | bytes 2097152 | tf_op jit(solution)/shard_map/back_project/reshape | solution.py:414
  108.4 5.4 %collective-permute-done.14.theirs_ref = f32[4,3,16,128]{3,2,1,0:T(8,128)S(1)} collective-permute-done((f32[4,3,16,128]{3,2,1,0:T(8,128)S(1)}, f32[4,3,16,128]{3,2,1,0:T(8,128)S(1)}, u32[]{:S(2)}, u32[]{:S(2)}) %collective-permute-start.14) | collective-permute-done | bytes 98336 | tf_op jit(solution)/shard_map/updates/ppermute | solution.py:309
  113.8 1.2 %updates.1 = (f32[128,128]{1,0:T(8,128)}, f32[128,128]{1,0:T(8,128)}) custom-call(s32[3]{0:T(128)S(1)} %pad_add_fusion.place_ref, f32[2,3,16,128]{3,2,1,0:T(8,128)S(1)} %get-tuple-element.74.own_ref, f32[2,3,16,128]{3,2,1,0:T(8,128)S(1)} %copy-done.7, f32[2,3,16,128]{3,2,1,0:T(8,128)S(1)} %copy-done.9, ...), custom_call_target="tpu_custom_call" | custom-call | flops 1000000 | bytes 1048576 | tf_op jit(solution)/shard_map/updates/updates/pallas_call | solution.py:409
  115.0 5.9 %all-to-all-done.3.picked_ref = bf16[32,4,16,256]{3,2,1,0:T(8,128)(2,1)S(1)} async-done(((bf16[32,4,16,256]{3,2,1,0:T(8,128)(2,1)}), bf16[32,4,16,256]{3,2,1,0:T(8,128)(2,1)S(1)}, u32[]{:S(2)}, u32[]{:S(2)}) %all-to-all-start.3) | async-done | bytes 1048608 | tf_op jit(solution)/shard_map/pick/all_to_all | solution.py:405
  120.9 1.1 back_project.1
  (71 shorter events, 4.0 us)
Async XLA Ops:
  0.6 7.1 %copy-start.4 = (f32[1,64,2,128]{3,2,1,0:T(2,128)S(1)}, f32[1,64,2,128]{3,2,1,0:T(2,128)}, u32[]{:S(2)}) copy-start(f32[1,64,2,128]{3,2,1,0:T(2,128)} %param.17) | copy-start | bytes 196612
  2.1 10.6 %collective-permute-start.2 = (s32[8]{0:T(128)S(1)}, s32[8]{0:T(128)S(1)}, u32[]{:S(2)}, u32[]{:S(2)}) collective-permute-start(s32[8]{0:T(128)S(1)} %get-tuple-element.82), channel_id=1, source_target_pairs={{0,192},{64,0},{128,64},{192,128},{1,193},{65,1},{129,65},{193,129... | collective-permute-start | bytes 104 | tf_op jit(solution)/shard_map/targets/ppermute | solution.py:309
  7.4 5.3 %collective-permute-start.1 = (s32[8]{0:T(128)S(1)}, s32[8]{0:T(128)S(1)}, u32[]{:S(2)}, u32[]{:S(2)}) collective-permute-start(s32[8]{0:T(128)S(1)} %get-tuple-element.83), channel_id=1, source_target_pairs={{0,128},{64,192},{128,0},{192,64},{1,129},{65,193},{129,1},{193,65... | collective-permute-start | bytes 104 | tf_op jit(solution)/shard_map/targets/ppermute | solution.py:309
  7.4 5.3 %collective-permute-start = (s32[8]{0:T(128)S(1)}, s32[8]{0:T(128)S(1)}, u32[]{:S(2)}, u32[]{:S(2)}) collective-permute-start(s32[8]{0:T(128)S(1)} %get-tuple-element.84), channel_id=1, source_target_pairs={{0,64},{64,128},{128,192},{192,0},{1,65},{65,129},{129,193},{193,1... | collective-permute-start | bytes 104 | tf_op jit(solution)/shard_map/targets/ppermute | solution.py:309
  7.8 9.1 %collective-permute-start.3 = (f32[128,128]{1,0:T(8,128)S(1)}, f32[128,128]{1,0:T(8,128)S(1)}, u32[]{:S(2)}, u32[]{:S(2)}) collective-permute-start(f32[128,128]{1,0:T(8,128)S(1)} %bitcast.29), channel_id=1, source_target_pairs={{0,4},{4,0},{1,5},{5,1},{2,6},{6,2},{3,7},{7,3},{8,12},{12,8},{9,1... | collective-permute-start | bytes 196616 | tf_op jit(solution)/shard_map/fields/ppermute | solution.py:309
  17.4 30.6 %copy-start.10 = (f32[1,8,128,128]{3,2,1,0:T(8,128)S(1)}, f32[1,8,128,128]{3,2,1,0:T(8,128)}, u32[]{:S(2)}) copy-start(f32[1,8,128,128]{3,2,1,0:T(8,128)} %param.14) | copy-start | bytes 1572868
  17.4 30.6 %copy-start.11 = (f32[2,128,128]{2,1,0:T(8,128)S(1)}, f32[2,128,128]{2,1,0:T(8,128)}, u32[]{:S(2)}) copy-start(f32[2,128,128]{2,1,0:T(8,128)} %probe_ref.1) | copy-start | bytes 393220
  17.5 30.6 %copy-start.13 = (bf16[256,256]{1,0:T(8,128)(2,1)S(1)}, bf16[256,256]{1,0:T(8,128)(2,1)}, u32[]{:S(2)}) copy-start(bf16[256,256]{1,0:T(8,128)(2,1)} %constant.91.clone.bl_ref) | copy-start | bytes 393220
  17.5 30.6 %copy-start.14 = (bf16[256,256]{1,0:T(8,128)(2,1)S(1)}, bf16[256,256]{1,0:T(8,128)(2,1)}, u32[]{:S(2)}) copy-start(bf16[256,256]{1,0:T(8,128)(2,1)} %constant.90.clone.bh_ref) | copy-start | bytes 393220
  17.5 30.6 %copy-start.15 = (bf16[256,256]{1,0:T(8,128)(2,1)S(1)}, bf16[256,256]{1,0:T(8,128)(2,1)}, u32[]{:S(2)}) copy-start(bf16[256,256]{1,0:T(8,128)(2,1)} %constant.89.clone.al_ref) | copy-start | bytes 393220
  17.5 30.6 %copy-start.16 = (bf16[256,256]{1,0:T(8,128)(2,1)S(1)}, bf16[256,256]{1,0:T(8,128)(2,1)}, u32[]{:S(2)}) copy-start(bf16[256,256]{1,0:T(8,128)(2,1)} %constant.88.clone.ah_ref) | copy-start | bytes 393220
  17.5 45.2 %all-to-all-start = ((bf16[32,4,16,256]{3,2,1,0:T(8,128)(2,1)}), bf16[32,4,16,256]{3,2,1,0:T(8,128)(2,1)S(1)}, u32[]{:S(2)}, u32[]{:S(2)}) async-start(bf16[32,4,16,256]{3,2,1,0:T(8,128)(2,1)} %ray_sums.1), calls=%async_computation | async-start | bytes 2097152 | tf_op jit(solution)/shard_map/ray_sums/all_to_all | solution.py:354
  26.5 17.9 %collective-permute-start.4 = (f32[296,128]{1,0:T(8,128)S(1)}, f32[296,128]{1,0:T(8,128)S(1)}, u32[]{:S(2)}, u32[]{:S(2)}) collective-permute-start(f32[296,128]{1,0:T(8,128)S(1)} %get-tuple-element.55), channel_id=1, source_target_pairs={{0,1},{1,2},{2,3},{3,0},{4,5},{5,6},{6,7},{7,4},{8,9},{9,10},{10,1... | collective-permute-start | bytes 454664 | tf_op jit(solution)/shard_map/fields/ppermute | solution.py:309
  28.0 20.0 %collective-permute-start.5 = (f32[296,128]{1,0:T(8,128)S(1)}, f32[296,128]{1,0:T(8,128)S(1)}, u32[]{:S(2)}, u32[]{:S(2)}) collective-permute-start(f32[296,128]{1,0:T(8,128)S(1)} %get-tuple-element.56), channel_id=1, source_target_pairs={{0,2},{1,3},{2,0},{3,1},{4,6},{5,7},{6,4},{7,5},{8,10},{9,11},{10,... | collective-permute-start | bytes 454664 | tf_op jit(solution)/shard_map/fields/ppermute | solution.py:309
  30.4 17.6 %collective-permute-start.6 = (f32[296,128]{1,0:T(8,128)S(1)}, f32[296,128]{1,0:T(8,128)S(1)}, u32[]{:S(2)}, u32[]{:S(2)}) collective-permute-start(f32[296,128]{1,0:T(8,128)S(1)} %get-tuple-element.57), channel_id=1, source_target_pairs={{0,3},{1,0},{2,1},{3,2},{4,7},{5,4},{6,5},{7,6},{8,11},{9,8},{10,9... | collective-permute-start | bytes 454664 | tf_op jit(solution)/shard_map/fields/ppermute | solution.py:309
  31.6 16.5 %copy-start.12 = (s32[1,8]{1,0:T(1,128)S(1)}, s32[1,8]{1,0:T(1,128)}, u32[]{:S(2)}) copy-start(s32[1,8]{1,0:T(1,128)} %starts_ref.1) | copy-start | bytes 100
  52.8 11.3 %collective-permute-start.10 = (f32[64,128]{1,0:T(8,128)S(1)}, f32[64,128]{1,0:T(8,128)S(1)}, u32[]{:S(2)}, u32[]{:S(2)}) collective-permute-start(f32[64,128]{1,0:T(8,128)S(1)} %get-tuple-element.64), channel_id=1, source_target_pairs={{0,4},{4,0},{1,5},{5,1},{2,6},{6,2},{3,7},{7,3},{8,12},{12,8},{9,1... | collective-permute-start | bytes 98312 | tf_op jit(solution)/shard_map/frames/ppermute | solution.py:309
  56.8 4.7 %collective-permute-start.7 = (bf16[2,128,128]{2,1,0:T(8,128)(2,1)S(1)}, bf16[2,128,128]{2,1,0:T(8,128)(2,1)S(1)}, u32[]{:S(2)}, u32[]{:S(2)}) collective-permute-start(bf16[2,128,128]{2,1,0:T(8,128)(2,1)S(1)} %get-tuple-element.60), channel_id=1, source_target_pairs={{0,1},{1,2},{2,3},{3,0},{4,5},{5,6},{6,7},{7,4},{8,9},{9,10},{10,1... | collective-permute-start | bytes 196616 | tf_op jit(solution)/shard_map/frames/ppermute | solution.py:309
  56.8 5.0 %collective-permute-start.8 = (bf16[2,128,128]{2,1,0:T(8,128)(2,1)S(1)}, bf16[2,128,128]{2,1,0:T(8,128)(2,1)S(1)}, u32[]{:S(2)}, u32[]{:S(2)}) collective-permute-start(bf16[2,128,128]{2,1,0:T(8,128)(2,1)S(1)} %get-tuple-element.61), channel_id=1, source_target_pairs={{0,2},{1,3},{2,0},{3,1},{4,6},{5,7},{6,4},{7,5},{8,10},{9,11},{10,... | collective-permute-start | bytes 196616 | tf_op jit(solution)/shard_map/frames/ppermute | solution.py:309
  58.2 4.5 %collective-permute-start.9 = (bf16[2,128,128]{2,1,0:T(8,128)(2,1)S(1)}, bf16[2,128,128]{2,1,0:T(8,128)(2,1)S(1)}, u32[]{:S(2)}, u32[]{:S(2)}) collective-permute-start(bf16[2,128,128]{2,1,0:T(8,128)(2,1)S(1)} %get-tuple-element.62), channel_id=1, source_target_pairs={{0,3},{1,0},{2,1},{3,2},{4,7},{5,4},{6,5},{7,6},{8,11},{9,8},{10,9... | collective-permute-start | bytes 196616 | tf_op jit(solution)/shard_map/frames/ppermute | solution.py:309
  78.5 12.8 %all-to-all-start.2 = ((bf16[8,128,128]{2,1,0:T(8,128)(2,1)}), bf16[8,128,128]{2,1,0:T(8,128)(2,1)S(1)}, u32[]{:S(2)}, u32[]{:S(2)}) async-start(bf16[8,128,128]{2,1,0:T(8,128)(2,1)} %get-tuple-element.69), calls=%async_computation.2 | async-start | bytes 524288 | tf_op jit(solution)/shard_map/residual/all_to_all | solution.py:393
  81.9 11.3 %collective-permute-start.11 = (f32[2,3,16,128]{3,2,1,0:T(8,128)S(1)}, f32[2,3,16,128]{3,2,1,0:T(8,128)S(1)}, u32[]{:S(2)}, u32[]{:S(2)}) collective-permute-start(f32[2,3,16,128]{3,2,1,0:T(8,128)S(1)} %get-tuple-element.71), channel_id=1, source_target_pairs={{0,1},{1,2},{2,3},{3,0},{4,5},{5,6},{6,7},{7,4},{8,9},{9,10},{10,1... | collective-permute-start | bytes 147464 | tf_op jit(solution)/shard_map/residual/ppermute | solution.py:309
  82.5 10.7 %collective-permute-start.12 = (f32[2,3,16,128]{3,2,1,0:T(8,128)S(1)}, f32[2,3,16,128]{3,2,1,0:T(8,128)S(1)}, u32[]{:S(2)}, u32[]{:S(2)}) collective-permute-start(f32[2,3,16,128]{3,2,1,0:T(8,128)S(1)} %get-tuple-element.72), channel_id=1, source_target_pairs={{0,2},{1,3},{2,0},{3,1},{4,6},{5,7},{6,4},{7,5},{8,10},{9,11},{10,... | collective-permute-start | bytes 147464 | tf_op jit(solution)/shard_map/residual/ppermute | solution.py:309
  85.3 8.0 %collective-permute-start.13 = (f32[2,3,16,128]{3,2,1,0:T(8,128)S(1)}, f32[2,3,16,128]{3,2,1,0:T(8,128)S(1)}, u32[]{:S(2)}, u32[]{:S(2)}) collective-permute-start(f32[2,3,16,128]{3,2,1,0:T(8,128)S(1)} %get-tuple-element.73), channel_id=1, source_target_pairs={{0,3},{1,0},{2,1},{3,2},{4,7},{5,4},{6,5},{7,6},{8,11},{9,8},{10,9... | collective-permute-start | bytes 147464 | tf_op jit(solution)/shard_map/residual/ppermute | solution.py:309
  93.2 11.4 %copy-start.6 = (f32[2,3,16,128]{3,2,1,0:T(8,128)}, f32[2,3,16,128]{3,2,1,0:T(8,128)S(1)}, u32[]{:S(2)}) copy-start(f32[2,3,16,128]{3,2,1,0:T(8,128)S(1)} %collective-permute-done.11.one_ref) | copy-start | bytes 147460
  93.2 11.4 %copy-start.8 = (f32[2,3,16,128]{3,2,1,0:T(8,128)}, f32[2,3,16,128]{3,2,1,0:T(8,128)S(1)}, u32[]{:S(2)}) copy-start(f32[2,3,16,128]{3,2,1,0:T(8,128)S(1)} %collective-permute-done.12.two_ref) | copy-start | bytes 147460
  93.3 12.5 %copy-start.1 = (bf16[1,32,2,32,256]{4,3,2,1,0:T(8,128)(2,1)S(1)}, bf16[1,32,2,32,256]{4,3,2,1,0:T(8,128)(2,1)}, u32[]{:S(2)}) copy-start(bf16[1,32,2,32,256]{4,3,2,1,0:T(8,128)(2,1)} %param.20) | copy-start | bytes 3145732
  93.3 27.6 %all-to-all-start.3 = ((bf16[32,4,16,256]{3,2,1,0:T(8,128)(2,1)}), bf16[32,4,16,256]{3,2,1,0:T(8,128)(2,1)S(1)}, u32[]{:S(2)}, u32[]{:S(2)}) async-start(bf16[32,4,16,256]{3,2,1,0:T(8,128)(2,1)} %pick_tiles.1), calls=%async_computation.3 | async-start | bytes 2097152 | tf_op jit(solution)/shard_map/pick/all_to_all | solution.py:405
  105.4 8.4 %collective-permute-start.14 = (f32[4,3,16,128]{3,2,1,0:T(8,128)S(1)}, f32[4,3,16,128]{3,2,1,0:T(8,128)S(1)}, u32[]{:S(2)}, u32[]{:S(2)}) collective-permute-start(f32[4,3,16,128]{3,2,1,0:T(8,128)S(1)} %pad_maximum_fusion), channel_id=1, source_target_pairs={{0,4},{4,0},{1,5},{5,1},{2,6},{6,2},{3,7},{7,3},{8,12},{12,8},{9,1... | collective-permute-start | bytes 294920 | tf_op jit(solution)/shard_map/updates/ppermute | solution.py:309
  106.9 6.9 %copy-start.7 = (f32[2,3,16,128]{3,2,1,0:T(8,128)S(1)}, f32[2,3,16,128]{3,2,1,0:T(8,128)}, u32[]{:S(2)}) copy-start(f32[2,3,16,128]{3,2,1,0:T(8,128)} %copy-done.6) | copy-start | bytes 147460
  106.9 6.9 %copy-start.9 = (f32[2,3,16,128]{3,2,1,0:T(8,128)S(1)}, f32[2,3,16,128]{3,2,1,0:T(8,128)}, u32[]{:S(2)}) copy-start(f32[2,3,16,128]{3,2,1,0:T(8,128)} %copy-done.8) | copy-start | bytes 147460
  108.4 12.5 %copy-start.3 = (f32[256,2,128]{2,1,0:T(2,128)S(1)}, f32[256,2,128]{2,1,0:T(2,128)}, u32[]{:S(2)}) copy-start(f32[256,2,128]{2,1,0:T(2,128)} %param.19) | copy-start | bytes 786436
  (6 other events, 6.2 us)

commit v4 on v3

--- a/solution.py
+++ b/solution.py
@@ -82,11 +82,11 @@
 
 
 def first_rows(place_ref, target_ref):
-    back_y = [lax.rem(place_ref[1] + Y - y, Y) for y in range(Y)]
-    back_zl = [lax.rem(place_ref[2] + ZL - zl, ZL) * XC for zl in range(ZL)]
+    back_y = [lax.rem(place_ref[1] + Y - y, Y) * XC for y in range(Y)]
+    back_zl = [lax.rem(place_ref[2] + ZL - zl, ZL) for zl in range(ZL)]
 
     def row(zl, y, xc):
-        return pl.multiple_of(target_ref[back_y[y], back_zl[zl] + xc] * QR, QR)
+        return pl.multiple_of(target_ref[back_zl[zl], back_y[y] + xc] * QR, QR)
 
     return row
 
@@ -212,11 +212,13 @@
 
 def pack(place_ref, object_ref, theirs_ref, dual_ref, target_ref, own_ref, one_ref, two_ref, three_ref, drift):
     y = place_ref[1]
+    targets = target_ref[...].astype(f32)
     drift[...] = object_ref[...] + dual_ref[...]
     for ahead, ref in enumerate((own_ref, one_ref, two_ref, three_ref)):
         ref[0:128, :] = object_ref[...]
         ref[128:256, :] = theirs_ref[...]
-        ref[FIELD_ROWS + DRIFT_ROWS :, :] = target_ref[...]
+        ref[FIELD_ROWS + DRIFT_ROWS :, :] = jnp.zeros((QR, NZ), f32)
+        ref[FIELD_ROWS + DRIFT_ROWS : FIELD_ROWS + DRIFT_ROWS + 1, : ZL * XC] = targets
         for part in range(2):
             for tile in range(2):
                 start = (tile * RAYS + lax.rem(y + ahead, Y) * QR) * 2 + part
@@ -328,33 +330,18 @@
     object_rows = object_field.reshape(128, NZ)
     dual_rows = dual_field.reshape(128, NZ)
 
-    with jax.named_scope("targets"):
-        own_targets = tile_range.reshape(ZL, XC)
-        ahead = [lax.dynamic_index_in_dim(own_targets, (zl + k) % ZL, 0, keepdims=False) for k in range(ZL)]
-        targets = jnp.stack([ahead[0]] + [shifted(ahead[k], "zl", ZL, k) for k in range(1, ZL)])
-        target_rows = jnp.zeros((QR, NZ), f32).at[0, : ZL * XC].set(targets.reshape(ZL * XC).astype(f32))
-
-    with jax.named_scope("fields"):
-        object_theirs = across(object_rows)
-
-    with jax.named_scope("ray_sums"):
-        radon_first, target_rows = lax.optimization_barrier((radon, target_rows))
-        sums = call(ray_sums, shape(NEAR, ZL, HITS * QR, 2 * NZ, dtype=bf16), 0, 2, flops=2 * 2048 * 256 * 256)(
-            radon_first, volume_rows
-        )
-
     with jax.named_scope("fields"):
         packed = call(
             pack, (shape(SENT_ROWS, NZ),) * Y, 1, 4, scratch=[pltpu.VMEM((128, NZ), f32)], flops=1_000_000
-        )(place, object_rows, object_theirs, dual_rows, target_rows)
-        sums, packed = lax.optimization_barrier((sums, packed))
+        )(place, object_rows, across(object_rows), dual_rows, tile_range.reshape(1, ZL * XC))
         fields = round_y(packed)
 
     with jax.named_scope("ray_sums"):
+        sums = call(ray_sums, shape(NEAR, ZL, HITS * QR, 2 * NZ, dtype=bf16), 0, 2, flops=2 * 2048 * 256 * 256)(
+            radon, volume_rows
+        )
+        sums, fields = lax.optimization_barrier((sums, fields))
         near_sums = lax.all_to_all(sums, CROSS, 0, 0, tiled=True)
-
-    with jax.named_scope("targets"):
-        tables = jnp.stack([field[FIELD_ROWS + DRIFT_ROWS, : ZL * XC] for field in fields]).astype(jnp.int32)
 
     with jax.named_scope("frames"):
         *inter_parts, drift_mine, drift_sent = call(
@@ -366,6 +353,14 @@
             flops=1_600_000_000,
         )(place, positions, *fields, probe_field, measured[0], ah, al, bh, bl)
         inter_parts = round_y(inter_parts)
+
+    with jax.named_scope("targets"):
+        tables = jnp.stack([field[FIELD_ROWS + DRIFT_ROWS, : ZL * XC] for field in fields])
+        tables, inter_parts[1] = lax.optimization_barrier((tables, inter_parts[1]))
+        tables = tables.astype(jnp.int32).reshape(Y, ZL, XC)
+        ahead = [lax.dynamic_index_in_dim(tables, (zl + k) % ZL, 1, keepdims=False) for k in range(ZL)]
+        tables = jnp.stack([ahead[0]] + [shifted(ahead[k], "zl", ZL, k) for k in range(1, ZL)])
+        tables = tables.reshape(ZL, Y * XC)
         drift_theirs = across(drift_sent)
 
     with jax.named_scope("near_sum"):

time: 123 us -> 118 us (0.959)
  waiting for transfers between devices: 36.7 us -> 25 us
  starting transfers between devices: 50 us -> 56.1 us
  local copies, waits for them, and re-layouts: 6.43 us -> 9.01 us
  blocking collectives: 13.1 us -> 11.8 us
    ppermute x15, waiting for transfers between devices: 24.7 us -> 15.8 us  [shifted(): lax.ppermute(value, axis, [(i, (i + step) % length) for i in range(length)])]
    ppermute x15, starting transfers between devices: 26.3 us -> 31.7 us  [shifted(): lax.ppermute(value, axis, [(i, (i + step) % length) for i in range(length)])]
    unnamed x37 -> x40, local copies, waits for them, and re-layouts: 2.91 us -> 5.16 us
    all_to_all x1, waiting for transfers between devices: 5.91 us -> 3.72 us  [body(): returned = lax.all_to_all(picked, CROSS, 0, 0, tiled=True)]
    all_to_all x1, blocking collectives: 13.1 us -> 11.8 us  [body(): far_sums = lax.all_to_all(dense, ALONG, 0, 0, tiled=True)]
  transfers between devices with their start and end apart: 18 -> 18, of which waited for: 8 -> 10; matrix products, arithmetic and copies ran while one was open for 2% -> 3% of each run, Pallas kernels for 9% -> 9%
where the time goes in v4:
time: 118 us; the launch traced here: 117 us
  starting transfers between devices  56.1 us (48%)
  waiting for transfers between devices  25 us (21%)
  Pallas kernels  14 us (12%)
  blocking collectives  11.8 us (10%)
  local copies, waits for them, and re-layouts  9.01 us (8%)
    ppermute x15, starting transfers between devices, shifted(): lax.ppermute(value, axis, [(i, (i + step) % length) for i in range(length)])  31.7 us
    ppermute x15, waiting for transfers between devices, shifted(): lax.ppermute(value, axis, [(i, (i + step) % length) for i in range(length)])  15.8 us
    all_to_all x1, blocking collectives, body(): far_sums = lax.all_to_all(dense, ALONG, 0, 0, tiled=True)  11.8 us
    all_to_all x1, starting transfers between devices, body(): returned = lax.all_to_all(picked, CROSS, 0, 0, tiled=True)  11.6 us
    all_to_all x1, starting transfers between devices, body(): near_sums = lax.all_to_all(sums, CROSS, 0, 0, tiled=True)  9.37 us
    all_to_all x1, waiting for transfers between devices, body(): residuals = lax.all_to_all(copies, ALONG, 0, 0, tiled=True)  5.49 us
    unnamed x40, local copies, waits for them, and re-layouts  5.16 us
    pallas_call x1, Pallas kernels, body(): call(frame_gradients, (shape(2, 128, NZ),) + (shape(2, 128, NZ, dtype=bf1...  4.65 us
  transfers between devices with their start and end apart: 18, of which 10 were waited for; matrix products, arithmetic and copies ran while one was open for 3% of the time, Pallas kernels for 9%

profile of v4, /device:TPU:1, one launch (start us, length us, event | category | flops | bytes accessed | tf_op | source)
XLA Modules:
  0.0 117.0 jit_solution(14333912782830201643)
XLA Ops:
  0.6 7.8 %collective-permute-start = (f32[128,128]{1,0:T(8,128)}, f32[128,128]{1,0:T(8,128)S(1)}, u32[]{:S(2)}, u32[]{:S(2)}) collective-permute-start(f32[128,128]{1,0:T(8,128)} %bitcast.23), channel_id=1, source_target_pairs={{0,4},{4,0},{1,5},{5,1},{2,6},{6,2},{3,7},{7,3},{8,12},{12,8},{9,1... | collective-permute-start | bytes 196616 | tf_op jit(solution)/shard_map/fields/ppermute | solution.py:311
  8.5 1.9 %collective-permute-done.theirs_ref = f32[128,128]{1,0:T(8,128)S(1)} collective-permute-done((f32[128,128]{1,0:T(8,128)}, f32[128,128]{1,0:T(8,128)S(1)}, u32[]{:S(2)}, u32[]{:S(2)}) %collective-permute-start) | collective-permute-done | bytes 65568 | tf_op jit(solution)/shard_map/fields/ppermute | solution.py:311
  13.3 1.4 %collective-permute-start.1 = (f32[296,128]{1,0:T(8,128)S(1)}, f32[296,128]{1,0:T(8,128)S(1)}, u32[]{:S(2)}, u32[]{:S(2)}) collective-permute-start(f32[296,128]{1,0:T(8,128)S(1)} %get-tuple-element.37), channel_id=1, source_target_pairs={{0,1},{1,2},{2,3},{3,0},{4,5},{5,6},{6,7},{7,4},{8,9},{9,10},{10,1... | collective-permute-start | bytes 454664 | tf_op jit(solution)/shard_map/fields/ppermute | solution.py:311
  14.7 2.6 %collective-permute-start.2 = (f32[296,128]{1,0:T(8,128)S(1)}, f32[296,128]{1,0:T(8,128)S(1)}, u32[]{:S(2)}, u32[]{:S(2)}) collective-permute-start(f32[296,128]{1,0:T(8,128)S(1)} %get-tuple-element.38), channel_id=1, source_target_pairs={{0,2},{1,3},{2,0},{3,1},{4,6},{5,7},{6,4},{7,5},{8,10},{9,11},{10,... | collective-permute-start | bytes 454664 | tf_op jit(solution)/shard_map/fields/ppermute | solution.py:311
  18.4 1.2 %copy-done = bf16[1,32,2,32,256]{4,3,2,1,0:T(8,128)(2,1)S(1)} copy-done((bf16[1,32,2,32,256]{4,3,2,1,0:T(8,128)(2,1)S(1)}, bf16[1,32,2,32,256]{4,3,2,1,0:T(8,128)(2,1)}, u32[]{:S(2)}) %copy-start) | copy-done | bytes 1048600
  20.6 1.8 %ray_sums.1 = bf16[32,4,16,256]{3,2,1,0:T(8,128)(2,1)} custom-call(bf16[32,2,32,256]{3,2,1,0:T(8,128)(2,1)S(1)} %bitcast.19, f32[512,128]{1,0:T(8,128)S(1)} %bitcast.21), custom_call_target="tpu_custom_call" | custom-call | flops 268435456 | bytes 1048576 | tf_op jit(solution)/shard_map/ray_sums/ray_sums/pallas_call | solution.py:340
  22.8 9.4 %all-to-all-start = ((bf16[32,4,16,256]{3,2,1,0:T(8,128)(2,1)}), bf16[32,4,16,256]{3,2,1,0:T(8,128)(2,1)S(1)}, u32[]{:S(2)}, u32[]{:S(2)}) async-start(bf16[32,4,16,256]{3,2,1,0:T(8,128)(2,1)} %ray_sums.1), calls=%async_computation | async-start | bytes 2097152 | tf_op jit(solution)/shard_map/ray_sums/all_to_all | solution.py:344
  32.9 4.6 %frame_gradients.1 = (f32[2,128,128]{2,1,0:T(8,128)S(1)}, bf16[2,128,128]{2,1,0:T(8,128)(2,1)S(1)}, bf16[2,128,128]{2,1,0:T(8,128)(2,1)S(1)}, bf16[2,128,128]{2,...) custom-call(s32[3]{0:T(128)S(1)} %pad_add_fusion.1.place_ref, s32[1,8]{1,0:T(1,128)S(1)} %copy-done.15, ...), custom_call_target="tpu_custom_call" | custom-call | flops 1600000000 | bytes 1048576 | tf_op jit(solution)/shard_map/frames/frame_gradients/pallas_call | solution.py:347
  37.5 5.5 %collective-permute-start.10 = (f32[64,128]{1,0:T(8,128)S(1)}, f32[64,128]{1,0:T(8,128)S(1)}, u32[]{:S(2)}, u32[]{:S(2)}) collective-permute-start(f32[64,128]{1,0:T(8,128)S(1)} %get-tuple-element.52), channel_id=1, source_target_pairs={{0,4},{4,0},{1,5},{5,1},{2,6},{6,2},{3,7},{7,3},{8,12},{12,8},{9,1... | collective-permute-start | bytes 98312 | tf_op jit(solution)/shard_map/targets/ppermute | solution.py:311
  43.0 1.4 %collective-permute-start.4 = (bf16[2,128,128]{2,1,0:T(8,128)(2,1)S(1)}, bf16[2,128,128]{2,1,0:T(8,128)(2,1)S(1)}, u32[]{:S(2)}, u32[]{:S(2)}) collective-permute-start(bf16[2,128,128]{2,1,0:T(8,128)(2,1)S(1)} %get-tuple-element.44), channel_id=1, source_target_pairs={{0,1},{1,2},{2,3},{3,0},{4,5},{5,6},{6,7},{7,4},{8,9},{9,10},{10,1... | collective-permute-start | bytes 196616 | tf_op jit(solution)/shard_map/frames/ppermute | solution.py:311
  44.4 2.4 %collective-permute-start.8 = (bf16[2,128,128]{2,1,0:T(8,128)(2,1)S(1)}, bf16[2,128,128]{2,1,0:T(8,128)(2,1)S(1)}, u32[]{:S(2)}, u32[]{:S(2)}) collective-permute-start(bf16[2,128,128]{2,1,0:T(8,128)(2,1)S(1)} %get-tuple-element.49), channel_id=1, source_target_pairs={{0,2},{1,3},{2,0},{3,1},{4,6},{5,7},{6,4},{7,5},{8,10},{9,11},{10,... | collective-permute-start | bytes 196616 | tf_op jit(solution)/shard_map/frames/ppermute | solution.py:311
  46.8 1.2 %collective-permute-start.9 = (bf16[2,128,128]{2,1,0:T(8,128)(2,1)S(1)}, bf16[2,128,128]{2,1,0:T(8,128)(2,1)S(1)}, u32[]{:S(2)}, u32[]{:S(2)}) collective-permute-start(bf16[2,128,128]{2,1,0:T(8,128)(2,1)S(1)} %get-tuple-element.50), channel_id=1, source_target_pairs={{0,3},{1,0},{2,1},{3,2},{4,7},{5,4},{6,5},{7,6},{8,11},{9,8},{10,9... | collective-permute-start | bytes 196616 | tf_op jit(solution)/shard_map/frames/ppermute | solution.py:311
  48.0 3.9 %collective-permute-done.4.one_ref = bf16[2,128,128]{2,1,0:T(8,128)(2,1)S(1)} collective-permute-done((bf16[2,128,128]{2,1,0:T(8,128)(2,1)S(1)}, bf16[2,128,128]{2,1,0:T(8,128)(2,1)S(1)}, u32[]{:S(2)}, u32[]{:S(2)}) %collective-permute-start.4) | collective-permute-done | bytes 65568 | tf_op jit(solution)/shard_map/frames/ppermute | solution.py:311
  52.1 1.2 collective-permute-start.7
  55.5 1.1 collective-permute-done.6
  56.7 2.1 %collective-permute-done.5 = s32[4,8]{1,0:T(4,128)S(1)} collective-permute-done((s32[4,8]{1,0:T(4,128)S(1)}, s32[4,8]{1,0:T(4,128)S(1)}, u32[]{:S(2)}, u32[]{:S(2)}) %collective-permute-start.5) | collective-permute-done | bytes 160 | tf_op jit(solution)/shard_map/targets/ppermute | solution.py:311
  58.9 1.3 %add_tiles.1 = (bf16[8,128,128]{2,1,0:T(8,128)(2,1)S(1)}, f32[2,128,128]{2,1,0:T(8,128)S(1)}) custom-call(s32[3]{0:T(128)S(1)} %pad_add_fusion.1.place_ref, s32[4,32]{1,0:T(4,128)S(1)} %pad_add_fusion.target_ref, bf16[32,4,16,256]{3,2,1,0:T(8,128)(2,1)S(1)} %all-to-all-done.sums_ref, f32[2,128,128]{2,1,0:T(8,128)S(1)} %get-tuple-element.47.own_ref, ...), custom_call_target="tpu_custom_call" | custom-call | flops 1000000 | bytes 1048576 | tf_op jit(solution)/shard_map/near_sum/add_tiles/pallas_call | solution.py:367
  60.2 11.8 %all_to_all.20.sums_ref = bf16[8,128,128]{2,1,0:T(8,128)(2,1)S(1)} all-to-all(bf16[8,128,128]{2,1,0:T(8,128)(2,1)S(1)} %get-tuple-element.53), channel_id=1, replica_groups=mesh['zl'=4,'x'=4,'c'=2,'zh'=2,'y'=4] {'zh','zl'}, dimensions={0} | all-to-all | bytes 524288 | tf_op jit(solution)/shard_map/near_sum/all_to_all | solution.py:376
  72.0 1.3 %residual_part.1 = (bf16[8,128,128]{2,1,0:T(8,128)(2,1)}, f32[2,3,16,128]{3,2,1,0:T(8,128)S(1)}, f32[2,3,16,128]{3,2,1,0:T(8,128)S(1)}, f32[2,3,16,128]{3,2,1,0:T(8,128)S(1)}, f32[2,3,16,128]{3,2,1,0:T(8,128)S(1)}) custom-call(s32[3]{0:T(128)S(1)} %pad_add_fusion.1.place_ref, bf16[8,128,128]{2,1,0:T(8,128)(2,1)S(1)} %all_to_all.20.sums_ref, ...), custom_call_target="tpu_custom_call" | custom-call | flops 1000000 | bytes 1048576 | tf_op jit(solution)/shard_map/residual/residual_part/pallas_call | solution.py:379
  73.3 3.4 %all-to-all-start.2 = ((bf16[8,128,128]{2,1,0:T(8,128)(2,1)}), bf16[8,128,128]{2,1,0:T(8,128)(2,1)S(1)}, u32[]{:S(2)}, u32[]{:S(2)}) async-start(bf16[8,128,128]{2,1,0:T(8,128)(2,1)} %get-tuple-element.57), calls=%async_computation.2 | async-start | bytes 524288 | tf_op jit(solution)/shard_map/residual/all_to_all | solution.py:388
  77.1 2.3 %collective-permute-start.12 = (f32[2,3,16,128]{3,2,1,0:T(8,128)S(1)}, f32[2,3,16,128]{3,2,1,0:T(8,128)S(1)}, u32[]{:S(2)}, u32[]{:S(2)}) collective-permute-start(f32[2,3,16,128]{3,2,1,0:T(8,128)S(1)} %get-tuple-element.60), channel_id=1, source_target_pairs={{0,2},{1,3},{2,0},{3,1},{4,6},{5,7},{6,4},{7,5},{8,10},{9,11},{10,... | collective-permute-start | bytes 147464 | tf_op jit(solution)/shard_map/residual/ppermute | solution.py:311
  79.4 1.1 collective-permute-start.13
  80.5 5.5 %all-to-all-done.2.residual_ref = bf16[8,128,128]{2,1,0:T(8,128)(2,1)S(1)} async-done(((bf16[8,128,128]{2,1,0:T(8,128)(2,1)}), bf16[8,128,128]{2,1,0:T(8,128)(2,1)S(1)}, u32[]{:S(2)}, u32[]{:S(2)}) %all-to-all-start.2) | async-done | bytes 262176 | tf_op jit(solution)/shard_map/residual/all_to_all | solution.py:388
  86.0 1.9 %pick_tiles.1 = bf16[32,4,16,256]{3,2,1,0:T(8,128)(2,1)} custom-call(s32[3]{0:T(128)S(1)} %pad_add_fusion.1.place_ref, s32[4,32]{1,0:T(4,128)S(1)} %pad_add_fusion.target_ref, bf16[8,128,128]{2,1,0:T(8,128)(2,1)S(1)} %all-to-all-done.2.residual_ref), custom_call_target="tpu_custom_call" | custom-call | flops 1000000 | bytes 1048576 | tf_op jit(solution)/shard_map/pick/pick_tiles/pallas_call | solution.py:391
  87.9 11.6 %all-to-all-start.3 = ((bf16[32,4,16,256]{3,2,1,0:T(8,128)(2,1)}), bf16[32,4,16,256]{3,2,1,0:T(8,128)(2,1)S(1)}, u32[]{:S(2)}, u32[]{:S(2)}) async-start(bf16[32,4,16,256]{3,2,1,0:T(8,128)(2,1)} %pick_tiles.1), calls=%async_computation.3 | async-start | bytes 2097152 | tf_op jit(solution)/shard_map/pick/all_to_all | solution.py:400
  100.3 1.7 %collective-permute-start.14 = (f32[4,3,16,128]{3,2,1,0:T(8,128)S(1)}, f32[4,3,16,128]{3,2,1,0:T(8,128)S(1)}, u32[]{:S(2)}, u32[]{:S(2)}) collective-permute-start(f32[4,3,16,128]{3,2,1,0:T(8,128)S(1)} %pad_maximum_fusion), channel_id=1, source_target_pairs={{0,4},{4,0},{1,5},{5,1},{2,6},{6,2},{3,7},{7,3},{8,12},{12,8},{9,1... | collective-permute-start | bytes 294920 | tf_op jit(solution)/shard_map/updates/ppermute | solution.py:311
  102.0 1.1 copy.17
  103.1 1.5 %copy.18.radon_ref = bf16[256,2048]{1,0:T(8,128)(2,1)S(1)} copy(bf16[256,2048]{0,1:T(8,128)(2,1)} %bitcast.30) | data formatting | bytes 2097152 | tf_op jit(solution)/shard_map/back_project/reshape | solution.py:409
  104.7 6.2 %collective-permute-done.14.theirs_ref = f32[4,3,16,128]{3,2,1,0:T(8,128)S(1)} collective-permute-done((f32[4,3,16,128]{3,2,1,0:T(8,128)S(1)}, f32[4,3,16,128]{3,2,1,0:T(8,128)S(1)}, u32[]{:S(2)}, u32[]{:S(2)}) %collective-permute-start.14) | collective-permute-done | bytes 98336 | tf_op jit(solution)/shard_map/updates/ppermute | solution.py:311
  110.9 1.2 %updates.1 = (f32[128,128]{1,0:T(8,128)}, f32[128,128]{1,0:T(8,128)}) custom-call(s32[3]{0:T(128)S(1)} %pad_add_fusion.1.place_ref, f32[2,3,16,128]{3,2,1,0:T(8,128)S(1)} %get-tuple-element.62.own_ref, f32[2,3,16,128]{3,2,1,0:T(8,128)S(1)} %copy-done.9, f32[2,3,16,128]{3,2,1,0:T(8,128)S(1)} %copy-done.11, ...), custom_call_target="tpu_custom_call" | custom-call | flops 1000000 | bytes 1048576 | tf_op jit(solution)/shard_map/updates/updates/pallas_call | solution.py:404
  112.1 3.7 %all-to-all-done.3.picked_ref = bf16[32,4,16,256]{3,2,1,0:T(8,128)(2,1)S(1)} async-done(((bf16[32,4,16,256]{3,2,1,0:T(8,128)(2,1)}), bf16[32,4,16,256]{3,2,1,0:T(8,128)(2,1)S(1)}, u32[]{:S(2)}, u32[]{:S(2)}) %all-to-all-start.3) | async-done | bytes 1048608 | tf_op jit(solution)/shard_map/pick/all_to_all | solution.py:400
  115.8 1.1 back_project.1
  (76 shorter events, 9.7 us)
Async XLA Ops:
  0.6 9.8 %collective-permute-start = (f32[128,128]{1,0:T(8,128)}, f32[128,128]{1,0:T(8,128)S(1)}, u32[]{:S(2)}, u32[]{:S(2)}) collective-permute-start(f32[128,128]{1,0:T(8,128)} %bitcast.23), channel_id=1, source_target_pairs={{0,4},{4,0},{1,5},{5,1},{2,6},{6,2},{3,7},{7,3},{8,12},{12,8},{9,1... | collective-permute-start | bytes 196616 | tf_op jit(solution)/shard_map/fields/ppermute | solution.py:311
  13.3 9.1 %collective-permute-start.1 = (f32[296,128]{1,0:T(8,128)S(1)}, f32[296,128]{1,0:T(8,128)S(1)}, u32[]{:S(2)}, u32[]{:S(2)}) collective-permute-start(f32[296,128]{1,0:T(8,128)S(1)} %get-tuple-element.37), channel_id=1, source_target_pairs={{0,1},{1,2},{2,3},{3,0},{4,5},{5,6},{6,7},{7,4},{8,9},{9,10},{10,1... | collective-permute-start | bytes 454664 | tf_op jit(solution)/shard_map/fields/ppermute | solution.py:311
  14.7 7.8 %collective-permute-start.2 = (f32[296,128]{1,0:T(8,128)S(1)}, f32[296,128]{1,0:T(8,128)S(1)}, u32[]{:S(2)}, u32[]{:S(2)}) collective-permute-start(f32[296,128]{1,0:T(8,128)S(1)} %get-tuple-element.38), channel_id=1, source_target_pairs={{0,2},{1,3},{2,0},{3,1},{4,6},{5,7},{6,4},{7,5},{8,10},{9,11},{10,... | collective-permute-start | bytes 454664 | tf_op jit(solution)/shard_map/fields/ppermute | solution.py:311
  17.3 5.4 %collective-permute-start.3 = (f32[296,128]{1,0:T(8,128)S(1)}, f32[296,128]{1,0:T(8,128)S(1)}, u32[]{:S(2)}, u32[]{:S(2)}) collective-permute-start(f32[296,128]{1,0:T(8,128)S(1)} %get-tuple-element.39), channel_id=1, source_target_pairs={{0,3},{1,0},{2,1},{3,2},{4,7},{5,4},{6,5},{7,6},{8,11},{9,8},{10,9... | collective-permute-start | bytes 454664 | tf_op jit(solution)/shard_map/fields/ppermute | solution.py:311
  22.7 9.5 %copy-start.13 = (f32[1,8,128,128]{3,2,1,0:T(8,128)S(1)}, f32[1,8,128,128]{3,2,1,0:T(8,128)}, u32[]{:S(2)}) copy-start(f32[1,8,128,128]{3,2,1,0:T(8,128)} %param.12) | copy-start | bytes 1572868
  22.7 9.5 %copy-start.14 = (f32[2,128,128]{2,1,0:T(8,128)S(1)}, f32[2,128,128]{2,1,0:T(8,128)}, u32[]{:S(2)}) copy-start(f32[2,128,128]{2,1,0:T(8,128)} %probe_ref.1) | copy-start | bytes 393220
  22.7 9.5 %copy-start.16 = (bf16[256,256]{1,0:T(8,128)(2,1)S(1)}, bf16[256,256]{1,0:T(8,128)(2,1)}, u32[]{:S(2)}) copy-start(bf16[256,256]{1,0:T(8,128)(2,1)} %constant.64.clone.bl_ref) | copy-start | bytes 393220
  22.7 9.5 %copy-start.17 = (bf16[256,256]{1,0:T(8,128)(2,1)S(1)}, bf16[256,256]{1,0:T(8,128)(2,1)}, u32[]{:S(2)}) copy-start(bf16[256,256]{1,0:T(8,128)(2,1)} %constant.63.clone.bh_ref) | copy-start | bytes 393220
  22.7 9.6 %copy-start.18 = (bf16[256,256]{1,0:T(8,128)(2,1)S(1)}, bf16[256,256]{1,0:T(8,128)(2,1)}, u32[]{:S(2)}) copy-start(bf16[256,256]{1,0:T(8,128)(2,1)} %constant.62.clone.al_ref) | copy-start | bytes 393220
  22.7 9.6 %copy-start.19 = (bf16[256,256]{1,0:T(8,128)(2,1)S(1)}, bf16[256,256]{1,0:T(8,128)(2,1)}, u32[]{:S(2)}) copy-start(bf16[256,256]{1,0:T(8,128)(2,1)} %constant.61.clone.ah_ref) | copy-start | bytes 393220
  22.8 36.1 %all-to-all-start = ((bf16[32,4,16,256]{3,2,1,0:T(8,128)(2,1)}), bf16[32,4,16,256]{3,2,1,0:T(8,128)(2,1)S(1)}, u32[]{:S(2)}, u32[]{:S(2)}) async-start(bf16[32,4,16,256]{3,2,1,0:T(8,128)(2,1)} %ray_sums.1), calls=%async_computation | async-start | bytes 2097152 | tf_op jit(solution)/shard_map/ray_sums/all_to_all | solution.py:344
  37.5 22.7 %collective-permute-start.10 = (f32[64,128]{1,0:T(8,128)S(1)}, f32[64,128]{1,0:T(8,128)S(1)}, u32[]{:S(2)}, u32[]{:S(2)}) collective-permute-start(f32[64,128]{1,0:T(8,128)S(1)} %get-tuple-element.52), channel_id=1, source_target_pairs={{0,4},{4,0},{1,5},{5,1},{2,6},{6,2},{3,7},{7,3},{8,12},{12,8},{9,1... | collective-permute-start | bytes 98312 | tf_op jit(solution)/shard_map/targets/ppermute | solution.py:311
  43.0 8.8 %collective-permute-start.4 = (bf16[2,128,128]{2,1,0:T(8,128)(2,1)S(1)}, bf16[2,128,128]{2,1,0:T(8,128)(2,1)S(1)}, u32[]{:S(2)}, u32[]{:S(2)}) collective-permute-start(bf16[2,128,128]{2,1,0:T(8,128)(2,1)S(1)} %get-tuple-element.44), channel_id=1, source_target_pairs={{0,1},{1,2},{2,3},{3,0},{4,5},{5,6},{6,7},{7,4},{8,9},{9,10},{10,1... | collective-permute-start | bytes 196616 | tf_op jit(solution)/shard_map/frames/ppermute | solution.py:311
  44.4 14.4 %collective-permute-start.8 = (bf16[2,128,128]{2,1,0:T(8,128)(2,1)S(1)}, bf16[2,128,128]{2,1,0:T(8,128)(2,1)S(1)}, u32[]{:S(2)}, u32[]{:S(2)}) collective-permute-start(bf16[2,128,128]{2,1,0:T(8,128)(2,1)S(1)} %get-tuple-element.49), channel_id=1, source_target_pairs={{0,2},{1,3},{2,0},{3,1},{4,6},{5,7},{6,4},{7,5},{8,10},{9,11},{10,... | collective-permute-start | bytes 196616 | tf_op jit(solution)/shard_map/frames/ppermute | solution.py:311
  46.8 12.0 %collective-permute-start.9 = (bf16[2,128,128]{2,1,0:T(8,128)(2,1)S(1)}, bf16[2,128,128]{2,1,0:T(8,128)(2,1)S(1)}, u32[]{:S(2)}, u32[]{:S(2)}) collective-permute-start(bf16[2,128,128]{2,1,0:T(8,128)(2,1)S(1)} %get-tuple-element.50), channel_id=1, source_target_pairs={{0,3},{1,0},{2,1},{3,2},{4,7},{5,4},{6,5},{7,6},{8,11},{9,8},{10,9... | collective-permute-start | bytes 196616 | tf_op jit(solution)/shard_map/frames/ppermute | solution.py:311
  52.1 2.4 %collective-permute-start.7 = (s32[4,8]{1,0:T(4,128)S(1)}, s32[4,8]{1,0:T(4,128)S(1)}, u32[]{:S(2)}, u32[]{:S(2)}) collective-permute-start(s32[4,8]{1,0:T(4,128)S(1)} %bitcast.34), channel_id=1, source_target_pairs={{0,192},{64,0},{128,64},{192,128},{1,193},{65,1},{129,65},{193,129... | collective-permute-start | bytes 392 | tf_op jit(solution)/shard_map/targets/ppermute | solution.py:311
  53.2 3.3 %collective-permute-start.6 = (s32[4,8]{1,0:T(4,128)S(1)}, s32[4,8]{1,0:T(4,128)S(1)}, u32[]{:S(2)}, u32[]{:S(2)}) collective-permute-start(s32[4,8]{1,0:T(4,128)S(1)} %bitcast.33), channel_id=1, source_target_pairs={{0,128},{64,192},{128,0},{192,64},{1,129},{65,193},{129,1},{193,65... | collective-permute-start | bytes 392 | tf_op jit(solution)/shard_map/targets/ppermute | solution.py:311
  54.5 4.2 %collective-permute-start.5 = (s32[4,8]{1,0:T(4,128)S(1)}, s32[4,8]{1,0:T(4,128)S(1)}, u32[]{:S(2)}, u32[]{:S(2)}) collective-permute-start(s32[4,8]{1,0:T(4,128)S(1)} %bitcast.32), channel_id=1, source_target_pairs={{0,64},{64,128},{128,192},{192,0},{1,65},{65,129},{129,193},{193,1... | collective-permute-start | bytes 392 | tf_op jit(solution)/shard_map/targets/ppermute | solution.py:311
  73.3 12.7 %all-to-all-start.2 = ((bf16[8,128,128]{2,1,0:T(8,128)(2,1)}), bf16[8,128,128]{2,1,0:T(8,128)(2,1)S(1)}, u32[]{:S(2)}, u32[]{:S(2)}) async-start(bf16[8,128,128]{2,1,0:T(8,128)(2,1)} %get-tuple-element.57), calls=%async_computation.2 | async-start | bytes 524288 | tf_op jit(solution)/shard_map/residual/all_to_all | solution.py:388
  76.7 11.1 %collective-permute-start.11 = (f32[2,3,16,128]{3,2,1,0:T(8,128)S(1)}, f32[2,3,16,128]{3,2,1,0:T(8,128)S(1)}, u32[]{:S(2)}, u32[]{:S(2)}) collective-permute-start(f32[2,3,16,128]{3,2,1,0:T(8,128)S(1)} %get-tuple-element.59), channel_id=1, source_target_pairs={{0,1},{1,2},{2,3},{3,0},{4,5},{5,6},{6,7},{7,4},{8,9},{9,10},{10,1... | collective-permute-start | bytes 147464 | tf_op jit(solution)/shard_map/residual/ppermute | solution.py:311
  77.1 10.8 %collective-permute-start.12 = (f32[2,3,16,128]{3,2,1,0:T(8,128)S(1)}, f32[2,3,16,128]{3,2,1,0:T(8,128)S(1)}, u32[]{:S(2)}, u32[]{:S(2)}) collective-permute-start(f32[2,3,16,128]{3,2,1,0:T(8,128)S(1)} %get-tuple-element.60), channel_id=1, source_target_pairs={{0,2},{1,3},{2,0},{3,1},{4,6},{5,7},{6,4},{7,5},{8,10},{9,11},{10,... | collective-permute-start | bytes 147464 | tf_op jit(solution)/shard_map/residual/ppermute | solution.py:311
  79.4 8.5 %collective-permute-start.13 = (f32[2,3,16,128]{3,2,1,0:T(8,128)S(1)}, f32[2,3,16,128]{3,2,1,0:T(8,128)S(1)}, u32[]{:S(2)}, u32[]{:S(2)}) collective-permute-start(f32[2,3,16,128]{3,2,1,0:T(8,128)S(1)} %get-tuple-element.61), channel_id=1, source_target_pairs={{0,3},{1,0},{2,1},{3,2},{4,7},{5,4},{6,5},{7,6},{8,11},{9,8},{10,9... | collective-permute-start | bytes 147464 | tf_op jit(solution)/shard_map/residual/ppermute | solution.py:311
  87.9 11.7 %copy-start.8 = (f32[2,3,16,128]{3,2,1,0:T(8,128)}, f32[2,3,16,128]{3,2,1,0:T(8,128)S(1)}, u32[]{:S(2)}) copy-start(f32[2,3,16,128]{3,2,1,0:T(8,128)S(1)} %collective-permute-done.11.one_ref) | copy-start | bytes 147460
  87.9 11.7 %copy-start.10 = (f32[2,3,16,128]{3,2,1,0:T(8,128)}, f32[2,3,16,128]{3,2,1,0:T(8,128)S(1)}, u32[]{:S(2)}) copy-start(f32[2,3,16,128]{3,2,1,0:T(8,128)S(1)} %collective-permute-done.12.two_ref) | copy-start | bytes 147460
  87.9 14.1 %copy-start.1 = (bf16[1,32,2,32,256]{4,3,2,1,0:T(8,128)(2,1)S(1)}, bf16[1,32,2,32,256]{4,3,2,1,0:T(8,128)(2,1)}, u32[]{:S(2)}) copy-start(bf16[1,32,2,32,256]{4,3,2,1,0:T(8,128)(2,1)} %param.18) | copy-start | bytes 3145732
  87.9 27.9 %all-to-all-start.3 = ((bf16[32,4,16,256]{3,2,1,0:T(8,128)(2,1)}), bf16[32,4,16,256]{3,2,1,0:T(8,128)(2,1)S(1)}, u32[]{:S(2)}, u32[]{:S(2)}) async-start(bf16[32,4,16,256]{3,2,1,0:T(8,128)(2,1)} %pick_tiles.1), calls=%async_computation.3 | async-start | bytes 2097152 | tf_op jit(solution)/shard_map/pick/all_to_all | solution.py:400
  100.3 10.5 %collective-permute-start.14 = (f32[4,3,16,128]{3,2,1,0:T(8,128)S(1)}, f32[4,3,16,128]{3,2,1,0:T(8,128)S(1)}, u32[]{:S(2)}, u32[]{:S(2)}) collective-permute-start(f32[4,3,16,128]{3,2,1,0:T(8,128)S(1)} %pad_maximum_fusion), channel_id=1, source_target_pairs={{0,4},{4,0},{1,5},{5,1},{2,6},{6,2},{3,7},{7,3},{8,12},{12,8},{9,1... | collective-permute-start | bytes 294920 | tf_op jit(solution)/shard_map/updates/ppermute | solution.py:311
  103.1 7.7 %copy-start.5 = (f32[1,64,2,128]{3,2,1,0:T(2,128)S(1)}, f32[1,64,2,128]{3,2,1,0:T(2,128)}, u32[]{:S(2)}) copy-start(f32[1,64,2,128]{3,2,1,0:T(2,128)} %param.15) | copy-start | bytes 196612
  103.1 7.7 %copy-start.7 = (f32[1,64,2,128]{3,2,1,0:T(2,128)S(1)}, f32[1,64,2,128]{3,2,1,0:T(2,128)}, u32[]{:S(2)}) copy-start(f32[1,64,2,128]{3,2,1,0:T(2,128)} %param.16) | copy-start | bytes 196612
  103.1 7.7 %copy-start.9 = (f32[2,3,16,128]{3,2,1,0:T(8,128)S(1)}, f32[2,3,16,128]{3,2,1,0:T(8,128)}, u32[]{:S(2)}) copy-start(f32[2,3,16,128]{3,2,1,0:T(8,128)} %copy-done.8) | copy-start | bytes 147460
  103.1 7.7 %copy-start.11 = (f32[2,3,16,128]{3,2,1,0:T(8,128)S(1)}, f32[2,3,16,128]{3,2,1,0:T(8,128)}, u32[]{:S(2)}) copy-start(f32[2,3,16,128]{3,2,1,0:T(8,128)} %copy-done.10) | copy-start | bytes 147460
  104.7 11.2 %copy-start.3 = (f32[256,2,128]{2,1,0:T(2,128)S(1)}, f32[256,2,128]{2,1,0:T(2,128)}, u32[]{:S(2)}) copy-start(f32[256,2,128]{2,1,0:T(2,128)} %param.17) | copy-start | bytes 786436
  (8 other events, 6.7 us)

commit v5 on v4

--- a/solution.py
+++ b/solution.py
@@ -108,7 +108,8 @@
 
 
 def residual_part(
-    place_ref, sums_ref, inter_ref, mine_ref, theirs_ref, residual_ref, own_ref, one_ref, two_ref, three_ref, joint
+    place_ref, sums_ref, inter_ref, mine_ref, theirs_ref, residual_ref, own_ref, one_ref, two_ref, three_ref,
+    joint, drift,
 ):
     zh = place_ref[0]
     y = place_ref[1]
@@ -116,15 +117,11 @@
     for source in range(1, DEEP):
         total = total + sums_ref[source].astype(f32)
     joint[...] = total
-    first = zh == 0
-    drift = jnp.concatenate(
-        [
-            jnp.where(first, mine_ref[...], theirs_ref[...]),
-            jnp.where(first, theirs_ref[...], mine_ref[...]),
-        ],
-        axis=0,
-    )
-    residual = (keep * (total - drift)).astype(bf16)
+    for other, ref in enumerate((mine_ref, theirs_ref)):
+        for back in range(Y):
+            owner = lax.rem(zh + other, ZH) * Y + lax.rem(y + Y - back, Y)
+            drift[pl.ds(pl.multiple_of(owner * 2 * QR, 2 * QR), 2 * QR), :] = ref[back]
+    residual = (keep * (total - drift[...])).astype(bf16)
     for copy in range(DEEP):
         residual_ref[copy] = residual
     for ahead, ref in enumerate((own_ref, one_ref, two_ref, three_ref)):
@@ -205,18 +202,17 @@
     )
 
 
-FIELD_ROWS = 4 * 64
+FIELD_ROWS = 128
 DRIFT_ROWS = 4 * QR
 SENT_ROWS = FIELD_ROWS + DRIFT_ROWS + QR
 
 
-def pack(place_ref, object_ref, theirs_ref, dual_ref, target_ref, own_ref, one_ref, two_ref, three_ref, drift):
+def pack(place_ref, object_ref, dual_ref, target_ref, own_ref, one_ref, two_ref, three_ref, drift):
     y = place_ref[1]
     targets = target_ref[...].astype(f32)
     drift[...] = object_ref[...] + dual_ref[...]
     for ahead, ref in enumerate((own_ref, one_ref, two_ref, three_ref)):
-        ref[0:128, :] = object_ref[...]
-        ref[128:256, :] = theirs_ref[...]
+        ref[0:FIELD_ROWS, :] = object_ref[...]
         ref[FIELD_ROWS + DRIFT_ROWS :, :] = jnp.zeros((QR, NZ), f32)
         ref[FIELD_ROWS + DRIFT_ROWS : FIELD_ROWS + DRIFT_ROWS + 1, : ZL * XC] = targets
         for part in range(2):
@@ -227,22 +223,18 @@
 
 
 def frame_gradients(
-    place_ref, starts_ref, own_field, one_field, two_field, three_field, probe_ref, measured_ref,
-    ah_ref, al_ref, bh_ref, bl_ref, own_ref, sent_one, sent_two, sent_three, mine_ref, theirs_ref,
+    place_ref, starts_ref, field_0, field_1, field_2, field_3, field_4, field_5, field_6, field_7,
+    probe_ref, measured_ref, ah_ref, al_ref, bh_ref, bl_ref, own_ref, sent_one, sent_two, sent_three,
     field_re, field_im, total_re, total_im,
 ):
     zh = place_ref[0]
     y = place_ref[1]
-    for back, field_ref in enumerate((own_field, one_field, two_field, three_field)):
-        source = lax.rem(y + Y - back, Y)
-        for other in range(ZH):
-            owner = lax.rem(zh + other, ZH) * Y + source
-            rows = pl.ds(pl.multiple_of(owner * 64, 64), 64)
-            field_re[rows, :] = field_ref[pl.ds(other * 128, 64, stride=2), :]
-            field_im[rows, :] = field_ref[pl.ds(other * 128 + 1, 64, stride=2), :]
-        rows = pl.ds(pl.multiple_of(source * 2 * QR, 2 * QR), 2 * QR)
-        mine_ref[rows, :] = field_ref[pl.ds(pl.multiple_of(FIELD_ROWS + zh * 2 * QR, 2 * QR), 2 * QR), :]
-        theirs_ref[rows, :] = field_ref[pl.ds(pl.multiple_of(FIELD_ROWS + (1 - zh) * 2 * QR, 2 * QR), 2 * QR), :]
+    fields = (field_0, field_1, field_2, field_3, field_4, field_5, field_6, field_7)
+    for place, field_ref in enumerate(fields):
+        owner = lax.rem(zh + place // Y, ZH) * Y + lax.rem(y + Y - place % Y, Y)
+        rows = pl.ds(pl.multiple_of(owner * 64, 64), 64)
+        field_re[rows, :] = field_ref[pl.ds(0, 64, stride=2), :]
+        field_im[rows, :] = field_ref[pl.ds(1, 64, stride=2), :]
     total_re[...] = jnp.zeros(total_re.shape, f32)
     total_im[...] = jnp.zeros(total_im.shape, f32)
     probe_re = probe_ref[0]
@@ -330,38 +322,44 @@
     object_rows = object_field.reshape(128, NZ)
     dual_rows = dual_field.reshape(128, NZ)
 
+    with jax.named_scope("ray_sums"):
+        object_theirs = across(object_rows)
+        sums = call(ray_sums, shape(NEAR, ZL, HITS * QR, 2 * NZ, dtype=bf16), 0, 2, flops=2 * 2048 * 256 * 256)(
+            radon, volume_rows
+        )
+
     with jax.named_scope("fields"):
         packed = call(
-            pack, (shape(SENT_ROWS, NZ),) * Y, 1, 4, scratch=[pltpu.VMEM((128, NZ), f32)], flops=1_000_000
-        )(place, object_rows, across(object_rows), dual_rows, tile_range.reshape(1, ZL * XC))
+            pack, (shape(SENT_ROWS, NZ),) * Y, 1, 3, scratch=[pltpu.VMEM((128, NZ), f32)], flops=1_000_000
+        )(place, object_rows, dual_rows, tile_range.reshape(1, ZL * XC))
         fields = round_y(packed)
+        far_fields = round_y([object_theirs] * Y)
 
     with jax.named_scope("ray_sums"):
-        sums = call(ray_sums, shape(NEAR, ZL, HITS * QR, 2 * NZ, dtype=bf16), 0, 2, flops=2 * 2048 * 256 * 256)(
-            radon, volume_rows
-        )
-        sums, fields = lax.optimization_barrier((sums, fields))
         near_sums = lax.all_to_all(sums, CROSS, 0, 0, tiled=True)
-
-    with jax.named_scope("frames"):
-        *inter_parts, drift_mine, drift_sent = call(
-            frame_gradients,
-            (shape(2, 128, NZ),) + (shape(2, 128, NZ, dtype=bf16),) * 3 + (shape(64, NZ),) * 2,
-            2,
-            10,
-            scratch=[pltpu.VMEM((NDET, NZ), f32)] * 4,
-            flops=1_600_000_000,
-        )(place, positions, *fields, probe_field, measured[0], ah, al, bh, bl)
-        inter_parts = round_y(inter_parts)
 
     with jax.named_scope("targets"):
         tables = jnp.stack([field[FIELD_ROWS + DRIFT_ROWS, : ZL * XC] for field in fields])
-        tables, inter_parts[1] = lax.optimization_barrier((tables, inter_parts[1]))
         tables = tables.astype(jnp.int32).reshape(Y, ZL, XC)
         ahead = [lax.dynamic_index_in_dim(tables, (zl + k) % ZL, 1, keepdims=False) for k in range(ZL)]
         tables = jnp.stack([ahead[0]] + [shifted(ahead[k], "zl", ZL, k) for k in range(1, ZL)])
         tables = tables.reshape(ZL, Y * XC)
-        drift_theirs = across(drift_sent)
+        drifts = jnp.stack([field[FIELD_ROWS : FIELD_ROWS + DRIFT_ROWS] for field in fields])
+        drifts = drifts.reshape(Y, 2, 2 * QR, NZ)
+        drift_mine = lax.dynamic_index_in_dim(drifts, zh, 1, keepdims=False)
+        drift_theirs = across(lax.dynamic_index_in_dim(drifts, 1 - zh, 1, keepdims=False))
+        far_fields, tables, drift_theirs = lax.optimization_barrier((far_fields, tables, drift_theirs))
+
+    with jax.named_scope("frames"):
+        inter_parts = call(
+            frame_gradients,
+            (shape(2, 128, NZ),) + (shape(2, 128, NZ, dtype=bf16),) * 3,
+            2,
+            14,
+            scratch=[pltpu.VMEM((NDET, NZ), f32)] * 4,
+            flops=1_600_000_000,
+        )(place, positions, *fields, *far_fields, probe_field, measured[0], ah, al, bh, bl)
+        inter_parts = round_y(inter_parts)
 
     with jax.named_scope("near_sum"):
         dense, inter = call(
@@ -372,7 +370,6 @@
             scratch=[pltpu.VMEM((ZL, 128, 2 * NZ), f32)],
             flops=1_000_000,
         )(place, tables, near_sums, *inter_parts)
-        dense, drift_theirs = lax.optimization_barrier((dense, drift_theirs))
         far_sums = lax.all_to_all(dense, ALONG, 0, 0, tiled=True)
 
     with jax.named_scope("residual"):
@@ -381,7 +378,7 @@
             (shape(DEEP, 128, NZ, dtype=bf16),) + (shape(ZH, 3, 2 * QR, NZ),) * Y,
             1,
             4,
-            scratch=[pltpu.VMEM((128, NZ), f32)],
+            scratch=[pltpu.VMEM((128, NZ), f32)] * 2,
             flops=1_000_000,
         )(place, far_sums, inter, drift_mine, drift_theirs)
         kept = round_y(kept)

time: 118 us -> 116 us (0.983)
  starting transfers between devices: 56.1 us -> 49.8 us
  waiting for transfers between devices: 25 us -> 29.3 us
    ppermute x15 -> x18, starting transfers between devices: 31.7 us -> 27.6 us  [shifted(): lax.ppermute(value, axis, [(i, (i + step) % length) for i in range(length)])]
    all_to_all x1, starting transfers between devices: 9.37 us -> 6.51 us  [body(): near_sums = lax.all_to_all(sums, CROSS, 0, 0, tiled=True)]
    ppermute x15 -> x18, waiting for transfers between devices: 15.8 us -> 18.3 us  [shifted(): lax.ppermute(value, axis, [(i, (i + step) % length) for i in range(length)])]
    all_to_all x1, waiting for transfers between devices: 3.72 us -> 4.92 us  [body(): returned = lax.all_to_all(picked, CROSS, 0, 0, tiled=True)]
  transfers between devices with their start and end apart: 18 -> 21, of which waited for: 10 -> 10; matrix products, arithmetic and copies ran while one was open for 3% -> 3% of each run, Pallas kernels for 9% -> 9%
where the time goes in v5:
time: 116 us; the launch traced here: 115 us
  starting transfers between devices  49.8 us (43%)
  waiting for transfers between devices  29.3 us (25%)
  Pallas kernels  13.9 us (12%)
  blocking collectives  12.3 us (11%)
  local copies, waits for them, and re-layouts  8.74 us (8%)
    ppermute x18, starting transfers between devices, shifted(): lax.ppermute(value, axis, [(i, (i + step) % length) for i in range(length)])  27.6 us
    ppermute x18, waiting for transfers between devices, shifted(): lax.ppermute(value, axis, [(i, (i + step) % length) for i in range(length)])  18.3 us
    all_to_all x1, starting transfers between devices, body(): returned = lax.all_to_all(picked, CROSS, 0, 0, tiled=True)  12.3 us
    all_to_all x1, blocking collectives, body(): far_sums = lax.all_to_all(dense, ALONG, 0, 0, tiled=True)  12.3 us
    all_to_all x1, starting transfers between devices, body(): near_sums = lax.all_to_all(sums, CROSS, 0, 0, tiled=True)  6.51 us
    all_to_all x1, waiting for transfers between devices, body(): residuals = lax.all_to_all(copies, ALONG, 0, 0, tiled=True)  6.06 us
    all_to_all x1, waiting for transfers between devices, body(): returned = lax.all_to_all(picked, CROSS, 0, 0, tiled=True)  4.92 us
    pallas_call x1, Pallas kernels, body(): call(frame_gradients, (shape(2, 128, NZ),) + (shape(2, 128, NZ, dtype=bf1...  4.66 us
  transfers between devices with their start and end apart: 21, of which 10 were waited for; matrix products, arithmetic and copies ran while one was open for 3% of the time, Pallas kernels for 9%

profile of v5, /device:TPU:1, one launch (start us, length us, event | category | flops | bytes accessed | tf_op | source)
XLA Modules:
  0.0 115.2 jit_solution(13953740830084624592)
XLA Ops:
  0.6 7.8 %collective-permute-start = (f32[128,128]{1,0:T(8,128)}, f32[128,128]{1,0:T(8,128)S(1)}, u32[]{:S(2)}, u32[]{:S(2)}) collective-permute-start(f32[128,128]{1,0:T(8,128)} %bitcast.39), channel_id=1, source_target_pairs={{0,4},{4,0},{1,5},{5,1},{2,6},{6,2},{3,7},{7,3},{8,12},{12,8},{9,1... | collective-permute-start | bytes 196616 | tf_op jit(solution)/shard_map/ray_sums/ppermute | solution.py:303
  11.4 1.4 %collective-permute-start.4 = (f32[168,128]{1,0:T(8,128)S(1)}, f32[168,128]{1,0:T(8,128)S(1)}, u32[]{:S(2)}, u32[]{:S(2)}) collective-permute-start(f32[168,128]{1,0:T(8,128)S(1)} %get-tuple-element.32), channel_id=1, source_target_pairs={{0,1},{1,2},{2,3},{3,0},{4,5},{5,6},{6,7},{7,4},{8,9},{9,10},{10,1... | collective-permute-start | bytes 258056 | tf_op jit(solution)/shard_map/fields/ppermute | solution.py:303
  12.8 2.6 %collective-permute-start.5 = (f32[168,128]{1,0:T(8,128)S(1)}, f32[168,128]{1,0:T(8,128)S(1)}, u32[]{:S(2)}, u32[]{:S(2)}) collective-permute-start(f32[168,128]{1,0:T(8,128)S(1)} %get-tuple-element.33), channel_id=1, source_target_pairs={{0,2},{1,3},{2,0},{3,1},{4,6},{5,7},{6,4},{7,5},{8,10},{9,11},{10,... | collective-permute-start | bytes 258056 | tf_op jit(solution)/shard_map/fields/ppermute | solution.py:303
  15.4 1.1 collective-permute-start.6
  16.5 1.2 %copy-done = bf16[1,32,2,32,256]{4,3,2,1,0:T(8,128)(2,1)S(1)} copy-done((bf16[1,32,2,32,256]{4,3,2,1,0:T(8,128)(2,1)S(1)}, bf16[1,32,2,32,256]{4,3,2,1,0:T(8,128)(2,1)}, u32[]{:S(2)}) %copy-start) | copy-done | bytes 1048600
  17.7 0.9 copy-done.2
  18.7 1.8 %ray_sums.1 = bf16[32,4,16,256]{3,2,1,0:T(8,128)(2,1)} custom-call(bf16[32,2,32,256]{3,2,1,0:T(8,128)(2,1)S(1)} %bitcast.35, f32[512,128]{1,0:T(8,128)S(1)} %bitcast.37), custom_call_target="tpu_custom_call" | custom-call | flops 268435456 | bytes 1048576 | tf_op jit(solution)/shard_map/ray_sums/ray_sums/pallas_call | solution.py:327
  20.5 6.5 %all-to-all-start = ((bf16[32,4,16,256]{3,2,1,0:T(8,128)(2,1)}), bf16[32,4,16,256]{3,2,1,0:T(8,128)(2,1)S(1)}, u32[]{:S(2)}, u32[]{:S(2)}) async-start(bf16[32,4,16,256]{3,2,1,0:T(8,128)(2,1)} %ray_sums.1), calls=%async_computation | async-start | bytes 2097152 | tf_op jit(solution)/shard_map/ray_sums/all_to_all | solution.py:339
  27.2 2.6 %collective-permute-start.3 = (f32[128,128]{1,0:T(8,128)S(1)}, f32[128,128]{1,0:T(8,128)S(1)}, u32[]{:S(2)}, u32[]{:S(2)}) collective-permute-start(f32[128,128]{1,0:T(8,128)S(1)} %collective-permute-done.field_4), channel_id=1, source_target_pairs={{0,3},{1,0},{2,1},{3,2},{4,7},{5,4},{6,5},{7,6},{8,11},{9,8},{10,9... | collective-permute-start | bytes 196616 | tf_op jit(solution)/shard_map/fields/ppermute | solution.py:303
  31.5 1.7 %collective-permute-start.9 = (s32[4,8]{1,0:T(4,128)S(1)}, s32[4,8]{1,0:T(4,128)S(1)}, u32[]{:S(2)}, u32[]{:S(2)}) collective-permute-start(s32[4,8]{1,0:T(4,128)S(1)} %bitcast.54), channel_id=1, source_target_pairs={{0,192},{64,0},{128,64},{192,128},{1,193},{65,1},{129,65},{193,129... | collective-permute-start | bytes 392 | tf_op jit(solution)/shard_map/targets/ppermute | solution.py:303
  35.0 1.9 %collective-permute-done.8 = s32[4,8]{1,0:T(4,128)S(1)} collective-permute-done((s32[4,8]{1,0:T(4,128)S(1)}, s32[4,8]{1,0:T(4,128)S(1)}, u32[]{:S(2)}, u32[]{:S(2)}) %collective-permute-start.8) | collective-permute-done | bytes 160 | tf_op jit(solution)/shard_map/targets/ppermute | solution.py:303
  36.9 1.2 %collective-permute-start.10 = (f32[4,16,128]{2,1,0:T(8,128)S(1)}, f32[4,16,128]{2,1,0:T(8,128)S(1)}, u32[]{:S(2)}, u32[]{:S(2)}) collective-permute-start(f32[4,16,128]{2,1,0:T(8,128)S(1)} %get-tuple-element.60), channel_id=1, source_target_pairs={{0,4},{4,0},{1,5},{5,1},{2,6},{6,2},{3,7},{7,3},{8,12},{12,8},{9,1... | collective-permute-start | bytes 98312 | tf_op jit(solution)/shard_map/targets/ppermute | solution.py:303
  39.0 4.8 %collective-permute-done.10.theirs_ref = f32[4,16,128]{2,1,0:T(8,128)S(1)} collective-permute-done((f32[4,16,128]{2,1,0:T(8,128)S(1)}, f32[4,16,128]{2,1,0:T(8,128)S(1)}, u32[]{:S(2)}, u32[]{:S(2)}) %collective-permute-start.10) | collective-permute-done | bytes 32800 | tf_op jit(solution)/shard_map/targets/ppermute | solution.py:303
  43.9 1.4 %collective-permute-done.1.field_5 = f32[128,128]{1,0:T(8,128)S(1)} collective-permute-done((f32[128,128]{1,0:T(8,128)S(1)}, f32[128,128]{1,0:T(8,128)S(1)}, u32[]{:S(2)}, u32[]{:S(2)}) %collective-permute-start.1) | collective-permute-done | bytes 65568 | tf_op jit(solution)/shard_map/fields/ppermute | solution.py:303
  45.3 4.7 %frame_gradients.1 = (f32[2,128,128]{2,1,0:T(8,128)S(1)}, bf16[2,128,128]{2,1,0:T(8,128)(2,1)S(1)}, bf16[2,128,128]{2,1,0:T(8,128)(2,1)S(1)}, bf16[2,128,128]{2,1,0:T(8,128)(2,1)S(1)}) custom-call(s32[3]{0:T(128)S(1)} %pad_add_fusion.1.place_ref, s32[1,8]{1,0:T(1,128)S(1)} %copy-done.15, f32[168,128]{1,0:T(8,128)S(1)} %get-tuple-element.31.field_0, ...), custom_call_target="tpu_custom_call" | custom-call | flops 1600000000 | bytes 1048576 | tf_op jit(solution)/shard_map/frames/frame_gradients/pallas_call | solution.py:354
  50.3 1.9 %collective-permute-start.12 = (bf16[2,128,128]{2,1,0:T(8,128)(2,1)S(1)}, bf16[2,128,128]{2,1,0:T(8,128)(2,1)S(1)}, u32[]{:S(2)}, u32[]{:S(2)}) collective-permute-start(bf16[2,128,128]{2,1,0:T(8,128)(2,1)S(1)} %get-tuple-element.42), channel_id=1, source_target_pairs={{0,2},{1,3},{2,0},{3,1},{4,6},{5,7},{6,4},{7,5},{8,10},{9,11},{10,... | collective-permute-start | bytes 196616 | tf_op jit(solution)/shard_map/frames/ppermute | solution.py:303
  52.9 2.3 %collective-permute-done.11.one_ref = bf16[2,128,128]{2,1,0:T(8,128)(2,1)S(1)} collective-permute-done((bf16[2,128,128]{2,1,0:T(8,128)(2,1)S(1)}, bf16[2,128,128]{2,1,0:T(8,128)(2,1)S(1)}, u32[]{:S(2)}, u32[]{:S(2)}) %collective-permute-start.11) | collective-permute-done | bytes 65568 | tf_op jit(solution)/shard_map/frames/ppermute | solution.py:303
  55.9 1.3 %add_tiles.1 = (bf16[8,128,128]{2,1,0:T(8,128)(2,1)S(1)}, f32[2,128,128]{2,1,0:T(8,128)S(1)}) custom-call(s32[3]{0:T(128)S(1)} %pad_add_fusion.1.place_ref, s32[4,32]{1,0:T(4,128)S(1)} %pad_add_fusion.target_ref, bf16[32,4,16,256]{3,2,1,0:T(8,128)(2,1)S(1)} %all-to-all-done.sums_ref, f32[2,128,128]{2,1,0:T(8,128)S(1)} %get-tuple-element.40.own_ref, ...), custom_call_target="tpu_custom_call" | custom-call | flops 1000000 | bytes 1048576 | tf_op jit(solution)/shard_map/near_sum/add_tiles/pallas_call | solution.py:365
  57.2 12.3 %all_to_all.20.sums_ref = bf16[8,128,128]{2,1,0:T(8,128)(2,1)S(1)} all-to-all(bf16[8,128,128]{2,1,0:T(8,128)(2,1)S(1)} %get-tuple-element.44), channel_id=1, replica_groups=mesh['zl'=4,'x'=4,'c'=2,'zh'=2,'y'=4] {'zh','zl'}, dimensions={0} | all-to-all | bytes 524288 | tf_op jit(solution)/shard_map/near_sum/all_to_all | solution.py:373
  69.5 1.3 %residual_part.1 = (bf16[8,128,128]{2,1,0:T(8,128)(2,1)}, f32[2,3,16,128]{3,2,1,0:T(8,128)S(1)}, f32[2,3,16,128]{3,2,1,0:T(8,128)S(1)}, f32[2,3,16,128]{3,2,1,0:T(8,128)S(1)}, f32[2,3,16,128]{3,2,1,0:T(8,128)S(1)}) custom-call(s32[3]{0:T(128)S(1)} %pad_add_fusion.1.place_ref, bf16[8,128,128]{2,1,0:T(8,128)(2,1)S(1)} %all_to_all.20.sums_ref, ...), custom_call_target="tpu_custom_call" | custom-call | flops 1000000 | bytes 1048576 | tf_op jit(solution)/shard_map/residual/residual_part/pallas_call | solution.py:376
  70.8 3.4 %all-to-all-start.2 = ((bf16[8,128,128]{2,1,0:T(8,128)(2,1)}), bf16[8,128,128]{2,1,0:T(8,128)(2,1)S(1)}, u32[]{:S(2)}, u32[]{:S(2)}) async-start(bf16[8,128,128]{2,1,0:T(8,128)(2,1)} %get-tuple-element.47), calls=%async_computation.2 | async-start | bytes 524288 | tf_op jit(solution)/shard_map/residual/all_to_all | solution.py:385
  74.9 2.4 %collective-permute-start.15 = (f32[2,3,16,128]{3,2,1,0:T(8,128)S(1)}, f32[2,3,16,128]{3,2,1,0:T(8,128)S(1)}, u32[]{:S(2)}, u32[]{:S(2)}) collective-permute-start(f32[2,3,16,128]{3,2,1,0:T(8,128)S(1)} %get-tuple-element.50), channel_id=1, source_target_pairs={{0,2},{1,3},{2,0},{3,1},{4,6},{5,7},{6,4},{7,5},{8,10},{9,11},{10,... | collective-permute-start | bytes 147464 | tf_op jit(solution)/shard_map/residual/ppermute | solution.py:303
  77.4 6.1 %all-to-all-done.2.residual_ref = bf16[8,128,128]{2,1,0:T(8,128)(2,1)S(1)} async-done(((bf16[8,128,128]{2,1,0:T(8,128)(2,1)}), bf16[8,128,128]{2,1,0:T(8,128)(2,1)S(1)}, u32[]{:S(2)}, u32[]{:S(2)}) %all-to-all-start.2) | async-done | bytes 262176 | tf_op jit(solution)/shard_map/residual/all_to_all | solution.py:385
  83.5 1.9 %pick_tiles.1 = bf16[32,4,16,256]{3,2,1,0:T(8,128)(2,1)} custom-call(s32[3]{0:T(128)S(1)} %pad_add_fusion.1.place_ref, s32[4,32]{1,0:T(4,128)S(1)} %pad_add_fusion.target_ref, bf16[8,128,128]{2,1,0:T(8,128)(2,1)S(1)} %all-to-all-done.2.residual_ref), custom_call_target="tpu_custom_call" | custom-call | flops 1000000 | bytes 1048576 | tf_op jit(solution)/shard_map/pick/pick_tiles/pallas_call | solution.py:388
  85.4 12.3 %all-to-all-start.3 = ((bf16[32,4,16,256]{3,2,1,0:T(8,128)(2,1)}), bf16[32,4,16,256]{3,2,1,0:T(8,128)(2,1)S(1)}, u32[]{:S(2)}, u32[]{:S(2)}) async-start(bf16[32,4,16,256]{3,2,1,0:T(8,128)(2,1)} %pick_tiles.1), calls=%async_computation.3 | async-start | bytes 2097152 | tf_op jit(solution)/shard_map/pick/all_to_all | solution.py:397
  98.6 0.9 collective-permute-start.17
  99.4 1.1 copy.29
  100.5 1.5 %copy.30.radon_ref = bf16[256,2048]{1,0:T(8,128)(2,1)S(1)} copy(bf16[256,2048]{0,1:T(8,128)(2,1)} %bitcast.46) | data formatting | bytes 2097152 | tf_op jit(solution)/shard_map/back_project/reshape | solution.py:406
  102.1 5.8 %collective-permute-done.17.theirs_ref = f32[4,3,16,128]{3,2,1,0:T(8,128)S(1)} collective-permute-done((f32[4,3,16,128]{3,2,1,0:T(8,128)S(1)}, f32[4,3,16,128]{3,2,1,0:T(8,128)S(1)}, u32[]{:S(2)}, u32[]{:S(2)}) %collective-permute-start.17) | collective-permute-done | bytes 98336 | tf_op jit(solution)/shard_map/updates/ppermute | solution.py:303
  107.9 1.2 %updates.1 = (f32[128,128]{1,0:T(8,128)}, f32[128,128]{1,0:T(8,128)}) custom-call(s32[3]{0:T(128)S(1)} %pad_add_fusion.1.place_ref, f32[2,3,16,128]{3,2,1,0:T(8,128)S(1)} %get-tuple-element.52.own_ref, f32[2,3,16,128]{3,2,1,0:T(8,128)S(1)} %copy-done.9, f32[2,3,16,128]{3,2,1,0:T(8,128)S(1)} %copy-done.11, ...), custom_call_target="tpu_custom_call" | custom-call | flops 1000000 | bytes 1048576 | tf_op jit(solution)/shard_map/updates/updates/pallas_call | solution.py:401
  109.2 4.9 %all-to-all-done.3.picked_ref = bf16[32,4,16,256]{3,2,1,0:T(8,128)(2,1)S(1)} async-done(((bf16[32,4,16,256]{3,2,1,0:T(8,128)(2,1)}), bf16[32,4,16,256]{3,2,1,0:T(8,128)(2,1)S(1)}, u32[]{:S(2)}, u32[]{:S(2)}) %all-to-all-start.3) | async-done | bytes 1048608 | tf_op jit(solution)/shard_map/pick/all_to_all | solution.py:397
  114.1 1.1 back_project.1
  (90 shorter events, 10.8 us)
Async XLA Ops:
  0.6 26.6 %collective-permute-start = (f32[128,128]{1,0:T(8,128)}, f32[128,128]{1,0:T(8,128)S(1)}, u32[]{:S(2)}, u32[]{:S(2)}) collective-permute-start(f32[128,128]{1,0:T(8,128)} %bitcast.39), channel_id=1, source_target_pairs={{0,4},{4,0},{1,5},{5,1},{2,6},{6,2},{3,7},{7,3},{8,12},{12,8},{9,1... | collective-permute-start | bytes 196616 | tf_op jit(solution)/shard_map/ray_sums/ppermute | solution.py:303
  11.4 19.0 %collective-permute-start.4 = (f32[168,128]{1,0:T(8,128)S(1)}, f32[168,128]{1,0:T(8,128)S(1)}, u32[]{:S(2)}, u32[]{:S(2)}) collective-permute-start(f32[168,128]{1,0:T(8,128)S(1)} %get-tuple-element.32), channel_id=1, source_target_pairs={{0,1},{1,2},{2,3},{3,0},{4,5},{5,6},{6,7},{7,4},{8,9},{9,10},{10,1... | collective-permute-start | bytes 258056 | tf_op jit(solution)/shard_map/fields/ppermute | solution.py:303
  12.8 18.3 %collective-permute-start.5 = (f32[168,128]{1,0:T(8,128)S(1)}, f32[168,128]{1,0:T(8,128)S(1)}, u32[]{:S(2)}, u32[]{:S(2)}) collective-permute-start(f32[168,128]{1,0:T(8,128)S(1)} %get-tuple-element.33), channel_id=1, source_target_pairs={{0,2},{1,3},{2,0},{3,1},{4,6},{5,7},{6,4},{7,5},{8,10},{9,11},{10,... | collective-permute-start | bytes 258056 | tf_op jit(solution)/shard_map/fields/ppermute | solution.py:303
  15.4 15.8 %collective-permute-start.6 = (f32[168,128]{1,0:T(8,128)S(1)}, f32[168,128]{1,0:T(8,128)S(1)}, u32[]{:S(2)}, u32[]{:S(2)}) collective-permute-start(f32[168,128]{1,0:T(8,128)S(1)} %get-tuple-element.34), channel_id=1, source_target_pairs={{0,3},{1,0},{2,1},{3,2},{4,7},{5,4},{6,5},{7,6},{8,11},{9,8},{10,9... | collective-permute-start | bytes 258056 | tf_op jit(solution)/shard_map/fields/ppermute | solution.py:303
  20.5 24.8 %copy-start.14 = (f32[2,128,128]{2,1,0:T(8,128)S(1)}, f32[2,128,128]{2,1,0:T(8,128)}, u32[]{:S(2)}) copy-start(f32[2,128,128]{2,1,0:T(8,128)} %probe_ref.1) | copy-start | bytes 393220
  20.5 24.8 %copy-start.16 = (bf16[256,256]{1,0:T(8,128)(2,1)S(1)}, bf16[256,256]{1,0:T(8,128)(2,1)}, u32[]{:S(2)}) copy-start(bf16[256,256]{1,0:T(8,128)(2,1)} %constant.71.clone.bl_ref) | copy-start | bytes 393220
  20.5 24.8 %copy-start.17 = (bf16[256,256]{1,0:T(8,128)(2,1)S(1)}, bf16[256,256]{1,0:T(8,128)(2,1)}, u32[]{:S(2)}) copy-start(bf16[256,256]{1,0:T(8,128)(2,1)} %constant.70.clone.bh_ref) | copy-start | bytes 393220
  20.5 24.8 %copy-start.18 = (bf16[256,256]{1,0:T(8,128)(2,1)S(1)}, bf16[256,256]{1,0:T(8,128)(2,1)}, u32[]{:S(2)}) copy-start(bf16[256,256]{1,0:T(8,128)(2,1)} %constant.69.clone.al_ref) | copy-start | bytes 393220
  20.5 24.8 %copy-start.19 = (bf16[256,256]{1,0:T(8,128)(2,1)S(1)}, bf16[256,256]{1,0:T(8,128)(2,1)}, u32[]{:S(2)}) copy-start(bf16[256,256]{1,0:T(8,128)(2,1)} %constant.68.clone.ah_ref) | copy-start | bytes 393220
  20.5 35.3 %all-to-all-start = ((bf16[32,4,16,256]{3,2,1,0:T(8,128)(2,1)}), bf16[32,4,16,256]{3,2,1,0:T(8,128)(2,1)S(1)}, u32[]{:S(2)}, u32[]{:S(2)}) async-start(bf16[32,4,16,256]{3,2,1,0:T(8,128)(2,1)} %ray_sums.1), calls=%async_computation | async-start | bytes 2097152 | tf_op jit(solution)/shard_map/ray_sums/all_to_all | solution.py:339
  27.0 18.2 %copy-start.13 = (f32[1,8,128,128]{3,2,1,0:T(8,128)S(1)}, f32[1,8,128,128]{3,2,1,0:T(8,128)}, u32[]{:S(2)}) copy-start(f32[1,8,128,128]{3,2,1,0:T(8,128)} %param.12) | copy-start | bytes 1572868
  27.2 16.6 %collective-permute-start.3 = (f32[128,128]{1,0:T(8,128)S(1)}, f32[128,128]{1,0:T(8,128)S(1)}, u32[]{:S(2)}, u32[]{:S(2)}) collective-permute-start(f32[128,128]{1,0:T(8,128)S(1)} %collective-permute-done.field_4), channel_id=1, source_target_pairs={{0,3},{1,0},{2,1},{3,2},{4,7},{5,4},{6,5},{7,6},{8,11},{9,8},{10,9... | collective-permute-start | bytes 196616 | tf_op jit(solution)/shard_map/fields/ppermute | solution.py:303
  29.9 14.0 %collective-permute-start.2 = (f32[128,128]{1,0:T(8,128)S(1)}, f32[128,128]{1,0:T(8,128)S(1)}, u32[]{:S(2)}, u32[]{:S(2)}) collective-permute-start(f32[128,128]{1,0:T(8,128)S(1)} %collective-permute-done.field_4), channel_id=1, source_target_pairs={{0,2},{1,3},{2,0},{3,1},{4,6},{5,7},{6,4},{7,5},{8,10},{9,11},{10,... | collective-permute-start | bytes 196616 | tf_op jit(solution)/shard_map/fields/ppermute | solution.py:303
  30.4 14.8 %collective-permute-start.1 = (f32[128,128]{1,0:T(8,128)S(1)}, f32[128,128]{1,0:T(8,128)S(1)}, u32[]{:S(2)}, u32[]{:S(2)}) collective-permute-start(f32[128,128]{1,0:T(8,128)S(1)} %collective-permute-done.field_4), channel_id=1, source_target_pairs={{0,1},{1,2},{2,3},{3,0},{4,5},{5,6},{6,7},{7,4},{8,9},{9,10},{10,1... | collective-permute-start | bytes 196616 | tf_op jit(solution)/shard_map/fields/ppermute | solution.py:303
  31.5 2.7 %collective-permute-start.9 = (s32[4,8]{1,0:T(4,128)S(1)}, s32[4,8]{1,0:T(4,128)S(1)}, u32[]{:S(2)}, u32[]{:S(2)}) collective-permute-start(s32[4,8]{1,0:T(4,128)S(1)} %bitcast.54), channel_id=1, source_target_pairs={{0,192},{64,0},{128,64},{192,128},{1,193},{65,1},{129,65},{193,129... | collective-permute-start | bytes 392 | tf_op jit(solution)/shard_map/targets/ppermute | solution.py:303
  33.2 3.7 %collective-permute-start.8 = (s32[4,8]{1,0:T(4,128)S(1)}, s32[4,8]{1,0:T(4,128)S(1)}, u32[]{:S(2)}, u32[]{:S(2)}) collective-permute-start(s32[4,8]{1,0:T(4,128)S(1)} %bitcast.53), channel_id=1, source_target_pairs={{0,128},{64,192},{128,0},{192,64},{1,129},{65,193},{129,1},{193,65... | collective-permute-start | bytes 392 | tf_op jit(solution)/shard_map/targets/ppermute | solution.py:303
  34.2 4.7 %collective-permute-start.7 = (s32[4,8]{1,0:T(4,128)S(1)}, s32[4,8]{1,0:T(4,128)S(1)}, u32[]{:S(2)}, u32[]{:S(2)}) collective-permute-start(s32[4,8]{1,0:T(4,128)S(1)} %bitcast.52), channel_id=1, source_target_pairs={{0,64},{64,128},{128,192},{192,0},{1,65},{65,129},{129,193},{193,1... | collective-permute-start | bytes 392 | tf_op jit(solution)/shard_map/targets/ppermute | solution.py:303
  36.9 7.0 %collective-permute-start.10 = (f32[4,16,128]{2,1,0:T(8,128)S(1)}, f32[4,16,128]{2,1,0:T(8,128)S(1)}, u32[]{:S(2)}, u32[]{:S(2)}) collective-permute-start(f32[4,16,128]{2,1,0:T(8,128)S(1)} %get-tuple-element.60), channel_id=1, source_target_pairs={{0,4},{4,0},{1,5},{5,1},{2,6},{6,2},{3,7},{7,3},{8,12},{12,8},{9,1... | collective-permute-start | bytes 98312 | tf_op jit(solution)/shard_map/targets/ppermute | solution.py:303
  50.0 5.3 %collective-permute-start.11 = (bf16[2,128,128]{2,1,0:T(8,128)(2,1)S(1)}, bf16[2,128,128]{2,1,0:T(8,128)(2,1)S(1)}, u32[]{:S(2)}, u32[]{:S(2)}) collective-permute-start(bf16[2,128,128]{2,1,0:T(8,128)(2,1)S(1)} %get-tuple-element.41), channel_id=1, source_target_pairs={{0,1},{1,2},{2,3},{3,0},{4,5},{5,6},{6,7},{7,4},{8,9},{9,10},{10,1... | collective-permute-start | bytes 196616 | tf_op jit(solution)/shard_map/frames/ppermute | solution.py:303
  50.3 5.0 %collective-permute-start.12 = (bf16[2,128,128]{2,1,0:T(8,128)(2,1)S(1)}, bf16[2,128,128]{2,1,0:T(8,128)(2,1)S(1)}, u32[]{:S(2)}, u32[]{:S(2)}) collective-permute-start(bf16[2,128,128]{2,1,0:T(8,128)(2,1)S(1)} %get-tuple-element.42), channel_id=1, source_target_pairs={{0,2},{1,3},{2,0},{3,1},{4,6},{5,7},{6,4},{7,5},{8,10},{9,11},{10,... | collective-permute-start | bytes 196616 | tf_op jit(solution)/shard_map/frames/ppermute | solution.py:303
  52.1 3.7 %collective-permute-start.13 = (bf16[2,128,128]{2,1,0:T(8,128)(2,1)S(1)}, bf16[2,128,128]{2,1,0:T(8,128)(2,1)S(1)}, u32[]{:S(2)}, u32[]{:S(2)}) collective-permute-start(bf16[2,128,128]{2,1,0:T(8,128)(2,1)S(1)} %get-tuple-element.43), channel_id=1, source_target_pairs={{0,3},{1,0},{2,1},{3,2},{4,7},{5,4},{6,5},{7,6},{8,11},{9,8},{10,9... | collective-permute-start | bytes 196616 | tf_op jit(solution)/shard_map/frames/ppermute | solution.py:303
  70.8 12.7 %all-to-all-start.2 = ((bf16[8,128,128]{2,1,0:T(8,128)(2,1)}), bf16[8,128,128]{2,1,0:T(8,128)(2,1)S(1)}, u32[]{:S(2)}, u32[]{:S(2)}) async-start(bf16[8,128,128]{2,1,0:T(8,128)(2,1)} %get-tuple-element.47), calls=%async_computation.2 | async-start | bytes 524288 | tf_op jit(solution)/shard_map/residual/all_to_all | solution.py:385
  74.2 11.1 %collective-permute-start.14 = (f32[2,3,16,128]{3,2,1,0:T(8,128)S(1)}, f32[2,3,16,128]{3,2,1,0:T(8,128)S(1)}, u32[]{:S(2)}, u32[]{:S(2)}) collective-permute-start(f32[2,3,16,128]{3,2,1,0:T(8,128)S(1)} %get-tuple-element.49), channel_id=1, source_target_pairs={{0,1},{1,2},{2,3},{3,0},{4,5},{5,6},{6,7},{7,4},{8,9},{9,10},{10,1... | collective-permute-start | bytes 147464 | tf_op jit(solution)/shard_map/residual/ppermute | solution.py:303
  74.9 10.4 %collective-permute-start.15 = (f32[2,3,16,128]{3,2,1,0:T(8,128)S(1)}, f32[2,3,16,128]{3,2,1,0:T(8,128)S(1)}, u32[]{:S(2)}, u32[]{:S(2)}) collective-permute-start(f32[2,3,16,128]{3,2,1,0:T(8,128)S(1)} %get-tuple-element.50), channel_id=1, source_target_pairs={{0,2},{1,3},{2,0},{3,1},{4,6},{5,7},{6,4},{7,5},{8,10},{9,11},{10,... | collective-permute-start | bytes 147464 | tf_op jit(solution)/shard_map/residual/ppermute | solution.py:303
  77.4 8.0 %collective-permute-start.16 = (f32[2,3,16,128]{3,2,1,0:T(8,128)S(1)}, f32[2,3,16,128]{3,2,1,0:T(8,128)S(1)}, u32[]{:S(2)}, u32[]{:S(2)}) collective-permute-start(f32[2,3,16,128]{3,2,1,0:T(8,128)S(1)} %get-tuple-element.51), channel_id=1, source_target_pairs={{0,3},{1,0},{2,1},{3,2},{4,7},{5,4},{6,5},{7,6},{8,11},{9,8},{10,9... | collective-permute-start | bytes 147464 | tf_op jit(solution)/shard_map/residual/ppermute | solution.py:303
  85.4 12.4 %copy-start.8 = (f32[2,3,16,128]{3,2,1,0:T(8,128)}, f32[2,3,16,128]{3,2,1,0:T(8,128)S(1)}, u32[]{:S(2)}) copy-start(f32[2,3,16,128]{3,2,1,0:T(8,128)S(1)} %collective-permute-done.14.one_ref) | copy-start | bytes 147460
  85.4 12.4 %copy-start.10 = (f32[2,3,16,128]{3,2,1,0:T(8,128)}, f32[2,3,16,128]{3,2,1,0:T(8,128)S(1)}, u32[]{:S(2)}) copy-start(f32[2,3,16,128]{3,2,1,0:T(8,128)S(1)} %collective-permute-done.15.two_ref) | copy-start | bytes 147460
  85.4 14.0 %copy-start.1 = (bf16[1,32,2,32,256]{4,3,2,1,0:T(8,128)(2,1)S(1)}, bf16[1,32,2,32,256]{4,3,2,1,0:T(8,128)(2,1)}, u32[]{:S(2)}) copy-start(bf16[1,32,2,32,256]{4,3,2,1,0:T(8,128)(2,1)} %param.18) | copy-start | bytes 3145732
  85.4 28.7 %all-to-all-start.3 = ((bf16[32,4,16,256]{3,2,1,0:T(8,128)(2,1)}), bf16[32,4,16,256]{3,2,1,0:T(8,128)(2,1)S(1)}, u32[]{:S(2)}, u32[]{:S(2)}) async-start(bf16[32,4,16,256]{3,2,1,0:T(8,128)(2,1)} %pick_tiles.1), calls=%async_computation.3 | async-start | bytes 2097152 | tf_op jit(solution)/shard_map/pick/all_to_all | solution.py:397
  98.6 9.3 %collective-permute-start.17 = (f32[4,3,16,128]{3,2,1,0:T(8,128)S(1)}, f32[4,3,16,128]{3,2,1,0:T(8,128)S(1)}, u32[]{:S(2)}, u32[]{:S(2)}) collective-permute-start(f32[4,3,16,128]{3,2,1,0:T(8,128)S(1)} %pad_maximum_fusion), channel_id=1, source_target_pairs={{0,4},{4,0},{1,5},{5,1},{2,6},{6,2},{3,7},{7,3},{8,12},{12,8},{9,1... | collective-permute-start | bytes 294920 | tf_op jit(solution)/shard_map/updates/ppermute | solution.py:303
  100.5 7.4 %copy-start.11 = (f32[2,3,16,128]{3,2,1,0:T(8,128)S(1)}, f32[2,3,16,128]{3,2,1,0:T(8,128)}, u32[]{:S(2)}) copy-start(f32[2,3,16,128]{3,2,1,0:T(8,128)} %copy-done.10) | copy-start | bytes 147460
  102.1 12.0 %copy-start.3 = (f32[256,2,128]{2,1,0:T(2,128)S(1)}, f32[256,2,128]{2,1,0:T(2,128)}, u32[]{:S(2)}) copy-start(f32[256,2,128]{2,1,0:T(2,128)} %param.17) | copy-start | bytes 786436
  (11 other events, 34.4 us)

commit v6 on v5

--- a/solution.py
+++ b/solution.py
@@ -25,6 +25,7 @@
 DEEP = ZH * ZL
 QR = RAYS // Y
 FR_DEV = 8
+FRAMES_COST = 20_000_000_000
 
 penalty = 1.0
 object_step = 0.1
@@ -36,14 +37,15 @@
 
 VM = pl.BlockSpec(memory_space=pltpu.VMEM)
 SM = pl.BlockSpec(memory_space=pltpu.SMEM)
-
-
-def call(kernel, outs, n_smem, n_vmem, scratch=(), flops=0, moved=1 << 20, limit=48 << 20):
+FAR = pl.BlockSpec(memory_space=pltpu.HBM)
+
+
+def call(kernel, outs, n_smem, n_vmem, scratch=(), flops=0, moved=1 << 20, limit=48 << 20, n_far=0):
     many = isinstance(outs, tuple)
     return pl.pallas_call(
         kernel,
         out_shape=outs,
-        in_specs=[SM] * n_smem + [VM] * n_vmem,
+        in_specs=[SM] * n_smem + [FAR] * n_far + [VM] * n_vmem,
         out_specs=tuple(VM for _ in outs) if many else VM,
         scratch_shapes=list(scratch),
         compiler_params=pltpu.CompilerParams(vmem_limit_bytes=limit),
@@ -67,11 +69,19 @@
     return jnp.asarray(high), jnp.asarray(low), jnp.asarray(high.T.copy()), jnp.asarray(low.T.copy())
 
 
-def ray_sums(radon_ref, volume_ref, out_ref):
+def ray_sums(radon_far, volume_far, out_ref, radon_ref, volume_ref, sems):
+    copies = [pltpu.make_async_copy(volume_far, volume_ref, sems.at[ZL])]
+    for zl in range(ZL):
+        angles = pl.ds(zl * XC, XC)
+        copies.append(pltpu.make_async_copy(radon_far.at[angles], radon_ref.at[angles], sems.at[zl]))
+    for copy in copies:
+        copy.start()
+    copies[0].wait()
     volume_half = jnp.concatenate(
         [volume_ref[pl.ds(0, TILE, stride=2), :], volume_ref[pl.ds(1, TILE, stride=2), :]], axis=1
     ).astype(bf16)
     for zl in range(ZL):
+        copies[1 + zl].wait()
         for xc in range(XC):
             rows = radon_ref[zl * XC + xc].reshape(HITS * RAYS, TILE)
             sums = jnp.dot(rows, volume_half, preferred_element_type=f32)
@@ -82,22 +92,36 @@
 
 
 def first_rows(place_ref, target_ref):
-    back_y = [lax.rem(place_ref[1] + Y - y, Y) * XC for y in range(Y)]
-    back_zl = [lax.rem(place_ref[2] + ZL - zl, ZL) for zl in range(ZL)]
+    zl_here = place_ref[2]
+    back_y = [lax.rem(place_ref[1] + Y - y, Y) * ZL for y in range(Y)]
+    back_zl = [lax.rem(zl_here + ZL - zl, ZL) for zl in range(ZL)]
 
     def row(zl, y, xc):
-        return pl.multiple_of(target_ref[back_zl[zl], back_y[y] + xc] * QR, QR)
+        return pl.multiple_of(target_ref[back_y[y] + back_zl[zl], zl_here * XC + xc] * QR, QR)
 
     return row
 
 
-def add_tiles(place_ref, target_ref, sums_ref, own_ref, one_ref, two_ref, three_ref, out_ref, inter_ref, total):
+def add_tiles(
+    place_ref, target_ref, sums_ref, inter_0, inter_1, inter_2, inter_3, field_0, field_1, field_2, field_3,
+    out_ref, inter_ref, total,
+):
+    zh = place_ref[0]
+    y_here = place_ref[1]
+    zl_here = place_ref[2]
     row = first_rows(place_ref, target_ref)
     total[...] = jnp.zeros(total.shape, f32)
     for part in range(2):
-        inter = (own_ref[part] + one_ref[part].astype(f32)) + (two_ref[part].astype(f32) + three_ref[part].astype(f32))
+        inter = (inter_0[part] + inter_1[part].astype(f32)) + (inter_2[part].astype(f32) + inter_3[part].astype(f32))
         inter_ref[part] = inter
-        total[place_ref[2], :, part * NZ : (part + 1) * NZ] = inter * share
+        total[zl_here, :, part * NZ : (part + 1) * NZ] = inter * share
+    for back, field_ref in enumerate((field_0, field_1, field_2, field_3)):
+        owner = zh * Y + lax.rem(y_here + Y - back, Y)
+        rows = pl.ds(pl.multiple_of(owner * 2 * QR, 2 * QR), 2 * QR)
+        base = FIELD_ROWS
+        total[zl_here, rows, :] -= jnp.concatenate(
+            [field_ref[base : base + 2 * QR, :], field_ref[base + 2 * QR : base + 4 * QR, :]], axis=1
+        )
     for xc in range(XC):
         for y in range(Y):
             for zl in range(ZL):
@@ -107,21 +131,14 @@
             out_ref[zh * ZL + zl] = total[zl, :, zh * NZ : (zh + 1) * NZ].astype(bf16)
 
 
-def residual_part(
-    place_ref, sums_ref, inter_ref, mine_ref, theirs_ref, residual_ref, own_ref, one_ref, two_ref, three_ref,
-    joint, drift,
-):
+def residual_part(place_ref, sums_ref, inter_ref, residual_ref, own_ref, one_ref, two_ref, three_ref, joint):
     zh = place_ref[0]
     y = place_ref[1]
     total = sums_ref[0].astype(f32)
     for source in range(1, DEEP):
         total = total + sums_ref[source].astype(f32)
     joint[...] = total
-    for other, ref in enumerate((mine_ref, theirs_ref)):
-        for back in range(Y):
-            owner = lax.rem(zh + other, ZH) * Y + lax.rem(y + Y - back, Y)
-            drift[pl.ds(pl.multiple_of(owner * 2 * QR, 2 * QR), 2 * QR), :] = ref[back]
-    residual = (keep * (total - drift[...])).astype(bf16)
+    residual = (keep * total).astype(bf16)
     for copy in range(DEEP):
         residual_ref[copy] = residual
     for ahead, ref in enumerate((own_ref, one_ref, two_ref, three_ref)):
@@ -170,10 +187,10 @@
                 piece = slice(tile * QR, (tile + 1) * QR)
                 inter = ref[0, 1 + part, piece, :] + theirs_ref[back, 1 + part, piece, :]
                 joint = theirs_ref[back, 0, piece, :] if other else ref[0, 0, piece, :]
-                projection = joint - share * inter
                 rows = pl.ds((tile * RAYS + source * QR) * 2 + part, QR, stride=2)
                 field = object_ref[rows, :]
                 dual = dual_ref[rows, :]
+                projection = joint + (field + dual) - share * inter
                 object_next = field - object_step * (inter + dual + penalty * (field - projection))
                 object_out[rows, :] = object_next
                 dual_out[rows, :] = dual + penalty * (object_next - projection)
@@ -203,23 +220,31 @@
 
 
 FIELD_ROWS = 128
-DRIFT_ROWS = 4 * QR
-SENT_ROWS = FIELD_ROWS + DRIFT_ROWS + QR
-
-
-def pack(place_ref, object_ref, dual_ref, target_ref, own_ref, one_ref, two_ref, three_ref, drift):
+SENT_ROWS = FIELD_ROWS + 4 * QR
+
+
+def pack(place_ref, object_far, dual_far, own_ref, one_ref, two_ref, three_ref, field, both, sems):
     y = place_ref[1]
-    targets = target_ref[...].astype(f32)
-    drift[...] = object_ref[...] + dual_ref[...]
+    copies = [pltpu.make_async_copy(object_far, field, sems.at[0]), pltpu.make_async_copy(dual_far, both, sems.at[1])]
+    for copy in copies:
+        copy.start()
+    for copy in copies:
+        copy.wait()
+    both[...] += field[...]
     for ahead, ref in enumerate((own_ref, one_ref, two_ref, three_ref)):
-        ref[0:FIELD_ROWS, :] = object_ref[...]
-        ref[FIELD_ROWS + DRIFT_ROWS :, :] = jnp.zeros((QR, NZ), f32)
-        ref[FIELD_ROWS + DRIFT_ROWS : FIELD_ROWS + DRIFT_ROWS + 1, : ZL * XC] = targets
+        ref[0:FIELD_ROWS, :] = field[...]
         for part in range(2):
             for tile in range(2):
                 start = (tile * RAYS + lax.rem(y + ahead, Y) * QR) * 2 + part
                 base = FIELD_ROWS + (part * 2 + tile) * QR
-                ref[base : base + QR, :] = drift[pl.ds(start, QR, stride=2), :]
+                ref[base : base + QR, :] = both[pl.ds(start, QR, stride=2), :]
+
+
+def pack_far(theirs_ref, own_ref, one_ref, two_ref, three_ref, out_ref):
+    out_ref[0:FIELD_ROWS, :] = theirs_ref[...]
+    out_ref[FIELD_ROWS:, :] = jnp.zeros((QR, NZ), f32)
+    for back, ref in enumerate((own_ref, one_ref, two_ref, three_ref)):
+        out_ref[FIELD_ROWS + back : FIELD_ROWS + back + 1, : ZL * XC] = ref[...].astype(f32)
 
 
 def frame_gradients(
@@ -322,33 +347,40 @@
     object_rows = object_field.reshape(128, NZ)
     dual_rows = dual_field.reshape(128, NZ)
 
+    with jax.named_scope("fields"):
+        object_theirs = across(object_rows)
+        own_targets = tile_range.reshape(1, ZL * XC)
+        targets = [own_targets] + [shifted(own_targets, "zl", ZL, k) for k in range(1, ZL)]
+        targets, radon = lax.optimization_barrier((targets, radon))
+
     with jax.named_scope("ray_sums"):
-        object_theirs = across(object_rows)
-        sums = call(ray_sums, shape(NEAR, ZL, HITS * QR, 2 * NZ, dtype=bf16), 0, 2, flops=2 * 2048 * 256 * 256)(
-            radon, volume_rows
-        )
+        sums = call(
+            ray_sums,
+            shape(NEAR, ZL, HITS * QR, 2 * NZ, dtype=bf16),
+            0,
+            0,
+            n_far=2,
+            scratch=[pltpu.VMEM(radon.shape, bf16), pltpu.VMEM((2 * TILE, NZ), f32), pltpu.SemaphoreType.DMA((ZL + 1,))],
+            flops=2 * 2048 * 256 * 256,
+        )(radon, volume_rows)
 
     with jax.named_scope("fields"):
         packed = call(
-            pack, (shape(SENT_ROWS, NZ),) * Y, 1, 3, scratch=[pltpu.VMEM((128, NZ), f32)], flops=1_000_000
-        )(place, object_rows, dual_rows, tile_range.reshape(1, ZL * XC))
+            pack,
+            (shape(SENT_ROWS, NZ),) * Y,
+            1,
+            0,
+            n_far=2,
+            scratch=[pltpu.VMEM((128, NZ), f32)] * 2 + [pltpu.SemaphoreType.DMA((2,))],
+            flops=1_000_000,
+        )(place, object_rows, dual_rows)
         fields = round_y(packed)
-        far_fields = round_y([object_theirs] * Y)
-
-    with jax.named_scope("ray_sums"):
+        object_theirs, sums = lax.optimization_barrier((object_theirs, sums))
         near_sums = lax.all_to_all(sums, CROSS, 0, 0, tiled=True)
-
-    with jax.named_scope("targets"):
-        tables = jnp.stack([field[FIELD_ROWS + DRIFT_ROWS, : ZL * XC] for field in fields])
-        tables = tables.astype(jnp.int32).reshape(Y, ZL, XC)
-        ahead = [lax.dynamic_index_in_dim(tables, (zl + k) % ZL, 1, keepdims=False) for k in range(ZL)]
-        tables = jnp.stack([ahead[0]] + [shifted(ahead[k], "zl", ZL, k) for k in range(1, ZL)])
-        tables = tables.reshape(ZL, Y * XC)
-        drifts = jnp.stack([field[FIELD_ROWS : FIELD_ROWS + DRIFT_ROWS] for field in fields])
-        drifts = drifts.reshape(Y, 2, 2 * QR, NZ)
-        drift_mine = lax.dynamic_index_in_dim(drifts, zh, 1, keepdims=False)
-        drift_theirs = across(lax.dynamic_index_in_dim(drifts, 1 - zh, 1, keepdims=False))
-        far_fields, tables, drift_theirs = lax.optimization_barrier((far_fields, tables, drift_theirs))
+        packed_far = call(pack_far, shape(FIELD_ROWS + QR, NZ), 0, 5, flops=1_000_000)(object_theirs, *targets)
+        far_fields = round_y([packed_far] * Y)
+        tables = jnp.concatenate([field[FIELD_ROWS : FIELD_ROWS + ZL, : ZL * XC] for field in far_fields])
+        tables = tables.astype(jnp.int32)
 
     with jax.named_scope("frames"):
         inter_parts = call(
@@ -357,7 +389,7 @@
             2,
             14,
             scratch=[pltpu.VMEM((NDET, NZ), f32)] * 4,
-            flops=1_600_000_000,
+            flops=FRAMES_COST,
         )(place, positions, *fields, *far_fields, probe_field, measured[0], ah, al, bh, bl)
         inter_parts = round_y(inter_parts)
 
@@ -366,10 +398,10 @@
             add_tiles,
             (shape(DEEP, 128, NZ, dtype=bf16), shape(2, 128, NZ)),
             2,
-            5,
+            9,
             scratch=[pltpu.VMEM((ZL, 128, 2 * NZ), f32)],
             flops=1_000_000,
-        )(place, tables, near_sums, *inter_parts)
+        )(place, tables, near_sums, *inter_parts, *fields)
         far_sums = lax.all_to_all(dense, ALONG, 0, 0, tiled=True)
 
     with jax.named_scope("residual"):
@@ -377,10 +409,10 @@
             residual_part,
             (shape(DEEP, 128, NZ, dtype=bf16),) + (shape(ZH, 3, 2 * QR, NZ),) * Y,
             1,
-            4,
-            scratch=[pltpu.VMEM((128, NZ), f32)] * 2,
+            2,
+            scratch=[pltpu.VMEM((128, NZ), f32)],
             flops=1_000_000,
-        )(place, far_sums, inter, drift_mine, drift_theirs)
+        )(place, far_sums, inter)
         kept = round_y(kept)
         residuals = lax.all_to_all(copies, ALONG, 0, 0, tiled=True)
 

time: 116 us -> 115 us (level)
  starting transfers between devices: 49.8 us -> 47.2 us
  blocking collectives: 12.3 us -> 14.7 us
  Pallas kernels: 13.9 us -> 15.9 us
  local copies, waits for them, and re-layouts: 8.74 us -> 7.08 us
    all_to_all x1, starting transfers between devices: 12.3 us -> 6.15 us  [body(): returned = lax.all_to_all(picked, CROSS, 0, 0, tiled=True)]
    ppermute x18 -> x17, waiting for transfers between devices: 18.3 us -> 13.9 us  [shifted(): lax.ppermute(value, axis, [(i, (i + step) % length) for i in range(length)])]
    all_to_all x1, starting transfers between devices: 6.51 us -> 10.9 us  [body(): near_sums = lax.all_to_all(sums, CROSS, 0, 0, tiled=True)]
    all_to_all x1, waiting for transfers between devices: 6.06 us -> 8.91 us  [body(): residuals = lax.all_to_all(copies, ALONG, 0, 0, tiled=True)]
    all_to_all x1, blocking collectives: 12.3 us -> 14.7 us  [body(): far_sums = lax.all_to_all(dense, ALONG, 0, 0, tiled=True)]
    pallas_call x2 -> x3, Pallas kernels: 2.39 us -> 3.77 us  [the longest x1 2.33 us: body(): call(ray_sums, shape(NEAR, ZL, HITS * QR, 2 * NZ, dtype=bf16), 0, 0, n_fa...]
    reshape x1 -> x2, local copies, waits for them, and re-layouts: 1.52 us -> 2.63 us  [body(): radon.reshape(ZL, XC, HITS, Y, QR, TILE).transpose(5, 1, 3, 0, 2, 4)]
    ppermute x18 -> x17, starting transfers between devices: 27.6 us -> 26.8 us  [shifted(): lax.ppermute(value, axis, [(i, (i + step) % length) for i in range(length)])]
  transfers between devices with their start and end apart: 21 -> 20, of which waited for: 10 -> 6; matrix products, arithmetic and copies ran while one was open for 3% -> 2% of each run, Pallas kernels for 9% -> 9%
where the time goes in v6:
time: 115 us; the launch traced here: 114 us
  starting transfers between devices  47.2 us (41%)
  waiting for transfers between devices  28.4 us (25%)
  Pallas kernels  15.9 us (14%)
  blocking collectives  14.7 us (13%)
  local copies, waits for them, and re-layouts  7.08 us (6%)
    ppermute x17, starting transfers between devices, shifted(): lax.ppermute(value, axis, [(i, (i + step) % length) for i in range(length)])  26.8 us
    all_to_all x1, blocking collectives, body(): far_sums = lax.all_to_all(dense, ALONG, 0, 0, tiled=True)  14.7 us
    ppermute x17, waiting for transfers between devices, shifted(): lax.ppermute(value, axis, [(i, (i + step) % length) for i in range(length)])  13.9 us
    all_to_all x1, starting transfers between devices, body(): near_sums = lax.all_to_all(sums, CROSS, 0, 0, tiled=True)  10.9 us
    all_to_all x1, waiting for transfers between devices, body(): residuals = lax.all_to_all(copies, ALONG, 0, 0, tiled=True)  8.91 us
    all_to_all x1, starting transfers between devices, body(): returned = lax.all_to_all(picked, CROSS, 0, 0, tiled=True)  6.15 us
    all_to_all x1, waiting for transfers between devices, body(): returned = lax.all_to_all(picked, CROSS, 0, 0, tiled=True)  5.57 us
    pallas_call x1, Pallas kernels, body(): call(frame_gradients, (shape(2, 128, NZ),) + (shape(2, 128, NZ, dtype=bf1...  4.65 us
  transfers between devices with their start and end apart: 20, of which 6 were waited for; matrix products, arithmetic and copies ran while one was open for 2% of the time, Pallas kernels for 9%

profile of v6, /device:TPU:1, one launch (start us, length us, event | category | flops | bytes accessed | tf_op | source)
XLA Modules:
  0.0 114.3 jit_solution(14041602160522764719)
XLA Ops:
  1.6 1.4 %pack.1 = (f32[160,128]{1,0:T(8,128)S(1)}, f32[160,128]{1,0:T(8,128)S(1)}, f32[160,128]{1,0:T(8,128)S(1)}, f32[160,128]{1,0:T(8,128)S(1)}) custom-call(s32[3]{0:T(128)S(1)} %pad_add_fusion.place_ref, f32[128,128]{1,0:T(8,128)} %bitcast.3.object_far.object_ref, f32[128,128]{1,0:T(8,128)S(1)} %bitcast.20), custom_call_target="tpu_custom_call" | custom-call | flops 1000000 | bytes 1048576 | tf_op jit(solution)/shard_map/fields/pack/pallas_call | solution.py:368
  3.0 2.2 %collective-permute-start.7 = (f32[160,128]{1,0:T(8,128)S(1)}, f32[160,128]{1,0:T(8,128)S(1)}, u32[]{:S(2)}, u32[]{:S(2)}) collective-permute-start(f32[160,128]{1,0:T(8,128)S(1)} %get-tuple-element.40), channel_id=1, source_target_pairs={{0,1},{1,2},{2,3},{3,0},{4,5},{5,6},{6,7},{7,4},{8,9},{9,10},{10,1... | collective-permute-start | bytes 245768 | tf_op jit(solution)/shard_map/fields/ppermute | solution.py:328
  5.2 6.9 %collective-permute-start = (f32[128,128]{1,0:T(8,128)}, f32[128,128]{1,0:T(8,128)S(1)}, u32[]{:S(2)}, u32[]{:S(2)}) collective-permute-start(f32[128,128]{1,0:T(8,128)} %bitcast.3.object_far.object_ref), channel_id=1, source_target_pairs={{0,4},{4,0},{1,5},{5,1},{2,6},{6,2},{3,7},{7,3},{8,12},{12,8},{9,1... | collective-permute-start | bytes 196616 | tf_op jit(solution)/shard_map/fields/ppermute | solution.py:328
  12.9 1.2 %collective-permute-start.2 = (s32[1,32]{1,0:T(1,128)S(1)}, s32[1,32]{1,0:T(1,128)S(1)}, u32[]{:S(2)}, u32[]{:S(2)}) collective-permute-start(s32[1,32]{1,0:T(1,128)S(1)} %bitcast.23), channel_id=1, source_target_pairs={{0,128},{64,192},{128,0},{192,64},{1,129},{65,193},{129,1},{193,65... | collective-permute-start | bytes 392 | tf_op jit(solution)/shard_map/fields/ppermute | solution.py:328
  14.1 1.6 %collective-permute-start.3 = (s32[1,32]{1,0:T(1,128)S(1)}, s32[1,32]{1,0:T(1,128)S(1)}, u32[]{:S(2)}, u32[]{:S(2)}) collective-permute-start(s32[1,32]{1,0:T(1,128)S(1)} %bitcast.24), channel_id=1, source_target_pairs={{0,192},{64,0},{128,64},{192,128},{1,193},{65,1},{129,65},{193,129... | collective-permute-start | bytes 392 | tf_op jit(solution)/shard_map/fields/ppermute | solution.py:328
  16.4 2.6 %collective-permute-start.8 = (f32[160,128]{1,0:T(8,128)S(1)}, f32[160,128]{1,0:T(8,128)S(1)}, u32[]{:S(2)}, u32[]{:S(2)}) collective-permute-start(f32[160,128]{1,0:T(8,128)S(1)} %get-tuple-element.41), channel_id=1, source_target_pairs={{0,2},{1,3},{2,0},{3,1},{4,6},{5,7},{6,4},{7,5},{8,10},{9,11},{10,... | collective-permute-start | bytes 245768 | tf_op jit(solution)/shard_map/fields/ppermute | solution.py:328
  19.0 1.1 collective-permute-start.9
  20.1 1.2 %copy-done = bf16[1,32,2,32,256]{4,3,2,1,0:T(8,128)(2,1)S(1)} copy-done((bf16[1,32,2,32,256]{4,3,2,1,0:T(8,128)(2,1)S(1)}, bf16[1,32,2,32,256]{4,3,2,1,0:T(8,128)(2,1)}, u32[]{:S(2)}) %copy-start) | copy-done | bytes 1048600
  22.2 2.3 %ray_sums.1 = bf16[32,4,16,256]{3,2,1,0:T(8,128)(2,1)} custom-call(bf16[32,2,32,256]{3,2,1,0:T(8,128)(2,1)S(1)} %bitcast.16, f32[512,128]{1,0:T(8,128)S(1)} %bitcast.18), custom_call_target="tpu_custom_call" | custom-call | flops 268435456 | bytes 1048576 | tf_op jit(solution)/shard_map/ray_sums/ray_sums/pallas_call | solution.py:357
  24.7 2.2 %collective-permute-start.5 = (f32[136,128]{1,0:T(8,128)S(1)}, f32[136,128]{1,0:T(8,128)S(1)}, u32[]{:S(2)}, u32[]{:S(2)}) collective-permute-start(f32[136,128]{1,0:T(8,128)S(1)} %pack_far.1.field_4), channel_id=1, source_target_pairs={{0,2},{1,3},{2,0},{3,1},{4,6},{5,7},{6,4},{7,5},{8,10},{9,11},{10,... | collective-permute-start | bytes 208904 | tf_op jit(solution)/shard_map/fields/ppermute | solution.py:328
  27.0 10.9 %all-to-all-start = ((bf16[32,4,16,256]{3,2,1,0:T(8,128)(2,1)}), bf16[32,4,16,256]{3,2,1,0:T(8,128)(2,1)S(1)}, u32[]{:S(2)}, u32[]{:S(2)}) async-start(bf16[32,4,16,256]{3,2,1,0:T(8,128)(2,1)} %ray_sums.1), calls=%async_computation | async-start | bytes 2097152 | tf_op jit(solution)/shard_map/fields/all_to_all | solution.py:379
  38.5 4.6 %frame_gradients.1 = (f32[2,128,128]{2,1,0:T(8,128)S(1)}, bf16[2,128,128]{2,1,0:T(8,128)(2,1)S(1)}, bf16[2,128,128]{2,1,0:T(8,128)(2,1)S(1)}, bf16[2,128,128]{2,1,0:T(8,128)(2,1)S(1)}) custom-call(s32[3]{0:T(128)S(1)} %pad_add_fusion.place_ref, s32[1,8]{1,0:T(1,128)S(1)} %copy-done.15, f32[160,128]{1,0:T(8,128)S(1)} %get-tuple-element.39.field_0, ...), custom_call_target="tpu_custom_call" | custom-call | flops 20000000000 | bytes 1048576 | tf_op jit(solution)/shard_map/frames/frame_gradients/pallas_call | solution.py:386
  43.2 1.4 %collective-permute-start.10 = (bf16[2,128,128]{2,1,0:T(8,128)(2,1)S(1)}, bf16[2,128,128]{2,1,0:T(8,128)(2,1)S(1)}, u32[]{:S(2)}, u32[]{:S(2)}) collective-permute-start(bf16[2,128,128]{2,1,0:T(8,128)(2,1)S(1)} %get-tuple-element.44), channel_id=1, source_target_pairs={{0,1},{1,2},{2,3},{3,0},{4,5},{5,6},{6,7},{7,4},{8,9},{9,10},{10,1... | collective-permute-start | bytes 196616 | tf_op jit(solution)/shard_map/frames/ppermute | solution.py:328
  44.6 2.4 %collective-permute-start.11 = (bf16[2,128,128]{2,1,0:T(8,128)(2,1)S(1)}, bf16[2,128,128]{2,1,0:T(8,128)(2,1)S(1)}, u32[]{:S(2)}, u32[]{:S(2)}) collective-permute-start(bf16[2,128,128]{2,1,0:T(8,128)(2,1)S(1)} %get-tuple-element.45), channel_id=1, source_target_pairs={{0,2},{1,3},{2,0},{3,1},{4,6},{5,7},{6,4},{7,5},{8,10},{9,11},{10,... | collective-permute-start | bytes 196616 | tf_op jit(solution)/shard_map/frames/ppermute | solution.py:328
  47.0 1.2 %collective-permute-start.12 = (bf16[2,128,128]{2,1,0:T(8,128)(2,1)S(1)}, bf16[2,128,128]{2,1,0:T(8,128)(2,1)S(1)}, u32[]{:S(2)}, u32[]{:S(2)}) collective-permute-start(bf16[2,128,128]{2,1,0:T(8,128)(2,1)S(1)} %get-tuple-element.46), channel_id=1, source_target_pairs={{0,3},{1,0},{2,1},{3,2},{4,7},{5,4},{6,5},{7,6},{8,11},{9,8},{10,9... | collective-permute-start | bytes 196616 | tf_op jit(solution)/shard_map/frames/ppermute | solution.py:328
  48.2 3.6 %collective-permute-done.10.inter_1 = bf16[2,128,128]{2,1,0:T(8,128)(2,1)S(1)} collective-permute-done((bf16[2,128,128]{2,1,0:T(8,128)(2,1)S(1)}, bf16[2,128,128]{2,1,0:T(8,128)(2,1)S(1)}, u32[]{:S(2)}, u32[]{:S(2)}) %collective-permute-start.10) | collective-permute-done | bytes 65568 | tf_op jit(solution)/shard_map/frames/ppermute | solution.py:328
  51.9 4.3 %collective-permute-done.11.inter_2 = bf16[2,128,128]{2,1,0:T(8,128)(2,1)S(1)} collective-permute-done((bf16[2,128,128]{2,1,0:T(8,128)(2,1)S(1)}, bf16[2,128,128]{2,1,0:T(8,128)(2,1)S(1)}, u32[]{:S(2)}, u32[]{:S(2)}) %collective-permute-start.11) | collective-permute-done | bytes 65568 | tf_op jit(solution)/shard_map/frames/ppermute | solution.py:328
  56.2 1.5 %add_tiles.1 = (bf16[8,128,128]{2,1,0:T(8,128)(2,1)S(1)}, f32[2,128,128]{2,1,0:T(8,128)S(1)}) custom-call(s32[3]{0:T(128)S(1)} %pad_add_fusion.place_ref, s32[16,32]{1,0:T(8,128)S(1)} %maximum_convert_fusion.target_ref, bf16[32,4,16,256]{3,2,1,0:T(8,128)(2,1)S(1)} %all-to-all-done.sums_ref, f32[2,128,128]{2,1,0:T(8,128)S(1)} %get-tuple-element.43.inter_0, ...), custom_call_target="tpu_custom_call" | custom-call | flops 1000000 | bytes 1048576 | tf_op jit(solution)/shard_map/near_sum/add_tiles/pallas_call | solution.py:397
  57.6 14.7 %all_to_all.20.sums_ref = bf16[8,128,128]{2,1,0:T(8,128)(2,1)S(1)} all-to-all(bf16[8,128,128]{2,1,0:T(8,128)(2,1)S(1)} %get-tuple-element.47), channel_id=1, replica_groups=mesh['zl'=4,'x'=4,'c'=2,'zh'=2,'y'=4] {'zh','zl'}, dimensions={0} | all-to-all | bytes 524288 | tf_op jit(solution)/shard_map/near_sum/all_to_all | solution.py:405
  72.3 1.3 %residual_part.1 = (bf16[8,128,128]{2,1,0:T(8,128)(2,1)}, f32[2,3,16,128]{3,2,1,0:T(8,128)S(1)}, f32[2,3,16,128]{3,2,1,0:T(8,128)S(1)}, f32[2,3,16,128]{3,2,1,0:T(8,128)S(1)}, f32[2,3,16,128]{3,2,1,0:T(8,128)S(1)}) custom-call(s32[3]{0:T(128)S(1)} %pad_add_fusion.place_ref, bf16[8,128,128]{2,1,0:T(8,128)(2,1)S(1)} %all_to_all.20.sums_ref, ...), custom_call_target="tpu_custom_call" | custom-call | flops 1000000 | bytes 1048576 | tf_op jit(solution)/shard_map/residual/residual_part/pallas_call | solution.py:408
  73.6 3.4 %all-to-all-start.2 = ((bf16[8,128,128]{2,1,0:T(8,128)(2,1)}), bf16[8,128,128]{2,1,0:T(8,128)(2,1)S(1)}, u32[]{:S(2)}, u32[]{:S(2)}) async-start(bf16[8,128,128]{2,1,0:T(8,128)(2,1)} %get-tuple-element.49), calls=%async_computation.2 | async-start | bytes 524288 | tf_op jit(solution)/shard_map/residual/all_to_all | solution.py:417
  77.1 1.6 %collective-permute-start.14 = (f32[2,3,16,128]{3,2,1,0:T(8,128)S(1)}, f32[2,3,16,128]{3,2,1,0:T(8,128)S(1)}, u32[]{:S(2)}, u32[]{:S(2)}) collective-permute-start(f32[2,3,16,128]{3,2,1,0:T(8,128)S(1)} %get-tuple-element.52), channel_id=1, source_target_pairs={{0,2},{1,3},{2,0},{3,1},{4,6},{5,7},{6,4},{7,5},{8,10},{9,11},{10,... | collective-permute-start | bytes 147464 | tf_op jit(solution)/shard_map/residual/ppermute | solution.py:328
  78.7 1.1 collective-permute-start.15
  79.8 8.9 %all-to-all-done.2.residual_ref = bf16[8,128,128]{2,1,0:T(8,128)(2,1)S(1)} async-done(((bf16[8,128,128]{2,1,0:T(8,128)(2,1)}), bf16[8,128,128]{2,1,0:T(8,128)(2,1)S(1)}, u32[]{:S(2)}, u32[]{:S(2)}) %all-to-all-start.2) | async-done | bytes 262176 | tf_op jit(solution)/shard_map/residual/all_to_all | solution.py:417
  88.7 2.0 %pick_tiles.1 = bf16[32,4,16,256]{3,2,1,0:T(8,128)(2,1)} custom-call(s32[3]{0:T(128)S(1)} %pad_add_fusion.place_ref, s32[16,32]{1,0:T(8,128)S(1)} %maximum_convert_fusion.target_ref, bf16[8,128,128]{2,1,0:T(8,128)(2,1)S(1)} %all-to-all-done.2.residual_ref), custom_call_target="tpu_custom_call" | custom-call | flops 1000000 | bytes 1048576 | tf_op jit(solution)/shard_map/pick/pick_tiles/pallas_call | solution.py:420
  90.7 6.1 %all-to-all-start.3 = ((bf16[32,4,16,256]{3,2,1,0:T(8,128)(2,1)}), bf16[32,4,16,256]{3,2,1,0:T(8,128)(2,1)S(1)}, u32[]{:S(2)}, u32[]{:S(2)}) async-start(bf16[32,4,16,256]{3,2,1,0:T(8,128)(2,1)} %pick_tiles.1), calls=%async_computation.3 | async-start | bytes 2097152 | tf_op jit(solution)/shard_map/pick/all_to_all | solution.py:429
  98.1 1.1 copy.16
  99.2 1.5 %copy.17.radon_ref = bf16[256,2048]{1,0:T(8,128)(2,1)S(1)} copy(bf16[256,2048]{0,1:T(8,128)(2,1)} %bitcast.27) | data formatting | bytes 2097152 | tf_op jit(solution)/shard_map/back_project/reshape | solution.py:438
  100.7 5.3 %collective-permute-done.16.theirs_ref = f32[4,3,16,128]{3,2,1,0:T(8,128)S(1)} collective-permute-done((f32[4,3,16,128]{3,2,1,0:T(8,128)S(1)}, f32[4,3,16,128]{3,2,1,0:T(8,128)S(1)}, u32[]{:S(2)}, u32[]{:S(2)}) %collective-permute-start.16) | collective-permute-done | bytes 98336 | tf_op jit(solution)/shard_map/updates/ppermute | solution.py:328
  106.1 1.6 %updates.1 = (f32[128,128]{1,0:T(8,128)}, f32[128,128]{1,0:T(8,128)}) custom-call(s32[3]{0:T(128)S(1)} %pad_add_fusion.place_ref, f32[2,3,16,128]{3,2,1,0:T(8,128)S(1)} %get-tuple-element.54.own_ref, f32[2,3,16,128]{3,2,1,0:T(8,128)S(1)} %copy-done.7, f32[2,3,16,128]{3,2,1,0:T(8,128)S(1)} %copy-done.9, f32[2,3,16,128]{3,2,1,0:T(8,128)S(1)} %copy-done.11, ...), custom_call_target="tpu_custom_call" | custom-call | flops 1000000 | bytes 1048576 | tf_op jit(solution)/shard_map/updates/updates/pallas_call | solution.py:433
  107.6 5.6 %all-to-all-done.3.picked_ref = bf16[32,4,16,256]{3,2,1,0:T(8,128)(2,1)S(1)} async-done(((bf16[32,4,16,256]{3,2,1,0:T(8,128)(2,1)}), bf16[32,4,16,256]{3,2,1,0:T(8,128)(2,1)S(1)}, u32[]{:S(2)}, u32[]{:S(2)}) %all-to-all-start.3) | async-done | bytes 1048608 | tf_op jit(solution)/shard_map/pick/all_to_all | solution.py:429
  113.2 1.1 back_project.1
  (74 shorter events, 5.3 us)
Async XLA Ops:
  3.0 9.1 %copy-start.12 = (s32[1,32,1,1]{1,3,2,0:T(1,128)S(1)}, s32[1,32,1,1]{1,3,2,0:T(1,128)}, u32[]{:S(2)}) copy-start(s32[1,32,1,1]{1,3,2,0:T(1,128)} %param.19) | copy-start | bytes 388
  3.0 23.9 %collective-permute-start.7 = (f32[160,128]{1,0:T(8,128)S(1)}, f32[160,128]{1,0:T(8,128)S(1)}, u32[]{:S(2)}, u32[]{:S(2)}) collective-permute-start(f32[160,128]{1,0:T(8,128)S(1)} %get-tuple-element.40), channel_id=1, source_target_pairs={{0,1},{1,2},{2,3},{3,0},{4,5},{5,6},{6,7},{7,4},{8,9},{9,10},{10,1... | collective-permute-start | bytes 245768 | tf_op jit(solution)/shard_map/fields/ppermute | solution.py:328
  5.2 19.4 %collective-permute-start = (f32[128,128]{1,0:T(8,128)}, f32[128,128]{1,0:T(8,128)S(1)}, u32[]{:S(2)}, u32[]{:S(2)}) collective-permute-start(f32[128,128]{1,0:T(8,128)} %bitcast.3.object_far.object_ref), channel_id=1, source_target_pairs={{0,4},{4,0},{1,5},{5,1},{2,6},{6,2},{3,7},{7,3},{8,12},{12,8},{9,1... | collective-permute-start | bytes 196616 | tf_op jit(solution)/shard_map/fields/ppermute | solution.py:328
  12.1 4.2 %collective-permute-start.1 = (s32[1,32]{1,0:T(1,128)S(1)}, s32[1,32]{1,0:T(1,128)S(1)}, u32[]{:S(2)}, u32[]{:S(2)}) collective-permute-start(s32[1,32]{1,0:T(1,128)S(1)} %bitcast.22), channel_id=1, source_target_pairs={{0,64},{64,128},{128,192},{192,0},{1,65},{65,129},{129,193},{193,1... | collective-permute-start | bytes 392 | tf_op jit(solution)/shard_map/fields/ppermute | solution.py:328
  12.9 6.1 %collective-permute-start.2 = (s32[1,32]{1,0:T(1,128)S(1)}, s32[1,32]{1,0:T(1,128)S(1)}, u32[]{:S(2)}, u32[]{:S(2)}) collective-permute-start(s32[1,32]{1,0:T(1,128)S(1)} %bitcast.23), channel_id=1, source_target_pairs={{0,128},{64,192},{128,0},{192,64},{1,129},{65,193},{129,1},{193,65... | collective-permute-start | bytes 392 | tf_op jit(solution)/shard_map/fields/ppermute | solution.py:328
  14.1 6.0 %collective-permute-start.3 = (s32[1,32]{1,0:T(1,128)S(1)}, s32[1,32]{1,0:T(1,128)S(1)}, u32[]{:S(2)}, u32[]{:S(2)}) collective-permute-start(s32[1,32]{1,0:T(1,128)S(1)} %bitcast.24), channel_id=1, source_target_pairs={{0,192},{64,0},{128,64},{192,128},{1,193},{65,1},{129,65},{193,129... | collective-permute-start | bytes 392 | tf_op jit(solution)/shard_map/fields/ppermute | solution.py:328
  16.4 21.5 %collective-permute-start.8 = (f32[160,128]{1,0:T(8,128)S(1)}, f32[160,128]{1,0:T(8,128)S(1)}, u32[]{:S(2)}, u32[]{:S(2)}) collective-permute-start(f32[160,128]{1,0:T(8,128)S(1)} %get-tuple-element.41), channel_id=1, source_target_pairs={{0,2},{1,3},{2,0},{3,1},{4,6},{5,7},{6,4},{7,5},{8,10},{9,11},{10,... | collective-permute-start | bytes 245768 | tf_op jit(solution)/shard_map/fields/ppermute | solution.py:328
  19.0 18.9 %collective-permute-start.9 = (f32[160,128]{1,0:T(8,128)S(1)}, f32[160,128]{1,0:T(8,128)S(1)}, u32[]{:S(2)}, u32[]{:S(2)}) collective-permute-start(f32[160,128]{1,0:T(8,128)S(1)} %get-tuple-element.42), channel_id=1, source_target_pairs={{0,3},{1,0},{2,1},{3,2},{4,7},{5,4},{6,5},{7,6},{8,11},{9,8},{10,9... | collective-permute-start | bytes 245768 | tf_op jit(solution)/shard_map/fields/ppermute | solution.py:328
  24.6 13.3 %collective-permute-start.6 = (f32[136,128]{1,0:T(8,128)S(1)}, f32[136,128]{1,0:T(8,128)S(1)}, u32[]{:S(2)}, u32[]{:S(2)}) collective-permute-start(f32[136,128]{1,0:T(8,128)S(1)} %pack_far.1.field_4), channel_id=1, source_target_pairs={{0,3},{1,0},{2,1},{3,2},{4,7},{5,4},{6,5},{7,6},{8,11},{9,8},{10,9... | collective-permute-start | bytes 208904 | tf_op jit(solution)/shard_map/fields/ppermute | solution.py:328
  24.7 13.2 %collective-permute-start.5 = (f32[136,128]{1,0:T(8,128)S(1)}, f32[136,128]{1,0:T(8,128)S(1)}, u32[]{:S(2)}, u32[]{:S(2)}) collective-permute-start(f32[136,128]{1,0:T(8,128)S(1)} %pack_far.1.field_4), channel_id=1, source_target_pairs={{0,2},{1,3},{2,0},{3,1},{4,6},{5,7},{6,4},{7,5},{8,10},{9,11},{10,... | collective-permute-start | bytes 208904 | tf_op jit(solution)/shard_map/fields/ppermute | solution.py:328
  26.9 11.0 %collective-permute-start.4 = (f32[136,128]{1,0:T(8,128)S(1)}, f32[136,128]{1,0:T(8,128)S(1)}, u32[]{:S(2)}, u32[]{:S(2)}) collective-permute-start(f32[136,128]{1,0:T(8,128)S(1)} %pack_far.1.field_4), channel_id=1, source_target_pairs={{0,1},{1,2},{2,3},{3,0},{4,5},{5,6},{6,7},{7,4},{8,9},{9,10},{10,1... | collective-permute-start | bytes 208904 | tf_op jit(solution)/shard_map/fields/ppermute | solution.py:328
  26.9 11.0 %copy-start.13 = (f32[1,8,128,128]{3,2,1,0:T(8,128)S(1)}, f32[1,8,128,128]{3,2,1,0:T(8,128)}, u32[]{:S(2)}) copy-start(f32[1,8,128,128]{3,2,1,0:T(8,128)} %param.12) | copy-start | bytes 1572868
  26.9 11.0 %copy-start.14 = (f32[2,128,128]{2,1,0:T(8,128)S(1)}, f32[2,128,128]{2,1,0:T(8,128)}, u32[]{:S(2)}) copy-start(f32[2,128,128]{2,1,0:T(8,128)} %probe_ref.1) | copy-start | bytes 393220
  26.9 11.0 %copy-start.16 = (bf16[256,256]{1,0:T(8,128)(2,1)S(1)}, bf16[256,256]{1,0:T(8,128)(2,1)}, u32[]{:S(2)}) copy-start(bf16[256,256]{1,0:T(8,128)(2,1)} %constant.21.clone.ah_ref) | copy-start | bytes 393220
  26.9 11.0 %copy-start.17 = (bf16[256,256]{1,0:T(8,128)(2,1)S(1)}, bf16[256,256]{1,0:T(8,128)(2,1)}, u32[]{:S(2)}) copy-start(bf16[256,256]{1,0:T(8,128)(2,1)} %constant.22.clone.al_ref) | copy-start | bytes 393220
  26.9 11.0 %copy-start.18 = (bf16[256,256]{1,0:T(8,128)(2,1)S(1)}, bf16[256,256]{1,0:T(8,128)(2,1)}, u32[]{:S(2)}) copy-start(bf16[256,256]{1,0:T(8,128)(2,1)} %constant.23.clone.bh_ref) | copy-start | bytes 393220
  26.9 11.0 %copy-start.19 = (bf16[256,256]{1,0:T(8,128)(2,1)S(1)}, bf16[256,256]{1,0:T(8,128)(2,1)}, u32[]{:S(2)}) copy-start(bf16[256,256]{1,0:T(8,128)(2,1)} %constant.24.clone.bl_ref) | copy-start | bytes 393220
  27.0 29.2 %all-to-all-start = ((bf16[32,4,16,256]{3,2,1,0:T(8,128)(2,1)}), bf16[32,4,16,256]{3,2,1,0:T(8,128)(2,1)S(1)}, u32[]{:S(2)}, u32[]{:S(2)}) async-start(bf16[32,4,16,256]{3,2,1,0:T(8,128)(2,1)} %ray_sums.1), calls=%async_computation | async-start | bytes 2097152 | tf_op jit(solution)/shard_map/fields/all_to_all | solution.py:379
  43.2 8.6 %collective-permute-start.10 = (bf16[2,128,128]{2,1,0:T(8,128)(2,1)S(1)}, bf16[2,128,128]{2,1,0:T(8,128)(2,1)S(1)}, u32[]{:S(2)}, u32[]{:S(2)}) collective-permute-start(bf16[2,128,128]{2,1,0:T(8,128)(2,1)S(1)} %get-tuple-element.44), channel_id=1, source_target_pairs={{0,1},{1,2},{2,3},{3,0},{4,5},{5,6},{6,7},{7,4},{8,9},{9,10},{10,1... | collective-permute-start | bytes 196616 | tf_op jit(solution)/shard_map/frames/ppermute | solution.py:328
  44.6 11.5 %collective-permute-start.11 = (bf16[2,128,128]{2,1,0:T(8,128)(2,1)S(1)}, bf16[2,128,128]{2,1,0:T(8,128)(2,1)S(1)}, u32[]{:S(2)}, u32[]{:S(2)}) collective-permute-start(bf16[2,128,128]{2,1,0:T(8,128)(2,1)S(1)} %get-tuple-element.45), channel_id=1, source_target_pairs={{0,2},{1,3},{2,0},{3,1},{4,6},{5,7},{6,4},{7,5},{8,10},{9,11},{10,... | collective-permute-start | bytes 196616 | tf_op jit(solution)/shard_map/frames/ppermute | solution.py:328
  47.0 9.1 %collective-permute-start.12 = (bf16[2,128,128]{2,1,0:T(8,128)(2,1)S(1)}, bf16[2,128,128]{2,1,0:T(8,128)(2,1)S(1)}, u32[]{:S(2)}, u32[]{:S(2)}) collective-permute-start(bf16[2,128,128]{2,1,0:T(8,128)(2,1)S(1)} %get-tuple-element.46), channel_id=1, source_target_pairs={{0,3},{1,0},{2,1},{3,2},{4,7},{5,4},{6,5},{7,6},{8,11},{9,8},{10,9... | collective-permute-start | bytes 196616 | tf_op jit(solution)/shard_map/frames/ppermute | solution.py:328
  73.6 15.1 %all-to-all-start.2 = ((bf16[8,128,128]{2,1,0:T(8,128)(2,1)}), bf16[8,128,128]{2,1,0:T(8,128)(2,1)S(1)}, u32[]{:S(2)}, u32[]{:S(2)}) async-start(bf16[8,128,128]{2,1,0:T(8,128)(2,1)} %get-tuple-element.49), calls=%async_computation.2 | async-start | bytes 524288 | tf_op jit(solution)/shard_map/residual/all_to_all | solution.py:417
  77.0 13.7 %collective-permute-start.13 = (f32[2,3,16,128]{3,2,1,0:T(8,128)S(1)}, f32[2,3,16,128]{3,2,1,0:T(8,128)S(1)}, u32[]{:S(2)}, u32[]{:S(2)}) collective-permute-start(f32[2,3,16,128]{3,2,1,0:T(8,128)S(1)} %get-tuple-element.51), channel_id=1, source_target_pairs={{0,1},{1,2},{2,3},{3,0},{4,5},{5,6},{6,7},{7,4},{8,9},{9,10},{10,1... | collective-permute-start | bytes 147464 | tf_op jit(solution)/shard_map/residual/ppermute | solution.py:328
  77.1 13.6 %collective-permute-start.14 = (f32[2,3,16,128]{3,2,1,0:T(8,128)S(1)}, f32[2,3,16,128]{3,2,1,0:T(8,128)S(1)}, u32[]{:S(2)}, u32[]{:S(2)}) collective-permute-start(f32[2,3,16,128]{3,2,1,0:T(8,128)S(1)} %get-tuple-element.52), channel_id=1, source_target_pairs={{0,2},{1,3},{2,0},{3,1},{4,6},{5,7},{6,4},{7,5},{8,10},{9,11},{10,... | collective-permute-start | bytes 147464 | tf_op jit(solution)/shard_map/residual/ppermute | solution.py:328
  78.7 12.0 %collective-permute-start.15 = (f32[2,3,16,128]{3,2,1,0:T(8,128)S(1)}, f32[2,3,16,128]{3,2,1,0:T(8,128)S(1)}, u32[]{:S(2)}, u32[]{:S(2)}) collective-permute-start(f32[2,3,16,128]{3,2,1,0:T(8,128)S(1)} %get-tuple-element.53), channel_id=1, source_target_pairs={{0,3},{1,0},{2,1},{3,2},{4,7},{5,4},{6,5},{7,6},{8,11},{9,8},{10,9... | collective-permute-start | bytes 147464 | tf_op jit(solution)/shard_map/residual/ppermute | solution.py:328
  90.7 7.3 %copy-start.1 = (bf16[1,32,2,32,256]{4,3,2,1,0:T(8,128)(2,1)S(1)}, bf16[1,32,2,32,256]{4,3,2,1,0:T(8,128)(2,1)}, u32[]{:S(2)}) copy-start(bf16[1,32,2,32,256]{4,3,2,1,0:T(8,128)(2,1)} %param.18) | copy-start | bytes 3145732
  90.7 22.5 %all-to-all-start.3 = ((bf16[32,4,16,256]{3,2,1,0:T(8,128)(2,1)}), bf16[32,4,16,256]{3,2,1,0:T(8,128)(2,1)S(1)}, u32[]{:S(2)}, u32[]{:S(2)}) async-start(bf16[32,4,16,256]{3,2,1,0:T(8,128)(2,1)} %pick_tiles.1), calls=%async_computation.3 | async-start | bytes 2097152 | tf_op jit(solution)/shard_map/pick/all_to_all | solution.py:429
  97.7 8.4 %collective-permute-start.16 = (f32[4,3,16,128]{3,2,1,0:T(8,128)S(1)}, f32[4,3,16,128]{3,2,1,0:T(8,128)S(1)}, u32[]{:S(2)}, u32[]{:S(2)}) collective-permute-start(f32[4,3,16,128]{3,2,1,0:T(8,128)S(1)} %pad_maximum_fusion), channel_id=1, source_target_pairs={{0,4},{4,0},{1,5},{5,1},{2,6},{6,2},{3,7},{7,3},{8,12},{12,8},{9,1... | collective-permute-start | bytes 294920 | tf_op jit(solution)/shard_map/updates/ppermute | solution.py:328
  99.2 6.9 %copy-start.7 = (f32[2,3,16,128]{3,2,1,0:T(8,128)S(1)}, f32[2,3,16,128]{3,2,1,0:T(8,128)}, u32[]{:S(2)}) copy-start(f32[2,3,16,128]{3,2,1,0:T(8,128)} %copy-done.6) | copy-start | bytes 147460
  99.2 6.9 %copy-start.9 = (f32[2,3,16,128]{3,2,1,0:T(8,128)S(1)}, f32[2,3,16,128]{3,2,1,0:T(8,128)}, u32[]{:S(2)}) copy-start(f32[2,3,16,128]{3,2,1,0:T(8,128)} %copy-done.8) | copy-start | bytes 147460
  99.2 6.9 %copy-start.11 = (f32[2,3,16,128]{3,2,1,0:T(8,128)S(1)}, f32[2,3,16,128]{3,2,1,0:T(8,128)}, u32[]{:S(2)}) copy-start(f32[2,3,16,128]{3,2,1,0:T(8,128)} %copy-done.10) | copy-start | bytes 147460
  100.7 12.5 %copy-start.3 = (f32[256,2,128]{2,1,0:T(2,128)S(1)}, f32[256,2,128]{2,1,0:T(2,128)}, u32[]{:S(2)}) copy-start(f32[256,2,128]{2,1,0:T(2,128)} %param.17) | copy-start | bytes 786436
  (11 other events, 31.4 us)

commit v7 on v6

--- a/solution.py
+++ b/solution.py
@@ -25,7 +25,8 @@
 DEEP = ZH * ZL
 QR = RAYS // Y
 FR_DEV = 8
-FRAMES_COST = 20_000_000_000
+FRAMES_COST = 6_000_000_000
+SUMS_LIMIT = 62 << 20
 
 penalty = 1.0
 object_step = 0.1
@@ -93,8 +94,8 @@
 
 def first_rows(place_ref, target_ref):
     zl_here = place_ref[2]
-    back_y = [lax.rem(place_ref[1] + Y - y, Y) * ZL for y in range(Y)]
-    back_zl = [lax.rem(zl_here + ZL - zl, ZL) for zl in range(ZL)]
+    back_y = [lax.rem(place_ref[1] + Y - y, Y) for y in range(Y)]
+    back_zl = [lax.rem(zl_here + ZL - zl, ZL) * Y for zl in range(ZL)]
 
     def row(zl, y, xc):
         return pl.multiple_of(target_ref[back_y[y] + back_zl[zl], zl_here * XC + xc] * QR, QR)
@@ -219,20 +220,20 @@
     )
 
 
-FIELD_ROWS = 128
-SENT_ROWS = FIELD_ROWS + 4 * QR
-
-
-def pack(place_ref, object_far, dual_far, own_ref, one_ref, two_ref, three_ref, field, both, sems):
+FIELD_ROWS = 2 * 128
+DRIFT_ROWS = 4 * QR
+SENT_ROWS = FIELD_ROWS + DRIFT_ROWS + QR
+
+
+def pack(place_ref, object_ref, theirs_ref, dual_ref, target_ref, own_ref, one_ref, two_ref, three_ref, both):
     y = place_ref[1]
-    copies = [pltpu.make_async_copy(object_far, field, sems.at[0]), pltpu.make_async_copy(dual_far, both, sems.at[1])]
-    for copy in copies:
-        copy.start()
-    for copy in copies:
-        copy.wait()
-    both[...] += field[...]
+    targets = target_ref[...].astype(f32)
+    both[...] = object_ref[...] + dual_ref[...]
     for ahead, ref in enumerate((own_ref, one_ref, two_ref, three_ref)):
-        ref[0:FIELD_ROWS, :] = field[...]
+        ref[0:128, :] = object_ref[...]
+        ref[128:256, :] = theirs_ref[...]
+        ref[FIELD_ROWS + DRIFT_ROWS :, :] = jnp.zeros((QR, NZ), f32)
+        ref[FIELD_ROWS + DRIFT_ROWS : FIELD_ROWS + DRIFT_ROWS + 1, : ZL * XC] = targets
         for part in range(2):
             for tile in range(2):
                 start = (tile * RAYS + lax.rem(y + ahead, Y) * QR) * 2 + part
@@ -240,26 +241,19 @@
                 ref[base : base + QR, :] = both[pl.ds(start, QR, stride=2), :]
 
 
-def pack_far(theirs_ref, own_ref, one_ref, two_ref, three_ref, out_ref):
-    out_ref[0:FIELD_ROWS, :] = theirs_ref[...]
-    out_ref[FIELD_ROWS:, :] = jnp.zeros((QR, NZ), f32)
-    for back, ref in enumerate((own_ref, one_ref, two_ref, three_ref)):
-        out_ref[FIELD_ROWS + back : FIELD_ROWS + back + 1, : ZL * XC] = ref[...].astype(f32)
-
-
 def frame_gradients(
-    place_ref, starts_ref, field_0, field_1, field_2, field_3, field_4, field_5, field_6, field_7,
-    probe_ref, measured_ref, ah_ref, al_ref, bh_ref, bl_ref, own_ref, sent_one, sent_two, sent_three,
+    place_ref, starts_ref, field_0, field_1, field_2, field_3, probe_ref,
+    measured_ref, ah_ref, al_ref, bh_ref, bl_ref, own_ref, sent_one, sent_two, sent_three,
     field_re, field_im, total_re, total_im,
 ):
     zh = place_ref[0]
     y = place_ref[1]
-    fields = (field_0, field_1, field_2, field_3, field_4, field_5, field_6, field_7)
-    for place, field_ref in enumerate(fields):
-        owner = lax.rem(zh + place // Y, ZH) * Y + lax.rem(y + Y - place % Y, Y)
-        rows = pl.ds(pl.multiple_of(owner * 64, 64), 64)
-        field_re[rows, :] = field_ref[pl.ds(0, 64, stride=2), :]
-        field_im[rows, :] = field_ref[pl.ds(1, 64, stride=2), :]
+    for back, field_ref in enumerate((field_0, field_1, field_2, field_3)):
+        for other in range(ZH):
+            owner = lax.rem(zh + other, ZH) * Y + lax.rem(y + Y - back, Y)
+            rows = pl.ds(pl.multiple_of(owner * 64, 64), 64)
+            field_re[rows, :] = field_ref[pl.ds(other * 128, 64, stride=2), :]
+            field_im[rows, :] = field_ref[pl.ds(other * 128 + 1, 64, stride=2), :]
     total_re[...] = jnp.zeros(total_re.shape, f32)
     total_im[...] = jnp.zeros(total_im.shape, f32)
     probe_re = probe_ref[0]
@@ -347,13 +341,8 @@
     object_rows = object_field.reshape(128, NZ)
     dual_rows = dual_field.reshape(128, NZ)
 
-    with jax.named_scope("fields"):
+    with jax.named_scope("ray_sums"):
         object_theirs = across(object_rows)
-        own_targets = tile_range.reshape(1, ZL * XC)
-        targets = [own_targets] + [shifted(own_targets, "zl", ZL, k) for k in range(1, ZL)]
-        targets, radon = lax.optimization_barrier((targets, radon))
-
-    with jax.named_scope("ray_sums"):
         sums = call(
             ray_sums,
             shape(NEAR, ZL, HITS * QR, 2 * NZ, dtype=bf16),
@@ -362,35 +351,33 @@
             n_far=2,
             scratch=[pltpu.VMEM(radon.shape, bf16), pltpu.VMEM((2 * TILE, NZ), f32), pltpu.SemaphoreType.DMA((ZL + 1,))],
             flops=2 * 2048 * 256 * 256,
+            limit=SUMS_LIMIT,
         )(radon, volume_rows)
+        near_sums = lax.all_to_all(sums, CROSS, 0, 0, tiled=True)
 
     with jax.named_scope("fields"):
+        object_theirs, sums = lax.optimization_barrier((object_theirs, sums))
         packed = call(
-            pack,
-            (shape(SENT_ROWS, NZ),) * Y,
-            1,
-            0,
-            n_far=2,
-            scratch=[pltpu.VMEM((128, NZ), f32)] * 2 + [pltpu.SemaphoreType.DMA((2,))],
-            flops=1_000_000,
-        )(place, object_rows, dual_rows)
+            pack, (shape(SENT_ROWS, NZ),) * Y, 1, 4, scratch=[pltpu.VMEM((128, NZ), f32)], flops=1_000_000
+        )(place, object_rows, object_theirs, dual_rows, tile_range.reshape(1, ZL * XC))
         fields = round_y(packed)
-        object_theirs, sums = lax.optimization_barrier((object_theirs, sums))
-        near_sums = lax.all_to_all(sums, CROSS, 0, 0, tiled=True)
-        packed_far = call(pack_far, shape(FIELD_ROWS + QR, NZ), 0, 5, flops=1_000_000)(object_theirs, *targets)
-        far_fields = round_y([packed_far] * Y)
-        tables = jnp.concatenate([field[FIELD_ROWS : FIELD_ROWS + ZL, : ZL * XC] for field in far_fields])
-        tables = tables.astype(jnp.int32)
 
     with jax.named_scope("frames"):
         inter_parts = call(
             frame_gradients,
             (shape(2, 128, NZ),) + (shape(2, 128, NZ, dtype=bf16),) * 3,
             2,
-            14,
+            10,
             scratch=[pltpu.VMEM((NDET, NZ), f32)] * 4,
             flops=FRAMES_COST,
-        )(place, positions, *fields, *far_fields, probe_field, measured[0], ah, al, bh, bl)
+        )(place, positions, *fields, probe_field, measured[0], ah, al, bh, bl)
+
+    with jax.named_scope("targets"):
+        tables = jnp.concatenate([field[FIELD_ROWS + DRIFT_ROWS :][:1, : ZL * XC] for field in fields])
+        tables, inter_parts = lax.optimization_barrier((tables.astype(jnp.int32), inter_parts))
+        tables = jnp.concatenate([tables] + [shifted(tables, "zl", ZL, k) for k in range(1, ZL)])
+
+    with jax.named_scope("frames"):
         inter_parts = round_y(inter_parts)
 
     with jax.named_scope("near_sum"):

time: 115 us -> 116 us (level)
  waiting for transfers between devices: 28.4 us -> 34.6 us
  local copies, waits for them, and re-layouts: 7.08 us -> 4.67 us
  blocking collectives: 14.7 us -> 13 us
    ppermute x17 -> x14, waiting for transfers between devices: 13.9 us -> 23.1 us  [shifted(): lax.ppermute(value, axis, [(i, (i + step) % length) for i in range(length)])]
    all_to_all x1, starting transfers between devices: 6.15 us -> 12.2 us  [body(): returned = lax.all_to_all(picked, CROSS, 0, 0, tiled=True)]
    ppermute x17 -> x14, starting transfers between devices: 26.8 us -> 22.8 us  [shifted(): lax.ppermute(value, axis, [(i, (i + step) % length) for i in range(length)])]
    all_to_all x1, waiting for transfers between devices: 8.91 us -> 5.51 us  [body(): residuals = lax.all_to_all(copies, ALONG, 0, 0, tiled=True)]
    all_to_all x1, starting transfers between devices: 10.9 us -> 8.19 us  [body(): near_sums = lax.all_to_all(sums, CROSS, 0, 0, tiled=True)]
    unnamed x40 -> x32, local copies, waits for them, and re-layouts: 3.7 us -> 1.32 us
    all_to_all x1, blocking collectives: 14.7 us -> 13 us  [body(): far_sums = lax.all_to_all(dense, ALONG, 0, 0, tiled=True)]
    reshape x2 -> x1, local copies, waits for them, and re-layouts: 2.63 us -> 1.49 us  [body(): radon.reshape(ZL, XC, HITS, Y, QR, TILE).transpose(5, 1, 3, 0, 2, 4)]
  transfers between devices with their start and end apart: 20 -> 17, of which waited for: 6 -> 9; matrix products, arithmetic and copies ran while one was open for 2% -> 2% of each run, Pallas kernels for 9% -> 10%
where the time goes in v7:
time: 116 us; the launch traced here: 115 us
  starting transfers between devices  46.6 us (40%)
  waiting for transfers between devices  34.6 us (30%)
  Pallas kernels  15.6 us (13%)
  blocking collectives  13 us (11%)
  local copies, waits for them, and re-layouts  4.67 us (4%)
    ppermute x14, waiting for transfers between devices, shifted(): lax.ppermute(value, axis, [(i, (i + step) % length) for i in range(length)])  23.1 us
    ppermute x14, starting transfers between devices, shifted(): lax.ppermute(value, axis, [(i, (i + step) % length) for i in range(length)])  22.8 us
    all_to_all x1, blocking collectives, body(): far_sums = lax.all_to_all(dense, ALONG, 0, 0, tiled=True)  13 us
    all_to_all x1, starting transfers between devices, body(): returned = lax.all_to_all(picked, CROSS, 0, 0, tiled=True)  12.2 us
    all_to_all x1, starting transfers between devices, body(): near_sums = lax.all_to_all(sums, CROSS, 0, 0, tiled=True)  8.19 us
    all_to_all x1, waiting for transfers between devices, body(): returned = lax.all_to_all(picked, CROSS, 0, 0, tiled=True)  5.92 us
    all_to_all x1, waiting for transfers between devices, body(): residuals = lax.all_to_all(copies, ALONG, 0, 0, tiled=True)  5.51 us
    pallas_call x1, Pallas kernels, body(): call(frame_gradients, (shape(2, 128, NZ),) + (shape(2, 128, NZ, dtype=bf1...  4.63 us
  transfers between devices with their start and end apart: 17, of which 9 were waited for; matrix products, arithmetic and copies ran while one was open for 2% of the time, Pallas kernels for 10%

profile of v7, /device:TPU:1, one launch (start us, length us, event | category | flops | bytes accessed | tf_op | source)
XLA Modules:
  0.0 115.4 jit_solution(14526937433804677891)
XLA Ops:
  0.6 7.8 %collective-permute-start = (f32[128,128]{1,0:T(8,128)}, f32[128,128]{1,0:T(8,128)S(1)}, u32[]{:S(2)}, u32[]{:S(2)}) collective-permute-start(f32[128,128]{1,0:T(8,128)} %bitcast.18), channel_id=1, source_target_pairs={{0,4},{4,0},{1,5},{5,1},{2,6},{6,2},{3,7},{7,3},{8,12},{12,8},{9,1... | collective-permute-start | bytes 196616 | tf_op jit(solution)/shard_map/ray_sums/ppermute | solution.py:322
  8.5 3.2 %ray_sums.1 = bf16[32,4,16,256]{3,2,1,0:T(8,128)(2,1)} custom-call(bf16[32,2,32,256]{3,2,1,0:T(8,128)(2,1)} %bitcast.25, f32[512,128]{1,0:T(8,128)} %bitcast.16), custom_call_target="tpu_custom_call" | custom-call | flops 268435456 | bytes 1048576 | tf_op jit(solution)/shard_map/ray_sums/ray_sums/pallas_call | solution.py:346
  11.8 8.2 %all-to-all-start = ((bf16[32,4,16,256]{3,2,1,0:T(8,128)(2,1)}), bf16[32,4,16,256]{3,2,1,0:T(8,128)(2,1)S(1)}, u32[]{:S(2)}, u32[]{:S(2)}) async-start(bf16[32,4,16,256]{3,2,1,0:T(8,128)(2,1)} %ray_sums.1), calls=%async_computation | async-start | bytes 2097152 | tf_op jit(solution)/shard_map/ray_sums/all_to_all | solution.py:356
  20.1 0.6 copy-done.7
  21.3 1.5 %collective-permute-start.1 = (f32[296,128]{1,0:T(8,128)S(1)}, f32[296,128]{1,0:T(8,128)S(1)}, u32[]{:S(2)}, u32[]{:S(2)}) collective-permute-start(f32[296,128]{1,0:T(8,128)S(1)} %get-tuple-element.33), channel_id=1, source_target_pairs={{0,1},{1,2},{2,3},{3,0},{4,5},{5,6},{6,7},{7,4},{8,9},{9,10},{10,1... | collective-permute-start | bytes 454664 | tf_op jit(solution)/shard_map/fields/ppermute | solution.py:322
  22.8 2.4 %collective-permute-start.2 = (f32[296,128]{1,0:T(8,128)S(1)}, f32[296,128]{1,0:T(8,128)S(1)}, u32[]{:S(2)}, u32[]{:S(2)}) collective-permute-start(f32[296,128]{1,0:T(8,128)S(1)} %get-tuple-element.34), channel_id=1, source_target_pairs={{0,2},{1,3},{2,0},{3,1},{4,6},{5,7},{6,4},{7,5},{8,10},{9,11},{10,... | collective-permute-start | bytes 454664 | tf_op jit(solution)/shard_map/fields/ppermute | solution.py:322
  25.2 1.2 %collective-permute-start.3 = (f32[296,128]{1,0:T(8,128)S(1)}, f32[296,128]{1,0:T(8,128)S(1)}, u32[]{:S(2)}, u32[]{:S(2)}) collective-permute-start(f32[296,128]{1,0:T(8,128)S(1)} %get-tuple-element.35), channel_id=1, source_target_pairs={{0,3},{1,0},{2,1},{3,2},{4,7},{5,4},{6,5},{7,6},{8,11},{9,8},{10,9... | collective-permute-start | bytes 454664 | tf_op jit(solution)/shard_map/fields/ppermute | solution.py:322
  26.4 11.9 %collective-permute-done.1.field_1 = f32[296,128]{1,0:T(8,128)S(1)} collective-permute-done((f32[296,128]{1,0:T(8,128)S(1)}, f32[296,128]{1,0:T(8,128)S(1)}, u32[]{:S(2)}, u32[]{:S(2)}) %collective-permute-start.1) | collective-permute-done | bytes 151584 | tf_op jit(solution)/shard_map/fields/ppermute | solution.py:322
  38.3 3.2 %collective-permute-done.2.field_2 = f32[296,128]{1,0:T(8,128)S(1)} collective-permute-done((f32[296,128]{1,0:T(8,128)S(1)}, f32[296,128]{1,0:T(8,128)S(1)}, u32[]{:S(2)}, u32[]{:S(2)}) %collective-permute-start.2) | collective-permute-done | bytes 151584 | tf_op jit(solution)/shard_map/fields/ppermute | solution.py:322
  41.6 0.6 copy-done.10
  42.2 4.6 %frame_gradients.1 = (f32[2,128,128]{2,1,0:T(8,128)S(1)}, bf16[2,128,128]{2,1,0:T(8,128)(2,1)S(1)}, bf16[2,128,128]{2,1,0:T(8,128)(2,1)S(1)}, bf16[2,128,128]{2,1,0:T(8,128)(2,1)S(1)}) custom-call(s32[3]{0:T(128)S(1)} %pad_add_fusion.1.place_ref, s32[1,8]{1,0:T(1,128)S(1)} %copy-done.10, f32[296,128]{1,0:T(8,128)S(1)} %get-tuple-element.32.field_0, ...), custom_call_target="tpu_custom_call" | custom-call | flops 6000000000 | bytes 1048576 | tf_op jit(solution)/shard_map/frames/frame_gradients/pallas_call | solution.py:366
  46.8 1.7 %collective-permute-start.6 = (s32[4,32]{1,0:T(4,128)S(1)}, s32[4,32]{1,0:T(4,128)S(1)}, u32[]{:S(2)}, u32[]{:S(2)}) collective-permute-start(s32[4,32]{1,0:T(4,128)S(1)} %maximum_convert_fusion), channel_id=1, source_target_pairs={{0,192},{64,0},{128,64},{192,128},{1,193},{65,1},{129,65},{193,129... | collective-permute-start | bytes 1544 | tf_op jit(solution)/shard_map/targets/ppermute | solution.py:322
  48.8 0.7 collective-permute-start.4
  49.5 1.2 %collective-permute-start.8 = (bf16[2,128,128]{2,1,0:T(8,128)(2,1)S(1)}, bf16[2,128,128]{2,1,0:T(8,128)(2,1)S(1)}, u32[]{:S(2)}, u32[]{:S(2)}) collective-permute-start(bf16[2,128,128]{2,1,0:T(8,128)(2,1)S(1)} %get-tuple-element.43), channel_id=1, source_target_pairs={{0,2},{1,3},{2,0},{3,1},{4,6},{5,7},{6,4},{7,5},{8,10},{9,11},{10,... | collective-permute-start | bytes 196616 | tf_op jit(solution)/shard_map/frames/ppermute | solution.py:322
  50.8 1.8 %collective-permute-start.9 = (bf16[2,128,128]{2,1,0:T(8,128)(2,1)S(1)}, bf16[2,128,128]{2,1,0:T(8,128)(2,1)S(1)}, u32[]{:S(2)}, u32[]{:S(2)}) collective-permute-start(bf16[2,128,128]{2,1,0:T(8,128)(2,1)S(1)} %get-tuple-element.44), channel_id=1, source_target_pairs={{0,3},{1,0},{2,1},{3,2},{4,7},{5,4},{6,5},{7,6},{8,11},{9,8},{10,9... | collective-permute-start | bytes 196616 | tf_op jit(solution)/shard_map/frames/ppermute | solution.py:322
  53.0 1.4 %collective-permute-done.7.inter_1 = bf16[2,128,128]{2,1,0:T(8,128)(2,1)S(1)} collective-permute-done((bf16[2,128,128]{2,1,0:T(8,128)(2,1)S(1)}, bf16[2,128,128]{2,1,0:T(8,128)(2,1)S(1)}, u32[]{:S(2)}, u32[]{:S(2)}) %collective-permute-start.7) | collective-permute-done | bytes 65568 | tf_op jit(solution)/shard_map/frames/ppermute | solution.py:322
  55.2 1.5 %add_tiles.1 = (bf16[8,128,128]{2,1,0:T(8,128)(2,1)S(1)}, f32[2,128,128]{2,1,0:T(8,128)S(1)}) custom-call(s32[3]{0:T(128)S(1)} %pad_add_fusion.1.place_ref, s32[16,32]{1,0:T(8,128)S(1)} %pad_add_fusion.target_ref, bf16[32,4,16,256]{3,2,1,0:T(8,128)(2,1)S(1)} %all-to-all-done.sums_ref, f32[2,128,128]{2,1,0:T(8,128)S(1)} %get-tuple-element.41.inter_0, ...), custom_call_target="tpu_custom_call" | custom-call | flops 1000000 | bytes 1048576 | tf_op jit(solution)/shard_map/near_sum/add_tiles/pallas_call | solution.py:384
  56.7 13.0 %all_to_all.20.sums_ref = bf16[8,128,128]{2,1,0:T(8,128)(2,1)S(1)} all-to-all(bf16[8,128,128]{2,1,0:T(8,128)(2,1)S(1)} %get-tuple-element.45), channel_id=1, replica_groups=mesh['zl'=4,'x'=4,'c'=2,'zh'=2,'y'=4] {'zh','zl'}, dimensions={0} | all-to-all | bytes 524288 | tf_op jit(solution)/shard_map/near_sum/all_to_all | solution.py:392
  69.7 1.3 %residual_part.1 = (bf16[8,128,128]{2,1,0:T(8,128)(2,1)}, f32[2,3,16,128]{3,2,1,0:T(8,128)S(1)}, f32[2,3,16,128]{3,2,1,0:T(8,128)S(1)}, f32[2,3,16,128]{3,2,1,0:T(8,128)S(1)}, f32[2,3,16,128]{3,2,1,0:T(8,128)S(1)}) custom-call(s32[3]{0:T(128)S(1)} %pad_add_fusion.1.place_ref, bf16[8,128,128]{2,1,0:T(8,128)(2,1)S(1)} %all_to_all.20.sums_ref, ...), custom_call_target="tpu_custom_call" | custom-call | flops 1000000 | bytes 1048576 | tf_op jit(solution)/shard_map/residual/residual_part/pallas_call | solution.py:395
  71.0 3.4 %all-to-all-start.2 = ((bf16[8,128,128]{2,1,0:T(8,128)(2,1)}), bf16[8,128,128]{2,1,0:T(8,128)(2,1)S(1)}, u32[]{:S(2)}, u32[]{:S(2)}) async-start(bf16[8,128,128]{2,1,0:T(8,128)(2,1)} %get-tuple-element.47), calls=%async_computation.2 | async-start | bytes 524288 | tf_op jit(solution)/shard_map/residual/all_to_all | solution.py:404
  74.4 1.1 collective-permute-start.10
  75.4 2.8 %collective-permute-start.11 = (f32[2,3,16,128]{3,2,1,0:T(8,128)S(1)}, f32[2,3,16,128]{3,2,1,0:T(8,128)S(1)}, u32[]{:S(2)}, u32[]{:S(2)}) collective-permute-start(f32[2,3,16,128]{3,2,1,0:T(8,128)S(1)} %get-tuple-element.50), channel_id=1, source_target_pairs={{0,2},{1,3},{2,0},{3,1},{4,6},{5,7},{6,4},{7,5},{8,10},{9,11},{10,... | collective-permute-start | bytes 147464 | tf_op jit(solution)/shard_map/residual/ppermute | solution.py:322
  78.2 5.5 %all-to-all-done.2.residual_ref = bf16[8,128,128]{2,1,0:T(8,128)(2,1)S(1)} async-done(((bf16[8,128,128]{2,1,0:T(8,128)(2,1)}), bf16[8,128,128]{2,1,0:T(8,128)(2,1)S(1)}, u32[]{:S(2)}, u32[]{:S(2)}) %all-to-all-start.2) | async-done | bytes 262176 | tf_op jit(solution)/shard_map/residual/all_to_all | solution.py:404
  83.7 2.0 %pick_tiles.1 = bf16[32,4,16,256]{3,2,1,0:T(8,128)(2,1)} custom-call(s32[3]{0:T(128)S(1)} %pad_add_fusion.1.place_ref, s32[16,32]{1,0:T(8,128)S(1)} %pad_add_fusion.target_ref, bf16[8,128,128]{2,1,0:T(8,128)(2,1)S(1)} %all-to-all-done.2.residual_ref), custom_call_target="tpu_custom_call" | custom-call | flops 1000000 | bytes 1048576 | tf_op jit(solution)/shard_map/pick/pick_tiles/pallas_call | solution.py:407
  85.8 12.2 %all-to-all-start.3 = ((bf16[32,4,16,256]{3,2,1,0:T(8,128)(2,1)}), bf16[32,4,16,256]{3,2,1,0:T(8,128)(2,1)S(1)}, u32[]{:S(2)}, u32[]{:S(2)}) async-start(bf16[32,4,16,256]{3,2,1,0:T(8,128)(2,1)} %pick_tiles.1), calls=%async_computation.3 | async-start | bytes 2097152 | tf_op jit(solution)/shard_map/pick/all_to_all | solution.py:416
  98.0 0.7 slice-done
  99.1 1.1 copy.17
  100.2 1.5 %copy.18.radon_ref = bf16[256,2048]{1,0:T(8,128)(2,1)S(1)} copy(bf16[256,2048]{0,1:T(8,128)(2,1)} %bitcast.27) | data formatting | bytes 2097152 | tf_op jit(solution)/shard_map/back_project/reshape | solution.py:425
  101.7 5.3 %collective-permute-done.13.theirs_ref = f32[4,3,16,128]{3,2,1,0:T(8,128)S(1)} collective-permute-done((f32[4,3,16,128]{3,2,1,0:T(8,128)S(1)}, f32[4,3,16,128]{3,2,1,0:T(8,128)S(1)}, u32[]{:S(2)}, u32[]{:S(2)}) %collective-permute-start.13) | collective-permute-done | bytes 98336 | tf_op jit(solution)/shard_map/updates/ppermute | solution.py:322
  107.1 1.2 %updates.1 = (f32[128,128]{1,0:T(8,128)}, f32[128,128]{1,0:T(8,128)}) custom-call(s32[3]{0:T(128)S(1)} %pad_add_fusion.1.place_ref, f32[2,3,16,128]{3,2,1,0:T(8,128)S(1)} %get-tuple-element.52.own_ref, f32[2,3,16,128]{3,2,1,0:T(8,128)S(1)} %copy-done.4, f32[2,3,16,128]{3,2,1,0:T(8,128)S(1)} %copy-done.6, ...), custom_call_target="tpu_custom_call" | custom-call | flops 1000000 | bytes 1048576 | tf_op jit(solution)/shard_map/updates/updates/pallas_call | solution.py:420
  108.3 5.9 %all-to-all-done.3.picked_ref = bf16[32,4,16,256]{3,2,1,0:T(8,128)(2,1)S(1)} async-done(((bf16[32,4,16,256]{3,2,1,0:T(8,128)(2,1)}), bf16[32,4,16,256]{3,2,1,0:T(8,128)(2,1)S(1)}, u32[]{:S(2)}, u32[]{:S(2)}) %all-to-all-start.3) | async-done | bytes 1048608 | tf_op jit(solution)/shard_map/pick/all_to_all | solution.py:416
  114.2 1.1 back_project.1
  (59 shorter events, 2.7 us)
Async XLA Ops:
  0.6 19.5 %collective-permute-start = (f32[128,128]{1,0:T(8,128)}, f32[128,128]{1,0:T(8,128)S(1)}, u32[]{:S(2)}, u32[]{:S(2)}) collective-permute-start(f32[128,128]{1,0:T(8,128)} %bitcast.18), channel_id=1, source_target_pairs={{0,4},{4,0},{1,5},{5,1},{2,6},{6,2},{3,7},{7,3},{8,12},{12,8},{9,1... | collective-permute-start | bytes 196616 | tf_op jit(solution)/shard_map/ray_sums/ppermute | solution.py:322
  11.7 8.4 %copy-start.1 = (f32[1,64,2,128]{3,2,1,0:T(2,128)S(1)}, f32[1,64,2,128]{3,2,1,0:T(2,128)}, u32[]{:S(2)}) copy-start(f32[1,64,2,128]{3,2,1,0:T(2,128)} %param.15) | copy-start | bytes 196612
  11.7 8.4 %copy-start.2 = (f32[1,64,2,128]{3,2,1,0:T(2,128)S(1)}, f32[1,64,2,128]{3,2,1,0:T(2,128)}, u32[]{:S(2)}) copy-start(f32[1,64,2,128]{3,2,1,0:T(2,128)} %param.16) | copy-start | bytes 196612
  11.7 29.8 %copy-start.8 = (f32[1,8,128,128]{3,2,1,0:T(8,128)S(1)}, f32[1,8,128,128]{3,2,1,0:T(8,128)}, u32[]{:S(2)}) copy-start(f32[1,8,128,128]{3,2,1,0:T(8,128)} %param.12) | copy-start | bytes 1572868
  11.7 29.8 %copy-start.9 = (f32[2,128,128]{2,1,0:T(8,128)S(1)}, f32[2,128,128]{2,1,0:T(8,128)}, u32[]{:S(2)}) copy-start(f32[2,128,128]{2,1,0:T(8,128)} %probe_ref.1) | copy-start | bytes 393220
  11.8 29.8 %copy-start.11 = (bf16[256,256]{1,0:T(8,128)(2,1)S(1)}, bf16[256,256]{1,0:T(8,128)(2,1)}, u32[]{:S(2)}) copy-start(bf16[256,256]{1,0:T(8,128)(2,1)} %constant.24.clone.bl_ref) | copy-start | bytes 393220
  11.8 29.8 %copy-start.12 = (bf16[256,256]{1,0:T(8,128)(2,1)S(1)}, bf16[256,256]{1,0:T(8,128)(2,1)}, u32[]{:S(2)}) copy-start(bf16[256,256]{1,0:T(8,128)(2,1)} %constant.23.clone.bh_ref) | copy-start | bytes 393220
  11.8 29.8 %copy-start.13 = (bf16[256,256]{1,0:T(8,128)(2,1)S(1)}, bf16[256,256]{1,0:T(8,128)(2,1)}, u32[]{:S(2)}) copy-start(bf16[256,256]{1,0:T(8,128)(2,1)} %constant.22.clone.al_ref) | copy-start | bytes 393220
  11.8 29.8 %copy-start.14 = (bf16[256,256]{1,0:T(8,128)(2,1)S(1)}, bf16[256,256]{1,0:T(8,128)(2,1)}, u32[]{:S(2)}) copy-start(bf16[256,256]{1,0:T(8,128)(2,1)} %constant.21.clone.ah_ref) | copy-start | bytes 393220
  11.8 43.4 %all-to-all-start = ((bf16[32,4,16,256]{3,2,1,0:T(8,128)(2,1)}), bf16[32,4,16,256]{3,2,1,0:T(8,128)(2,1)S(1)}, u32[]{:S(2)}, u32[]{:S(2)}) async-start(bf16[32,4,16,256]{3,2,1,0:T(8,128)(2,1)} %ray_sums.1), calls=%async_computation | async-start | bytes 2097152 | tf_op jit(solution)/shard_map/ray_sums/all_to_all | solution.py:356
  21.3 16.9 %collective-permute-start.1 = (f32[296,128]{1,0:T(8,128)S(1)}, f32[296,128]{1,0:T(8,128)S(1)}, u32[]{:S(2)}, u32[]{:S(2)}) collective-permute-start(f32[296,128]{1,0:T(8,128)S(1)} %get-tuple-element.33), channel_id=1, source_target_pairs={{0,1},{1,2},{2,3},{3,0},{4,5},{5,6},{6,7},{7,4},{8,9},{9,10},{10,1... | collective-permute-start | bytes 454664 | tf_op jit(solution)/shard_map/fields/ppermute | solution.py:322
  22.8 18.7 %collective-permute-start.2 = (f32[296,128]{1,0:T(8,128)S(1)}, f32[296,128]{1,0:T(8,128)S(1)}, u32[]{:S(2)}, u32[]{:S(2)}) collective-permute-start(f32[296,128]{1,0:T(8,128)S(1)} %get-tuple-element.34), channel_id=1, source_target_pairs={{0,2},{1,3},{2,0},{3,1},{4,6},{5,7},{6,4},{7,5},{8,10},{9,11},{10,... | collective-permute-start | bytes 454664 | tf_op jit(solution)/shard_map/fields/ppermute | solution.py:322
  25.2 16.3 %collective-permute-start.3 = (f32[296,128]{1,0:T(8,128)S(1)}, f32[296,128]{1,0:T(8,128)S(1)}, u32[]{:S(2)}, u32[]{:S(2)}) collective-permute-start(f32[296,128]{1,0:T(8,128)S(1)} %get-tuple-element.35), channel_id=1, source_target_pairs={{0,3},{1,0},{2,1},{3,2},{4,7},{5,4},{6,5},{7,6},{8,11},{9,8},{10,9... | collective-permute-start | bytes 454664 | tf_op jit(solution)/shard_map/fields/ppermute | solution.py:322
  46.8 4.0 %collective-permute-start.6 = (s32[4,32]{1,0:T(4,128)S(1)}, s32[4,32]{1,0:T(4,128)S(1)}, u32[]{:S(2)}, u32[]{:S(2)}) collective-permute-start(s32[4,32]{1,0:T(4,128)S(1)} %maximum_convert_fusion), channel_id=1, source_target_pairs={{0,192},{64,0},{128,64},{192,128},{1,193},{65,1},{129,65},{193,129... | collective-permute-start | bytes 1544 | tf_op jit(solution)/shard_map/targets/ppermute | solution.py:322
  48.5 4.0 %collective-permute-start.5 = (s32[4,32]{1,0:T(4,128)S(1)}, s32[4,32]{1,0:T(4,128)S(1)}, u32[]{:S(2)}, u32[]{:S(2)}) collective-permute-start(s32[4,32]{1,0:T(4,128)S(1)} %maximum_convert_fusion), channel_id=1, source_target_pairs={{0,128},{64,192},{128,0},{192,64},{1,129},{65,193},{129,1},{193,65... | collective-permute-start | bytes 1544 | tf_op jit(solution)/shard_map/targets/ppermute | solution.py:322
  48.8 4.2 %collective-permute-start.4 = (s32[4,32]{1,0:T(4,128)S(1)}, s32[4,32]{1,0:T(4,128)S(1)}, u32[]{:S(2)}, u32[]{:S(2)}) collective-permute-start(s32[4,32]{1,0:T(4,128)S(1)} %maximum_convert_fusion), channel_id=1, source_target_pairs={{0,64},{64,128},{128,192},{192,0},{1,65},{65,129},{129,193},{193,1... | collective-permute-start | bytes 1544 | tf_op jit(solution)/shard_map/targets/ppermute | solution.py:322
  49.5 4.9 %collective-permute-start.7 = (bf16[2,128,128]{2,1,0:T(8,128)(2,1)S(1)}, bf16[2,128,128]{2,1,0:T(8,128)(2,1)S(1)}, u32[]{:S(2)}, u32[]{:S(2)}) collective-permute-start(bf16[2,128,128]{2,1,0:T(8,128)(2,1)S(1)} %get-tuple-element.42), channel_id=1, source_target_pairs={{0,1},{1,2},{2,3},{3,0},{4,5},{5,6},{6,7},{7,4},{8,9},{9,10},{10,1... | collective-permute-start | bytes 196616 | tf_op jit(solution)/shard_map/frames/ppermute | solution.py:322
  49.5 5.1 %collective-permute-start.8 = (bf16[2,128,128]{2,1,0:T(8,128)(2,1)S(1)}, bf16[2,128,128]{2,1,0:T(8,128)(2,1)S(1)}, u32[]{:S(2)}, u32[]{:S(2)}) collective-permute-start(bf16[2,128,128]{2,1,0:T(8,128)(2,1)S(1)} %get-tuple-element.43), channel_id=1, source_target_pairs={{0,2},{1,3},{2,0},{3,1},{4,6},{5,7},{6,4},{7,5},{8,10},{9,11},{10,... | collective-permute-start | bytes 196616 | tf_op jit(solution)/shard_map/frames/ppermute | solution.py:322
  50.8 4.5 %collective-permute-start.9 = (bf16[2,128,128]{2,1,0:T(8,128)(2,1)S(1)}, bf16[2,128,128]{2,1,0:T(8,128)(2,1)S(1)}, u32[]{:S(2)}, u32[]{:S(2)}) collective-permute-start(bf16[2,128,128]{2,1,0:T(8,128)(2,1)S(1)} %get-tuple-element.44), channel_id=1, source_target_pairs={{0,3},{1,0},{2,1},{3,2},{4,7},{5,4},{6,5},{7,6},{8,11},{9,8},{10,9... | collective-permute-start | bytes 196616 | tf_op jit(solution)/shard_map/frames/ppermute | solution.py:322
  71.0 12.8 %all-to-all-start.2 = ((bf16[8,128,128]{2,1,0:T(8,128)(2,1)}), bf16[8,128,128]{2,1,0:T(8,128)(2,1)S(1)}, u32[]{:S(2)}, u32[]{:S(2)}) async-start(bf16[8,128,128]{2,1,0:T(8,128)(2,1)} %get-tuple-element.47), calls=%async_computation.2 | async-start | bytes 524288 | tf_op jit(solution)/shard_map/residual/all_to_all | solution.py:404
  74.4 11.3 %collective-permute-start.10 = (f32[2,3,16,128]{3,2,1,0:T(8,128)S(1)}, f32[2,3,16,128]{3,2,1,0:T(8,128)S(1)}, u32[]{:S(2)}, u32[]{:S(2)}) collective-permute-start(f32[2,3,16,128]{3,2,1,0:T(8,128)S(1)} %get-tuple-element.49), channel_id=1, source_target_pairs={{0,1},{1,2},{2,3},{3,0},{4,5},{5,6},{6,7},{7,4},{8,9},{9,10},{10,1... | collective-permute-start | bytes 147464 | tf_op jit(solution)/shard_map/residual/ppermute | solution.py:322
  75.4 10.3 %collective-permute-start.11 = (f32[2,3,16,128]{3,2,1,0:T(8,128)S(1)}, f32[2,3,16,128]{3,2,1,0:T(8,128)S(1)}, u32[]{:S(2)}, u32[]{:S(2)}) collective-permute-start(f32[2,3,16,128]{3,2,1,0:T(8,128)S(1)} %get-tuple-element.50), channel_id=1, source_target_pairs={{0,2},{1,3},{2,0},{3,1},{4,6},{5,7},{6,4},{7,5},{8,10},{9,11},{10,... | collective-permute-start | bytes 147464 | tf_op jit(solution)/shard_map/residual/ppermute | solution.py:322
  78.2 7.5 %collective-permute-start.12 = (f32[2,3,16,128]{3,2,1,0:T(8,128)S(1)}, f32[2,3,16,128]{3,2,1,0:T(8,128)S(1)}, u32[]{:S(2)}, u32[]{:S(2)}) collective-permute-start(f32[2,3,16,128]{3,2,1,0:T(8,128)S(1)} %get-tuple-element.51), channel_id=1, source_target_pairs={{0,3},{1,0},{2,1},{3,2},{4,7},{5,4},{6,5},{7,6},{8,11},{9,8},{10,9... | collective-permute-start | bytes 147464 | tf_op jit(solution)/shard_map/residual/ppermute | solution.py:322
  85.7 12.2 %copy-start.3 = (f32[2,3,16,128]{3,2,1,0:T(8,128)}, f32[2,3,16,128]{3,2,1,0:T(8,128)S(1)}, u32[]{:S(2)}) copy-start(f32[2,3,16,128]{3,2,1,0:T(8,128)S(1)} %collective-permute-done.10.one_ref) | copy-start | bytes 147460
  85.7 12.2 %copy-start.5 = (f32[2,3,16,128]{3,2,1,0:T(8,128)}, f32[2,3,16,128]{3,2,1,0:T(8,128)S(1)}, u32[]{:S(2)}) copy-start(f32[2,3,16,128]{3,2,1,0:T(8,128)S(1)} %collective-permute-done.11.two_ref) | copy-start | bytes 147460
  85.7 13.3 %copy-start.15 = (bf16[1,32,2,32,256]{4,3,2,1,0:T(8,128)(2,1)S(1)}, bf16[1,32,2,32,256]{4,3,2,1,0:T(8,128)(2,1)}, u32[]{:S(2)}) copy-start(bf16[1,32,2,32,256]{4,3,2,1,0:T(8,128)(2,1)} %param.18) | copy-start | bytes 3145732
  85.8 28.5 %all-to-all-start.3 = ((bf16[32,4,16,256]{3,2,1,0:T(8,128)(2,1)}), bf16[32,4,16,256]{3,2,1,0:T(8,128)(2,1)S(1)}, u32[]{:S(2)}, u32[]{:S(2)}) async-start(bf16[32,4,16,256]{3,2,1,0:T(8,128)(2,1)} %pick_tiles.1), calls=%async_computation.3 | async-start | bytes 2097152 | tf_op jit(solution)/shard_map/pick/all_to_all | solution.py:416
  98.0 0.7 slice-start.1
  98.7 8.3 %collective-permute-start.13 = (f32[4,3,16,128]{3,2,1,0:T(8,128)S(1)}, f32[4,3,16,128]{3,2,1,0:T(8,128)S(1)}, u32[]{:S(2)}, u32[]{:S(2)}) collective-permute-start(f32[4,3,16,128]{3,2,1,0:T(8,128)S(1)} %pad_maximum_fusion), channel_id=1, source_target_pairs={{0,4},{4,0},{1,5},{5,1},{2,6},{6,2},{3,7},{7,3},{8,12},{12,8},{9,1... | collective-permute-start | bytes 294920 | tf_op jit(solution)/shard_map/updates/ppermute | solution.py:322
  100.2 6.9 %copy-start.4 = (f32[2,3,16,128]{3,2,1,0:T(8,128)S(1)}, f32[2,3,16,128]{3,2,1,0:T(8,128)}, u32[]{:S(2)}) copy-start(f32[2,3,16,128]{3,2,1,0:T(8,128)} %copy-done.3) | copy-start | bytes 147460
  100.2 6.9 %copy-start.6 = (f32[2,3,16,128]{3,2,1,0:T(8,128)S(1)}, f32[2,3,16,128]{3,2,1,0:T(8,128)}, u32[]{:S(2)}) copy-start(f32[2,3,16,128]{3,2,1,0:T(8,128)} %copy-done.5) | copy-start | bytes 147460
  101.7 12.5 %copy-start = (f32[256,2,128]{2,1,0:T(2,128)S(1)}, f32[256,2,128]{2,1,0:T(2,128)}, u32[]{:S(2)}) copy-start(f32[256,2,128]{2,1,0:T(2,128)} %param.17) | copy-start | bytes 786436
  (3 other events, 2.1 us)

commit v8 on v7

--- a/solution.py
+++ b/solution.py
@@ -25,7 +25,7 @@
 DEEP = ZH * ZL
 QR = RAYS // Y
 FR_DEV = 8
-FRAMES_COST = 6_000_000_000
+FRAMES_COST = 20_000_000_000
 SUMS_LIMIT = 62 << 20
 
 penalty = 1.0

time: 116 us -> 104 us (0.90)
  waiting for transfers between devices: 34.6 us -> 21 us
  blocking collectives: 13 us -> 16.2 us
  starting transfers between devices: 46.6 us -> 44.3 us
    ppermute x14, waiting for transfers between devices: 23.1 us -> 10.6 us  [shifted(): lax.ppermute(value, axis, [(i, (i + step) % length) for i in range(length)])]
    all_to_all x1, starting transfers between devices: 12.2 us -> 8.34 us  [body(): returned = lax.all_to_all(picked, CROSS, 0, 0, tiled=True)]
    ppermute x14, starting transfers between devices: 22.8 us -> 26.2 us  [shifted(): lax.ppermute(value, axis, [(i, (i + step) % length) for i in range(length)])]
    all_to_all x1, blocking collectives: 13 us -> 16.2 us  [body(): far_sums = lax.all_to_all(dense, ALONG, 0, 0, tiled=True)]
    all_to_all x1, starting transfers between devices: 8.19 us -> 6.37 us  [body(): near_sums = lax.all_to_all(sums, CROSS, 0, 0, tiled=True)]
  transfers between devices with their start and end apart: 17 -> 17, of which waited for: 9 -> 5; matrix products, arithmetic and copies ran while one was open for 2% -> 3% of each run, Pallas kernels for 10% -> 11%
where the time goes in v8:
time: 104 us
  starting transfers between devices  44.3 us (43%)
  waiting for transfers between devices  21 us (20%)
  blocking collectives  16.2 us (16%)
  Pallas kernels  15.6 us (15%)
  local copies, waits for them, and re-layouts  5.52 us (5%)
    ppermute x14, starting transfers between devices, shifted(): lax.ppermute(value, axis, [(i, (i + step) % length) for i in range(length)])  26.2 us
    all_to_all x1, blocking collectives, body(): far_sums = lax.all_to_all(dense, ALONG, 0, 0, tiled=True)  16.2 us
    ppermute x14, waiting for transfers between devices, shifted(): lax.ppermute(value, axis, [(i, (i + step) % length) for i in range(length)])  10.6 us
    all_to_all x1, starting transfers between devices, body(): returned = lax.all_to_all(picked, CROSS, 0, 0, tiled=True)  8.34 us
    all_to_all x1, starting transfers between devices, body(): near_sums = lax.all_to_all(sums, CROSS, 0, 0, tiled=True)  6.37 us
    all_to_all x1, waiting for transfers between devices, body(): residuals = lax.all_to_all(copies, ALONG, 0, 0, tiled=True)  5.18 us
    all_to_all x1, waiting for transfers between devices, body(): returned = lax.all_to_all(picked, CROSS, 0, 0, tiled=True)  5.16 us
    pallas_call x1, Pallas kernels, body(): call(frame_gradients, (shape(2, 128, NZ),) + (shape(2, 128, NZ, dtype=bf1...  4.65 us
  transfers between devices with their start and end apart: 17, of which 5 were waited for; matrix products, arithmetic and copies ran while one was open for 3% of the time, Pallas kernels for 11%

profile of v8, /device:TPU:1, one launch (start us, length us, event | category | flops | bytes accessed | tf_op | source)
XLA Modules:
  0.0 103.7 jit_solution(4232653167122098603)
XLA Ops:
  0.6 7.8 %collective-permute-start = (f32[128,128]{1,0:T(8,128)}, f32[128,128]{1,0:T(8,128)S(1)}, u32[]{:S(2)}, u32[]{:S(2)}) collective-permute-start(f32[128,128]{1,0:T(8,128)} %bitcast.18), channel_id=1, source_target_pairs={{0,4},{4,0},{1,5},{5,1},{2,6},{6,2},{3,7},{7,3},{8,12},{12,8},{9,1... | collective-permute-start | bytes 196616 | tf_op jit(solution)/shard_map/ray_sums/ppermute | solution.py:322
  8.5 3.3 %ray_sums.1 = bf16[32,4,16,256]{3,2,1,0:T(8,128)(2,1)} custom-call(bf16[32,2,32,256]{3,2,1,0:T(8,128)(2,1)} %bitcast.25, f32[512,128]{1,0:T(8,128)} %bitcast.16), custom_call_target="tpu_custom_call" | custom-call | flops 268435456 | bytes 1048576 | tf_op jit(solution)/shard_map/ray_sums/ray_sums/pallas_call | solution.py:346
  13.1 1.4 %collective-permute-start.1 = (f32[296,128]{1,0:T(8,128)S(1)}, f32[296,128]{1,0:T(8,128)S(1)}, u32[]{:S(2)}, u32[]{:S(2)}) collective-permute-start(f32[296,128]{1,0:T(8,128)S(1)} %get-tuple-element.33), channel_id=1, source_target_pairs={{0,1},{1,2},{2,3},{3,0},{4,5},{5,6},{6,7},{7,4},{8,9},{9,10},{10,1... | collective-permute-start | bytes 454664 | tf_op jit(solution)/shard_map/fields/ppermute | solution.py:322
  14.5 2.6 %collective-permute-start.2 = (f32[296,128]{1,0:T(8,128)S(1)}, f32[296,128]{1,0:T(8,128)S(1)}, u32[]{:S(2)}, u32[]{:S(2)}) collective-permute-start(f32[296,128]{1,0:T(8,128)S(1)} %get-tuple-element.34), channel_id=1, source_target_pairs={{0,2},{1,3},{2,0},{3,1},{4,6},{5,7},{6,4},{7,5},{8,10},{9,11},{10,... | collective-permute-start | bytes 454664 | tf_op jit(solution)/shard_map/fields/ppermute | solution.py:322
  17.1 1.1 %collective-permute-start.3 = (f32[296,128]{1,0:T(8,128)S(1)}, f32[296,128]{1,0:T(8,128)S(1)}, u32[]{:S(2)}, u32[]{:S(2)}) collective-permute-start(f32[296,128]{1,0:T(8,128)S(1)} %get-tuple-element.35), channel_id=1, source_target_pairs={{0,3},{1,0},{2,1},{3,2},{4,7},{5,4},{6,5},{7,6},{8,11},{9,8},{10,9... | collective-permute-start | bytes 454664 | tf_op jit(solution)/shard_map/fields/ppermute | solution.py:322
  18.3 6.4 %all-to-all-start = ((bf16[32,4,16,256]{3,2,1,0:T(8,128)(2,1)}), bf16[32,4,16,256]{3,2,1,0:T(8,128)(2,1)S(1)}, u32[]{:S(2)}, u32[]{:S(2)}) async-start(bf16[32,4,16,256]{3,2,1,0:T(8,128)(2,1)} %ray_sums.1), calls=%async_computation | async-start | bytes 2097152 | tf_op jit(solution)/shard_map/ray_sums/all_to_all | solution.py:356
  25.3 0.9 copy-done.14
  26.2 4.7 %frame_gradients.1 = (f32[2,128,128]{2,1,0:T(8,128)S(1)}, bf16[2,128,128]{2,1,0:T(8,128)(2,1)S(1)}, bf16[2,128,128]{2,1,0:T(8,128)(2,1)S(1)}, bf16[2,128,128]{2,1,0:T(8,128)(2,1)S(1)}) custom-call(s32[3]{0:T(128)S(1)} %pad_add_fusion.1.place_ref, s32[1,8]{1,0:T(1,128)S(1)} %copy-done.10, f32[296,128]{1,0:T(8,128)S(1)} %get-tuple-element.32.field_0, ...), custom_call_target="tpu_custom_call" | custom-call | flops 20000000000 | bytes 1048576 | tf_op jit(solution)/shard_map/frames/frame_gradients/pallas_call | solution.py:366
  30.9 2.2 %collective-permute-start.6 = (s32[4,32]{1,0:T(4,128)S(1)}, s32[4,32]{1,0:T(4,128)S(1)}, u32[]{:S(2)}, u32[]{:S(2)}) collective-permute-start(s32[4,32]{1,0:T(4,128)S(1)} %maximum_convert_fusion), channel_id=1, source_target_pairs={{0,192},{64,0},{128,64},{192,128},{1,193},{65,1},{129,65},{193,129... | collective-permute-start | bytes 1544 | tf_op jit(solution)/shard_map/targets/ppermute | solution.py:322
  33.1 1.2 %collective-permute-start.4 = (s32[4,32]{1,0:T(4,128)S(1)}, s32[4,32]{1,0:T(4,128)S(1)}, u32[]{:S(2)}, u32[]{:S(2)}) collective-permute-start(s32[4,32]{1,0:T(4,128)S(1)} %maximum_convert_fusion), channel_id=1, source_target_pairs={{0,64},{64,128},{128,192},{192,0},{1,65},{65,129},{129,193},{193,1... | collective-permute-start | bytes 1544 | tf_op jit(solution)/shard_map/targets/ppermute | solution.py:322
  34.3 1.4 %collective-permute-start.7 = (bf16[2,128,128]{2,1,0:T(8,128)(2,1)S(1)}, bf16[2,128,128]{2,1,0:T(8,128)(2,1)S(1)}, u32[]{:S(2)}, u32[]{:S(2)}) collective-permute-start(bf16[2,128,128]{2,1,0:T(8,128)(2,1)S(1)} %get-tuple-element.42), channel_id=1, source_target_pairs={{0,1},{1,2},{2,3},{3,0},{4,5},{5,6},{6,7},{7,4},{8,9},{9,10},{10,1... | collective-permute-start | bytes 196616 | tf_op jit(solution)/shard_map/frames/ppermute | solution.py:322
  35.7 2.4 %collective-permute-start.8 = (bf16[2,128,128]{2,1,0:T(8,128)(2,1)S(1)}, bf16[2,128,128]{2,1,0:T(8,128)(2,1)S(1)}, u32[]{:S(2)}, u32[]{:S(2)}) collective-permute-start(bf16[2,128,128]{2,1,0:T(8,128)(2,1)S(1)} %get-tuple-element.43), channel_id=1, source_target_pairs={{0,2},{1,3},{2,0},{3,1},{4,6},{5,7},{6,4},{7,5},{8,10},{9,11},{10,... | collective-permute-start | bytes 196616 | tf_op jit(solution)/shard_map/frames/ppermute | solution.py:322
  38.1 1.2 %collective-permute-start.9 = (bf16[2,128,128]{2,1,0:T(8,128)(2,1)S(1)}, bf16[2,128,128]{2,1,0:T(8,128)(2,1)S(1)}, u32[]{:S(2)}, u32[]{:S(2)}) collective-permute-start(bf16[2,128,128]{2,1,0:T(8,128)(2,1)S(1)} %get-tuple-element.44), channel_id=1, source_target_pairs={{0,3},{1,0},{2,1},{3,2},{4,7},{5,4},{6,5},{7,6},{8,11},{9,8},{10,9... | collective-permute-start | bytes 196616 | tf_op jit(solution)/shard_map/frames/ppermute | solution.py:322
  39.3 3.1 %collective-permute-done.7.inter_1 = bf16[2,128,128]{2,1,0:T(8,128)(2,1)S(1)} collective-permute-done((bf16[2,128,128]{2,1,0:T(8,128)(2,1)S(1)}, bf16[2,128,128]{2,1,0:T(8,128)(2,1)S(1)}, u32[]{:S(2)}, u32[]{:S(2)}) %collective-permute-start.7) | collective-permute-done | bytes 65568 | tf_op jit(solution)/shard_map/frames/ppermute | solution.py:322
  42.4 1.7 %collective-permute-done.8.inter_2 = bf16[2,128,128]{2,1,0:T(8,128)(2,1)S(1)} collective-permute-done((bf16[2,128,128]{2,1,0:T(8,128)(2,1)S(1)}, bf16[2,128,128]{2,1,0:T(8,128)(2,1)S(1)}, u32[]{:S(2)}, u32[]{:S(2)}) %collective-permute-start.8) | collective-permute-done | bytes 65568 | tf_op jit(solution)/shard_map/frames/ppermute | solution.py:322
  44.2 1.5 %add_tiles.1 = (bf16[8,128,128]{2,1,0:T(8,128)(2,1)S(1)}, f32[2,128,128]{2,1,0:T(8,128)S(1)}) custom-call(s32[3]{0:T(128)S(1)} %pad_add_fusion.1.place_ref, s32[16,32]{1,0:T(8,128)S(1)} %pad_add_fusion.target_ref, bf16[32,4,16,256]{3,2,1,0:T(8,128)(2,1)S(1)} %all-to-all-done.sums_ref, f32[2,128,128]{2,1,0:T(8,128)S(1)} %get-tuple-element.41.inter_0, ...), custom_call_target="tpu_custom_call" | custom-call | flops 1000000 | bytes 1048576 | tf_op jit(solution)/shard_map/near_sum/add_tiles/pallas_call | solution.py:384
  45.7 16.2 %all_to_all.20.sums_ref = bf16[8,128,128]{2,1,0:T(8,128)(2,1)S(1)} all-to-all(bf16[8,128,128]{2,1,0:T(8,128)(2,1)S(1)} %get-tuple-element.45), channel_id=1, replica_groups=mesh['zl'=4,'x'=4,'c'=2,'zh'=2,'y'=4] {'zh','zl'}, dimensions={0} | all-to-all | bytes 524288 | tf_op jit(solution)/shard_map/near_sum/all_to_all | solution.py:392
  61.8 1.3 %residual_part.1 = (bf16[8,128,128]{2,1,0:T(8,128)(2,1)}, f32[2,3,16,128]{3,2,1,0:T(8,128)S(1)}, f32[2,3,16,128]{3,2,1,0:T(8,128)S(1)}, f32[2,3,16,128]{3,2,1,0:T(8,128)S(1)}, f32[2,3,16,128]{3,2,1,0:T(8,128)S(1)}) custom-call(s32[3]{0:T(128)S(1)} %pad_add_fusion.1.place_ref, bf16[8,128,128]{2,1,0:T(8,128)(2,1)S(1)} %all_to_all.20.sums_ref, ...), custom_call_target="tpu_custom_call" | custom-call | flops 1000000 | bytes 1048576 | tf_op jit(solution)/shard_map/residual/residual_part/pallas_call | solution.py:395
  63.1 3.4 %all-to-all-start.2 = ((bf16[8,128,128]{2,1,0:T(8,128)(2,1)}), bf16[8,128,128]{2,1,0:T(8,128)(2,1)S(1)}, u32[]{:S(2)}, u32[]{:S(2)}) async-start(bf16[8,128,128]{2,1,0:T(8,128)(2,1)} %get-tuple-element.47), calls=%async_computation.2 | async-start | bytes 524288 | tf_op jit(solution)/shard_map/residual/all_to_all | solution.py:404
  67.1 1.6 %collective-permute-start.11 = (f32[2,3,16,128]{3,2,1,0:T(8,128)S(1)}, f32[2,3,16,128]{3,2,1,0:T(8,128)S(1)}, u32[]{:S(2)}, u32[]{:S(2)}) collective-permute-start(f32[2,3,16,128]{3,2,1,0:T(8,128)S(1)} %get-tuple-element.50), channel_id=1, source_target_pairs={{0,2},{1,3},{2,0},{3,1},{4,6},{5,7},{6,4},{7,5},{8,10},{9,11},{10,... | collective-permute-start | bytes 147464 | tf_op jit(solution)/shard_map/residual/ppermute | solution.py:322
  68.7 2.0 %collective-permute-start.12 = (f32[2,3,16,128]{3,2,1,0:T(8,128)S(1)}, f32[2,3,16,128]{3,2,1,0:T(8,128)S(1)}, u32[]{:S(2)}, u32[]{:S(2)}) collective-permute-start(f32[2,3,16,128]{3,2,1,0:T(8,128)S(1)} %get-tuple-element.51), channel_id=1, source_target_pairs={{0,3},{1,0},{2,1},{3,2},{4,7},{5,4},{6,5},{7,6},{8,11},{9,8},{10,9... | collective-permute-start | bytes 147464 | tf_op jit(solution)/shard_map/residual/ppermute | solution.py:322
  70.7 5.2 %all-to-all-done.2.residual_ref = bf16[8,128,128]{2,1,0:T(8,128)(2,1)S(1)} async-done(((bf16[8,128,128]{2,1,0:T(8,128)(2,1)}), bf16[8,128,128]{2,1,0:T(8,128)(2,1)S(1)}, u32[]{:S(2)}, u32[]{:S(2)}) %all-to-all-start.2) | async-done | bytes 262176 | tf_op jit(solution)/shard_map/residual/all_to_all | solution.py:404
  75.9 2.0 %pick_tiles.1 = bf16[32,4,16,256]{3,2,1,0:T(8,128)(2,1)} custom-call(s32[3]{0:T(128)S(1)} %pad_add_fusion.1.place_ref, s32[16,32]{1,0:T(8,128)S(1)} %pad_add_fusion.target_ref, bf16[8,128,128]{2,1,0:T(8,128)(2,1)S(1)} %all-to-all-done.2.residual_ref), custom_call_target="tpu_custom_call" | custom-call | flops 1000000 | bytes 1048576 | tf_op jit(solution)/shard_map/pick/pick_tiles/pallas_call | solution.py:407
  77.9 8.3 %all-to-all-start.3 = ((bf16[32,4,16,256]{3,2,1,0:T(8,128)(2,1)}), bf16[32,4,16,256]{3,2,1,0:T(8,128)(2,1)S(1)}, u32[]{:S(2)}, u32[]{:S(2)}) async-start(bf16[32,4,16,256]{3,2,1,0:T(8,128)(2,1)} %pick_tiles.1), calls=%async_computation.3 | async-start | bytes 2097152 | tf_op jit(solution)/shard_map/pick/all_to_all | solution.py:416
  86.3 0.7 slice-done
  87.0 0.8 collective-permute-start.13
  87.8 1.1 %copy.17 = bf16[256,8,4,4,2,8]{0,5,4,3,2,1:T(8,128)(2,1)} copy(bf16[256,8,4,4,2,8]{0,5,2,4,1,3:T(8,128)(2,1)S(1)} %bitcast.26) | data formatting | bytes 2097152 | tf_op jit(solution)/shard_map/back_project/transpose | solution.py:425
  88.9 1.5 %copy.18.radon_ref = bf16[256,2048]{1,0:T(8,128)(2,1)S(1)} copy(bf16[256,2048]{0,1:T(8,128)(2,1)} %bitcast.27) | data formatting | bytes 2097152 | tf_op jit(solution)/shard_map/back_project/reshape | solution.py:425
  90.4 5.7 %collective-permute-done.13.theirs_ref = f32[4,3,16,128]{3,2,1,0:T(8,128)S(1)} collective-permute-done((f32[4,3,16,128]{3,2,1,0:T(8,128)S(1)}, f32[4,3,16,128]{3,2,1,0:T(8,128)S(1)}, u32[]{:S(2)}, u32[]{:S(2)}) %collective-permute-start.13) | collective-permute-done | bytes 98336 | tf_op jit(solution)/shard_map/updates/ppermute | solution.py:322
  96.2 1.2 %updates.1 = (f32[128,128]{1,0:T(8,128)}, f32[128,128]{1,0:T(8,128)}) custom-call(s32[3]{0:T(128)S(1)} %pad_add_fusion.1.place_ref, f32[2,3,16,128]{3,2,1,0:T(8,128)S(1)} %get-tuple-element.52.own_ref, f32[2,3,16,128]{3,2,1,0:T(8,128)S(1)} %copy-done.4, f32[2,3,16,128]{3,2,1,0:T(8,128)S(1)} %copy-done.6, ...), custom_call_target="tpu_custom_call" | custom-call | flops 1000000 | bytes 1048576 | tf_op jit(solution)/shard_map/updates/updates/pallas_call | solution.py:420
  97.4 5.2 %all-to-all-done.3.picked_ref = bf16[32,4,16,256]{3,2,1,0:T(8,128)(2,1)S(1)} async-done(((bf16[32,4,16,256]{3,2,1,0:T(8,128)(2,1)}), bf16[32,4,16,256]{3,2,1,0:T(8,128)(2,1)S(1)}, u32[]{:S(2)}, u32[]{:S(2)}) %all-to-all-start.3) | async-done | bytes 1048608 | tf_op jit(solution)/shard_map/pick/all_to_all | solution.py:416
  102.6 1.1 %back_project.1 = f32[512,128]{1,0:T(8,128)} custom-call(bf16[256,2048]{1,0:T(8,128)(2,1)S(1)} %copy.18.radon_ref, bf16[32,4,16,256]{3,2,1,0:T(8,128)(2,1)S(1)} %all-to-all-done.3.picked_ref, f32[512,128]{1,0:T(8,128)S(1)} %bitcast.17), custom_call_target="tpu_custom_call" | custom-call | flops 268435456 | bytes 1048576 | tf_op jit(solution)/shard_map/back_project/back_project/pallas_call | solution.py:426
  (59 shorter events, 2.6 us)
Async XLA Ops:
  0.6 11.2 %collective-permute-start = (f32[128,128]{1,0:T(8,128)}, f32[128,128]{1,0:T(8,128)S(1)}, u32[]{:S(2)}, u32[]{:S(2)}) collective-permute-start(f32[128,128]{1,0:T(8,128)} %bitcast.18), channel_id=1, source_target_pairs={{0,4},{4,0},{1,5},{5,1},{2,6},{6,2},{3,7},{7,3},{8,12},{12,8},{9,1... | collective-permute-start | bytes 196616 | tf_op jit(solution)/shard_map/ray_sums/ppermute | solution.py:322
  8.5 3.3 %copy-start.1 = (f32[1,64,2,128]{3,2,1,0:T(2,128)S(1)}, f32[1,64,2,128]{3,2,1,0:T(2,128)}, u32[]{:S(2)}) copy-start(f32[1,64,2,128]{3,2,1,0:T(2,128)} %param.15) | copy-start | bytes 196612
  8.5 3.3 %copy-start.2 = (f32[1,64,2,128]{3,2,1,0:T(2,128)S(1)}, f32[1,64,2,128]{3,2,1,0:T(2,128)}, u32[]{:S(2)}) copy-start(f32[1,64,2,128]{3,2,1,0:T(2,128)} %param.16) | copy-start | bytes 196612
  13.1 11.6 %collective-permute-start.1 = (f32[296,128]{1,0:T(8,128)S(1)}, f32[296,128]{1,0:T(8,128)S(1)}, u32[]{:S(2)}, u32[]{:S(2)}) collective-permute-start(f32[296,128]{1,0:T(8,128)S(1)} %get-tuple-element.33), channel_id=1, source_target_pairs={{0,1},{1,2},{2,3},{3,0},{4,5},{5,6},{6,7},{7,4},{8,9},{9,10},{10,1... | collective-permute-start | bytes 454664 | tf_op jit(solution)/shard_map/fields/ppermute | solution.py:322
  14.5 10.2 %collective-permute-start.2 = (f32[296,128]{1,0:T(8,128)S(1)}, f32[296,128]{1,0:T(8,128)S(1)}, u32[]{:S(2)}, u32[]{:S(2)}) collective-permute-start(f32[296,128]{1,0:T(8,128)S(1)} %get-tuple-element.34), channel_id=1, source_target_pairs={{0,2},{1,3},{2,0},{3,1},{4,6},{5,7},{6,4},{7,5},{8,10},{9,11},{10,... | collective-permute-start | bytes 454664 | tf_op jit(solution)/shard_map/fields/ppermute | solution.py:322
  17.1 7.6 %copy-start.8 = (f32[1,8,128,128]{3,2,1,0:T(8,128)S(1)}, f32[1,8,128,128]{3,2,1,0:T(8,128)}, u32[]{:S(2)}) copy-start(f32[1,8,128,128]{3,2,1,0:T(8,128)} %param.12) | copy-start | bytes 1572868
  17.1 7.6 %copy-start.9 = (f32[2,128,128]{2,1,0:T(8,128)S(1)}, f32[2,128,128]{2,1,0:T(8,128)}, u32[]{:S(2)}) copy-start(f32[2,128,128]{2,1,0:T(8,128)} %probe_ref.1) | copy-start | bytes 393220
  17.1 7.6 %copy-start.11 = (bf16[256,256]{1,0:T(8,128)(2,1)S(1)}, bf16[256,256]{1,0:T(8,128)(2,1)}, u32[]{:S(2)}) copy-start(bf16[256,256]{1,0:T(8,128)(2,1)} %constant.24.clone.bl_ref) | copy-start | bytes 393220
  17.1 7.6 %copy-start.12 = (bf16[256,256]{1,0:T(8,128)(2,1)S(1)}, bf16[256,256]{1,0:T(8,128)(2,1)}, u32[]{:S(2)}) copy-start(bf16[256,256]{1,0:T(8,128)(2,1)} %constant.23.clone.bh_ref) | copy-start | bytes 393220
  17.1 7.6 %copy-start.13 = (bf16[256,256]{1,0:T(8,128)(2,1)S(1)}, bf16[256,256]{1,0:T(8,128)(2,1)}, u32[]{:S(2)}) copy-start(bf16[256,256]{1,0:T(8,128)(2,1)} %constant.22.clone.al_ref) | copy-start | bytes 393220
  17.1 7.6 %collective-permute-start.3 = (f32[296,128]{1,0:T(8,128)S(1)}, f32[296,128]{1,0:T(8,128)S(1)}, u32[]{:S(2)}, u32[]{:S(2)}) collective-permute-start(f32[296,128]{1,0:T(8,128)S(1)} %get-tuple-element.35), channel_id=1, source_target_pairs={{0,3},{1,0},{2,1},{3,2},{4,7},{5,4},{6,5},{7,6},{8,11},{9,8},{10,9... | collective-permute-start | bytes 454664 | tf_op jit(solution)/shard_map/fields/ppermute | solution.py:322
  18.3 25.9 %all-to-all-start = ((bf16[32,4,16,256]{3,2,1,0:T(8,128)(2,1)}), bf16[32,4,16,256]{3,2,1,0:T(8,128)(2,1)S(1)}, u32[]{:S(2)}, u32[]{:S(2)}) async-start(bf16[32,4,16,256]{3,2,1,0:T(8,128)(2,1)} %ray_sums.1), calls=%async_computation | async-start | bytes 2097152 | tf_op jit(solution)/shard_map/ray_sums/all_to_all | solution.py:356
  25.3 0.9 copy-start.14
  30.9 7.2 %collective-permute-start.6 = (s32[4,32]{1,0:T(4,128)S(1)}, s32[4,32]{1,0:T(4,128)S(1)}, u32[]{:S(2)}, u32[]{:S(2)}) collective-permute-start(s32[4,32]{1,0:T(4,128)S(1)} %maximum_convert_fusion), channel_id=1, source_target_pairs={{0,192},{64,0},{128,64},{192,128},{1,193},{65,1},{129,65},{193,129... | collective-permute-start | bytes 1544 | tf_op jit(solution)/shard_map/targets/ppermute | solution.py:322
  33.1 6.2 %collective-permute-start.5 = (s32[4,32]{1,0:T(4,128)S(1)}, s32[4,32]{1,0:T(4,128)S(1)}, u32[]{:S(2)}, u32[]{:S(2)}) collective-permute-start(s32[4,32]{1,0:T(4,128)S(1)} %maximum_convert_fusion), channel_id=1, source_target_pairs={{0,128},{64,192},{128,0},{192,64},{1,129},{65,193},{129,1},{193,65... | collective-permute-start | bytes 1544 | tf_op jit(solution)/shard_map/targets/ppermute | solution.py:322
  33.1 6.2 %collective-permute-start.4 = (s32[4,32]{1,0:T(4,128)S(1)}, s32[4,32]{1,0:T(4,128)S(1)}, u32[]{:S(2)}, u32[]{:S(2)}) collective-permute-start(s32[4,32]{1,0:T(4,128)S(1)} %maximum_convert_fusion), channel_id=1, source_target_pairs={{0,64},{64,128},{128,192},{192,0},{1,65},{65,129},{129,193},{193,1... | collective-permute-start | bytes 1544 | tf_op jit(solution)/shard_map/targets/ppermute | solution.py:322
  34.3 8.1 %collective-permute-start.7 = (bf16[2,128,128]{2,1,0:T(8,128)(2,1)S(1)}, bf16[2,128,128]{2,1,0:T(8,128)(2,1)S(1)}, u32[]{:S(2)}, u32[]{:S(2)}) collective-permute-start(bf16[2,128,128]{2,1,0:T(8,128)(2,1)S(1)} %get-tuple-element.42), channel_id=1, source_target_pairs={{0,1},{1,2},{2,3},{3,0},{4,5},{5,6},{6,7},{7,4},{8,9},{9,10},{10,1... | collective-permute-start | bytes 196616 | tf_op jit(solution)/shard_map/frames/ppermute | solution.py:322
  35.7 8.5 %collective-permute-start.8 = (bf16[2,128,128]{2,1,0:T(8,128)(2,1)S(1)}, bf16[2,128,128]{2,1,0:T(8,128)(2,1)S(1)}, u32[]{:S(2)}, u32[]{:S(2)}) collective-permute-start(bf16[2,128,128]{2,1,0:T(8,128)(2,1)S(1)} %get-tuple-element.43), channel_id=1, source_target_pairs={{0,2},{1,3},{2,0},{3,1},{4,6},{5,7},{6,4},{7,5},{8,10},{9,11},{10,... | collective-permute-start | bytes 196616 | tf_op jit(solution)/shard_map/frames/ppermute | solution.py:322
  38.1 6.1 %collective-permute-start.9 = (bf16[2,128,128]{2,1,0:T(8,128)(2,1)S(1)}, bf16[2,128,128]{2,1,0:T(8,128)(2,1)S(1)}, u32[]{:S(2)}, u32[]{:S(2)}) collective-permute-start(bf16[2,128,128]{2,1,0:T(8,128)(2,1)S(1)} %get-tuple-element.44), channel_id=1, source_target_pairs={{0,3},{1,0},{2,1},{3,2},{4,7},{5,4},{6,5},{7,6},{8,11},{9,8},{10,9... | collective-permute-start | bytes 196616 | tf_op jit(solution)/shard_map/frames/ppermute | solution.py:322
  63.1 12.7 %all-to-all-start.2 = ((bf16[8,128,128]{2,1,0:T(8,128)(2,1)}), bf16[8,128,128]{2,1,0:T(8,128)(2,1)S(1)}, u32[]{:S(2)}, u32[]{:S(2)}) async-start(bf16[8,128,128]{2,1,0:T(8,128)(2,1)} %get-tuple-element.47), calls=%async_computation.2 | async-start | bytes 524288 | tf_op jit(solution)/shard_map/residual/all_to_all | solution.py:404
  66.5 11.3 %collective-permute-start.10 = (f32[2,3,16,128]{3,2,1,0:T(8,128)S(1)}, f32[2,3,16,128]{3,2,1,0:T(8,128)S(1)}, u32[]{:S(2)}, u32[]{:S(2)}) collective-permute-start(f32[2,3,16,128]{3,2,1,0:T(8,128)S(1)} %get-tuple-element.49), channel_id=1, source_target_pairs={{0,1},{1,2},{2,3},{3,0},{4,5},{5,6},{6,7},{7,4},{8,9},{9,10},{10,1... | collective-permute-start | bytes 147464 | tf_op jit(solution)/shard_map/residual/ppermute | solution.py:322
  67.1 10.8 %collective-permute-start.11 = (f32[2,3,16,128]{3,2,1,0:T(8,128)S(1)}, f32[2,3,16,128]{3,2,1,0:T(8,128)S(1)}, u32[]{:S(2)}, u32[]{:S(2)}) collective-permute-start(f32[2,3,16,128]{3,2,1,0:T(8,128)S(1)} %get-tuple-element.50), channel_id=1, source_target_pairs={{0,2},{1,3},{2,0},{3,1},{4,6},{5,7},{6,4},{7,5},{8,10},{9,11},{10,... | collective-permute-start | bytes 147464 | tf_op jit(solution)/shard_map/residual/ppermute | solution.py:322
  68.7 9.2 %collective-permute-start.12 = (f32[2,3,16,128]{3,2,1,0:T(8,128)S(1)}, f32[2,3,16,128]{3,2,1,0:T(8,128)S(1)}, u32[]{:S(2)}, u32[]{:S(2)}) collective-permute-start(f32[2,3,16,128]{3,2,1,0:T(8,128)S(1)} %get-tuple-element.51), channel_id=1, source_target_pairs={{0,3},{1,0},{2,1},{3,2},{4,7},{5,4},{6,5},{7,6},{8,11},{9,8},{10,9... | collective-permute-start | bytes 147464 | tf_op jit(solution)/shard_map/residual/ppermute | solution.py:322
  77.8 8.4 %copy-start.3 = (f32[2,3,16,128]{3,2,1,0:T(8,128)}, f32[2,3,16,128]{3,2,1,0:T(8,128)S(1)}, u32[]{:S(2)}) copy-start(f32[2,3,16,128]{3,2,1,0:T(8,128)S(1)} %collective-permute-done.10.one_ref) | copy-start | bytes 147460
  77.8 8.4 %copy-start.5 = (f32[2,3,16,128]{3,2,1,0:T(8,128)}, f32[2,3,16,128]{3,2,1,0:T(8,128)S(1)}, u32[]{:S(2)}) copy-start(f32[2,3,16,128]{3,2,1,0:T(8,128)S(1)} %collective-permute-done.11.two_ref) | copy-start | bytes 147460
  77.9 9.9 %copy-start.15 = (bf16[1,32,2,32,256]{4,3,2,1,0:T(8,128)(2,1)S(1)}, bf16[1,32,2,32,256]{4,3,2,1,0:T(8,128)(2,1)}, u32[]{:S(2)}) copy-start(bf16[1,32,2,32,256]{4,3,2,1,0:T(8,128)(2,1)} %param.18) | copy-start | bytes 3145732
  77.9 24.7 %all-to-all-start.3 = ((bf16[32,4,16,256]{3,2,1,0:T(8,128)(2,1)}), bf16[32,4,16,256]{3,2,1,0:T(8,128)(2,1)S(1)}, u32[]{:S(2)}, u32[]{:S(2)}) async-start(bf16[32,4,16,256]{3,2,1,0:T(8,128)(2,1)} %pick_tiles.1), calls=%async_computation.3 | async-start | bytes 2097152 | tf_op jit(solution)/shard_map/pick/all_to_all | solution.py:416
  86.3 0.7 slice-start.1
  87.0 9.1 %collective-permute-start.13 = (f32[4,3,16,128]{3,2,1,0:T(8,128)S(1)}, f32[4,3,16,128]{3,2,1,0:T(8,128)S(1)}, u32[]{:S(2)}, u32[]{:S(2)}) collective-permute-start(f32[4,3,16,128]{3,2,1,0:T(8,128)S(1)} %pad_maximum_fusion), channel_id=1, source_target_pairs={{0,4},{4,0},{1,5},{5,1},{2,6},{6,2},{3,7},{7,3},{8,12},{12,8},{9,1... | collective-permute-start | bytes 294920 | tf_op jit(solution)/shard_map/updates/ppermute | solution.py:322
  88.9 7.2 %copy-start.4 = (f32[2,3,16,128]{3,2,1,0:T(8,128)S(1)}, f32[2,3,16,128]{3,2,1,0:T(8,128)}, u32[]{:S(2)}) copy-start(f32[2,3,16,128]{3,2,1,0:T(8,128)} %copy-done.3) | copy-start | bytes 147460
  88.9 7.2 %copy-start.6 = (f32[2,3,16,128]{3,2,1,0:T(8,128)S(1)}, f32[2,3,16,128]{3,2,1,0:T(8,128)}, u32[]{:S(2)}) copy-start(f32[2,3,16,128]{3,2,1,0:T(8,128)} %copy-done.5) | copy-start | bytes 147460
  90.4 12.1 %copy-start = (f32[256,2,128]{2,1,0:T(2,128)S(1)}, f32[256,2,128]{2,1,0:T(2,128)}, u32[]{:S(2)}) copy-start(f32[256,2,128]{2,1,0:T(2,128)} %param.17) | copy-start | bytes 786436
  (3 other events, 2.1 us)

commit v9 on v8

--- a/solution.py
+++ b/solution.py
@@ -94,8 +94,8 @@
 
 def first_rows(place_ref, target_ref):
     zl_here = place_ref[2]
-    back_y = [lax.rem(place_ref[1] + Y - y, Y) for y in range(Y)]
-    back_zl = [lax.rem(zl_here + ZL - zl, ZL) * Y for zl in range(ZL)]
+    back_y = [lax.rem(place_ref[1] + Y - y, Y) * ZL for y in range(Y)]
+    back_zl = [lax.rem(zl_here + ZL - zl, ZL) for zl in range(ZL)]
 
     def row(zl, y, xc):
         return pl.multiple_of(target_ref[back_y[y] + back_zl[zl], zl_here * XC + xc] * QR, QR)
@@ -132,21 +132,24 @@
             out_ref[zh * ZL + zl] = total[zl, :, zh * NZ : (zh + 1) * NZ].astype(bf16)
 
 
-def residual_part(place_ref, sums_ref, inter_ref, residual_ref, own_ref, one_ref, two_ref, three_ref, joint):
-    zh = place_ref[0]
-    y = place_ref[1]
+def residual_part(sums_ref, residual_ref, joint_ref):
     total = sums_ref[0].astype(f32)
     for source in range(1, DEEP):
         total = total + sums_ref[source].astype(f32)
-    joint[...] = total
+    joint_ref[...] = total
     residual = (keep * total).astype(bf16)
     for copy in range(DEEP):
         residual_ref[copy] = residual
+
+
+def share_out(place_ref, joint_ref, inter_ref, own_ref, one_ref, two_ref, three_ref):
+    zh = place_ref[0]
+    y = place_ref[1]
     for ahead, ref in enumerate((own_ref, one_ref, two_ref, three_ref)):
         for other in range(ZH):
             owner = lax.rem(zh + other, ZH) * Y + lax.rem(y + ahead, Y)
             rows = pl.ds(pl.multiple_of(owner * 2 * QR, 2 * QR), 2 * QR)
-            ref[other, 0] = joint[rows, :]
+            ref[other, 0] = joint_ref[rows, :]
             for part in range(2):
                 ref[other, 1 + part] = inter_ref[part, rows, :]
 
@@ -227,13 +230,11 @@
 
 def pack(place_ref, object_ref, theirs_ref, dual_ref, target_ref, own_ref, one_ref, two_ref, three_ref, both):
     y = place_ref[1]
-    targets = target_ref[...].astype(f32)
     both[...] = object_ref[...] + dual_ref[...]
     for ahead, ref in enumerate((own_ref, one_ref, two_ref, three_ref)):
         ref[0:128, :] = object_ref[...]
         ref[128:256, :] = theirs_ref[...]
-        ref[FIELD_ROWS + DRIFT_ROWS :, :] = jnp.zeros((QR, NZ), f32)
-        ref[FIELD_ROWS + DRIFT_ROWS : FIELD_ROWS + DRIFT_ROWS + 1, : ZL * XC] = targets
+        ref[FIELD_ROWS + DRIFT_ROWS :, :] = target_ref[...]
         for part in range(2):
             for tile in range(2):
                 start = (tile * RAYS + lax.rem(y + ahead, Y) * QR) * 2 + part
@@ -355,11 +356,16 @@
         )(radon, volume_rows)
         near_sums = lax.all_to_all(sums, CROSS, 0, 0, tiled=True)
 
+    with jax.named_scope("targets"):
+        own_targets, sums = lax.optimization_barrier((tile_range.reshape(1, ZL * XC), sums))
+        targets = jnp.concatenate([own_targets] + [shifted(own_targets, "zl", ZL, k) for k in range(1, ZL)])
+        targets = jnp.pad(targets.astype(f32), ((0, QR - ZL), (0, NZ - ZL * XC)))
+
     with jax.named_scope("fields"):
-        object_theirs, sums = lax.optimization_barrier((object_theirs, sums))
+        object_theirs, sums, targets = lax.optimization_barrier((object_theirs, sums, targets))
         packed = call(
             pack, (shape(SENT_ROWS, NZ),) * Y, 1, 4, scratch=[pltpu.VMEM((128, NZ), f32)], flops=1_000_000
-        )(place, object_rows, object_theirs, dual_rows, tile_range.reshape(1, ZL * XC))
+        )(place, object_rows, object_theirs, dual_rows, targets)
         fields = round_y(packed)
 
     with jax.named_scope("frames"):
@@ -371,14 +377,11 @@
             scratch=[pltpu.VMEM((NDET, NZ), f32)] * 4,
             flops=FRAMES_COST,
         )(place, positions, *fields, probe_field, measured[0], ah, al, bh, bl)
+        inter_parts = round_y(inter_parts)
 
     with jax.named_scope("targets"):
-        tables = jnp.concatenate([field[FIELD_ROWS + DRIFT_ROWS :][:1, : ZL * XC] for field in fields])
-        tables, inter_parts = lax.optimization_barrier((tables.astype(jnp.int32), inter_parts))
-        tables = jnp.concatenate([tables] + [shifted(tables, "zl", ZL, k) for k in range(1, ZL)])
-
-    with jax.named_scope("frames"):
-        inter_parts = round_y(inter_parts)
+        base = FIELD_ROWS + DRIFT_ROWS
+        tables = jnp.concatenate([field[base : base + ZL, : ZL * XC] for field in fields]).astype(jnp.int32)
 
     with jax.named_scope("near_sum"):
         dense, inter = call(
@@ -392,16 +395,12 @@
         far_sums = lax.all_to_all(dense, ALONG, 0, 0, tiled=True)
 
     with jax.named_scope("residual"):
-        copies, *kept = call(
-            residual_part,
-            (shape(DEEP, 128, NZ, dtype=bf16),) + (shape(ZH, 3, 2 * QR, NZ),) * Y,
-            1,
-            2,
-            scratch=[pltpu.VMEM((128, NZ), f32)],
-            flops=1_000_000,
-        )(place, far_sums, inter)
+        copies, joint = call(
+            residual_part, (shape(DEEP, 128, NZ, dtype=bf16), shape(128, NZ)), 0, 1, flops=1_000_000
+        )(far_sums)
+        residuals = lax.all_to_all(copies, ALONG, 0, 0, tiled=True)
+        kept = call(share_out, (shape(ZH, 3, 2 * QR, NZ),) * Y, 1, 2, flops=1_000_000)(place, joint, inter)
         kept = round_y(kept)
-        residuals = lax.all_to_all(copies, ALONG, 0, 0, tiled=True)
 
     with jax.named_scope("pick"):
         picked = call(

time: 104 us -> 110 us (1.058)
  waiting for transfers between devices: 21 us -> 23.9 us
  starting transfers between devices: 44.3 us -> 46.2 us
  blocking collectives: 16.2 us -> 17.4 us
    ppermute x14, waiting for transfers between devices: 10.6 us -> 15.3 us  [shifted(): lax.ppermute(value, axis, [(i, (i + step) % length) for i in range(length)])]
    all_to_all x1, starting transfers between devices: 6.37 us -> 7.92 us  [body(): near_sums = lax.all_to_all(sums, CROSS, 0, 0, tiled=True)]
    all_to_all x1, waiting for transfers between devices: 5.16 us -> 3.64 us  [body(): returned = lax.all_to_all(picked, CROSS, 0, 0, tiled=True)]
    all_to_all x1, blocking collectives: 16.2 us -> 17.4 us  [body(): far_sums = lax.all_to_all(dense, ALONG, 0, 0, tiled=True)]
  transfers between devices with their start and end apart: 17 -> 17, of which waited for: 5 -> 6; matrix products, arithmetic and copies ran while one was open for 3% -> 2% of each run, Pallas kernels for 11% -> 8%
where the time goes in v9:
time: 110 us
  starting transfers between devices  46.2 us (42%)
  waiting for transfers between devices  23.9 us (22%)
  blocking collectives  17.4 us (16%)
  Pallas kernels  15.7 us (14%)
  local copies, waits for them, and re-layouts  5.54 us (5%)
    ppermute x14, starting transfers between devices, shifted(): lax.ppermute(value, axis, [(i, (i + step) % length) for i in range(length)])  26.1 us
    all_to_all x1, blocking collectives, body(): far_sums = lax.all_to_all(dense, ALONG, 0, 0, tiled=True)  17.4 us
    ppermute x14, waiting for transfers between devices, shifted(): lax.ppermute(value, axis, [(i, (i + step) % length) for i in range(length)])  15.3 us
    all_to_all x1, starting transfers between devices, body(): returned = lax.all_to_all(picked, CROSS, 0, 0, tiled=True)  8.74 us
    all_to_all x1, starting transfers between devices, body(): near_sums = lax.all_to_all(sums, CROSS, 0, 0, tiled=True)  7.92 us
    all_to_all x1, waiting for transfers between devices, body(): residuals = lax.all_to_all(copies, ALONG, 0, 0, tiled=True)  4.9 us
    pallas_call x1, Pallas kernels, body(): call(frame_gradients, (shape(2, 128, NZ),) + (shape(2, 128, NZ, dtype=bf1...  4.64 us
    all_to_all x1, waiting for transfers between devices, body(): returned = lax.all_to_all(picked, CROSS, 0, 0, tiled=True)  3.64 us
  transfers between devices with their start and end apart: 17, of which 6 were waited for; matrix products, arithmetic and copies ran while one was open for 2% of the time, Pallas kernels for 8%

profile of v9, /device:TPU:1, one launch (start us, length us, event | category | flops | bytes accessed | tf_op | source)
XLA Modules:
  0.0 109.8 jit_solution(6822745876950366214)
XLA Ops:
  0.7 3.3 %ray_sums.1 = bf16[32,4,16,256]{3,2,1,0:T(8,128)(2,1)} custom-call(bf16[32,2,32,256]{3,2,1,0:T(8,128)(2,1)} %bitcast.24, f32[512,128]{1,0:T(8,128)} %bitcast.16), custom_call_target="tpu_custom_call" | custom-call | flops 268435456 | bytes 1048576 | tf_op jit(solution)/shard_map/ray_sums/ray_sums/pallas_call | solution.py:347
  4.6 5.2 %collective-permute-start.3 = (s32[1,32]{1,0:T(1,128)S(1)}, s32[1,32]{1,0:T(1,128)S(1)}, u32[]{:S(2)}, u32[]{:S(2)}) collective-permute-start(s32[1,32]{1,0:T(1,128)S(1)} %bitcast.28), channel_id=1, source_target_pairs={{0,192},{64,0},{128,64},{192,128},{1,193},{65,1},{129,65},{193,129... | collective-permute-start | bytes 392 | tf_op jit(solution)/shard_map/targets/ppermute | solution.py:323
  10.1 4.9 %collective-permute-start = (f32[128,128]{1,0:T(8,128)S(1)}, f32[128,128]{1,0:T(8,128)S(1)}, u32[]{:S(2)}, u32[]{:S(2)}) collective-permute-start(f32[128,128]{1,0:T(8,128)S(1)} %bitcast.18), channel_id=1, source_target_pairs={{0,4},{4,0},{1,5},{5,1},{2,6},{6,2},{3,7},{7,3},{8,12},{12,8},{9,1... | collective-permute-start | bytes 196616 | tf_op jit(solution)/shard_map/ray_sums/ppermute | solution.py:323
  15.1 2.0 %collective-permute-done.theirs_ref = f32[128,128]{1,0:T(8,128)S(1)} collective-permute-done((f32[128,128]{1,0:T(8,128)S(1)}, f32[128,128]{1,0:T(8,128)S(1)}, u32[]{:S(2)}, u32[]{:S(2)}) %collective-permute-start) | collective-permute-done | bytes 65568 | tf_op jit(solution)/shard_map/ray_sums/ppermute | solution.py:323
  17.8 1.4 %collective-permute-start.4 = (f32[296,128]{1,0:T(8,128)S(1)}, f32[296,128]{1,0:T(8,128)S(1)}, u32[]{:S(2)}, u32[]{:S(2)}) collective-permute-start(f32[296,128]{1,0:T(8,128)S(1)} %get-tuple-element.33), channel_id=1, source_target_pairs={{0,1},{1,2},{2,3},{3,0},{4,5},{5,6},{6,7},{7,4},{8,9},{9,10},{10,1... | collective-permute-start | bytes 454664 | tf_op jit(solution)/shard_map/fields/ppermute | solution.py:323
  19.2 2.6 %collective-permute-start.5 = (f32[296,128]{1,0:T(8,128)S(1)}, f32[296,128]{1,0:T(8,128)S(1)}, u32[]{:S(2)}, u32[]{:S(2)}) collective-permute-start(f32[296,128]{1,0:T(8,128)S(1)} %get-tuple-element.34), channel_id=1, source_target_pairs={{0,2},{1,3},{2,0},{3,1},{4,6},{5,7},{6,4},{7,5},{8,10},{9,11},{10,... | collective-permute-start | bytes 454664 | tf_op jit(solution)/shard_map/fields/ppermute | solution.py:323
  21.8 1.1 %collective-permute-start.6 = (f32[296,128]{1,0:T(8,128)S(1)}, f32[296,128]{1,0:T(8,128)S(1)}, u32[]{:S(2)}, u32[]{:S(2)}) collective-permute-start(f32[296,128]{1,0:T(8,128)S(1)} %get-tuple-element.35), channel_id=1, source_target_pairs={{0,3},{1,0},{2,1},{3,2},{4,7},{5,4},{6,5},{7,6},{8,11},{9,8},{10,9... | collective-permute-start | bytes 454664 | tf_op jit(solution)/shard_map/fields/ppermute | solution.py:323
  22.9 7.9 %all-to-all-start = ((bf16[32,4,16,256]{3,2,1,0:T(8,128)(2,1)}), bf16[32,4,16,256]{3,2,1,0:T(8,128)(2,1)S(1)}, u32[]{:S(2)}, u32[]{:S(2)}) async-start(bf16[32,4,16,256]{3,2,1,0:T(8,128)(2,1)} %ray_sums.1), calls=%async_computation | async-start | bytes 2097152 | tf_op jit(solution)/shard_map/ray_sums/all_to_all | solution.py:357
  31.5 0.9 copy-done.13
  32.4 4.6 %frame_gradients.1 = (f32[2,128,128]{2,1,0:T(8,128)S(1)}, bf16[2,128,128]{2,1,0:T(8,128)(2,1)S(1)}, bf16[2,128,128]{2,1,0:T(8,128)(2,1)S(1)}, bf16[2,128,128]{2,1,0:T(8,128)(2,1)S(1)}) custom-call(s32[3]{0:T(128)S(1)} %pad_add_fusion.place_ref, s32[1,8]{1,0:T(1,128)S(1)} %copy-done.9, f32[296,128]{1,0:T(8,128)S(1)} %get-tuple-element.32.field_0, ...), custom_call_target="tpu_custom_call" | custom-call | flops 20000000000 | bytes 1048576 | tf_op jit(solution)/shard_map/frames/frame_gradients/pallas_call | solution.py:372
  37.1 1.5 %collective-permute-start.7 = (bf16[2,128,128]{2,1,0:T(8,128)(2,1)S(1)}, bf16[2,128,128]{2,1,0:T(8,128)(2,1)S(1)}, u32[]{:S(2)}, u32[]{:S(2)}) collective-permute-start(bf16[2,128,128]{2,1,0:T(8,128)(2,1)S(1)} %get-tuple-element.37), channel_id=1, source_target_pairs={{0,1},{1,2},{2,3},{3,0},{4,5},{5,6},{6,7},{7,4},{8,9},{9,10},{10,1... | collective-permute-start | bytes 196616 | tf_op jit(solution)/shard_map/frames/ppermute | solution.py:323
  38.6 2.4 %collective-permute-start.8 = (bf16[2,128,128]{2,1,0:T(8,128)(2,1)S(1)}, bf16[2,128,128]{2,1,0:T(8,128)(2,1)S(1)}, u32[]{:S(2)}, u32[]{:S(2)}) collective-permute-start(bf16[2,128,128]{2,1,0:T(8,128)(2,1)S(1)} %get-tuple-element.38), channel_id=1, source_target_pairs={{0,2},{1,3},{2,0},{3,1},{4,6},{5,7},{6,4},{7,5},{8,10},{9,11},{10,... | collective-permute-start | bytes 196616 | tf_op jit(solution)/shard_map/frames/ppermute | solution.py:323
  41.0 1.2 %collective-permute-start.9 = (bf16[2,128,128]{2,1,0:T(8,128)(2,1)S(1)}, bf16[2,128,128]{2,1,0:T(8,128)(2,1)S(1)}, u32[]{:S(2)}, u32[]{:S(2)}) collective-permute-start(bf16[2,128,128]{2,1,0:T(8,128)(2,1)S(1)} %get-tuple-element.39), channel_id=1, source_target_pairs={{0,3},{1,0},{2,1},{3,2},{4,7},{5,4},{6,5},{7,6},{8,11},{9,8},{10,9... | collective-permute-start | bytes 196616 | tf_op jit(solution)/shard_map/frames/ppermute | solution.py:323
  42.2 2.7 %collective-permute-done.7.inter_1 = bf16[2,128,128]{2,1,0:T(8,128)(2,1)S(1)} collective-permute-done((bf16[2,128,128]{2,1,0:T(8,128)(2,1)S(1)}, bf16[2,128,128]{2,1,0:T(8,128)(2,1)S(1)}, u32[]{:S(2)}, u32[]{:S(2)}) %collective-permute-start.7) | collective-permute-done | bytes 65568 | tf_op jit(solution)/shard_map/frames/ppermute | solution.py:323
  44.9 4.2 %collective-permute-done.8.inter_2 = bf16[2,128,128]{2,1,0:T(8,128)(2,1)S(1)} collective-permute-done((bf16[2,128,128]{2,1,0:T(8,128)(2,1)S(1)}, bf16[2,128,128]{2,1,0:T(8,128)(2,1)S(1)}, u32[]{:S(2)}, u32[]{:S(2)}) %collective-permute-start.8) | collective-permute-done | bytes 65568 | tf_op jit(solution)/shard_map/frames/ppermute | solution.py:323
  49.1 1.5 %add_tiles.1 = (bf16[8,128,128]{2,1,0:T(8,128)(2,1)S(1)}, f32[2,128,128]{2,1,0:T(8,128)S(1)}) custom-call(s32[3]{0:T(128)S(1)} %pad_add_fusion.place_ref, s32[16,32]{1,0:T(8,128)S(1)} %maximum_convert_fusion.target_ref, bf16[32,4,16,256]{3,2,1,0:T(8,128)(2,1)S(1)} %all-to-all-done.sums_ref, f32[2,128,128]{2,1,0:T(8,128)S(1)} %get-tuple-element.36.inter_0, ...), custom_call_target="tpu_custom_call" | custom-call | flops 1000000 | bytes 1048576 | tf_op jit(solution)/shard_map/near_sum/add_tiles/pallas_call | solution.py:387
  50.5 17.4 %all_to_all.20.sums_ref = bf16[8,128,128]{2,1,0:T(8,128)(2,1)S(1)} all-to-all(bf16[8,128,128]{2,1,0:T(8,128)(2,1)S(1)} %get-tuple-element.40), channel_id=1, replica_groups=mesh['zl'=4,'x'=4,'c'=2,'zh'=2,'y'=4] {'zh','zl'}, dimensions={0} | all-to-all | bytes 524288 | tf_op jit(solution)/shard_map/near_sum/all_to_all | solution.py:395
  68.0 0.8 residual_part.1
  68.7 3.4 %all-to-all-start.2 = ((bf16[8,128,128]{2,1,0:T(8,128)(2,1)}), bf16[8,128,128]{2,1,0:T(8,128)(2,1)S(1)}, u32[]{:S(2)}, u32[]{:S(2)}) async-start(bf16[8,128,128]{2,1,0:T(8,128)(2,1)} %get-tuple-element.41), calls=%async_computation.2 | async-start | bytes 524288 | tf_op jit(solution)/shard_map/residual/all_to_all | solution.py:401
  72.7 0.8 collective-permute-start.10
  73.5 1.5 %collective-permute-start.11 = (f32[2,3,16,128]{3,2,1,0:T(8,128)S(1)}, f32[2,3,16,128]{3,2,1,0:T(8,128)S(1)}, u32[]{:S(2)}, u32[]{:S(2)}) collective-permute-start(f32[2,3,16,128]{3,2,1,0:T(8,128)S(1)} %get-tuple-element.46), channel_id=1, source_target_pairs={{0,2},{1,3},{2,0},{3,1},{4,6},{5,7},{6,4},{7,5},{8,10},{9,11},{10,... | collective-permute-start | bytes 147464 | tf_op jit(solution)/shard_map/residual/ppermute | solution.py:323
  75.0 1.6 %collective-permute-start.12 = (f32[2,3,16,128]{3,2,1,0:T(8,128)S(1)}, f32[2,3,16,128]{3,2,1,0:T(8,128)S(1)}, u32[]{:S(2)}, u32[]{:S(2)}) collective-permute-start(f32[2,3,16,128]{3,2,1,0:T(8,128)S(1)} %get-tuple-element.47), channel_id=1, source_target_pairs={{0,3},{1,0},{2,1},{3,2},{4,7},{5,4},{6,5},{7,6},{8,11},{9,8},{10,9... | collective-permute-start | bytes 147464 | tf_op jit(solution)/shard_map/residual/ppermute | solution.py:323
  76.6 4.9 %all-to-all-done.2.residual_ref = bf16[8,128,128]{2,1,0:T(8,128)(2,1)S(1)} async-done(((bf16[8,128,128]{2,1,0:T(8,128)(2,1)}), bf16[8,128,128]{2,1,0:T(8,128)(2,1)S(1)}, u32[]{:S(2)}, u32[]{:S(2)}) %all-to-all-start.2) | async-done | bytes 262176 | tf_op jit(solution)/shard_map/residual/all_to_all | solution.py:401
  81.5 2.0 %pick_tiles.1 = bf16[32,4,16,256]{3,2,1,0:T(8,128)(2,1)} custom-call(s32[3]{0:T(128)S(1)} %pad_add_fusion.place_ref, s32[16,32]{1,0:T(8,128)S(1)} %maximum_convert_fusion.target_ref, bf16[8,128,128]{2,1,0:T(8,128)(2,1)S(1)} %all-to-all-done.2.residual_ref), custom_call_target="tpu_custom_call" | custom-call | flops 1000000 | bytes 1048576 | tf_op jit(solution)/shard_map/pick/pick_tiles/pallas_call | solution.py:406
  83.6 8.7 %all-to-all-start.3 = ((bf16[32,4,16,256]{3,2,1,0:T(8,128)(2,1)}), bf16[32,4,16,256]{3,2,1,0:T(8,128)(2,1)S(1)}, u32[]{:S(2)}, u32[]{:S(2)}) async-start(bf16[32,4,16,256]{3,2,1,0:T(8,128)(2,1)} %pick_tiles.1), calls=%async_computation.3 | async-start | bytes 2097152 | tf_op jit(solution)/shard_map/pick/all_to_all | solution.py:415
  93.1 1.6 %collective-permute-start.13 = (f32[4,3,16,128]{3,2,1,0:T(8,128)S(1)}, f32[4,3,16,128]{3,2,1,0:T(8,128)S(1)}, u32[]{:S(2)}, u32[]{:S(2)}) collective-permute-start(f32[4,3,16,128]{3,2,1,0:T(8,128)S(1)} %pad_maximum_fusion), channel_id=1, source_target_pairs={{0,4},{4,0},{1,5},{5,1},{2,6},{6,2},{3,7},{7,3},{8,12},{12,8},{9,1... | collective-permute-start | bytes 294920 | tf_op jit(solution)/shard_map/updates/ppermute | solution.py:323
  94.8 1.1 %copy.17 = bf16[256,8,4,4,2,8]{0,5,4,3,2,1:T(8,128)(2,1)} copy(bf16[256,8,4,4,2,8]{0,5,2,4,1,3:T(8,128)(2,1)S(1)} %bitcast.25) | data formatting | bytes 2097152 | tf_op jit(solution)/shard_map/back_project/transpose | solution.py:424
  95.9 1.5 %copy.18.radon_ref = bf16[256,2048]{1,0:T(8,128)(2,1)S(1)} copy(bf16[256,2048]{0,1:T(8,128)(2,1)} %bitcast.26) | data formatting | bytes 2097152 | tf_op jit(solution)/shard_map/back_project/reshape | solution.py:424
  97.4 6.4 %collective-permute-done.13.theirs_ref = f32[4,3,16,128]{3,2,1,0:T(8,128)S(1)} collective-permute-done((f32[4,3,16,128]{3,2,1,0:T(8,128)S(1)}, f32[4,3,16,128]{3,2,1,0:T(8,128)S(1)}, u32[]{:S(2)}, u32[]{:S(2)}) %collective-permute-start.13) | collective-permute-done | bytes 98336 | tf_op jit(solution)/shard_map/updates/ppermute | solution.py:323
  103.8 1.2 %updates.1 = (f32[128,128]{1,0:T(8,128)}, f32[128,128]{1,0:T(8,128)}) custom-call(s32[3]{0:T(128)S(1)} %pad_add_fusion.place_ref, f32[2,3,16,128]{3,2,1,0:T(8,128)S(1)} %get-tuple-element.48.own_ref, f32[2,3,16,128]{3,2,1,0:T(8,128)S(1)} %copy-done.4, f32[2,3,16,128]{3,2,1,0:T(8,128)S(1)} %copy-done.6, ...), custom_call_target="tpu_custom_call" | custom-call | flops 1000000 | bytes 1048576 | tf_op jit(solution)/shard_map/updates/updates/pallas_call | solution.py:419
  105.0 3.6 %all-to-all-done.3.picked_ref = bf16[32,4,16,256]{3,2,1,0:T(8,128)(2,1)S(1)} async-done(((bf16[32,4,16,256]{3,2,1,0:T(8,128)(2,1)}), bf16[32,4,16,256]{3,2,1,0:T(8,128)(2,1)S(1)}, u32[]{:S(2)}, u32[]{:S(2)}) %all-to-all-start.3) | async-done | bytes 1048608 | tf_op jit(solution)/shard_map/pick/all_to_all | solution.py:415
  108.7 1.1 %back_project.1 = f32[512,128]{1,0:T(8,128)} custom-call(bf16[256,2048]{1,0:T(8,128)(2,1)S(1)} %copy.18.radon_ref, bf16[32,4,16,256]{3,2,1,0:T(8,128)(2,1)S(1)} %all-to-all-done.3.picked_ref, f32[512,128]{1,0:T(8,128)S(1)} %bitcast.17), custom_call_target="tpu_custom_call" | custom-call | flops 268435456 | bytes 1048576 | tf_op jit(solution)/shard_map/back_project/back_project/pallas_call | solution.py:425
  (61 shorter events, 3.6 us)
Async XLA Ops:
  0.6 9.4 %copy-start.1 = (f32[1,64,2,128]{3,2,1,0:T(2,128)S(1)}, f32[1,64,2,128]{3,2,1,0:T(2,128)}, u32[]{:S(2)}) copy-start(f32[1,64,2,128]{3,2,1,0:T(2,128)} %param.15) | copy-start | bytes 196612
  0.6 16.5 %copy-start.2 = (f32[1,64,2,128]{3,2,1,0:T(2,128)S(1)}, f32[1,64,2,128]{3,2,1,0:T(2,128)}, u32[]{:S(2)}) copy-start(f32[1,64,2,128]{3,2,1,0:T(2,128)} %param.16) | copy-start | bytes 196612
  4.6 10.5 %collective-permute-start.3 = (s32[1,32]{1,0:T(1,128)S(1)}, s32[1,32]{1,0:T(1,128)S(1)}, u32[]{:S(2)}, u32[]{:S(2)}) collective-permute-start(s32[1,32]{1,0:T(1,128)S(1)} %bitcast.28), channel_id=1, source_target_pairs={{0,192},{64,0},{128,64},{192,128},{1,193},{65,1},{129,65},{193,129... | collective-permute-start | bytes 392 | tf_op jit(solution)/shard_map/targets/ppermute | solution.py:323
  9.8 5.3 %collective-permute-start.2 = (s32[1,32]{1,0:T(1,128)S(1)}, s32[1,32]{1,0:T(1,128)S(1)}, u32[]{:S(2)}, u32[]{:S(2)}) collective-permute-start(s32[1,32]{1,0:T(1,128)S(1)} %bitcast.29), channel_id=1, source_target_pairs={{0,128},{64,192},{128,0},{192,64},{1,129},{65,193},{129,1},{193,65... | collective-permute-start | bytes 392 | tf_op jit(solution)/shard_map/targets/ppermute | solution.py:323
  9.8 5.3 %collective-permute-start.1 = (s32[1,32]{1,0:T(1,128)S(1)}, s32[1,32]{1,0:T(1,128)S(1)}, u32[]{:S(2)}, u32[]{:S(2)}) collective-permute-start(s32[1,32]{1,0:T(1,128)S(1)} %bitcast.30), channel_id=1, source_target_pairs={{0,64},{64,128},{128,192},{192,0},{1,65},{65,129},{129,193},{193,1... | collective-permute-start | bytes 392 | tf_op jit(solution)/shard_map/targets/ppermute | solution.py:323
  10.1 7.1 %collective-permute-start = (f32[128,128]{1,0:T(8,128)S(1)}, f32[128,128]{1,0:T(8,128)S(1)}, u32[]{:S(2)}, u32[]{:S(2)}) collective-permute-start(f32[128,128]{1,0:T(8,128)S(1)} %bitcast.18), channel_id=1, source_target_pairs={{0,4},{4,0},{1,5},{5,1},{2,6},{6,2},{3,7},{7,3},{8,12},{12,8},{9,1... | collective-permute-start | bytes 196616 | tf_op jit(solution)/shard_map/ray_sums/ppermute | solution.py:323
  17.8 13.1 %collective-permute-start.4 = (f32[296,128]{1,0:T(8,128)S(1)}, f32[296,128]{1,0:T(8,128)S(1)}, u32[]{:S(2)}, u32[]{:S(2)}) collective-permute-start(f32[296,128]{1,0:T(8,128)S(1)} %get-tuple-element.33), channel_id=1, source_target_pairs={{0,1},{1,2},{2,3},{3,0},{4,5},{5,6},{6,7},{7,4},{8,9},{9,10},{10,1... | collective-permute-start | bytes 454664 | tf_op jit(solution)/shard_map/fields/ppermute | solution.py:323
  19.2 11.8 %collective-permute-start.5 = (f32[296,128]{1,0:T(8,128)S(1)}, f32[296,128]{1,0:T(8,128)S(1)}, u32[]{:S(2)}, u32[]{:S(2)}) collective-permute-start(f32[296,128]{1,0:T(8,128)S(1)} %get-tuple-element.34), channel_id=1, source_target_pairs={{0,2},{1,3},{2,0},{3,1},{4,6},{5,7},{6,4},{7,5},{8,10},{9,11},{10,... | collective-permute-start | bytes 454664 | tf_op jit(solution)/shard_map/fields/ppermute | solution.py:323
  21.8 9.2 %copy-start.7 = (f32[1,8,128,128]{3,2,1,0:T(8,128)S(1)}, f32[1,8,128,128]{3,2,1,0:T(8,128)}, u32[]{:S(2)}) copy-start(f32[1,8,128,128]{3,2,1,0:T(8,128)} %param.12) | copy-start | bytes 1572868
  21.8 9.2 %copy-start.8 = (f32[2,128,128]{2,1,0:T(8,128)S(1)}, f32[2,128,128]{2,1,0:T(8,128)}, u32[]{:S(2)}) copy-start(f32[2,128,128]{2,1,0:T(8,128)} %probe_ref.1) | copy-start | bytes 393220
  21.8 9.2 %copy-start.10 = (bf16[256,256]{1,0:T(8,128)(2,1)S(1)}, bf16[256,256]{1,0:T(8,128)(2,1)}, u32[]{:S(2)}) copy-start(bf16[256,256]{1,0:T(8,128)(2,1)} %constant.27.clone.bl_ref) | copy-start | bytes 393220
  21.8 9.2 %copy-start.11 = (bf16[256,256]{1,0:T(8,128)(2,1)S(1)}, bf16[256,256]{1,0:T(8,128)(2,1)}, u32[]{:S(2)}) copy-start(bf16[256,256]{1,0:T(8,128)(2,1)} %constant.26.clone.bh_ref) | copy-start | bytes 393220
  21.8 9.2 %copy-start.12 = (bf16[256,256]{1,0:T(8,128)(2,1)S(1)}, bf16[256,256]{1,0:T(8,128)(2,1)}, u32[]{:S(2)}) copy-start(bf16[256,256]{1,0:T(8,128)(2,1)} %constant.25.clone.al_ref) | copy-start | bytes 393220
  21.8 9.1 %collective-permute-start.6 = (f32[296,128]{1,0:T(8,128)S(1)}, f32[296,128]{1,0:T(8,128)S(1)}, u32[]{:S(2)}, u32[]{:S(2)}) collective-permute-start(f32[296,128]{1,0:T(8,128)S(1)} %get-tuple-element.35), channel_id=1, source_target_pairs={{0,3},{1,0},{2,1},{3,2},{4,7},{5,4},{6,5},{7,6},{8,11},{9,8},{10,9... | collective-permute-start | bytes 454664 | tf_op jit(solution)/shard_map/fields/ppermute | solution.py:323
  22.9 26.1 %all-to-all-start = ((bf16[32,4,16,256]{3,2,1,0:T(8,128)(2,1)}), bf16[32,4,16,256]{3,2,1,0:T(8,128)(2,1)S(1)}, u32[]{:S(2)}, u32[]{:S(2)}) async-start(bf16[32,4,16,256]{3,2,1,0:T(8,128)(2,1)} %ray_sums.1), calls=%async_computation | async-start | bytes 2097152 | tf_op jit(solution)/shard_map/ray_sums/all_to_all | solution.py:357
  31.5 0.9 copy-start.13
  37.1 7.8 %collective-permute-start.7 = (bf16[2,128,128]{2,1,0:T(8,128)(2,1)S(1)}, bf16[2,128,128]{2,1,0:T(8,128)(2,1)S(1)}, u32[]{:S(2)}, u32[]{:S(2)}) collective-permute-start(bf16[2,128,128]{2,1,0:T(8,128)(2,1)S(1)} %get-tuple-element.37), channel_id=1, source_target_pairs={{0,1},{1,2},{2,3},{3,0},{4,5},{5,6},{6,7},{7,4},{8,9},{9,10},{10,1... | collective-permute-start | bytes 196616 | tf_op jit(solution)/shard_map/frames/ppermute | solution.py:323
  38.6 10.5 %collective-permute-start.8 = (bf16[2,128,128]{2,1,0:T(8,128)(2,1)S(1)}, bf16[2,128,128]{2,1,0:T(8,128)(2,1)S(1)}, u32[]{:S(2)}, u32[]{:S(2)}) collective-permute-start(bf16[2,128,128]{2,1,0:T(8,128)(2,1)S(1)} %get-tuple-element.38), channel_id=1, source_target_pairs={{0,2},{1,3},{2,0},{3,1},{4,6},{5,7},{6,4},{7,5},{8,10},{9,11},{10,... | collective-permute-start | bytes 196616 | tf_op jit(solution)/shard_map/frames/ppermute | solution.py:323
  41.0 8.1 %collective-permute-start.9 = (bf16[2,128,128]{2,1,0:T(8,128)(2,1)S(1)}, bf16[2,128,128]{2,1,0:T(8,128)(2,1)S(1)}, u32[]{:S(2)}, u32[]{:S(2)}) collective-permute-start(bf16[2,128,128]{2,1,0:T(8,128)(2,1)S(1)} %get-tuple-element.39), channel_id=1, source_target_pairs={{0,3},{1,0},{2,1},{3,2},{4,7},{5,4},{6,5},{7,6},{8,11},{9,8},{10,9... | collective-permute-start | bytes 196616 | tf_op jit(solution)/shard_map/frames/ppermute | solution.py:323
  68.7 12.8 %all-to-all-start.2 = ((bf16[8,128,128]{2,1,0:T(8,128)(2,1)}), bf16[8,128,128]{2,1,0:T(8,128)(2,1)S(1)}, u32[]{:S(2)}, u32[]{:S(2)}) async-start(bf16[8,128,128]{2,1,0:T(8,128)(2,1)} %get-tuple-element.41), calls=%async_computation.2 | async-start | bytes 524288 | tf_op jit(solution)/shard_map/residual/all_to_all | solution.py:401
  72.7 10.8 %collective-permute-start.10 = (f32[2,3,16,128]{3,2,1,0:T(8,128)S(1)}, f32[2,3,16,128]{3,2,1,0:T(8,128)S(1)}, u32[]{:S(2)}, u32[]{:S(2)}) collective-permute-start(f32[2,3,16,128]{3,2,1,0:T(8,128)S(1)} %get-tuple-element.45), channel_id=1, source_target_pairs={{0,1},{1,2},{2,3},{3,0},{4,5},{5,6},{6,7},{7,4},{8,9},{9,10},{10,1... | collective-permute-start | bytes 147464 | tf_op jit(solution)/shard_map/residual/ppermute | solution.py:323
  73.5 10.1 %collective-permute-start.11 = (f32[2,3,16,128]{3,2,1,0:T(8,128)S(1)}, f32[2,3,16,128]{3,2,1,0:T(8,128)S(1)}, u32[]{:S(2)}, u32[]{:S(2)}) collective-permute-start(f32[2,3,16,128]{3,2,1,0:T(8,128)S(1)} %get-tuple-element.46), channel_id=1, source_target_pairs={{0,2},{1,3},{2,0},{3,1},{4,6},{5,7},{6,4},{7,5},{8,10},{9,11},{10,... | collective-permute-start | bytes 147464 | tf_op jit(solution)/shard_map/residual/ppermute | solution.py:323
  75.0 8.6 %collective-permute-start.12 = (f32[2,3,16,128]{3,2,1,0:T(8,128)S(1)}, f32[2,3,16,128]{3,2,1,0:T(8,128)S(1)}, u32[]{:S(2)}, u32[]{:S(2)}) collective-permute-start(f32[2,3,16,128]{3,2,1,0:T(8,128)S(1)} %get-tuple-element.47), channel_id=1, source_target_pairs={{0,3},{1,0},{2,1},{3,2},{4,7},{5,4},{6,5},{7,6},{8,11},{9,8},{10,9... | collective-permute-start | bytes 147464 | tf_op jit(solution)/shard_map/residual/ppermute | solution.py:323
  83.5 8.8 %copy-start.3 = (f32[2,3,16,128]{3,2,1,0:T(8,128)}, f32[2,3,16,128]{3,2,1,0:T(8,128)S(1)}, u32[]{:S(2)}) copy-start(f32[2,3,16,128]{3,2,1,0:T(8,128)S(1)} %collective-permute-done.10.one_ref) | copy-start | bytes 147460
  83.6 8.8 %copy-start.5 = (f32[2,3,16,128]{3,2,1,0:T(8,128)}, f32[2,3,16,128]{3,2,1,0:T(8,128)S(1)}, u32[]{:S(2)}) copy-start(f32[2,3,16,128]{3,2,1,0:T(8,128)S(1)} %collective-permute-done.11.two_ref) | copy-start | bytes 147460
  83.6 11.2 %copy-start.14 = (bf16[1,32,2,32,256]{4,3,2,1,0:T(8,128)(2,1)S(1)}, bf16[1,32,2,32,256]{4,3,2,1,0:T(8,128)(2,1)}, u32[]{:S(2)}) copy-start(bf16[1,32,2,32,256]{4,3,2,1,0:T(8,128)(2,1)} %param.18) | copy-start | bytes 3145732
  83.6 25.1 %all-to-all-start.3 = ((bf16[32,4,16,256]{3,2,1,0:T(8,128)(2,1)}), bf16[32,4,16,256]{3,2,1,0:T(8,128)(2,1)S(1)}, u32[]{:S(2)}, u32[]{:S(2)}) async-start(bf16[32,4,16,256]{3,2,1,0:T(8,128)(2,1)} %pick_tiles.1), calls=%async_computation.3 | async-start | bytes 2097152 | tf_op jit(solution)/shard_map/pick/all_to_all | solution.py:415
  92.4 0.7 slice-start.1
  93.1 10.6 %collective-permute-start.13 = (f32[4,3,16,128]{3,2,1,0:T(8,128)S(1)}, f32[4,3,16,128]{3,2,1,0:T(8,128)S(1)}, u32[]{:S(2)}, u32[]{:S(2)}) collective-permute-start(f32[4,3,16,128]{3,2,1,0:T(8,128)S(1)} %pad_maximum_fusion), channel_id=1, source_target_pairs={{0,4},{4,0},{1,5},{5,1},{2,6},{6,2},{3,7},{7,3},{8,12},{12,8},{9,1... | collective-permute-start | bytes 294920 | tf_op jit(solution)/shard_map/updates/ppermute | solution.py:323
  95.9 7.9 %copy-start.4 = (f32[2,3,16,128]{3,2,1,0:T(8,128)S(1)}, f32[2,3,16,128]{3,2,1,0:T(8,128)}, u32[]{:S(2)}) copy-start(f32[2,3,16,128]{3,2,1,0:T(8,128)} %copy-done.3) | copy-start | bytes 147460
  95.9 7.9 %copy-start.6 = (f32[2,3,16,128]{3,2,1,0:T(8,128)S(1)}, f32[2,3,16,128]{3,2,1,0:T(8,128)}, u32[]{:S(2)}) copy-start(f32[2,3,16,128]{3,2,1,0:T(8,128)} %copy-done.5) | copy-start | bytes 147460
  97.4 11.3 %copy-start = (f32[256,2,128]{2,1,0:T(2,128)S(1)}, f32[256,2,128]{2,1,0:T(2,128)}, u32[]{:S(2)}) copy-start(f32[256,2,128]{2,1,0:T(2,128)} %param.17) | copy-start | bytes 786436
  (3 other events, 2.1 us)

commit v10 on v9

--- a/solution.py
+++ b/solution.py
@@ -64,13 +64,15 @@
     angles = (k[:, None] * k[None, :] % PROBE) * (2.0 * math.pi / PROBE)
     cosine = np.cos(angles) / math.sqrt(PROBE)
     sine = np.sin(angles) / math.sqrt(PROBE)
-    left = np.block([[cosine, sine], [-sine, cosine]]).astype(np.float32)
-    high = left.astype(jnp.bfloat16)
-    low = (left - high.astype(np.float32)).astype(jnp.bfloat16)
-    return jnp.asarray(high), jnp.asarray(low), jnp.asarray(high.T.copy()), jnp.asarray(low.T.copy())
-
-
-def ray_sums(radon_far, volume_far, out_ref, radon_ref, volume_ref, sems):
+    both = np.stack([cosine, sine]).astype(np.float32)
+    high = both.astype(jnp.bfloat16)
+    low = (both - high.astype(np.float32)).astype(jnp.bfloat16)
+    return jnp.asarray(np.concatenate([high, low]))
+
+
+def ray_sums(radon_far, volume_far, target_far, out_ref, target_out, radon_ref, volume_ref, target_ref, sems):
+    targets = pltpu.make_async_copy(target_far, target_ref, sems.at[ZL + 1])
+    targets.start()
     copies = [pltpu.make_async_copy(volume_far, volume_ref, sems.at[ZL])]
     for zl in range(ZL):
         angles = pl.ds(zl * XC, XC)
@@ -90,27 +92,28 @@
                 low = sums[y * QR : (y + 1) * QR]
                 high = sums[RAYS + y * QR : RAYS + (y + 1) * QR]
                 out_ref[xc * Y + y, zl] = jnp.concatenate([low, high], axis=0).astype(bf16)
-
-
-def first_rows(place_ref, target_ref):
+    targets.wait()
+    target_out[...] = jnp.zeros(target_out.shape, f32)
+    target_out[0:1, : ZL * XC] = target_ref[...].astype(f32)
+
+
+def each_tile(place_ref, tables):
     zl_here = place_ref[2]
-    back_y = [lax.rem(place_ref[1] + Y - y, Y) * ZL for y in range(Y)]
-    back_zl = [lax.rem(zl_here + ZL - zl, ZL) for zl in range(ZL)]
-
-    def row(zl, y, xc):
-        return pl.multiple_of(target_ref[back_y[y] + back_zl[zl], zl_here * XC + xc] * QR, QR)
-
-    return row
+    for back_zl, table in enumerate(tables):
+        zl = lax.rem(zl_here + ZL - back_zl, ZL)
+        for back_y in range(Y):
+            y = lax.rem(place_ref[1] + Y - back_y, Y)
+            for xc in range(XC):
+                yield zl, xc * Y + y, pl.multiple_of(table[back_y, zl_here * XC + xc] * QR, QR)
 
 
 def add_tiles(
-    place_ref, target_ref, sums_ref, inter_0, inter_1, inter_2, inter_3, field_0, field_1, field_2, field_3,
-    out_ref, inter_ref, total,
+    place_ref, table_0, table_1, table_2, table_3, sums_ref, inter_0, inter_1, inter_2, inter_3,
+    field_0, field_1, field_2, field_3, out_ref, inter_ref, total,
 ):
     zh = place_ref[0]
     y_here = place_ref[1]
     zl_here = place_ref[2]
-    row = first_rows(place_ref, target_ref)
     total[...] = jnp.zeros(total.shape, f32)
     for part in range(2):
         inter = (inter_0[part] + inter_1[part].astype(f32)) + (inter_2[part].astype(f32) + inter_3[part].astype(f32))
@@ -123,10 +126,8 @@
         total[zl_here, rows, :] -= jnp.concatenate(
             [field_ref[base : base + 2 * QR, :], field_ref[base + 2 * QR : base + 4 * QR, :]], axis=1
         )
-    for xc in range(XC):
-        for y in range(Y):
-            for zl in range(ZL):
-                total[zl, pl.ds(row(zl, y, xc), HITS * QR), :] += sums_ref[xc * Y + y, zl].astype(f32)
+    for zl, near, row in each_tile(place_ref, (table_0, table_1, table_2, table_3)):
+        total[zl, pl.ds(row, HITS * QR), :] += sums_ref[near, zl].astype(f32)
     for zh in range(ZH):
         for zl in range(ZL):
             out_ref[zh * ZL + zl] = total[zl, :, zh * NZ : (zh + 1) * NZ].astype(bf16)
@@ -154,17 +155,14 @@
                 ref[other, 1 + part] = inter_ref[part, rows, :]
 
 
-def pick_tiles(place_ref, target_ref, residual_ref, out_ref, rows_ref):
+def pick_tiles(place_ref, table_0, table_1, table_2, table_3, residual_ref, out_ref, rows_ref):
     for zl in range(ZL):
         rows_ref[zl] = jnp.concatenate(
             [residual_ref[zl].astype(f32), residual_ref[ZL + zl].astype(f32)], axis=1
         )
 
-    row = first_rows(place_ref, target_ref)
-    for xc in range(XC):
-        for y in range(Y):
-            for zl in range(ZL):
-                out_ref[xc * Y + y, zl] = rows_ref[zl, pl.ds(row(zl, y, xc), HITS * QR), :].astype(bf16)
+    for zl, near, row in each_tile(place_ref, (table_0, table_1, table_2, table_3)):
+        out_ref[near, zl] = rows_ref[zl, pl.ds(row, HITS * QR), :].astype(bf16)
 
 
 def back_project(radon_ref, picked_ref, volume_ref, out_ref):
@@ -205,6 +203,16 @@
     return high, (value - high.astype(f32)).astype(bf16)
 
 
+def complex_blocks(cosine, sine):
+    forward = jnp.concatenate(
+        [jnp.concatenate([cosine, sine], axis=1), jnp.concatenate([-sine, cosine], axis=1)], axis=0
+    )
+    backward = jnp.concatenate(
+        [jnp.concatenate([cosine, -sine], axis=1), jnp.concatenate([sine, cosine], axis=1)], axis=0
+    )
+    return forward, backward
+
+
 def from_left(high_table, low_table, value):
     high, low = split(value)
     return (
@@ -243,8 +251,7 @@
 
 
 def frame_gradients(
-    place_ref, starts_ref, field_0, field_1, field_2, field_3, probe_ref,
-    measured_ref, ah_ref, al_ref, bh_ref, bl_ref, own_ref, sent_one, sent_two, sent_three,
+    place_ref, field_0, field_1, field_2, field_3, probe_ref, measured_ref, dft_ref, own_ref, sent_one, sent_two, sent_three,
     field_re, field_im, total_re, total_im,
 ):
     zh = place_ref[0]
@@ -259,11 +266,12 @@
     total_im[...] = jnp.zeros(total_im.shape, f32)
     probe_re = probe_ref[0]
     probe_im = probe_ref[1]
-    ah, al, bh, bl = ah_ref[...], al_ref[...], bh_ref[...], bl_ref[...]
+    ah, bh = complex_blocks(dft_ref[0], dft_ref[1])
+    al, bl = complex_blocks(dft_ref[2], dft_ref[3])
     for pair in range(FR_DEV // 2):
         waves = []
         for frame in (2 * pair, 2 * pair + 1):
-            rows = pl.ds(starts_ref[0, frame], PROBE)
+            rows = pl.ds(place_ref[3 + frame], PROBE)
             object_re = field_re[rows, :]
             object_im = field_im[rows, :]
             waves.append(
@@ -302,7 +310,7 @@
         for i in range(2):
             back_re = backs[:PROBE, i * NZ : (i + 1) * NZ]
             back_im = backs[PROBE:, i * NZ : (i + 1) * NZ]
-            rows = pl.ds(starts_ref[0, 2 * pair + i], PROBE)
+            rows = pl.ds(place_ref[3 + 2 * pair + i], PROBE)
             total_re[rows, :] += probe_re * back_re + probe_im * back_im
             total_im[rows, :] += probe_re * back_im - probe_im * back_re
     for ahead in range(Y):
@@ -335,8 +343,7 @@
     zh = lax.axis_index("zh")
     zl = lax.axis_index("zl")
     y = lax.axis_index("y")
-    place = jnp.stack([zh, y, zl]).astype(jnp.int32)
-    ah, al, bh, bl = dft_blocks()
+    place = jnp.concatenate([jnp.stack([zh, y, zl]).astype(jnp.int32), positions.reshape(FR_DEV)])
     radon = radon_tiles.reshape(ZL * XC, HITS, RAYS, TILE)
     volume_rows = volume.reshape(2 * TILE, NZ)
     object_rows = object_field.reshape(128, NZ)
@@ -344,22 +351,22 @@
 
     with jax.named_scope("ray_sums"):
         object_theirs = across(object_rows)
-        sums = call(
+        sums, targets = call(
             ray_sums,
-            shape(NEAR, ZL, HITS * QR, 2 * NZ, dtype=bf16),
+            (shape(NEAR, ZL, HITS * QR, 2 * NZ, dtype=bf16), shape(QR, NZ)),
             0,
             0,
-            n_far=2,
-            scratch=[pltpu.VMEM(radon.shape, bf16), pltpu.VMEM((2 * TILE, NZ), f32), pltpu.SemaphoreType.DMA((ZL + 1,))],
+            n_far=3,
+            scratch=[
+                pltpu.VMEM(radon.shape, bf16),
+                pltpu.VMEM((2 * TILE, NZ), f32),
+                pltpu.VMEM((1, ZL * XC), jnp.int32),
+                pltpu.SemaphoreType.DMA((ZL + 2,)),
+            ],
             flops=2 * 2048 * 256 * 256,
             limit=SUMS_LIMIT,
-        )(radon, volume_rows)
+        )(radon, volume_rows, tile_range.reshape(1, ZL * XC))
         near_sums = lax.all_to_all(sums, CROSS, 0, 0, tiled=True)
-
-    with jax.named_scope("targets"):
-        own_targets, sums = lax.optimization_barrier((tile_range.reshape(1, ZL * XC), sums))
-        targets = jnp.concatenate([own_targets] + [shifted(own_targets, "zl", ZL, k) for k in range(1, ZL)])
-        targets = jnp.pad(targets.astype(f32), ((0, QR - ZL), (0, NZ - ZL * XC)))
 
     with jax.named_scope("fields"):
         object_theirs, sums, targets = lax.optimization_barrier((object_theirs, sums, targets))
@@ -372,26 +379,29 @@
         inter_parts = call(
             frame_gradients,
             (shape(2, 128, NZ),) + (shape(2, 128, NZ, dtype=bf16),) * 3,
-            2,
-            10,
+            1,
+            7,
             scratch=[pltpu.VMEM((NDET, NZ), f32)] * 4,
             flops=FRAMES_COST,
-        )(place, positions, *fields, probe_field, measured[0], ah, al, bh, bl)
+        )(place, *fields, probe_field, measured[0], dft_blocks())
+        inter_own = inter_parts[0]
         inter_parts = round_y(inter_parts)
 
     with jax.named_scope("targets"):
         base = FIELD_ROWS + DRIFT_ROWS
-        tables = jnp.concatenate([field[base : base + ZL, : ZL * XC] for field in fields]).astype(jnp.int32)
+        table = jnp.concatenate([field[base : base + 1, : ZL * XC] for field in fields]).astype(jnp.int32)
+        table, inter_own = lax.optimization_barrier((table, inter_own))
+        tables = [table] + [shifted(table, "zl", ZL, k) for k in range(1, ZL)]
 
     with jax.named_scope("near_sum"):
         dense, inter = call(
             add_tiles,
             (shape(DEEP, 128, NZ, dtype=bf16), shape(2, 128, NZ)),
-            2,
+            5,
             9,
             scratch=[pltpu.VMEM((ZL, 128, 2 * NZ), f32)],
             flops=1_000_000,
-        )(place, tables, near_sums, *inter_parts, *fields)
+        )(place, *tables, near_sums, *inter_parts, *fields)
         far_sums = lax.all_to_all(dense, ALONG, 0, 0, tiled=True)
 
     with jax.named_scope("residual"):
@@ -406,11 +416,11 @@
         picked = call(
             pick_tiles,
             shape(NEAR, ZL, HITS * QR, 2 * NZ, dtype=bf16),
-            2,
+            5,
             1,
             scratch=[pltpu.VMEM((ZL, 128, 2 * NZ), f32)],
             flops=1_000_000,
-        )(place, tables, residuals)
+        )(place, *tables, residuals)
         picked, kept = lax.optimization_barrier((picked, kept))
         returned = lax.all_to_all(picked, CROSS, 0, 0, tiled=True)
 

time: 110 us -> 103 us (0.936)
  starting transfers between devices: 46.2 us -> 42.7 us
  blocking collectives: 17.4 us -> 15.1 us
    ppermute x14, starting transfers between devices: 26.1 us -> 21.9 us  [shifted(): lax.ppermute(value, axis, [(i, (i + step) % length) for i in range(length)])]
    all_to_all x1, blocking collectives: 17.4 us -> 15.1 us  [body(): far_sums = lax.all_to_all(dense, ALONG, 0, 0, tiled=True)]
    ppermute x14, waiting for transfers between devices: 15.3 us -> 14.2 us  [shifted(): lax.ppermute(value, axis, [(i, (i + step) % length) for i in range(length)])]
  transfers between devices with their start and end apart: 17 -> 17, of which waited for: 6 -> 7; matrix products, arithmetic and copies ran while one was open for 2% -> 3% of each run, Pallas kernels for 8% -> 12%
where the time goes in v10:
time: 103 us
  starting transfers between devices  42.7 us (41%)
  waiting for transfers between devices  23.5 us (23%)
  Pallas kernels  15.8 us (15%)
  blocking collectives  15.1 us (15%)
  local copies, waits for them, and re-layouts  4.73 us (5%)
    ppermute x14, starting transfers between devices, shifted(): lax.ppermute(value, axis, [(i, (i + step) % length) for i in range(length)])  21.9 us
    all_to_all x1, blocking collectives, body(): far_sums = lax.all_to_all(dense, ALONG, 0, 0, tiled=True)  15.1 us
    ppermute x14, waiting for transfers between devices, shifted(): lax.ppermute(value, axis, [(i, (i + step) % length) for i in range(length)])  14.2 us
    all_to_all x1, starting transfers between devices, body(): returned = lax.all_to_all(picked, CROSS, 0, 0, tiled=True)  9.2 us
    all_to_all x1, starting transfers between devices, body(): near_sums = lax.all_to_all(sums, CROSS, 0, 0, tiled=True)  7.95 us
    all_to_all x1, waiting for transfers between devices, body(): residuals = lax.all_to_all(copies, ALONG, 0, 0, tiled=True)  5.7 us
    pallas_call x1, Pallas kernels, body(): call(frame_gradients, (shape(2, 128, NZ),) + (shape(2, 128, NZ, dtype=bf1...  4.63 us
    all_to_all x1, waiting for transfers between devices, body(): returned = lax.all_to_all(picked, CROSS, 0, 0, tiled=True)  3.65 us
  transfers between devices with their start and end apart: 17, of which 7 were waited for; matrix products, arithmetic and copies ran while one was open for 3% of the time, Pallas kernels for 12%

profile of v10, /device:TPU:1, one launch (start us, length us, event | category | flops | bytes accessed | tf_op | source)
XLA Modules:
  0.0 102.8 jit_solution(8745150438264882429)
XLA Ops:
  0.6 7.8 %collective-permute-start = (f32[128,128]{1,0:T(8,128)}, f32[128,128]{1,0:T(8,128)S(1)}, u32[]{:S(2)}, u32[]{:S(2)}) collective-permute-start(f32[128,128]{1,0:T(8,128)} %bitcast.19), channel_id=1, source_target_pairs={{0,4},{4,0},{1,5},{5,1},{2,6},{6,2},{3,7},{7,3},{8,12},{12,8},{9,1... | collective-permute-start | bytes 196616 | tf_op jit(solution)/shard_map/ray_sums/ppermute | solution.py:331
  8.5 0.7 copy-done.14
  9.2 3.3 %ray_sums.1 = (bf16[32,4,16,256]{3,2,1,0:T(8,128)(2,1)}, f32[8,128]{1,0:T(8,128)}) custom-call(bf16[32,2,32,256]{3,2,1,0:T(8,128)(2,1)} %bitcast.25, f32[512,128]{1,0:T(8,128)} %bitcast.17, s32[1,32]{1,0:T(1,128)} %bitcast.29), custom_call_target="tpu_custom_call" | custom-call | flops 268435456 | bytes 1048576 | tf_op jit(solution)/shard_map/ray_sums/ray_sums/pallas_call | solution.py:354
  13.8 2.8 %collective-permute-start.3 = (f32[296,128]{1,0:T(8,128)S(1)}, f32[296,128]{1,0:T(8,128)S(1)}, u32[]{:S(2)}, u32[]{:S(2)}) collective-permute-start(f32[296,128]{1,0:T(8,128)S(1)} %get-tuple-element.38), channel_id=1, source_target_pairs={{0,3},{1,0},{2,1},{3,2},{4,7},{5,4},{6,5},{7,6},{8,11},{9,8},{10,9... | collective-permute-start | bytes 454664 | tf_op jit(solution)/shard_map/fields/ppermute | solution.py:331
  17.0 0.7 collective-permute-start.1
  17.7 7.9 %all-to-all-start = ((bf16[32,4,16,256]{3,2,1,0:T(8,128)(2,1)}), bf16[32,4,16,256]{3,2,1,0:T(8,128)(2,1)S(1)}, u32[]{:S(2)}, u32[]{:S(2)}) async-start(bf16[32,4,16,256]{3,2,1,0:T(8,128)(2,1)} %get-tuple-element.31), calls=%async_computation | async-start | bytes 2097152 | tf_op jit(solution)/shard_map/ray_sums/all_to_all | solution.py:369
  25.7 1.4 %collective-permute-done.1.field_1 = f32[296,128]{1,0:T(8,128)S(1)} collective-permute-done((f32[296,128]{1,0:T(8,128)S(1)}, f32[296,128]{1,0:T(8,128)S(1)}, u32[]{:S(2)}, u32[]{:S(2)}) %collective-permute-start.1) | collective-permute-done | bytes 151584 | tf_op jit(solution)/shard_map/fields/ppermute | solution.py:331
  27.1 4.6 %frame_gradients.1 = (f32[2,128,128]{2,1,0:T(8,128)S(1)}, bf16[2,128,128]{2,1,0:T(8,128)(2,1)S(1)}, bf16[2,128,128]{2,1,0:T(8,128)(2,1)S(1)}, bf16[2,128,128]{2,1,0:T(8,128)(2,1)S(1)}) custom-call(s32[11]{0:T(128)S(1)} %pad_add_fusion.place_ref, f32[296,128]{1,0:T(8,128)S(1)} %get-tuple-element.35.field_0, f32[296,128]{1,0:T(8,128)S(1)} %collective-permute-done.1.field_1, ...), custom_call_target="tpu_custom_call" | custom-call | flops 20000000000 | bytes 1048576 | tf_op jit(solution)/shard_map/frames/frame_gradients/pallas_call | solution.py:379
  31.8 2.4 %collective-permute-start.8 = (bf16[2,128,128]{2,1,0:T(8,128)(2,1)S(1)}, bf16[2,128,128]{2,1,0:T(8,128)(2,1)S(1)}, u32[]{:S(2)}, u32[]{:S(2)}) collective-permute-start(bf16[2,128,128]{2,1,0:T(8,128)(2,1)S(1)} %get-tuple-element.42), channel_id=1, source_target_pairs={{0,2},{1,3},{2,0},{3,1},{4,6},{5,7},{6,4},{7,5},{8,10},{9,11},{10,... | collective-permute-start | bytes 196616 | tf_op jit(solution)/shard_map/frames/ppermute | solution.py:331
  34.2 1.2 %collective-permute-start.9 = (bf16[2,128,128]{2,1,0:T(8,128)(2,1)S(1)}, bf16[2,128,128]{2,1,0:T(8,128)(2,1)S(1)}, u32[]{:S(2)}, u32[]{:S(2)}) collective-permute-start(bf16[2,128,128]{2,1,0:T(8,128)(2,1)S(1)} %get-tuple-element.43), channel_id=1, source_target_pairs={{0,3},{1,0},{2,1},{3,2},{4,7},{5,4},{6,5},{7,6},{8,11},{9,8},{10,9... | collective-permute-start | bytes 196616 | tf_op jit(solution)/shard_map/frames/ppermute | solution.py:331
  35.4 0.8 collective-permute-start.4
  36.2 1.2 %collective-permute-start.5 = (s32[4,32]{1,0:T(4,128)S(1)}, s32[4,32]{1,0:T(4,128)S(1)}, u32[]{:S(2)}, u32[]{:S(2)}) collective-permute-start(s32[4,32]{1,0:T(4,128)S(1)} %maximum_convert_fusion.table_0), channel_id=1, source_target_pairs={{0,128},{64,192},{128,0},{192,64},{1,129},{65,193},{129,1},{193,65... | collective-permute-start | bytes 1544 | tf_op jit(solution)/shard_map/targets/ppermute | solution.py:331
  37.4 2.6 %collective-permute-done.4.table_1 = s32[4,32]{1,0:T(4,128)S(1)} collective-permute-done((s32[4,32]{1,0:T(4,128)S(1)}, s32[4,32]{1,0:T(4,128)S(1)}, u32[]{:S(2)}, u32[]{:S(2)}) %collective-permute-start.4) | collective-permute-done | bytes 544 | tf_op jit(solution)/shard_map/targets/ppermute | solution.py:331
  40.0 2.7 %collective-permute-done.6.table_3 = s32[4,32]{1,0:T(4,128)S(1)} collective-permute-done((s32[4,32]{1,0:T(4,128)S(1)}, s32[4,32]{1,0:T(4,128)S(1)}, u32[]{:S(2)}, u32[]{:S(2)}) %collective-permute-start.6) | collective-permute-done | bytes 544 | tf_op jit(solution)/shard_map/targets/ppermute | solution.py:331
  42.7 1.2 %collective-permute-done.8.inter_2 = bf16[2,128,128]{2,1,0:T(8,128)(2,1)S(1)} collective-permute-done((bf16[2,128,128]{2,1,0:T(8,128)(2,1)S(1)}, bf16[2,128,128]{2,1,0:T(8,128)(2,1)S(1)}, u32[]{:S(2)}, u32[]{:S(2)}) %collective-permute-start.8) | collective-permute-done | bytes 65568 | tf_op jit(solution)/shard_map/frames/ppermute | solution.py:331
  44.0 1.5 %add_tiles.1 = (bf16[8,128,128]{2,1,0:T(8,128)(2,1)S(1)}, f32[2,128,128]{2,1,0:T(8,128)S(1)}) custom-call(s32[11]{0:T(128)S(1)} %pad_add_fusion.place_ref, s32[4,32]{1,0:T(4,128)S(1)} %maximum_convert_fusion.table_0, s32[4,32]{1,0:T(4,128)S(1)} %collective-permute-done.4.table_1, s32[4,32]{1,0:T(4,128)S(1)} %collective-permute-done.5.table_2, ...), custom_call_target="tpu_custom_call" | custom-call | flops 1000000 | bytes 1048576 | tf_op jit(solution)/shard_map/near_sum/add_tiles/pallas_call | solution.py:397
  45.4 15.1 %all_to_all.20.sums_ref = bf16[8,128,128]{2,1,0:T(8,128)(2,1)S(1)} all-to-all(bf16[8,128,128]{2,1,0:T(8,128)(2,1)S(1)} %get-tuple-element.44), channel_id=1, replica_groups=mesh['zl'=4,'x'=4,'c'=2,'zh'=2,'y'=4] {'zh','zl'}, dimensions={0} | all-to-all | bytes 524288 | tf_op jit(solution)/shard_map/near_sum/all_to_all | solution.py:405
  60.5 0.8 residual_part.1
  61.3 3.6 %all-to-all-start.2 = ((bf16[8,128,128]{2,1,0:T(8,128)(2,1)}), bf16[8,128,128]{2,1,0:T(8,128)(2,1)S(1)}, u32[]{:S(2)}, u32[]{:S(2)}) async-start(bf16[8,128,128]{2,1,0:T(8,128)(2,1)} %get-tuple-element.45), calls=%async_computation.2 | async-start | bytes 524288 | tf_op jit(solution)/shard_map/residual/all_to_all | solution.py:411
  65.6 1.5 %collective-permute-start.11 = (f32[2,3,16,128]{3,2,1,0:T(8,128)S(1)}, f32[2,3,16,128]{3,2,1,0:T(8,128)S(1)}, u32[]{:S(2)}, u32[]{:S(2)}) collective-permute-start(f32[2,3,16,128]{3,2,1,0:T(8,128)S(1)} %get-tuple-element.50), channel_id=1, source_target_pairs={{0,2},{1,3},{2,0},{3,1},{4,6},{5,7},{6,4},{7,5},{8,10},{9,11},{10,... | collective-permute-start | bytes 147464 | tf_op jit(solution)/shard_map/residual/ppermute | solution.py:331
  67.1 1.2 %collective-permute-start.12 = (f32[2,3,16,128]{3,2,1,0:T(8,128)S(1)}, f32[2,3,16,128]{3,2,1,0:T(8,128)S(1)}, u32[]{:S(2)}, u32[]{:S(2)}) collective-permute-start(f32[2,3,16,128]{3,2,1,0:T(8,128)S(1)} %get-tuple-element.51), channel_id=1, source_target_pairs={{0,3},{1,0},{2,1},{3,2},{4,7},{5,4},{6,5},{7,6},{8,11},{9,8},{10,9... | collective-permute-start | bytes 147464 | tf_op jit(solution)/shard_map/residual/ppermute | solution.py:331
  68.3 5.7 %all-to-all-done.2.residual_ref = bf16[8,128,128]{2,1,0:T(8,128)(2,1)S(1)} async-done(((bf16[8,128,128]{2,1,0:T(8,128)(2,1)}), bf16[8,128,128]{2,1,0:T(8,128)(2,1)S(1)}, u32[]{:S(2)}, u32[]{:S(2)}) %all-to-all-start.2) | async-done | bytes 262176 | tf_op jit(solution)/shard_map/residual/all_to_all | solution.py:411
  74.0 2.1 %pick_tiles.1 = bf16[32,4,16,256]{3,2,1,0:T(8,128)(2,1)} custom-call(s32[11]{0:T(128)S(1)} %pad_add_fusion.place_ref, s32[4,32]{1,0:T(4,128)S(1)} %maximum_convert_fusion.table_0, s32[4,32]{1,0:T(4,128)S(1)} %collective-permute-done.4.table_1, s32[4,32]{1,0:T(4,128)S(1)} %collective-permute-done.5.table_2, s32[4,32]{1,0:T(4,128)S(1)} %collective-permute-done.6.table_3, ...), custom_call_target="tpu_custom_call" | custom-call | flops 1000000 | bytes 1048576 | tf_op jit(solution)/shard_map/pick/pick_tiles/pallas_call | solution.py:416
  76.1 9.2 %all-to-all-start.3 = ((bf16[32,4,16,256]{3,2,1,0:T(8,128)(2,1)}), bf16[32,4,16,256]{3,2,1,0:T(8,128)(2,1)S(1)}, u32[]{:S(2)}, u32[]{:S(2)}) async-start(bf16[32,4,16,256]{3,2,1,0:T(8,128)(2,1)} %pick_tiles.1), calls=%async_computation.3 | async-start | bytes 2097152 | tf_op jit(solution)/shard_map/pick/all_to_all | solution.py:425
  85.4 0.7 slice-done.2
  86.2 1.7 %collective-permute-start.13 = (f32[4,3,16,128]{3,2,1,0:T(8,128)S(1)}, f32[4,3,16,128]{3,2,1,0:T(8,128)S(1)}, u32[]{:S(2)}, u32[]{:S(2)}) collective-permute-start(f32[4,3,16,128]{3,2,1,0:T(8,128)S(1)} %pad_maximum_fusion), channel_id=1, source_target_pairs={{0,4},{4,0},{1,5},{5,1},{2,6},{6,2},{3,7},{7,3},{8,12},{12,8},{9,1... | collective-permute-start | bytes 294920 | tf_op jit(solution)/shard_map/updates/ppermute | solution.py:331
  87.9 1.1 %copy.14 = bf16[256,8,4,4,2,8]{0,5,4,3,2,1:T(8,128)(2,1)} copy(bf16[256,8,4,4,2,8]{0,5,2,4,1,3:T(8,128)(2,1)S(1)} %bitcast.26) | data formatting | bytes 2097152 | tf_op jit(solution)/shard_map/back_project/transpose | solution.py:434
  89.0 1.5 %copy.15.radon_ref = bf16[256,2048]{1,0:T(8,128)(2,1)S(1)} copy(bf16[256,2048]{0,1:T(8,128)(2,1)} %bitcast.27) | data formatting | bytes 2097152 | tf_op jit(solution)/shard_map/back_project/reshape | solution.py:434
  90.5 6.2 %collective-permute-done.13.theirs_ref = f32[4,3,16,128]{3,2,1,0:T(8,128)S(1)} collective-permute-done((f32[4,3,16,128]{3,2,1,0:T(8,128)S(1)}, f32[4,3,16,128]{3,2,1,0:T(8,128)S(1)}, u32[]{:S(2)}, u32[]{:S(2)}) %collective-permute-start.13) | collective-permute-done | bytes 98336 | tf_op jit(solution)/shard_map/updates/ppermute | solution.py:331
  96.8 1.2 %updates.1 = (f32[128,128]{1,0:T(8,128)}, f32[128,128]{1,0:T(8,128)}) custom-call(s32[11]{0:T(128)S(1)} %pad_add_fusion.place_ref, f32[2,3,16,128]{3,2,1,0:T(8,128)S(1)} %get-tuple-element.52.own_ref, f32[2,3,16,128]{3,2,1,0:T(8,128)S(1)} %copy-done.4, f32[2,3,16,128]{3,2,1,0:T(8,128)S(1)} %copy-done.6, f32[2,3,16,128]{3,2,1,0:T(8,128)S(1)} %copy-done.8, ...), custom_call_target="tpu_custom_call" | custom-call | flops 1000000 | bytes 1048576 | tf_op jit(solution)/shard_map/updates/updates/pallas_call | solution.py:429
  98.0 3.6 %all-to-all-done.3.picked_ref = bf16[32,4,16,256]{3,2,1,0:T(8,128)(2,1)S(1)} async-done(((bf16[32,4,16,256]{3,2,1,0:T(8,128)(2,1)}), bf16[32,4,16,256]{3,2,1,0:T(8,128)(2,1)S(1)}, u32[]{:S(2)}, u32[]{:S(2)}) %all-to-all-start.3) | async-done | bytes 1048608 | tf_op jit(solution)/shard_map/pick/all_to_all | solution.py:425
  101.7 1.1 %back_project.1 = f32[512,128]{1,0:T(8,128)} custom-call(bf16[256,2048]{1,0:T(8,128)(2,1)S(1)} %copy.15.radon_ref, bf16[32,4,16,256]{3,2,1,0:T(8,128)(2,1)S(1)} %all-to-all-done.3.picked_ref, f32[512,128]{1,0:T(8,128)S(1)} %bitcast.18), custom_call_target="tpu_custom_call" | custom-call | flops 268435456 | bytes 1048576 | tf_op jit(solution)/shard_map/back_project/back_project/pallas_call | solution.py:435
  (58 shorter events, 2.6 us)
Async XLA Ops:
  0.6 11.9 %collective-permute-start = (f32[128,128]{1,0:T(8,128)}, f32[128,128]{1,0:T(8,128)S(1)}, u32[]{:S(2)}, u32[]{:S(2)}) collective-permute-start(f32[128,128]{1,0:T(8,128)} %bitcast.19), channel_id=1, source_target_pairs={{0,4},{4,0},{1,5},{5,1},{2,6},{6,2},{3,7},{7,3},{8,12},{12,8},{9,1... | collective-permute-start | bytes 196616 | tf_op jit(solution)/shard_map/ray_sums/ppermute | solution.py:331
  9.2 3.4 %copy-start.1 = (f32[1,64,2,128]{3,2,1,0:T(2,128)S(1)}, f32[1,64,2,128]{3,2,1,0:T(2,128)}, u32[]{:S(2)}) copy-start(f32[1,64,2,128]{3,2,1,0:T(2,128)} %param.12) | copy-start | bytes 196612
  9.2 3.4 %copy-start.2 = (f32[1,64,2,128]{3,2,1,0:T(2,128)S(1)}, f32[1,64,2,128]{3,2,1,0:T(2,128)}, u32[]{:S(2)}) copy-start(f32[1,64,2,128]{3,2,1,0:T(2,128)} %param.13) | copy-start | bytes 196612
  13.8 11.8 %collective-permute-start.3 = (f32[296,128]{1,0:T(8,128)S(1)}, f32[296,128]{1,0:T(8,128)S(1)}, u32[]{:S(2)}, u32[]{:S(2)}) collective-permute-start(f32[296,128]{1,0:T(8,128)S(1)} %get-tuple-element.38), channel_id=1, source_target_pairs={{0,3},{1,0},{2,1},{3,2},{4,7},{5,4},{6,5},{7,6},{8,11},{9,8},{10,9... | collective-permute-start | bytes 454664 | tf_op jit(solution)/shard_map/fields/ppermute | solution.py:331
  16.6 9.0 %collective-permute-start.2 = (f32[296,128]{1,0:T(8,128)S(1)}, f32[296,128]{1,0:T(8,128)S(1)}, u32[]{:S(2)}, u32[]{:S(2)}) collective-permute-start(f32[296,128]{1,0:T(8,128)S(1)} %get-tuple-element.37), channel_id=1, source_target_pairs={{0,2},{1,3},{2,0},{3,1},{4,6},{5,7},{6,4},{7,5},{8,10},{9,11},{10,... | collective-permute-start | bytes 454664 | tf_op jit(solution)/shard_map/fields/ppermute | solution.py:331
  17.0 10.1 %copy-start.10 = (f32[1,8,128,128]{3,2,1,0:T(8,128)S(1)}, f32[1,8,128,128]{3,2,1,0:T(8,128)}, u32[]{:S(2)}) copy-start(f32[1,8,128,128]{3,2,1,0:T(8,128)} %param.9) | copy-start | bytes 1572868
  17.0 10.1 %copy-start.11 = (f32[2,128,128]{2,1,0:T(8,128)S(1)}, f32[2,128,128]{2,1,0:T(8,128)}, u32[]{:S(2)}) copy-start(f32[2,128,128]{2,1,0:T(8,128)} %probe_ref.1) | copy-start | bytes 393220
  17.0 10.1 %copy-start.12 = (bf16[4,128,128]{2,1,0:T(8,128)(2,1)S(1)}, bf16[4,128,128]{2,1,0:T(8,128)(2,1)}, u32[]{:S(2)}) copy-start(bf16[4,128,128]{2,1,0:T(8,128)(2,1)} %constant.15.clone.dft_ref) | copy-start | bytes 393220
  17.0 10.1 %collective-permute-start.1 = (f32[296,128]{1,0:T(8,128)S(1)}, f32[296,128]{1,0:T(8,128)S(1)}, u32[]{:S(2)}, u32[]{:S(2)}) collective-permute-start(f32[296,128]{1,0:T(8,128)S(1)} %get-tuple-element.36), channel_id=1, source_target_pairs={{0,1},{1,2},{2,3},{3,0},{4,5},{5,6},{6,7},{7,4},{8,9},{9,10},{10,1... | collective-permute-start | bytes 454664 | tf_op jit(solution)/shard_map/fields/ppermute | solution.py:331
  17.7 26.3 %all-to-all-start = ((bf16[32,4,16,256]{3,2,1,0:T(8,128)(2,1)}), bf16[32,4,16,256]{3,2,1,0:T(8,128)(2,1)S(1)}, u32[]{:S(2)}, u32[]{:S(2)}) async-start(bf16[32,4,16,256]{3,2,1,0:T(8,128)(2,1)} %get-tuple-element.31), calls=%async_computation | async-start | bytes 2097152 | tf_op jit(solution)/shard_map/ray_sums/all_to_all | solution.py:369
  31.7 11.0 %collective-permute-start.7 = (bf16[2,128,128]{2,1,0:T(8,128)(2,1)S(1)}, bf16[2,128,128]{2,1,0:T(8,128)(2,1)S(1)}, u32[]{:S(2)}, u32[]{:S(2)}) collective-permute-start(bf16[2,128,128]{2,1,0:T(8,128)(2,1)S(1)} %get-tuple-element.41), channel_id=1, source_target_pairs={{0,1},{1,2},{2,3},{3,0},{4,5},{5,6},{6,7},{7,4},{8,9},{9,10},{10,1... | collective-permute-start | bytes 196616 | tf_op jit(solution)/shard_map/frames/ppermute | solution.py:331
  31.8 12.1 %collective-permute-start.8 = (bf16[2,128,128]{2,1,0:T(8,128)(2,1)S(1)}, bf16[2,128,128]{2,1,0:T(8,128)(2,1)S(1)}, u32[]{:S(2)}, u32[]{:S(2)}) collective-permute-start(bf16[2,128,128]{2,1,0:T(8,128)(2,1)S(1)} %get-tuple-element.42), channel_id=1, source_target_pairs={{0,2},{1,3},{2,0},{3,1},{4,6},{5,7},{6,4},{7,5},{8,10},{9,11},{10,... | collective-permute-start | bytes 196616 | tf_op jit(solution)/shard_map/frames/ppermute | solution.py:331
  34.2 9.7 %collective-permute-start.9 = (bf16[2,128,128]{2,1,0:T(8,128)(2,1)S(1)}, bf16[2,128,128]{2,1,0:T(8,128)(2,1)S(1)}, u32[]{:S(2)}, u32[]{:S(2)}) collective-permute-start(bf16[2,128,128]{2,1,0:T(8,128)(2,1)S(1)} %get-tuple-element.43), channel_id=1, source_target_pairs={{0,3},{1,0},{2,1},{3,2},{4,7},{5,4},{6,5},{7,6},{8,11},{9,8},{10,9... | collective-permute-start | bytes 196616 | tf_op jit(solution)/shard_map/frames/ppermute | solution.py:331
  35.4 4.6 %collective-permute-start.4 = (s32[4,32]{1,0:T(4,128)S(1)}, s32[4,32]{1,0:T(4,128)S(1)}, u32[]{:S(2)}, u32[]{:S(2)}) collective-permute-start(s32[4,32]{1,0:T(4,128)S(1)} %maximum_convert_fusion.table_0), channel_id=1, source_target_pairs={{0,64},{64,128},{128,192},{192,0},{1,65},{65,129},{129,193},{193,1... | collective-permute-start | bytes 1544 | tf_op jit(solution)/shard_map/targets/ppermute | solution.py:331
  36.2 3.8 %collective-permute-start.5 = (s32[4,32]{1,0:T(4,128)S(1)}, s32[4,32]{1,0:T(4,128)S(1)}, u32[]{:S(2)}, u32[]{:S(2)}) collective-permute-start(s32[4,32]{1,0:T(4,128)S(1)} %maximum_convert_fusion.table_0), channel_id=1, source_target_pairs={{0,128},{64,192},{128,0},{192,64},{1,129},{65,193},{129,1},{193,65... | collective-permute-start | bytes 1544 | tf_op jit(solution)/shard_map/targets/ppermute | solution.py:331
  40.0 2.7 %collective-permute-start.6 = (s32[4,32]{1,0:T(4,128)S(1)}, s32[4,32]{1,0:T(4,128)S(1)}, u32[]{:S(2)}, u32[]{:S(2)}) collective-permute-start(s32[4,32]{1,0:T(4,128)S(1)} %maximum_convert_fusion.table_0), channel_id=1, source_target_pairs={{0,192},{64,0},{128,64},{192,128},{1,193},{65,1},{129,65},{193,129... | collective-permute-start | bytes 1544 | tf_op jit(solution)/shard_map/targets/ppermute | solution.py:331
  61.3 12.7 %all-to-all-start.2 = ((bf16[8,128,128]{2,1,0:T(8,128)(2,1)}), bf16[8,128,128]{2,1,0:T(8,128)(2,1)S(1)}, u32[]{:S(2)}, u32[]{:S(2)}) async-start(bf16[8,128,128]{2,1,0:T(8,128)(2,1)} %get-tuple-element.45), calls=%async_computation.2 | async-start | bytes 524288 | tf_op jit(solution)/shard_map/residual/all_to_all | solution.py:411
  65.5 10.6 %collective-permute-start.10 = (f32[2,3,16,128]{3,2,1,0:T(8,128)S(1)}, f32[2,3,16,128]{3,2,1,0:T(8,128)S(1)}, u32[]{:S(2)}, u32[]{:S(2)}) collective-permute-start(f32[2,3,16,128]{3,2,1,0:T(8,128)S(1)} %get-tuple-element.49), channel_id=1, source_target_pairs={{0,1},{1,2},{2,3},{3,0},{4,5},{5,6},{6,7},{7,4},{8,9},{9,10},{10,1... | collective-permute-start | bytes 147464 | tf_op jit(solution)/shard_map/residual/ppermute | solution.py:331
  65.6 10.5 %collective-permute-start.11 = (f32[2,3,16,128]{3,2,1,0:T(8,128)S(1)}, f32[2,3,16,128]{3,2,1,0:T(8,128)S(1)}, u32[]{:S(2)}, u32[]{:S(2)}) collective-permute-start(f32[2,3,16,128]{3,2,1,0:T(8,128)S(1)} %get-tuple-element.50), channel_id=1, source_target_pairs={{0,2},{1,3},{2,0},{3,1},{4,6},{5,7},{6,4},{7,5},{8,10},{9,11},{10,... | collective-permute-start | bytes 147464 | tf_op jit(solution)/shard_map/residual/ppermute | solution.py:331
  67.1 9.0 %collective-permute-start.12 = (f32[2,3,16,128]{3,2,1,0:T(8,128)S(1)}, f32[2,3,16,128]{3,2,1,0:T(8,128)S(1)}, u32[]{:S(2)}, u32[]{:S(2)}) collective-permute-start(f32[2,3,16,128]{3,2,1,0:T(8,128)S(1)} %get-tuple-element.51), channel_id=1, source_target_pairs={{0,3},{1,0},{2,1},{3,2},{4,7},{5,4},{6,5},{7,6},{8,11},{9,8},{10,9... | collective-permute-start | bytes 147464 | tf_op jit(solution)/shard_map/residual/ppermute | solution.py:331
  76.1 9.3 %copy-start.3 = (f32[2,3,16,128]{3,2,1,0:T(8,128)}, f32[2,3,16,128]{3,2,1,0:T(8,128)S(1)}, u32[]{:S(2)}) copy-start(f32[2,3,16,128]{3,2,1,0:T(8,128)S(1)} %collective-permute-done.10.one_ref) | copy-start | bytes 147460
  76.1 9.3 %copy-start.5 = (f32[2,3,16,128]{3,2,1,0:T(8,128)}, f32[2,3,16,128]{3,2,1,0:T(8,128)S(1)}, u32[]{:S(2)}) copy-start(f32[2,3,16,128]{3,2,1,0:T(8,128)S(1)} %collective-permute-done.11.two_ref) | copy-start | bytes 147460
  76.1 9.2 %copy-start.7 = (f32[2,3,16,128]{3,2,1,0:T(8,128)}, f32[2,3,16,128]{3,2,1,0:T(8,128)S(1)}, u32[]{:S(2)}) copy-start(f32[2,3,16,128]{3,2,1,0:T(8,128)S(1)} %collective-permute-done.12.three_ref) | copy-start | bytes 147460
  76.1 11.8 %copy-start.13 = (bf16[1,32,2,32,256]{4,3,2,1,0:T(8,128)(2,1)S(1)}, bf16[1,32,2,32,256]{4,3,2,1,0:T(8,128)(2,1)}, u32[]{:S(2)}) copy-start(bf16[1,32,2,32,256]{4,3,2,1,0:T(8,128)(2,1)} %param.15) | copy-start | bytes 3145732
  76.1 25.5 %all-to-all-start.3 = ((bf16[32,4,16,256]{3,2,1,0:T(8,128)(2,1)}), bf16[32,4,16,256]{3,2,1,0:T(8,128)(2,1)S(1)}, u32[]{:S(2)}, u32[]{:S(2)}) async-start(bf16[32,4,16,256]{3,2,1,0:T(8,128)(2,1)} %pick_tiles.1), calls=%async_computation.3 | async-start | bytes 2097152 | tf_op jit(solution)/shard_map/pick/all_to_all | solution.py:425
  85.4 0.7 slice-start
  85.4 0.8 slice-start.1
  86.2 10.6 %collective-permute-start.13 = (f32[4,3,16,128]{3,2,1,0:T(8,128)S(1)}, f32[4,3,16,128]{3,2,1,0:T(8,128)S(1)}, u32[]{:S(2)}, u32[]{:S(2)}) collective-permute-start(f32[4,3,16,128]{3,2,1,0:T(8,128)S(1)} %pad_maximum_fusion), channel_id=1, source_target_pairs={{0,4},{4,0},{1,5},{5,1},{2,6},{6,2},{3,7},{7,3},{8,12},{12,8},{9,1... | collective-permute-start | bytes 294920 | tf_op jit(solution)/shard_map/updates/ppermute | solution.py:331
  89.0 7.8 %copy-start.4 = (f32[2,3,16,128]{3,2,1,0:T(8,128)S(1)}, f32[2,3,16,128]{3,2,1,0:T(8,128)}, u32[]{:S(2)}) copy-start(f32[2,3,16,128]{3,2,1,0:T(8,128)} %copy-done.3) | copy-start | bytes 147460
  89.0 7.8 %copy-start.6 = (f32[2,3,16,128]{3,2,1,0:T(8,128)S(1)}, f32[2,3,16,128]{3,2,1,0:T(8,128)}, u32[]{:S(2)}) copy-start(f32[2,3,16,128]{3,2,1,0:T(8,128)} %copy-done.5) | copy-start | bytes 147460
  89.0 7.8 %copy-start.8 = (f32[2,3,16,128]{3,2,1,0:T(8,128)S(1)}, f32[2,3,16,128]{3,2,1,0:T(8,128)}, u32[]{:S(2)}) copy-start(f32[2,3,16,128]{3,2,1,0:T(8,128)} %copy-done.7) | copy-start | bytes 147460
  90.5 11.2 %copy-start = (f32[256,2,128]{2,1,0:T(2,128)S(1)}, f32[256,2,128]{2,1,0:T(2,128)}, u32[]{:S(2)}) copy-start(f32[256,2,128]{2,1,0:T(2,128)} %param.14) | copy-start | bytes 786436
  (3 other events, 2.1 us)

commit v11 on v10

--- a/solution.py
+++ b/solution.py
@@ -70,9 +70,7 @@
     return jnp.asarray(np.concatenate([high, low]))
 
 
-def ray_sums(radon_far, volume_far, target_far, out_ref, target_out, radon_ref, volume_ref, target_ref, sems):
-    targets = pltpu.make_async_copy(target_far, target_ref, sems.at[ZL + 1])
-    targets.start()
+def ray_sums(radon_far, volume_far, out_ref, radon_ref, volume_ref, sems):
     copies = [pltpu.make_async_copy(volume_far, volume_ref, sems.at[ZL])]
     for zl in range(ZL):
         angles = pl.ds(zl * XC, XC)
@@ -92,23 +90,21 @@
                 low = sums[y * QR : (y + 1) * QR]
                 high = sums[RAYS + y * QR : RAYS + (y + 1) * QR]
                 out_ref[xc * Y + y, zl] = jnp.concatenate([low, high], axis=0).astype(bf16)
-    targets.wait()
-    target_out[...] = jnp.zeros(target_out.shape, f32)
-    target_out[0:1, : ZL * XC] = target_ref[...].astype(f32)
-
-
-def each_tile(place_ref, tables):
+
+
+def each_tile(place_ref, table_ref):
     zl_here = place_ref[2]
-    for back_zl, table in enumerate(tables):
-        zl = lax.rem(zl_here + ZL - back_zl, ZL)
+    for apart in range(ZL):
+        zl = jnp.bitwise_xor(zl_here, apart)
         for back_y in range(Y):
             y = lax.rem(place_ref[1] + Y - back_y, Y)
             for xc in range(XC):
-                yield zl, xc * Y + y, pl.multiple_of(table[back_y, zl_here * XC + xc] * QR, QR)
+                row = table_ref[back_y * ZL + apart, zl_here * XC + xc] * QR
+                yield zl, xc * Y + y, pl.multiple_of(row, QR)
 
 
 def add_tiles(
-    place_ref, table_0, table_1, table_2, table_3, sums_ref, inter_0, inter_1, inter_2, inter_3,
+    place_ref, table_ref, sums_ref, inter_0, inter_1, inter_2, inter_3,
     field_0, field_1, field_2, field_3, out_ref, inter_ref, total,
 ):
     zh = place_ref[0]
@@ -126,7 +122,7 @@
         total[zl_here, rows, :] -= jnp.concatenate(
             [field_ref[base : base + 2 * QR, :], field_ref[base + 2 * QR : base + 4 * QR, :]], axis=1
         )
-    for zl, near, row in each_tile(place_ref, (table_0, table_1, table_2, table_3)):
+    for zl, near, row in each_tile(place_ref, table_ref):
         total[zl, pl.ds(row, HITS * QR), :] += sums_ref[near, zl].astype(f32)
     for zh in range(ZH):
         for zl in range(ZL):
@@ -155,13 +151,13 @@
                 ref[other, 1 + part] = inter_ref[part, rows, :]
 
 
-def pick_tiles(place_ref, table_0, table_1, table_2, table_3, residual_ref, out_ref, rows_ref):
+def pick_tiles(place_ref, table_ref, residual_ref, out_ref, rows_ref):
     for zl in range(ZL):
         rows_ref[zl] = jnp.concatenate(
             [residual_ref[zl].astype(f32), residual_ref[ZL + zl].astype(f32)], axis=1
         )
 
-    for zl, near, row in each_tile(place_ref, (table_0, table_1, table_2, table_3)):
+    for zl, near, row in each_tile(place_ref, table_ref):
         out_ref[near, zl] = rows_ref[zl, pl.ds(row, HITS * QR), :].astype(bf16)
 
 
@@ -236,13 +232,19 @@
 SENT_ROWS = FIELD_ROWS + DRIFT_ROWS + QR
 
 
-def pack(place_ref, object_ref, theirs_ref, dual_ref, target_ref, own_ref, one_ref, two_ref, three_ref, both):
+def pack(
+    place_ref, object_ref, theirs_ref, dual_ref, near_ref, far_ref,
+    own_ref, one_ref, two_ref, three_ref, both,
+):
     y = place_ref[1]
     both[...] = object_ref[...] + dual_ref[...]
     for ahead, ref in enumerate((own_ref, one_ref, two_ref, three_ref)):
         ref[0:128, :] = object_ref[...]
         ref[128:256, :] = theirs_ref[...]
-        ref[FIELD_ROWS + DRIFT_ROWS :, :] = target_ref[...]
+        base = FIELD_ROWS + DRIFT_ROWS
+        ref[base:, :] = jnp.zeros((QR, NZ), f32)
+        ref[base : base + 2, : ZL * XC] = near_ref[...].astype(f32)
+        ref[base + 2 : base + 4, : ZL * XC] = far_ref[...].astype(f32)
         for part in range(2):
             for tile in range(2):
                 start = (tile * RAYS + lax.rem(y + ahead, Y) * QR) * 2 + part
@@ -331,6 +333,10 @@
     return lax.ppermute(value, axis, [(i, (i + step) % length) for i in range(length)])
 
 
+def swapped(value, apart):
+    return lax.ppermute(value, "zl", [(i, i ^ apart) for i in range(ZL)])
+
+
 def across(value):
     return shifted(value, "zh", ZH, 1)
 
@@ -351,28 +357,28 @@
 
     with jax.named_scope("ray_sums"):
         object_theirs = across(object_rows)
-        sums, targets = call(
+        sums = call(
             ray_sums,
-            (shape(NEAR, ZL, HITS * QR, 2 * NZ, dtype=bf16), shape(QR, NZ)),
+            shape(NEAR, ZL, HITS * QR, 2 * NZ, dtype=bf16),
             0,
             0,
-            n_far=3,
-            scratch=[
-                pltpu.VMEM(radon.shape, bf16),
-                pltpu.VMEM((2 * TILE, NZ), f32),
-                pltpu.VMEM((1, ZL * XC), jnp.int32),
-                pltpu.SemaphoreType.DMA((ZL + 2,)),
-            ],
+            n_far=2,
+            scratch=[pltpu.VMEM(radon.shape, bf16), pltpu.VMEM((2 * TILE, NZ), f32), pltpu.SemaphoreType.DMA((ZL + 1,))],
             flops=2 * 2048 * 256 * 256,
             limit=SUMS_LIMIT,
-        )(radon, volume_rows, tile_range.reshape(1, ZL * XC))
+        )(radon, volume_rows)
         near_sums = lax.all_to_all(sums, CROSS, 0, 0, tiled=True)
 
+    with jax.named_scope("targets"):
+        table, sums = lax.optimization_barrier((tile_range.reshape(1, ZL * XC), sums))
+        near = jnp.concatenate([table, swapped(table, 1)])
+        far = swapped(near, 2)
+
     with jax.named_scope("fields"):
-        object_theirs, sums, targets = lax.optimization_barrier((object_theirs, sums, targets))
+        object_theirs, sums = lax.optimization_barrier((object_theirs, sums))
         packed = call(
-            pack, (shape(SENT_ROWS, NZ),) * Y, 1, 4, scratch=[pltpu.VMEM((128, NZ), f32)], flops=1_000_000
-        )(place, object_rows, object_theirs, dual_rows, targets)
+            pack, (shape(SENT_ROWS, NZ),) * Y, 1, 5, scratch=[pltpu.VMEM((128, NZ), f32)], flops=1_000_000
+        )(place, object_rows, object_theirs, dual_rows, near, far)
         fields = round_y(packed)
 
     with jax.named_scope("frames"):
@@ -384,24 +390,21 @@
             scratch=[pltpu.VMEM((NDET, NZ), f32)] * 4,
             flops=FRAMES_COST,
         )(place, *fields, probe_field, measured[0], dft_blocks())
-        inter_own = inter_parts[0]
         inter_parts = round_y(inter_parts)
 
     with jax.named_scope("targets"):
         base = FIELD_ROWS + DRIFT_ROWS
-        table = jnp.concatenate([field[base : base + 1, : ZL * XC] for field in fields]).astype(jnp.int32)
-        table, inter_own = lax.optimization_barrier((table, inter_own))
-        tables = [table] + [shifted(table, "zl", ZL, k) for k in range(1, ZL)]
+        tables = jnp.concatenate([field[base : base + ZL, : ZL * XC] for field in fields]).astype(jnp.int32)
 
     with jax.named_scope("near_sum"):
         dense, inter = call(
             add_tiles,
             (shape(DEEP, 128, NZ, dtype=bf16), shape(2, 128, NZ)),
-            5,
+            2,
             9,
             scratch=[pltpu.VMEM((ZL, 128, 2 * NZ), f32)],
             flops=1_000_000,
-        )(place, *tables, near_sums, *inter_parts, *fields)
+        )(place, tables, near_sums, *inter_parts, *fields)
         far_sums = lax.all_to_all(dense, ALONG, 0, 0, tiled=True)
 
     with jax.named_scope("residual"):
@@ -416,11 +419,11 @@
         picked = call(
             pick_tiles,
             shape(NEAR, ZL, HITS * QR, 2 * NZ, dtype=bf16),
-            5,
+            2,
             1,
             scratch=[pltpu.VMEM((ZL, 128, 2 * NZ), f32)],
             flops=1_000_000,
-        )(place, *tables, residuals)
+        )(place, tables, residuals)
         picked, kept = lax.optimization_barrier((picked, kept))
         returned = lax.all_to_all(picked, CROSS, 0, 0, tiled=True)
 

time: 103 us -> 108 us (1.049)
  waiting for transfers between devices: 23.5 us -> 27.7 us
  starting transfers between devices: 42.7 us -> 44.8 us
  blocking collectives: 15.1 us -> 13.5 us
    ppermute x0 -> x2, waiting for transfers between devices: none -> 3.04 us  [swapped(): return lax.ppermute(value, 'zl', [(i, i ^ apart) for i in range(ZL)])]
    ppermute x0 -> x2, starting transfers between devices: none -> 2.01 us  [swapped(): return lax.ppermute(value, 'zl', [(i, i ^ apart) for i in range(ZL)])]
    all_to_all x1, blocking collectives: 15.1 us -> 13.5 us  [body(): far_sums = lax.all_to_all(dense, ALONG, 0, 0, tiled=True)]
    ppermute x14 -> x11, waiting for transfers between devices: 14.2 us -> 15.2 us  [shifted(): lax.ppermute(value, axis, [(i, (i + step) % length) for i in range(length)])]
    ppermute x14 -> x11, starting transfers between devices: 21.9 us -> 22 us  [shifted(): lax.ppermute(value, axis, [(i, (i + step) % length) for i in range(length)])]
  transfers between devices with their start and end apart: 17 -> 16, of which waited for: 7 -> 7; matrix products, arithmetic and copies ran while one was open for 3% -> 3% of each run, Pallas kernels for 12% -> 11%
where the time goes in v11:
time: 108 us; the launch traced here: 107 us
  starting transfers between devices  44.8 us (41%)
  waiting for transfers between devices  27.7 us (26%)
  Pallas kernels  15.8 us (15%)
  blocking collectives  13.5 us (12%)
  local copies, waits for them, and re-layouts  4.69 us (4%)
    ppermute x11, starting transfers between devices, shifted(): lax.ppermute(value, axis, [(i, (i + step) % length) for i in range(length)])  22 us
    ppermute x11, waiting for transfers between devices, shifted(): lax.ppermute(value, axis, [(i, (i + step) % length) for i in range(length)])  15.2 us
    all_to_all x1, blocking collectives, body(): far_sums = lax.all_to_all(dense, ALONG, 0, 0, tiled=True)  13.5 us
    all_to_all x1, starting transfers between devices, body(): returned = lax.all_to_all(picked, CROSS, 0, 0, tiled=True)  8.73 us
    all_to_all x1, starting transfers between devices, body(): near_sums = lax.all_to_all(sums, CROSS, 0, 0, tiled=True)  8.66 us
    all_to_all x1, waiting for transfers between devices, body(): residuals = lax.all_to_all(copies, ALONG, 0, 0, tiled=True)  5.77 us
    pallas_call x1, Pallas kernels, body(): call(frame_gradients, (shape(2, 128, NZ),) + (shape(2, 128, NZ, dtype=bf1...  4.64 us
    all_to_all x1, waiting for transfers between devices, body(): returned = lax.all_to_all(picked, CROSS, 0, 0, tiled=True)  3.65 us
  transfers between devices with their start and end apart: 16, of which 7 were waited for; matrix products, arithmetic and copies ran while one was open for 3% of the time, Pallas kernels for 11%

profile of v11, /device:TPU:1, one launch (start us, length us, event | category | flops | bytes accessed | tf_op | source)
XLA Modules:
  0.0 107.5 jit_solution(18348947880688827166)
XLA Ops:
  0.6 7.8 %collective-permute-start = (f32[128,128]{1,0:T(8,128)}, f32[128,128]{1,0:T(8,128)S(1)}, u32[]{:S(2)}, u32[]{:S(2)}) collective-permute-start(f32[128,128]{1,0:T(8,128)} %bitcast.19), channel_id=1, source_target_pairs={{0,4},{4,0},{1,5},{5,1},{2,6},{6,2},{3,7},{7,3},{8,12},{12,8},{9,1... | collective-permute-start | bytes 196616 | tf_op jit(solution)/shard_map/ray_sums/ppermute | solution.py:333
  8.5 3.3 %ray_sums.1 = bf16[32,4,16,256]{3,2,1,0:T(8,128)(2,1)} custom-call(bf16[32,2,32,256]{3,2,1,0:T(8,128)(2,1)} %bitcast.25, f32[512,128]{1,0:T(8,128)} %bitcast.17), custom_call_target="tpu_custom_call" | custom-call | flops 268435456 | bytes 1048576 | tf_op jit(solution)/shard_map/ray_sums/ray_sums/pallas_call | solution.py:360
  12.4 0.7 collective-permute-start.1
  13.2 1.7 %collective-permute-done.1 = s32[1,32]{1,0:T(1,128)S(1)} collective-permute-done((s32[1,32]{1,0:T(1,128)S(1)}, s32[1,32]{1,0:T(1,128)S(1)}, u32[]{:S(2)}, u32[]{:S(2)}) %collective-permute-start.1) | collective-permute-done | bytes 160 | tf_op jit(solution)/shard_map/targets/ppermute | solution.py:337
  14.8 1.3 %collective-permute-start.2 = (s32[2,32]{1,0:T(2,128)S(1)}, s32[2,32]{1,0:T(2,128)S(1)}, u32[]{:S(2)}, u32[]{:S(2)}) collective-permute-start(s32[2,32]{1,0:T(2,128)S(1)} %pad_add_fusion.near_ref), channel_id=1, source_target_pairs={{0,128},{64,192},{128,0},{192,64},{1,129},{65,193},{129,1},{193,65... | collective-permute-start | bytes 776 | tf_op jit(solution)/shard_map/targets/ppermute | solution.py:337
  16.8 1.4 %collective-permute-done.2.far_ref = s32[2,32]{1,0:T(2,128)S(1)} collective-permute-done((s32[2,32]{1,0:T(2,128)S(1)}, s32[2,32]{1,0:T(2,128)S(1)}, u32[]{:S(2)}, u32[]{:S(2)}) %collective-permute-start.2) | collective-permute-done | bytes 288 | tf_op jit(solution)/shard_map/targets/ppermute | solution.py:337
  18.8 1.4 %collective-permute-start.3 = (f32[296,128]{1,0:T(8,128)S(1)}, f32[296,128]{1,0:T(8,128)S(1)}, u32[]{:S(2)}, u32[]{:S(2)}) collective-permute-start(f32[296,128]{1,0:T(8,128)S(1)} %get-tuple-element.29), channel_id=1, source_target_pairs={{0,1},{1,2},{2,3},{3,0},{4,5},{5,6},{6,7},{7,4},{8,9},{9,10},{10,1... | collective-permute-start | bytes 454664 | tf_op jit(solution)/shard_map/fields/ppermute | solution.py:333
  20.2 2.6 %collective-permute-start.4 = (f32[296,128]{1,0:T(8,128)S(1)}, f32[296,128]{1,0:T(8,128)S(1)}, u32[]{:S(2)}, u32[]{:S(2)}) collective-permute-start(f32[296,128]{1,0:T(8,128)S(1)} %get-tuple-element.30), channel_id=1, source_target_pairs={{0,2},{1,3},{2,0},{3,1},{4,6},{5,7},{6,4},{7,5},{8,10},{9,11},{10,... | collective-permute-start | bytes 454664 | tf_op jit(solution)/shard_map/fields/ppermute | solution.py:333
  22.8 1.1 collective-permute-start.5
  23.9 8.7 %all-to-all-start = ((bf16[32,4,16,256]{3,2,1,0:T(8,128)(2,1)}), bf16[32,4,16,256]{3,2,1,0:T(8,128)(2,1)S(1)}, u32[]{:S(2)}, u32[]{:S(2)}) async-start(bf16[32,4,16,256]{3,2,1,0:T(8,128)(2,1)} %ray_sums.1), calls=%async_computation | async-start | bytes 2097152 | tf_op jit(solution)/shard_map/ray_sums/all_to_all | solution.py:370
  32.6 4.6 %frame_gradients.1 = (f32[2,128,128]{2,1,0:T(8,128)S(1)}, bf16[2,128,128]{2,1,0:T(8,128)(2,1)S(1)}, bf16[2,128,128]{2,1,0:T(8,128)(2,1)S(1)}, bf16[2,128,128]{2,1,0:T(8,128)(2,1)S(1)}) custom-call(s32[11]{0:T(128)S(1)} %pad_add_fusion.1.place_ref, f32[296,128]{1,0:T(8,128)S(1)} %get-tuple-element.28.field_0, f32[296,128]{1,0:T(8,128)S(1)} %collective-permute-done.3.field_1, ...), custom_call_target="tpu_custom_call" | custom-call | flops 20000000000 | bytes 1048576 | tf_op jit(solution)/shard_map/frames/frame_gradients/pallas_call | solution.py:385
  37.3 1.4 %collective-permute-start.6 = (bf16[2,128,128]{2,1,0:T(8,128)(2,1)S(1)}, bf16[2,128,128]{2,1,0:T(8,128)(2,1)S(1)}, u32[]{:S(2)}, u32[]{:S(2)}) collective-permute-start(bf16[2,128,128]{2,1,0:T(8,128)(2,1)S(1)} %get-tuple-element.33), channel_id=1, source_target_pairs={{0,1},{1,2},{2,3},{3,0},{4,5},{5,6},{6,7},{7,4},{8,9},{9,10},{10,1... | collective-permute-start | bytes 196616 | tf_op jit(solution)/shard_map/frames/ppermute | solution.py:333
  38.7 2.4 %collective-permute-start.7 = (bf16[2,128,128]{2,1,0:T(8,128)(2,1)S(1)}, bf16[2,128,128]{2,1,0:T(8,128)(2,1)S(1)}, u32[]{:S(2)}, u32[]{:S(2)}) collective-permute-start(bf16[2,128,128]{2,1,0:T(8,128)(2,1)S(1)} %get-tuple-element.34), channel_id=1, source_target_pairs={{0,2},{1,3},{2,0},{3,1},{4,6},{5,7},{6,4},{7,5},{8,10},{9,11},{10,... | collective-permute-start | bytes 196616 | tf_op jit(solution)/shard_map/frames/ppermute | solution.py:333
  41.1 1.2 %collective-permute-start.8 = (bf16[2,128,128]{2,1,0:T(8,128)(2,1)S(1)}, bf16[2,128,128]{2,1,0:T(8,128)(2,1)S(1)}, u32[]{:S(2)}, u32[]{:S(2)}) collective-permute-start(bf16[2,128,128]{2,1,0:T(8,128)(2,1)S(1)} %get-tuple-element.35), channel_id=1, source_target_pairs={{0,3},{1,0},{2,1},{3,2},{4,7},{5,4},{6,5},{7,6},{8,11},{9,8},{10,9... | collective-permute-start | bytes 196616 | tf_op jit(solution)/shard_map/frames/ppermute | solution.py:333
  42.3 4.2 %collective-permute-done.6.inter_1 = bf16[2,128,128]{2,1,0:T(8,128)(2,1)S(1)} collective-permute-done((bf16[2,128,128]{2,1,0:T(8,128)(2,1)S(1)}, bf16[2,128,128]{2,1,0:T(8,128)(2,1)S(1)}, u32[]{:S(2)}, u32[]{:S(2)}) %collective-permute-start.6) | collective-permute-done | bytes 65568 | tf_op jit(solution)/shard_map/frames/ppermute | solution.py:333
  46.6 4.3 %collective-permute-done.7.inter_2 = bf16[2,128,128]{2,1,0:T(8,128)(2,1)S(1)} collective-permute-done((bf16[2,128,128]{2,1,0:T(8,128)(2,1)S(1)}, bf16[2,128,128]{2,1,0:T(8,128)(2,1)S(1)}, u32[]{:S(2)}, u32[]{:S(2)}) %collective-permute-start.7) | collective-permute-done | bytes 65568 | tf_op jit(solution)/shard_map/frames/ppermute | solution.py:333
  50.9 1.5 %add_tiles.1 = (bf16[8,128,128]{2,1,0:T(8,128)(2,1)S(1)}, f32[2,128,128]{2,1,0:T(8,128)S(1)}) custom-call(s32[11]{0:T(128)S(1)} %pad_add_fusion.1.place_ref, s32[16,32]{1,0:T(8,128)S(1)} %maximum_convert_fusion.table_ref, bf16[32,4,16,256]{3,2,1,0:T(8,128)(2,1)S(1)} %all-to-all-done.sums_ref, f32[2,128,128]{2,1,0:T(8,128)S(1)} %get-tuple-element.32.inter_0, ...), custom_call_target="tpu_custom_call" | custom-call | flops 1000000 | bytes 1048576 | tf_op jit(solution)/shard_map/near_sum/add_tiles/pallas_call | solution.py:400
  52.4 13.5 %all_to_all.20.sums_ref = bf16[8,128,128]{2,1,0:T(8,128)(2,1)S(1)} all-to-all(bf16[8,128,128]{2,1,0:T(8,128)(2,1)S(1)} %get-tuple-element.36), channel_id=1, replica_groups=mesh['zl'=4,'x'=4,'c'=2,'zh'=2,'y'=4] {'zh','zl'}, dimensions={0} | all-to-all | bytes 524288 | tf_op jit(solution)/shard_map/near_sum/all_to_all | solution.py:408
  65.9 0.8 residual_part.1
  66.6 3.4 %all-to-all-start.2 = ((bf16[8,128,128]{2,1,0:T(8,128)(2,1)}), bf16[8,128,128]{2,1,0:T(8,128)(2,1)S(1)}, u32[]{:S(2)}, u32[]{:S(2)}) async-start(bf16[8,128,128]{2,1,0:T(8,128)(2,1)} %get-tuple-element.37), calls=%async_computation.2 | async-start | bytes 524288 | tf_op jit(solution)/shard_map/residual/all_to_all | solution.py:414
  70.7 0.9 collective-permute-start.10
  71.6 1.7 %collective-permute-start.11 = (f32[2,3,16,128]{3,2,1,0:T(8,128)S(1)}, f32[2,3,16,128]{3,2,1,0:T(8,128)S(1)}, u32[]{:S(2)}, u32[]{:S(2)}) collective-permute-start(f32[2,3,16,128]{3,2,1,0:T(8,128)S(1)} %get-tuple-element.43), channel_id=1, source_target_pairs={{0,3},{1,0},{2,1},{3,2},{4,7},{5,4},{6,5},{7,6},{8,11},{9,8},{10,9... | collective-permute-start | bytes 147464 | tf_op jit(solution)/shard_map/residual/ppermute | solution.py:333
  73.4 5.8 %all-to-all-done.2.residual_ref = bf16[8,128,128]{2,1,0:T(8,128)(2,1)S(1)} async-done(((bf16[8,128,128]{2,1,0:T(8,128)(2,1)}), bf16[8,128,128]{2,1,0:T(8,128)(2,1)S(1)}, u32[]{:S(2)}, u32[]{:S(2)}) %all-to-all-start.2) | async-done | bytes 262176 | tf_op jit(solution)/shard_map/residual/all_to_all | solution.py:414
  79.1 2.1 %pick_tiles.1 = bf16[32,4,16,256]{3,2,1,0:T(8,128)(2,1)} custom-call(s32[11]{0:T(128)S(1)} %pad_add_fusion.1.place_ref, s32[16,32]{1,0:T(8,128)S(1)} %maximum_convert_fusion.table_ref, bf16[8,128,128]{2,1,0:T(8,128)(2,1)S(1)} %all-to-all-done.2.residual_ref), custom_call_target="tpu_custom_call" | custom-call | flops 1000000 | bytes 1048576 | tf_op jit(solution)/shard_map/pick/pick_tiles/pallas_call | solution.py:419
  81.3 8.7 %all-to-all-start.3 = ((bf16[32,4,16,256]{3,2,1,0:T(8,128)(2,1)}), bf16[32,4,16,256]{3,2,1,0:T(8,128)(2,1)S(1)}, u32[]{:S(2)}, u32[]{:S(2)}) async-start(bf16[32,4,16,256]{3,2,1,0:T(8,128)(2,1)} %pick_tiles.1), calls=%async_computation.3 | async-start | bytes 2097152 | tf_op jit(solution)/shard_map/pick/all_to_all | solution.py:428
  90.8 1.4 %collective-permute-start.12 = (f32[4,3,16,128]{3,2,1,0:T(8,128)S(1)}, f32[4,3,16,128]{3,2,1,0:T(8,128)S(1)}, u32[]{:S(2)}, u32[]{:S(2)}) collective-permute-start(f32[4,3,16,128]{3,2,1,0:T(8,128)S(1)} %pad_maximum_fusion), channel_id=1, source_target_pairs={{0,4},{4,0},{1,5},{5,1},{2,6},{6,2},{3,7},{7,3},{8,12},{12,8},{9,1... | collective-permute-start | bytes 294920 | tf_op jit(solution)/shard_map/updates/ppermute | solution.py:333
  92.2 1.1 %copy.14 = bf16[256,8,4,4,2,8]{0,5,4,3,2,1:T(8,128)(2,1)} copy(bf16[256,8,4,4,2,8]{0,5,2,4,1,3:T(8,128)(2,1)S(1)} %bitcast.26) | data formatting | bytes 2097152 | tf_op jit(solution)/shard_map/back_project/transpose | solution.py:437
  93.3 1.5 %copy.15.radon_ref = bf16[256,2048]{1,0:T(8,128)(2,1)S(1)} copy(bf16[256,2048]{0,1:T(8,128)(2,1)} %bitcast.27) | data formatting | bytes 2097152 | tf_op jit(solution)/shard_map/back_project/reshape | solution.py:437
  94.8 6.6 %collective-permute-done.12.theirs_ref = f32[4,3,16,128]{3,2,1,0:T(8,128)S(1)} collective-permute-done((f32[4,3,16,128]{3,2,1,0:T(8,128)S(1)}, f32[4,3,16,128]{3,2,1,0:T(8,128)S(1)}, u32[]{:S(2)}, u32[]{:S(2)}) %collective-permute-start.12) | collective-permute-done | bytes 98336 | tf_op jit(solution)/shard_map/updates/ppermute | solution.py:333
  101.4 1.2 %updates.1 = (f32[128,128]{1,0:T(8,128)}, f32[128,128]{1,0:T(8,128)}) custom-call(s32[11]{0:T(128)S(1)} %pad_add_fusion.1.place_ref, f32[2,3,16,128]{3,2,1,0:T(8,128)S(1)} %get-tuple-element.44.own_ref, f32[2,3,16,128]{3,2,1,0:T(8,128)S(1)} %copy-done.4, f32[2,3,16,128]{3,2,1,0:T(8,128)S(1)} %copy-done.6, ...), custom_call_target="tpu_custom_call" | custom-call | flops 1000000 | bytes 1048576 | tf_op jit(solution)/shard_map/updates/updates/pallas_call | solution.py:432
  102.7 3.6 %all-to-all-done.3.picked_ref = bf16[32,4,16,256]{3,2,1,0:T(8,128)(2,1)S(1)} async-done(((bf16[32,4,16,256]{3,2,1,0:T(8,128)(2,1)}), bf16[32,4,16,256]{3,2,1,0:T(8,128)(2,1)S(1)}, u32[]{:S(2)}, u32[]{:S(2)}) %all-to-all-start.3) | async-done | bytes 1048608 | tf_op jit(solution)/shard_map/pick/all_to_all | solution.py:428
  106.3 1.1 %back_project.1 = f32[512,128]{1,0:T(8,128)} custom-call(bf16[256,2048]{1,0:T(8,128)(2,1)S(1)} %copy.15.radon_ref, bf16[32,4,16,256]{3,2,1,0:T(8,128)(2,1)S(1)} %all-to-all-done.3.picked_ref, f32[512,128]{1,0:T(8,128)S(1)} %bitcast.18), custom_call_target="tpu_custom_call" | custom-call | flops 268435456 | bytes 1048576 | tf_op jit(solution)/shard_map/back_project/back_project/pallas_call | solution.py:438
  (52 shorter events, 3.5 us)
Async XLA Ops:
  0.6 16.2 %collective-permute-start = (f32[128,128]{1,0:T(8,128)}, f32[128,128]{1,0:T(8,128)S(1)}, u32[]{:S(2)}, u32[]{:S(2)}) collective-permute-start(f32[128,128]{1,0:T(8,128)} %bitcast.19), channel_id=1, source_target_pairs={{0,4},{4,0},{1,5},{5,1},{2,6},{6,2},{3,7},{7,3},{8,12},{12,8},{9,1... | collective-permute-start | bytes 196616 | tf_op jit(solution)/shard_map/ray_sums/ppermute | solution.py:333
  8.5 9.8 %copy-start.1 = (f32[1,64,2,128]{3,2,1,0:T(2,128)S(1)}, f32[1,64,2,128]{3,2,1,0:T(2,128)}, u32[]{:S(2)}) copy-start(f32[1,64,2,128]{3,2,1,0:T(2,128)} %param.12) | copy-start | bytes 196612
  8.5 9.8 %copy-start.2 = (f32[1,64,2,128]{3,2,1,0:T(2,128)S(1)}, f32[1,64,2,128]{3,2,1,0:T(2,128)}, u32[]{:S(2)}) copy-start(f32[1,64,2,128]{3,2,1,0:T(2,128)} %param.13) | copy-start | bytes 196612
  11.8 0.7 copy-start.12
  12.4 2.4 %collective-permute-start.1 = (s32[1,32]{1,0:T(1,128)S(1)}, s32[1,32]{1,0:T(1,128)S(1)}, u32[]{:S(2)}, u32[]{:S(2)}) collective-permute-start(s32[1,32]{1,0:T(1,128)S(1)} %bitcast.30), channel_id=1, source_target_pairs={{0,64},{64,0},{128,192},{192,128},{1,65},{65,1},{129,193},{193,129... | collective-permute-start | bytes 392 | tf_op jit(solution)/shard_map/targets/ppermute | solution.py:337
  14.8 3.4 %collective-permute-start.2 = (s32[2,32]{1,0:T(2,128)S(1)}, s32[2,32]{1,0:T(2,128)S(1)}, u32[]{:S(2)}, u32[]{:S(2)}) collective-permute-start(s32[2,32]{1,0:T(2,128)S(1)} %pad_add_fusion.near_ref), channel_id=1, source_target_pairs={{0,128},{64,192},{128,0},{192,64},{1,129},{65,193},{129,1},{193,65... | collective-permute-start | bytes 776 | tf_op jit(solution)/shard_map/targets/ppermute | solution.py:337
  16.1 0.7 copy-start.11
  18.8 13.8 %collective-permute-start.3 = (f32[296,128]{1,0:T(8,128)S(1)}, f32[296,128]{1,0:T(8,128)S(1)}, u32[]{:S(2)}, u32[]{:S(2)}) collective-permute-start(f32[296,128]{1,0:T(8,128)S(1)} %get-tuple-element.29), channel_id=1, source_target_pairs={{0,1},{1,2},{2,3},{3,0},{4,5},{5,6},{6,7},{7,4},{8,9},{9,10},{10,1... | collective-permute-start | bytes 454664 | tf_op jit(solution)/shard_map/fields/ppermute | solution.py:333
  20.2 12.4 %collective-permute-start.4 = (f32[296,128]{1,0:T(8,128)S(1)}, f32[296,128]{1,0:T(8,128)S(1)}, u32[]{:S(2)}, u32[]{:S(2)}) collective-permute-start(f32[296,128]{1,0:T(8,128)S(1)} %get-tuple-element.30), channel_id=1, source_target_pairs={{0,2},{1,3},{2,0},{3,1},{4,6},{5,7},{6,4},{7,5},{8,10},{9,11},{10,... | collective-permute-start | bytes 454664 | tf_op jit(solution)/shard_map/fields/ppermute | solution.py:333
  22.8 9.8 %copy-start.7 = (f32[1,8,128,128]{3,2,1,0:T(8,128)S(1)}, f32[1,8,128,128]{3,2,1,0:T(8,128)}, u32[]{:S(2)}) copy-start(f32[1,8,128,128]{3,2,1,0:T(8,128)} %param.9) | copy-start | bytes 1572868
  22.8 9.8 %copy-start.8 = (f32[2,128,128]{2,1,0:T(8,128)S(1)}, f32[2,128,128]{2,1,0:T(8,128)}, u32[]{:S(2)}) copy-start(f32[2,128,128]{2,1,0:T(8,128)} %probe_ref.1) | copy-start | bytes 393220
  22.8 9.8 %copy-start.9 = (bf16[4,128,128]{2,1,0:T(8,128)(2,1)S(1)}, bf16[4,128,128]{2,1,0:T(8,128)(2,1)}, u32[]{:S(2)}) copy-start(bf16[4,128,128]{2,1,0:T(8,128)(2,1)} %constant.15.clone.dft_ref) | copy-start | bytes 393220
  22.8 9.8 %collective-permute-start.5 = (f32[296,128]{1,0:T(8,128)S(1)}, f32[296,128]{1,0:T(8,128)S(1)}, u32[]{:S(2)}, u32[]{:S(2)}) collective-permute-start(f32[296,128]{1,0:T(8,128)S(1)} %get-tuple-element.31), channel_id=1, source_target_pairs={{0,3},{1,0},{2,1},{3,2},{4,7},{5,4},{6,5},{7,6},{8,11},{9,8},{10,9... | collective-permute-start | bytes 454664 | tf_op jit(solution)/shard_map/fields/ppermute | solution.py:333
  23.9 27.0 %all-to-all-start = ((bf16[32,4,16,256]{3,2,1,0:T(8,128)(2,1)}), bf16[32,4,16,256]{3,2,1,0:T(8,128)(2,1)S(1)}, u32[]{:S(2)}, u32[]{:S(2)}) async-start(bf16[32,4,16,256]{3,2,1,0:T(8,128)(2,1)} %ray_sums.1), calls=%async_computation | async-start | bytes 2097152 | tf_op jit(solution)/shard_map/ray_sums/all_to_all | solution.py:370
  37.3 9.3 %collective-permute-start.6 = (bf16[2,128,128]{2,1,0:T(8,128)(2,1)S(1)}, bf16[2,128,128]{2,1,0:T(8,128)(2,1)S(1)}, u32[]{:S(2)}, u32[]{:S(2)}) collective-permute-start(bf16[2,128,128]{2,1,0:T(8,128)(2,1)S(1)} %get-tuple-element.33), channel_id=1, source_target_pairs={{0,1},{1,2},{2,3},{3,0},{4,5},{5,6},{6,7},{7,4},{8,9},{9,10},{10,1... | collective-permute-start | bytes 196616 | tf_op jit(solution)/shard_map/frames/ppermute | solution.py:333
  38.7 12.1 %collective-permute-start.7 = (bf16[2,128,128]{2,1,0:T(8,128)(2,1)S(1)}, bf16[2,128,128]{2,1,0:T(8,128)(2,1)S(1)}, u32[]{:S(2)}, u32[]{:S(2)}) collective-permute-start(bf16[2,128,128]{2,1,0:T(8,128)(2,1)S(1)} %get-tuple-element.34), channel_id=1, source_target_pairs={{0,2},{1,3},{2,0},{3,1},{4,6},{5,7},{6,4},{7,5},{8,10},{9,11},{10,... | collective-permute-start | bytes 196616 | tf_op jit(solution)/shard_map/frames/ppermute | solution.py:333
  41.1 9.7 %collective-permute-start.8 = (bf16[2,128,128]{2,1,0:T(8,128)(2,1)S(1)}, bf16[2,128,128]{2,1,0:T(8,128)(2,1)S(1)}, u32[]{:S(2)}, u32[]{:S(2)}) collective-permute-start(bf16[2,128,128]{2,1,0:T(8,128)(2,1)S(1)} %get-tuple-element.35), channel_id=1, source_target_pairs={{0,3},{1,0},{2,1},{3,2},{4,7},{5,4},{6,5},{7,6},{8,11},{9,8},{10,9... | collective-permute-start | bytes 196616 | tf_op jit(solution)/shard_map/frames/ppermute | solution.py:333
  66.6 12.5 %all-to-all-start.2 = ((bf16[8,128,128]{2,1,0:T(8,128)(2,1)}), bf16[8,128,128]{2,1,0:T(8,128)(2,1)S(1)}, u32[]{:S(2)}, u32[]{:S(2)}) async-start(bf16[8,128,128]{2,1,0:T(8,128)(2,1)} %get-tuple-element.37), calls=%async_computation.2 | async-start | bytes 524288 | tf_op jit(solution)/shard_map/residual/all_to_all | solution.py:414
  70.6 10.6 %collective-permute-start.9 = (f32[2,3,16,128]{3,2,1,0:T(8,128)S(1)}, f32[2,3,16,128]{3,2,1,0:T(8,128)S(1)}, u32[]{:S(2)}, u32[]{:S(2)}) collective-permute-start(f32[2,3,16,128]{3,2,1,0:T(8,128)S(1)} %get-tuple-element.41), channel_id=1, source_target_pairs={{0,1},{1,2},{2,3},{3,0},{4,5},{5,6},{6,7},{7,4},{8,9},{9,10},{10,1... | collective-permute-start | bytes 147464 | tf_op jit(solution)/shard_map/residual/ppermute | solution.py:333
  70.7 10.5 %collective-permute-start.10 = (f32[2,3,16,128]{3,2,1,0:T(8,128)S(1)}, f32[2,3,16,128]{3,2,1,0:T(8,128)S(1)}, u32[]{:S(2)}, u32[]{:S(2)}) collective-permute-start(f32[2,3,16,128]{3,2,1,0:T(8,128)S(1)} %get-tuple-element.42), channel_id=1, source_target_pairs={{0,2},{1,3},{2,0},{3,1},{4,6},{5,7},{6,4},{7,5},{8,10},{9,11},{10,... | collective-permute-start | bytes 147464 | tf_op jit(solution)/shard_map/residual/ppermute | solution.py:333
  71.6 9.6 %collective-permute-start.11 = (f32[2,3,16,128]{3,2,1,0:T(8,128)S(1)}, f32[2,3,16,128]{3,2,1,0:T(8,128)S(1)}, u32[]{:S(2)}, u32[]{:S(2)}) collective-permute-start(f32[2,3,16,128]{3,2,1,0:T(8,128)S(1)} %get-tuple-element.43), channel_id=1, source_target_pairs={{0,3},{1,0},{2,1},{3,2},{4,7},{5,4},{6,5},{7,6},{8,11},{9,8},{10,9... | collective-permute-start | bytes 147464 | tf_op jit(solution)/shard_map/residual/ppermute | solution.py:333
  81.2 8.8 %copy-start.3 = (f32[2,3,16,128]{3,2,1,0:T(8,128)}, f32[2,3,16,128]{3,2,1,0:T(8,128)S(1)}, u32[]{:S(2)}) copy-start(f32[2,3,16,128]{3,2,1,0:T(8,128)S(1)} %collective-permute-done.9.one_ref) | copy-start | bytes 147460
  81.2 8.8 %copy-start.5 = (f32[2,3,16,128]{3,2,1,0:T(8,128)}, f32[2,3,16,128]{3,2,1,0:T(8,128)S(1)}, u32[]{:S(2)}) copy-start(f32[2,3,16,128]{3,2,1,0:T(8,128)S(1)} %collective-permute-done.10.two_ref) | copy-start | bytes 147460
  81.3 10.9 %copy-start.10 = (bf16[1,32,2,32,256]{4,3,2,1,0:T(8,128)(2,1)S(1)}, bf16[1,32,2,32,256]{4,3,2,1,0:T(8,128)(2,1)}, u32[]{:S(2)}) copy-start(bf16[1,32,2,32,256]{4,3,2,1,0:T(8,128)(2,1)} %param.15) | copy-start | bytes 3145732
  81.3 25.1 %all-to-all-start.3 = ((bf16[32,4,16,256]{3,2,1,0:T(8,128)(2,1)}), bf16[32,4,16,256]{3,2,1,0:T(8,128)(2,1)S(1)}, u32[]{:S(2)}, u32[]{:S(2)}) async-start(bf16[32,4,16,256]{3,2,1,0:T(8,128)(2,1)} %pick_tiles.1), calls=%async_computation.3 | async-start | bytes 2097152 | tf_op jit(solution)/shard_map/pick/all_to_all | solution.py:428
  90.0 0.7 slice-start
  90.1 0.7 slice-start.1
  90.8 10.6 %collective-permute-start.12 = (f32[4,3,16,128]{3,2,1,0:T(8,128)S(1)}, f32[4,3,16,128]{3,2,1,0:T(8,128)S(1)}, u32[]{:S(2)}, u32[]{:S(2)}) collective-permute-start(f32[4,3,16,128]{3,2,1,0:T(8,128)S(1)} %pad_maximum_fusion), channel_id=1, source_target_pairs={{0,4},{4,0},{1,5},{5,1},{2,6},{6,2},{3,7},{7,3},{8,12},{12,8},{9,1... | collective-permute-start | bytes 294920 | tf_op jit(solution)/shard_map/updates/ppermute | solution.py:333
  93.3 8.2 %copy-start.4 = (f32[2,3,16,128]{3,2,1,0:T(8,128)S(1)}, f32[2,3,16,128]{3,2,1,0:T(8,128)}, u32[]{:S(2)}) copy-start(f32[2,3,16,128]{3,2,1,0:T(8,128)} %copy-done.3) | copy-start | bytes 147460
  93.3 8.2 %copy-start.6 = (f32[2,3,16,128]{3,2,1,0:T(8,128)S(1)}, f32[2,3,16,128]{3,2,1,0:T(8,128)}, u32[]{:S(2)}) copy-start(f32[2,3,16,128]{3,2,1,0:T(8,128)} %copy-done.5) | copy-start | bytes 147460
  94.8 11.6 %copy-start = (f32[256,2,128]{2,1,0:T(2,128)S(1)}, f32[256,2,128]{2,1,0:T(2,128)}, u32[]{:S(2)}) copy-start(f32[256,2,128]{2,1,0:T(2,128)} %param.14) | copy-start | bytes 786436

commit v12 on v10

--- a/solution.py
+++ b/solution.py
@@ -155,14 +155,26 @@
                 ref[other, 1 + part] = inter_ref[part, rows, :]
 
 
-def pick_tiles(place_ref, table_0, table_1, table_2, table_3, residual_ref, out_ref, rows_ref):
+def pick_tiles(place_ref, table_0, table_1, table_2, table_3, residual_ref, out_far, rows_ref, out_ref, sems):
+    tables = (table_0, table_1, table_2, table_3)
+    zl_here = place_ref[2]
     for zl in range(ZL):
         rows_ref[zl] = jnp.concatenate(
             [residual_ref[zl].astype(f32), residual_ref[ZL + zl].astype(f32)], axis=1
         )
-
-    for zl, near, row in each_tile(place_ref, (table_0, table_1, table_2, table_3)):
-        out_ref[near, zl] = rows_ref[zl, pl.ds(row, HITS * QR), :].astype(bf16)
+    copies = []
+    for back_y in range(Y):
+        y = lax.rem(place_ref[1] + Y - back_y, Y)
+        for xc in range(XC):
+            near = xc * Y + y
+            for back_zl in range(ZL):
+                zl = lax.rem(zl_here + ZL - back_zl, ZL)
+                row = pl.multiple_of(tables[back_zl][back_y, zl_here * XC + xc] * QR, QR)
+                out_ref[near, zl] = rows_ref[zl, pl.ds(row, HITS * QR), :].astype(bf16)
+            copies.append(pltpu.make_async_copy(out_ref.at[near], out_far.at[near], sems.at[back_y * XC + xc]))
+            copies[-1].start()
+    for copy in copies:
+        copy.wait()
 
 
 def back_project(radon_ref, picked_ref, volume_ref, out_ref):
@@ -413,13 +425,19 @@
         kept = round_y(kept)
 
     with jax.named_scope("pick"):
-        picked = call(
+        picked = pl.pallas_call(
             pick_tiles,
-            shape(NEAR, ZL, HITS * QR, 2 * NZ, dtype=bf16),
-            5,
-            1,
-            scratch=[pltpu.VMEM((ZL, 128, 2 * NZ), f32)],
-            flops=1_000_000,
+            out_shape=shape(NEAR, ZL, HITS * QR, 2 * NZ, dtype=bf16),
+            in_specs=[SM] * 5 + [VM],
+            out_specs=FAR,
+            scratch_shapes=[
+                pltpu.VMEM((ZL, 128, 2 * NZ), f32),
+                pltpu.VMEM((NEAR, ZL, HITS * QR, 2 * NZ), bf16),
+                pltpu.SemaphoreType.DMA((NEAR,)),
+            ],
+            compiler_params=pltpu.CompilerParams(vmem_limit_bytes=48 << 20),
+            cost_estimate=pl.CostEstimate(flops=1_000_000, bytes_accessed=1 << 20, transcendentals=0),
+            name="pick_tiles",
         )(place, *tables, residuals)
         picked, kept = lax.optimization_barrier((picked, kept))
         returned = lax.all_to_all(picked, CROSS, 0, 0, tiled=True)

time: 103 us -> 103 us (level)
  transfers between devices with their start and end apart: 17 -> 17, of which waited for: 7 -> 7; matrix products, arithmetic and copies ran while one was open for 3% -> 3% of each run, Pallas kernels for 12% -> 11%
where the time goes in v12:
time: 103 us
  starting transfers between devices  42.7 us (41%)
  waiting for transfers between devices  23.5 us (23%)
  Pallas kernels  15.7 us (15%)
  blocking collectives  15.1 us (15%)
  local copies, waits for them, and re-layouts  4.73 us (5%)
    ppermute x14, starting transfers between devices, shifted(): lax.ppermute(value, axis, [(i, (i + step) % length) for i in range(length)])  22 us
    all_to_all x1, blocking collectives, body(): far_sums = lax.all_to_all(dense, ALONG, 0, 0, tiled=True)  15.1 us
    ppermute x14, waiting for transfers between devices, shifted(): lax.ppermute(value, axis, [(i, (i + step) % length) for i in range(length)])  14.2 us
    all_to_all x1, starting transfers between devices, body(): returned = lax.all_to_all(picked, CROSS, 0, 0, tiled=True)  9.23 us
    all_to_all x1, starting transfers between devices, body(): near_sums = lax.all_to_all(sums, CROSS, 0, 0, tiled=True)  7.95 us
    all_to_all x1, waiting for transfers between devices, body(): residuals = lax.all_to_all(copies, ALONG, 0, 0, tiled=True)  5.68 us
    pallas_call x1, Pallas kernels, body(): call(frame_gradients, (shape(2, 128, NZ),) + (shape(2, 128, NZ, dtype=bf1...  4.63 us
    all_to_all x1, waiting for transfers between devices, body(): returned = lax.all_to_all(picked, CROSS, 0, 0, tiled=True)  3.65 us
  transfers between devices with their start and end apart: 17, of which 7 were waited for; matrix products, arithmetic and copies ran while one was open for 3% of the time, Pallas kernels for 11%

profile of v12, /device:TPU:1, one launch (start us, length us, event | category | flops | bytes accessed | tf_op | source)
XLA Modules:
  0.0 102.8 jit_solution(664366331890911797)
XLA Ops:
  0.6 7.8 %collective-permute-start = (f32[128,128]{1,0:T(8,128)}, f32[128,128]{1,0:T(8,128)S(1)}, u32[]{:S(2)}, u32[]{:S(2)}) collective-permute-start(f32[128,128]{1,0:T(8,128)} %bitcast.19), channel_id=1, source_target_pairs={{0,4},{4,0},{1,5},{5,1},{2,6},{6,2},{3,7},{7,3},{8,12},{12,8},{9,1... | collective-permute-start | bytes 196616 | tf_op jit(solution)/shard_map/ray_sums/ppermute | solution.py:343
  8.5 0.7 copy-done.14
  9.2 3.3 %ray_sums.1 = (bf16[32,4,16,256]{3,2,1,0:T(8,128)(2,1)}, f32[8,128]{1,0:T(8,128)}) custom-call(bf16[32,2,32,256]{3,2,1,0:T(8,128)(2,1)} %bitcast.25, f32[512,128]{1,0:T(8,128)} %bitcast.17, s32[1,32]{1,0:T(1,128)} %bitcast.29), custom_call_target="tpu_custom_call" | custom-call | flops 268435456 | bytes 1048576 | tf_op jit(solution)/shard_map/ray_sums/ray_sums/pallas_call | solution.py:366
  13.8 2.8 %collective-permute-start.3 = (f32[296,128]{1,0:T(8,128)S(1)}, f32[296,128]{1,0:T(8,128)S(1)}, u32[]{:S(2)}, u32[]{:S(2)}) collective-permute-start(f32[296,128]{1,0:T(8,128)S(1)} %get-tuple-element.38), channel_id=1, source_target_pairs={{0,3},{1,0},{2,1},{3,2},{4,7},{5,4},{6,5},{7,6},{8,11},{9,8},{10,9... | collective-permute-start | bytes 454664 | tf_op jit(solution)/shard_map/fields/ppermute | solution.py:343
  17.0 0.7 collective-permute-start.1
  17.7 7.9 %all-to-all-start = ((bf16[32,4,16,256]{3,2,1,0:T(8,128)(2,1)}), bf16[32,4,16,256]{3,2,1,0:T(8,128)(2,1)S(1)}, u32[]{:S(2)}, u32[]{:S(2)}) async-start(bf16[32,4,16,256]{3,2,1,0:T(8,128)(2,1)} %get-tuple-element.31), calls=%async_computation | async-start | bytes 2097152 | tf_op jit(solution)/shard_map/ray_sums/all_to_all | solution.py:381
  25.7 1.4 %collective-permute-done.1.field_1 = f32[296,128]{1,0:T(8,128)S(1)} collective-permute-done((f32[296,128]{1,0:T(8,128)S(1)}, f32[296,128]{1,0:T(8,128)S(1)}, u32[]{:S(2)}, u32[]{:S(2)}) %collective-permute-start.1) | collective-permute-done | bytes 151584 | tf_op jit(solution)/shard_map/fields/ppermute | solution.py:343
  27.1 4.6 %frame_gradients.1 = (f32[2,128,128]{2,1,0:T(8,128)S(1)}, bf16[2,128,128]{2,1,0:T(8,128)(2,1)S(1)}, bf16[2,128,128]{2,1,0:T(8,128)(2,1)S(1)}, bf16[2,128,128]{2,1,0:T(8,128)(2,1)S(1)}) custom-call(s32[11]{0:T(128)S(1)} %pad_add_fusion.place_ref, f32[296,128]{1,0:T(8,128)S(1)} %get-tuple-element.35.field_0, f32[296,128]{1,0:T(8,128)S(1)} %collective-permute-done.1.field_1, ...), custom_call_target="tpu_custom_call" | custom-call | flops 20000000000 | bytes 1048576 | tf_op jit(solution)/shard_map/frames/frame_gradients/pallas_call | solution.py:391
  31.8 2.4 %collective-permute-start.8 = (bf16[2,128,128]{2,1,0:T(8,128)(2,1)S(1)}, bf16[2,128,128]{2,1,0:T(8,128)(2,1)S(1)}, u32[]{:S(2)}, u32[]{:S(2)}) collective-permute-start(bf16[2,128,128]{2,1,0:T(8,128)(2,1)S(1)} %get-tuple-element.42), channel_id=1, source_target_pairs={{0,2},{1,3},{2,0},{3,1},{4,6},{5,7},{6,4},{7,5},{8,10},{9,11},{10,... | collective-permute-start | bytes 196616 | tf_op jit(solution)/shard_map/frames/ppermute | solution.py:343
  34.2 1.2 %collective-permute-start.9 = (bf16[2,128,128]{2,1,0:T(8,128)(2,1)S(1)}, bf16[2,128,128]{2,1,0:T(8,128)(2,1)S(1)}, u32[]{:S(2)}, u32[]{:S(2)}) collective-permute-start(bf16[2,128,128]{2,1,0:T(8,128)(2,1)S(1)} %get-tuple-element.43), channel_id=1, source_target_pairs={{0,3},{1,0},{2,1},{3,2},{4,7},{5,4},{6,5},{7,6},{8,11},{9,8},{10,9... | collective-permute-start | bytes 196616 | tf_op jit(solution)/shard_map/frames/ppermute | solution.py:343
  35.4 0.8 collective-permute-start.4
  36.2 1.2 %collective-permute-start.5 = (s32[4,32]{1,0:T(4,128)S(1)}, s32[4,32]{1,0:T(4,128)S(1)}, u32[]{:S(2)}, u32[]{:S(2)}) collective-permute-start(s32[4,32]{1,0:T(4,128)S(1)} %maximum_convert_fusion.table_0), channel_id=1, source_target_pairs={{0,128},{64,192},{128,0},{192,64},{1,129},{65,193},{129,1},{193,65... | collective-permute-start | bytes 1544 | tf_op jit(solution)/shard_map/targets/ppermute | solution.py:343
  37.4 2.6 %collective-permute-done.4.table_1 = s32[4,32]{1,0:T(4,128)S(1)} collective-permute-done((s32[4,32]{1,0:T(4,128)S(1)}, s32[4,32]{1,0:T(4,128)S(1)}, u32[]{:S(2)}, u32[]{:S(2)}) %collective-permute-start.4) | collective-permute-done | bytes 544 | tf_op jit(solution)/shard_map/targets/ppermute | solution.py:343
  40.0 2.7 %collective-permute-done.6.table_3 = s32[4,32]{1,0:T(4,128)S(1)} collective-permute-done((s32[4,32]{1,0:T(4,128)S(1)}, s32[4,32]{1,0:T(4,128)S(1)}, u32[]{:S(2)}, u32[]{:S(2)}) %collective-permute-start.6) | collective-permute-done | bytes 544 | tf_op jit(solution)/shard_map/targets/ppermute | solution.py:343
  42.7 1.2 %collective-permute-done.8.inter_2 = bf16[2,128,128]{2,1,0:T(8,128)(2,1)S(1)} collective-permute-done((bf16[2,128,128]{2,1,0:T(8,128)(2,1)S(1)}, bf16[2,128,128]{2,1,0:T(8,128)(2,1)S(1)}, u32[]{:S(2)}, u32[]{:S(2)}) %collective-permute-start.8) | collective-permute-done | bytes 65568 | tf_op jit(solution)/shard_map/frames/ppermute | solution.py:343
  44.0 1.5 %add_tiles.1 = (bf16[8,128,128]{2,1,0:T(8,128)(2,1)S(1)}, f32[2,128,128]{2,1,0:T(8,128)S(1)}) custom-call(s32[11]{0:T(128)S(1)} %pad_add_fusion.place_ref, s32[4,32]{1,0:T(4,128)S(1)} %maximum_convert_fusion.table_0, s32[4,32]{1,0:T(4,128)S(1)} %collective-permute-done.4.table_1, s32[4,32]{1,0:T(4,128)S(1)} %collective-permute-done.5.table_2, ...), custom_call_target="tpu_custom_call" | custom-call | flops 1000000 | bytes 1048576 | tf_op jit(solution)/shard_map/near_sum/add_tiles/pallas_call | solution.py:409
  45.4 15.1 %all_to_all.20.sums_ref = bf16[8,128,128]{2,1,0:T(8,128)(2,1)S(1)} all-to-all(bf16[8,128,128]{2,1,0:T(8,128)(2,1)S(1)} %get-tuple-element.44), channel_id=1, replica_groups=mesh['zl'=4,'x'=4,'c'=2,'zh'=2,'y'=4] {'zh','zl'}, dimensions={0} | all-to-all | bytes 524288 | tf_op jit(solution)/shard_map/near_sum/all_to_all | solution.py:417
  60.5 0.8 residual_part.1
  61.3 3.6 %all-to-all-start.2 = ((bf16[8,128,128]{2,1,0:T(8,128)(2,1)}), bf16[8,128,128]{2,1,0:T(8,128)(2,1)S(1)}, u32[]{:S(2)}, u32[]{:S(2)}) async-start(bf16[8,128,128]{2,1,0:T(8,128)(2,1)} %get-tuple-element.45), calls=%async_computation.2 | async-start | bytes 524288 | tf_op jit(solution)/shard_map/residual/all_to_all | solution.py:423
  65.5 1.6 %collective-permute-start.11 = (f32[2,3,16,128]{3,2,1,0:T(8,128)S(1)}, f32[2,3,16,128]{3,2,1,0:T(8,128)S(1)}, u32[]{:S(2)}, u32[]{:S(2)}) collective-permute-start(f32[2,3,16,128]{3,2,1,0:T(8,128)S(1)} %get-tuple-element.50), channel_id=1, source_target_pairs={{0,2},{1,3},{2,0},{3,1},{4,6},{5,7},{6,4},{7,5},{8,10},{9,11},{10,... | collective-permute-start | bytes 147464 | tf_op jit(solution)/shard_map/residual/ppermute | solution.py:343
  67.1 1.2 %collective-permute-start.12 = (f32[2,3,16,128]{3,2,1,0:T(8,128)S(1)}, f32[2,3,16,128]{3,2,1,0:T(8,128)S(1)}, u32[]{:S(2)}, u32[]{:S(2)}) collective-permute-start(f32[2,3,16,128]{3,2,1,0:T(8,128)S(1)} %get-tuple-element.51), channel_id=1, source_target_pairs={{0,3},{1,0},{2,1},{3,2},{4,7},{5,4},{6,5},{7,6},{8,11},{9,8},{10,9... | collective-permute-start | bytes 147464 | tf_op jit(solution)/shard_map/residual/ppermute | solution.py:343
  68.3 5.7 %all-to-all-done.2.residual_ref = bf16[8,128,128]{2,1,0:T(8,128)(2,1)S(1)} async-done(((bf16[8,128,128]{2,1,0:T(8,128)(2,1)}), bf16[8,128,128]{2,1,0:T(8,128)(2,1)S(1)}, u32[]{:S(2)}, u32[]{:S(2)}) %all-to-all-start.2) | async-done | bytes 262176 | tf_op jit(solution)/shard_map/residual/all_to_all | solution.py:423
  74.0 2.0 %pick_tiles.1 = bf16[32,4,16,256]{3,2,1,0:T(8,128)(2,1)} custom-call(s32[11]{0:T(128)S(1)} %pad_add_fusion.place_ref, s32[4,32]{1,0:T(4,128)S(1)} %maximum_convert_fusion.table_0, s32[4,32]{1,0:T(4,128)S(1)} %collective-permute-done.4.table_1, s32[4,32]{1,0:T(4,128)S(1)} %collective-permute-done.5.table_2, s32[4,32]{1,0:T(4,128)S(1)} %collective-permute-done.6.table_3, ...), custom_call_target="tpu_custom_call" | custom-call | flops 1000000 | bytes 1048576 | tf_op jit(solution)/shard_map/pick/pick_tiles/pallas_call | solution.py:428
  76.1 9.2 %all-to-all-start.3 = ((bf16[32,4,16,256]{3,2,1,0:T(8,128)(2,1)}), bf16[32,4,16,256]{3,2,1,0:T(8,128)(2,1)S(1)}, u32[]{:S(2)}, u32[]{:S(2)}) async-start(bf16[32,4,16,256]{3,2,1,0:T(8,128)(2,1)} %pick_tiles.1), calls=%async_computation.3 | async-start | bytes 2097152 | tf_op jit(solution)/shard_map/pick/all_to_all | solution.py:443
  85.4 0.7 slice-done.2
  86.2 1.7 %collective-permute-start.13 = (f32[4,3,16,128]{3,2,1,0:T(8,128)S(1)}, f32[4,3,16,128]{3,2,1,0:T(8,128)S(1)}, u32[]{:S(2)}, u32[]{:S(2)}) collective-permute-start(f32[4,3,16,128]{3,2,1,0:T(8,128)S(1)} %pad_maximum_fusion), channel_id=1, source_target_pairs={{0,4},{4,0},{1,5},{5,1},{2,6},{6,2},{3,7},{7,3},{8,12},{12,8},{9,1... | collective-permute-start | bytes 294920 | tf_op jit(solution)/shard_map/updates/ppermute | solution.py:343
  87.9 1.1 %copy.14 = bf16[256,8,4,4,2,8]{0,5,4,3,2,1:T(8,128)(2,1)} copy(bf16[256,8,4,4,2,8]{0,5,2,4,1,3:T(8,128)(2,1)S(1)} %bitcast.26) | data formatting | bytes 2097152 | tf_op jit(solution)/shard_map/back_project/transpose | solution.py:452
  89.0 1.5 %copy.15.radon_ref = bf16[256,2048]{1,0:T(8,128)(2,1)S(1)} copy(bf16[256,2048]{0,1:T(8,128)(2,1)} %bitcast.27) | data formatting | bytes 2097152 | tf_op jit(solution)/shard_map/back_project/reshape | solution.py:452
  90.5 6.2 %collective-permute-done.13.theirs_ref = f32[4,3,16,128]{3,2,1,0:T(8,128)S(1)} collective-permute-done((f32[4,3,16,128]{3,2,1,0:T(8,128)S(1)}, f32[4,3,16,128]{3,2,1,0:T(8,128)S(1)}, u32[]{:S(2)}, u32[]{:S(2)}) %collective-permute-start.13) | collective-permute-done | bytes 98336 | tf_op jit(solution)/shard_map/updates/ppermute | solution.py:343
  96.8 1.2 %updates.1 = (f32[128,128]{1,0:T(8,128)}, f32[128,128]{1,0:T(8,128)}) custom-call(s32[11]{0:T(128)S(1)} %pad_add_fusion.place_ref, f32[2,3,16,128]{3,2,1,0:T(8,128)S(1)} %get-tuple-element.52.own_ref, f32[2,3,16,128]{3,2,1,0:T(8,128)S(1)} %copy-done.4, f32[2,3,16,128]{3,2,1,0:T(8,128)S(1)} %copy-done.6, f32[2,3,16,128]{3,2,1,0:T(8,128)S(1)} %copy-done.8, ...), custom_call_target="tpu_custom_call" | custom-call | flops 1000000 | bytes 1048576 | tf_op jit(solution)/shard_map/updates/updates/pallas_call | solution.py:447
  98.0 3.6 %all-to-all-done.3.picked_ref = bf16[32,4,16,256]{3,2,1,0:T(8,128)(2,1)S(1)} async-done(((bf16[32,4,16,256]{3,2,1,0:T(8,128)(2,1)}), bf16[32,4,16,256]{3,2,1,0:T(8,128)(2,1)S(1)}, u32[]{:S(2)}, u32[]{:S(2)}) %all-to-all-start.3) | async-done | bytes 1048608 | tf_op jit(solution)/shard_map/pick/all_to_all | solution.py:443
  101.7 1.1 %back_project.1 = f32[512,128]{1,0:T(8,128)} custom-call(bf16[256,2048]{1,0:T(8,128)(2,1)S(1)} %copy.15.radon_ref, bf16[32,4,16,256]{3,2,1,0:T(8,128)(2,1)S(1)} %all-to-all-done.3.picked_ref, f32[512,128]{1,0:T(8,128)S(1)} %bitcast.18), custom_call_target="tpu_custom_call" | custom-call | flops 268435456 | bytes 1048576 | tf_op jit(solution)/shard_map/back_project/back_project/pallas_call | solution.py:453
  (58 shorter events, 2.6 us)
Async XLA Ops:
  0.6 11.9 %collective-permute-start = (f32[128,128]{1,0:T(8,128)}, f32[128,128]{1,0:T(8,128)S(1)}, u32[]{:S(2)}, u32[]{:S(2)}) collective-permute-start(f32[128,128]{1,0:T(8,128)} %bitcast.19), channel_id=1, source_target_pairs={{0,4},{4,0},{1,5},{5,1},{2,6},{6,2},{3,7},{7,3},{8,12},{12,8},{9,1... | collective-permute-start | bytes 196616 | tf_op jit(solution)/shard_map/ray_sums/ppermute | solution.py:343
  9.2 3.4 %copy-start.1 = (f32[1,64,2,128]{3,2,1,0:T(2,128)S(1)}, f32[1,64,2,128]{3,2,1,0:T(2,128)}, u32[]{:S(2)}) copy-start(f32[1,64,2,128]{3,2,1,0:T(2,128)} %param.12) | copy-start | bytes 196612
  9.2 3.4 %copy-start.2 = (f32[1,64,2,128]{3,2,1,0:T(2,128)S(1)}, f32[1,64,2,128]{3,2,1,0:T(2,128)}, u32[]{:S(2)}) copy-start(f32[1,64,2,128]{3,2,1,0:T(2,128)} %param.13) | copy-start | bytes 196612
  13.8 11.8 %collective-permute-start.3 = (f32[296,128]{1,0:T(8,128)S(1)}, f32[296,128]{1,0:T(8,128)S(1)}, u32[]{:S(2)}, u32[]{:S(2)}) collective-permute-start(f32[296,128]{1,0:T(8,128)S(1)} %get-tuple-element.38), channel_id=1, source_target_pairs={{0,3},{1,0},{2,1},{3,2},{4,7},{5,4},{6,5},{7,6},{8,11},{9,8},{10,9... | collective-permute-start | bytes 454664 | tf_op jit(solution)/shard_map/fields/ppermute | solution.py:343
  16.6 9.0 %collective-permute-start.2 = (f32[296,128]{1,0:T(8,128)S(1)}, f32[296,128]{1,0:T(8,128)S(1)}, u32[]{:S(2)}, u32[]{:S(2)}) collective-permute-start(f32[296,128]{1,0:T(8,128)S(1)} %get-tuple-element.37), channel_id=1, source_target_pairs={{0,2},{1,3},{2,0},{3,1},{4,6},{5,7},{6,4},{7,5},{8,10},{9,11},{10,... | collective-permute-start | bytes 454664 | tf_op jit(solution)/shard_map/fields/ppermute | solution.py:343
  17.0 10.1 %copy-start.10 = (f32[1,8,128,128]{3,2,1,0:T(8,128)S(1)}, f32[1,8,128,128]{3,2,1,0:T(8,128)}, u32[]{:S(2)}) copy-start(f32[1,8,128,128]{3,2,1,0:T(8,128)} %param.9) | copy-start | bytes 1572868
  17.0 10.1 %copy-start.11 = (f32[2,128,128]{2,1,0:T(8,128)S(1)}, f32[2,128,128]{2,1,0:T(8,128)}, u32[]{:S(2)}) copy-start(f32[2,128,128]{2,1,0:T(8,128)} %probe_ref.1) | copy-start | bytes 393220
  17.0 10.1 %copy-start.12 = (bf16[4,128,128]{2,1,0:T(8,128)(2,1)S(1)}, bf16[4,128,128]{2,1,0:T(8,128)(2,1)}, u32[]{:S(2)}) copy-start(bf16[4,128,128]{2,1,0:T(8,128)(2,1)} %constant.15.clone.dft_ref) | copy-start | bytes 393220
  17.0 10.1 %collective-permute-start.1 = (f32[296,128]{1,0:T(8,128)S(1)}, f32[296,128]{1,0:T(8,128)S(1)}, u32[]{:S(2)}, u32[]{:S(2)}) collective-permute-start(f32[296,128]{1,0:T(8,128)S(1)} %get-tuple-element.36), channel_id=1, source_target_pairs={{0,1},{1,2},{2,3},{3,0},{4,5},{5,6},{6,7},{7,4},{8,9},{9,10},{10,1... | collective-permute-start | bytes 454664 | tf_op jit(solution)/shard_map/fields/ppermute | solution.py:343
  17.7 26.3 %all-to-all-start = ((bf16[32,4,16,256]{3,2,1,0:T(8,128)(2,1)}), bf16[32,4,16,256]{3,2,1,0:T(8,128)(2,1)S(1)}, u32[]{:S(2)}, u32[]{:S(2)}) async-start(bf16[32,4,16,256]{3,2,1,0:T(8,128)(2,1)} %get-tuple-element.31), calls=%async_computation | async-start | bytes 2097152 | tf_op jit(solution)/shard_map/ray_sums/all_to_all | solution.py:381
  31.7 11.0 %collective-permute-start.7 = (bf16[2,128,128]{2,1,0:T(8,128)(2,1)S(1)}, bf16[2,128,128]{2,1,0:T(8,128)(2,1)S(1)}, u32[]{:S(2)}, u32[]{:S(2)}) collective-permute-start(bf16[2,128,128]{2,1,0:T(8,128)(2,1)S(1)} %get-tuple-element.41), channel_id=1, source_target_pairs={{0,1},{1,2},{2,3},{3,0},{4,5},{5,6},{6,7},{7,4},{8,9},{9,10},{10,1... | collective-permute-start | bytes 196616 | tf_op jit(solution)/shard_map/frames/ppermute | solution.py:343
  31.8 12.1 %collective-permute-start.8 = (bf16[2,128,128]{2,1,0:T(8,128)(2,1)S(1)}, bf16[2,128,128]{2,1,0:T(8,128)(2,1)S(1)}, u32[]{:S(2)}, u32[]{:S(2)}) collective-permute-start(bf16[2,128,128]{2,1,0:T(8,128)(2,1)S(1)} %get-tuple-element.42), channel_id=1, source_target_pairs={{0,2},{1,3},{2,0},{3,1},{4,6},{5,7},{6,4},{7,5},{8,10},{9,11},{10,... | collective-permute-start | bytes 196616 | tf_op jit(solution)/shard_map/frames/ppermute | solution.py:343
  34.2 9.7 %collective-permute-start.9 = (bf16[2,128,128]{2,1,0:T(8,128)(2,1)S(1)}, bf16[2,128,128]{2,1,0:T(8,128)(2,1)S(1)}, u32[]{:S(2)}, u32[]{:S(2)}) collective-permute-start(bf16[2,128,128]{2,1,0:T(8,128)(2,1)S(1)} %get-tuple-element.43), channel_id=1, source_target_pairs={{0,3},{1,0},{2,1},{3,2},{4,7},{5,4},{6,5},{7,6},{8,11},{9,8},{10,9... | collective-permute-start | bytes 196616 | tf_op jit(solution)/shard_map/frames/ppermute | solution.py:343
  35.4 4.6 %collective-permute-start.4 = (s32[4,32]{1,0:T(4,128)S(1)}, s32[4,32]{1,0:T(4,128)S(1)}, u32[]{:S(2)}, u32[]{:S(2)}) collective-permute-start(s32[4,32]{1,0:T(4,128)S(1)} %maximum_convert_fusion.table_0), channel_id=1, source_target_pairs={{0,64},{64,128},{128,192},{192,0},{1,65},{65,129},{129,193},{193,1... | collective-permute-start | bytes 1544 | tf_op jit(solution)/shard_map/targets/ppermute | solution.py:343
  36.2 3.8 %collective-permute-start.5 = (s32[4,32]{1,0:T(4,128)S(1)}, s32[4,32]{1,0:T(4,128)S(1)}, u32[]{:S(2)}, u32[]{:S(2)}) collective-permute-start(s32[4,32]{1,0:T(4,128)S(1)} %maximum_convert_fusion.table_0), channel_id=1, source_target_pairs={{0,128},{64,192},{128,0},{192,64},{1,129},{65,193},{129,1},{193,65... | collective-permute-start | bytes 1544 | tf_op jit(solution)/shard_map/targets/ppermute | solution.py:343
  40.0 2.7 %collective-permute-start.6 = (s32[4,32]{1,0:T(4,128)S(1)}, s32[4,32]{1,0:T(4,128)S(1)}, u32[]{:S(2)}, u32[]{:S(2)}) collective-permute-start(s32[4,32]{1,0:T(4,128)S(1)} %maximum_convert_fusion.table_0), channel_id=1, source_target_pairs={{0,192},{64,0},{128,64},{192,128},{1,193},{65,1},{129,65},{193,129... | collective-permute-start | bytes 1544 | tf_op jit(solution)/shard_map/targets/ppermute | solution.py:343
  61.3 12.7 %all-to-all-start.2 = ((bf16[8,128,128]{2,1,0:T(8,128)(2,1)}), bf16[8,128,128]{2,1,0:T(8,128)(2,1)S(1)}, u32[]{:S(2)}, u32[]{:S(2)}) async-start(bf16[8,128,128]{2,1,0:T(8,128)(2,1)} %get-tuple-element.45), calls=%async_computation.2 | async-start | bytes 524288 | tf_op jit(solution)/shard_map/residual/all_to_all | solution.py:423
  65.5 10.6 %collective-permute-start.10 = (f32[2,3,16,128]{3,2,1,0:T(8,128)S(1)}, f32[2,3,16,128]{3,2,1,0:T(8,128)S(1)}, u32[]{:S(2)}, u32[]{:S(2)}) collective-permute-start(f32[2,3,16,128]{3,2,1,0:T(8,128)S(1)} %get-tuple-element.49), channel_id=1, source_target_pairs={{0,1},{1,2},{2,3},{3,0},{4,5},{5,6},{6,7},{7,4},{8,9},{9,10},{10,1... | collective-permute-start | bytes 147464 | tf_op jit(solution)/shard_map/residual/ppermute | solution.py:343
  65.5 10.5 %collective-permute-start.11 = (f32[2,3,16,128]{3,2,1,0:T(8,128)S(1)}, f32[2,3,16,128]{3,2,1,0:T(8,128)S(1)}, u32[]{:S(2)}, u32[]{:S(2)}) collective-permute-start(f32[2,3,16,128]{3,2,1,0:T(8,128)S(1)} %get-tuple-element.50), channel_id=1, source_target_pairs={{0,2},{1,3},{2,0},{3,1},{4,6},{5,7},{6,4},{7,5},{8,10},{9,11},{10,... | collective-permute-start | bytes 147464 | tf_op jit(solution)/shard_map/residual/ppermute | solution.py:343
  67.1 9.0 %collective-permute-start.12 = (f32[2,3,16,128]{3,2,1,0:T(8,128)S(1)}, f32[2,3,16,128]{3,2,1,0:T(8,128)S(1)}, u32[]{:S(2)}, u32[]{:S(2)}) collective-permute-start(f32[2,3,16,128]{3,2,1,0:T(8,128)S(1)} %get-tuple-element.51), channel_id=1, source_target_pairs={{0,3},{1,0},{2,1},{3,2},{4,7},{5,4},{6,5},{7,6},{8,11},{9,8},{10,9... | collective-permute-start | bytes 147464 | tf_op jit(solution)/shard_map/residual/ppermute | solution.py:343
  76.0 9.3 %copy-start.3 = (f32[2,3,16,128]{3,2,1,0:T(8,128)}, f32[2,3,16,128]{3,2,1,0:T(8,128)S(1)}, u32[]{:S(2)}) copy-start(f32[2,3,16,128]{3,2,1,0:T(8,128)S(1)} %collective-permute-done.10.one_ref) | copy-start | bytes 147460
  76.1 9.3 %copy-start.5 = (f32[2,3,16,128]{3,2,1,0:T(8,128)}, f32[2,3,16,128]{3,2,1,0:T(8,128)S(1)}, u32[]{:S(2)}) copy-start(f32[2,3,16,128]{3,2,1,0:T(8,128)S(1)} %collective-permute-done.11.two_ref) | copy-start | bytes 147460
  76.1 9.3 %copy-start.7 = (f32[2,3,16,128]{3,2,1,0:T(8,128)}, f32[2,3,16,128]{3,2,1,0:T(8,128)S(1)}, u32[]{:S(2)}) copy-start(f32[2,3,16,128]{3,2,1,0:T(8,128)S(1)} %collective-permute-done.12.three_ref) | copy-start | bytes 147460
  76.1 11.8 %copy-start.13 = (bf16[1,32,2,32,256]{4,3,2,1,0:T(8,128)(2,1)S(1)}, bf16[1,32,2,32,256]{4,3,2,1,0:T(8,128)(2,1)}, u32[]{:S(2)}) copy-start(bf16[1,32,2,32,256]{4,3,2,1,0:T(8,128)(2,1)} %param.15) | copy-start | bytes 3145732
  76.1 25.6 %all-to-all-start.3 = ((bf16[32,4,16,256]{3,2,1,0:T(8,128)(2,1)}), bf16[32,4,16,256]{3,2,1,0:T(8,128)(2,1)S(1)}, u32[]{:S(2)}, u32[]{:S(2)}) async-start(bf16[32,4,16,256]{3,2,1,0:T(8,128)(2,1)} %pick_tiles.1), calls=%async_computation.3 | async-start | bytes 2097152 | tf_op jit(solution)/shard_map/pick/all_to_all | solution.py:443
  85.4 0.7 slice-start
  85.4 0.8 slice-start.1
  86.2 10.6 %collective-permute-start.13 = (f32[4,3,16,128]{3,2,1,0:T(8,128)S(1)}, f32[4,3,16,128]{3,2,1,0:T(8,128)S(1)}, u32[]{:S(2)}, u32[]{:S(2)}) collective-permute-start(f32[4,3,16,128]{3,2,1,0:T(8,128)S(1)} %pad_maximum_fusion), channel_id=1, source_target_pairs={{0,4},{4,0},{1,5},{5,1},{2,6},{6,2},{3,7},{7,3},{8,12},{12,8},{9,1... | collective-permute-start | bytes 294920 | tf_op jit(solution)/shard_map/updates/ppermute | solution.py:343
  89.0 7.7 %copy-start.4 = (f32[2,3,16,128]{3,2,1,0:T(8,128)S(1)}, f32[2,3,16,128]{3,2,1,0:T(8,128)}, u32[]{:S(2)}) copy-start(f32[2,3,16,128]{3,2,1,0:T(8,128)} %copy-done.3) | copy-start | bytes 147460
  89.0 7.7 %copy-start.6 = (f32[2,3,16,128]{3,2,1,0:T(8,128)S(1)}, f32[2,3,16,128]{3,2,1,0:T(8,128)}, u32[]{:S(2)}) copy-start(f32[2,3,16,128]{3,2,1,0:T(8,128)} %copy-done.5) | copy-start | bytes 147460
  89.0 7.7 %copy-start.8 = (f32[2,3,16,128]{3,2,1,0:T(8,128)S(1)}, f32[2,3,16,128]{3,2,1,0:T(8,128)}, u32[]{:S(2)}) copy-start(f32[2,3,16,128]{3,2,1,0:T(8,128)} %copy-done.7) | copy-start | bytes 147460
  90.5 11.1 %copy-start = (f32[256,2,128]{2,1,0:T(2,128)S(1)}, f32[256,2,128]{2,1,0:T(2,128)}, u32[]{:S(2)}) copy-start(f32[256,2,128]{2,1,0:T(2,128)} %param.14) | copy-start | bytes 786436
  (3 other events, 2.1 us)

commit v13 on v10

--- a/solution.py
+++ b/solution.py
@@ -97,14 +97,19 @@
     target_out[0:1, : ZL * XC] = target_ref[...].astype(f32)
 
 
-def each_tile(place_ref, tables):
+def tile_groups(place_ref, tables, count):
     zl_here = place_ref[2]
-    for back_zl, table in enumerate(tables):
-        zl = lax.rem(zl_here + ZL - back_zl, ZL)
-        for back_y in range(Y):
-            y = lax.rem(place_ref[1] + Y - back_y, Y)
-            for xc in range(XC):
-                yield zl, xc * Y + y, pl.multiple_of(table[back_y, zl_here * XC + xc] * QR, QR)
+    angles = [lax.rem(zl_here + ZL - back_zl, ZL) for back_zl in range(ZL)]
+    groups = []
+    for back_y in range(Y):
+        y = lax.rem(place_ref[1] + Y - back_y, Y)
+        for xc in range(XC):
+            for zl, table in zip(angles, tables):
+                row = table[back_y, zl_here * XC + xc] * QR
+                groups.append((zl, xc * Y + y, pl.ds(pl.multiple_of(row, QR), HITS * QR)))
+                if len(groups) == count:
+                    yield groups
+                    groups = []
 
 
 def add_tiles(
@@ -126,8 +131,10 @@
         total[zl_here, rows, :] -= jnp.concatenate(
             [field_ref[base : base + 2 * QR, :], field_ref[base + 2 * QR : base + 4 * QR, :]], axis=1
         )
-    for zl, near, row in each_tile(place_ref, (table_0, table_1, table_2, table_3)):
-        total[zl, pl.ds(row, HITS * QR), :] += sums_ref[near, zl].astype(f32)
+    for group in tile_groups(place_ref, (table_0, table_1, table_2, table_3), ZL):
+        added = [total[zl, rows, :] + sums_ref[near, zl].astype(f32) for zl, near, rows in group]
+        for (zl, near, rows), value in zip(group, added):
+            total[zl, rows, :] = value
     for zh in range(ZH):
         for zl in range(ZL):
             out_ref[zh * ZL + zl] = total[zl, :, zh * NZ : (zh + 1) * NZ].astype(bf16)
@@ -161,8 +168,10 @@
             [residual_ref[zl].astype(f32), residual_ref[ZL + zl].astype(f32)], axis=1
         )
 
-    for zl, near, row in each_tile(place_ref, (table_0, table_1, table_2, table_3)):
-        out_ref[near, zl] = rows_ref[zl, pl.ds(row, HITS * QR), :].astype(bf16)
+    for group in tile_groups(place_ref, (table_0, table_1, table_2, table_3), 2 * ZL):
+        picked = [rows_ref[zl, rows, :].astype(bf16) for zl, near, rows in group]
+        for (zl, near, rows), value in zip(group, picked):
+            out_ref[near, zl] = value
 
 
 def back_project(radon_ref, picked_ref, volume_ref, out_ref):
@@ -268,51 +277,44 @@
     probe_im = probe_ref[1]
     ah, bh = complex_blocks(dft_ref[0], dft_ref[1])
     al, bl = complex_blocks(dft_ref[2], dft_ref[3])
-    for pair in range(FR_DEV // 2):
-        waves = []
-        for frame in (2 * pair, 2 * pair + 1):
-            rows = pl.ds(place_ref[3 + frame], PROBE)
-            object_re = field_re[rows, :]
-            object_im = field_im[rows, :]
-            waves.append(
-                jnp.concatenate(
-                    [
-                        probe_re * object_re - probe_im * object_im,
-                        probe_re * object_im + probe_im * object_re,
-                    ],
-                    axis=0,
-                )
+    frames = [pl.ds(place_ref[3 + frame], PROBE) for frame in range(FR_DEV)]
+    waves = []
+    for rows in frames:
+        object_re = field_re[rows, :]
+        object_im = field_im[rows, :]
+        waves.append(
+            jnp.concatenate(
+                [probe_re * object_re - probe_im * object_im, probe_re * object_im + probe_im * object_re], axis=0
             )
-        lefts = from_left(ah, al, jnp.concatenate(waves, axis=1))
-        sides = jnp.concatenate(
-            [
-                jnp.concatenate([lefts[:PROBE, i * NZ : (i + 1) * NZ], lefts[PROBE:, i * NZ : (i + 1) * NZ]], axis=1)
-                for i in range(2)
-            ],
-            axis=0,
         )
-        far = from_right(sides, bh, bl)
-        far_re = far[:, :NZ]
-        far_im = far[:, NZ:]
-        modulus = jnp.sqrt(far_re * far_re + far_im * far_im)
-        intensity = measured_ref[2 * pair : 2 * pair + 2].reshape(2 * PROBE, NZ)
-        shrink = 1.0 - jnp.sqrt(intensity) / jnp.maximum(modulus, 1.0)
-        diff = jnp.concatenate([far_re * shrink, far_im * shrink], axis=1)
-        half = from_right(diff, ah, al)
-        stacked = jnp.concatenate(
-            [
-                jnp.concatenate([half[i * PROBE : (i + 1) * PROBE, :NZ], half[i * PROBE : (i + 1) * PROBE, NZ:]], axis=0)
-                for i in range(2)
-            ],
-            axis=1,
-        )
-        backs = from_left(bh, bl, stacked)
-        for i in range(2):
-            back_re = backs[:PROBE, i * NZ : (i + 1) * NZ]
-            back_im = backs[PROBE:, i * NZ : (i + 1) * NZ]
-            rows = pl.ds(place_ref[3 + 2 * pair + i], PROBE)
-            total_re[rows, :] += probe_re * back_re + probe_im * back_im
-            total_im[rows, :] += probe_re * back_im - probe_im * back_re
+    lefts = from_left(ah, al, jnp.concatenate(waves, axis=1))
+    sides = jnp.concatenate(
+        [
+            jnp.concatenate([lefts[:PROBE, i * NZ : (i + 1) * NZ], lefts[PROBE:, i * NZ : (i + 1) * NZ]], axis=1)
+            for i in range(FR_DEV)
+        ],
+        axis=0,
+    )
+    far = from_right(sides, bh, bl)
+    far_re = far[:, :NZ]
+    far_im = far[:, NZ:]
+    modulus = jnp.sqrt(far_re * far_re + far_im * far_im)
+    intensity = measured_ref[...].reshape(FR_DEV * PROBE, NZ)
+    shrink = 1.0 - jnp.sqrt(intensity) / jnp.maximum(modulus, 1.0)
+    half = from_right(jnp.concatenate([far_re * shrink, far_im * shrink], axis=1), ah, al)
+    stacked = jnp.concatenate(
+        [
+            jnp.concatenate([half[i * PROBE : (i + 1) * PROBE, :NZ], half[i * PROBE : (i + 1) * PROBE, NZ:]], axis=0)
+            for i in range(FR_DEV)
+        ],
+        axis=1,
+    )
+    backs = from_left(bh, bl, stacked)
+    for i, rows in enumerate(frames):
+        back_re = backs[:PROBE, i * NZ : (i + 1) * NZ]
+        back_im = backs[PROBE:, i * NZ : (i + 1) * NZ]
+        total_re[rows, :] += probe_re * back_re + probe_im * back_im
+        total_im[rows, :] += probe_re * back_im - probe_im * back_re
     for ahead in range(Y):
         owner = lax.rem(y + ahead, Y)
         for tile in range(0, NR, 2):

time: 103 us -> 103 us (level)
  waiting for transfers between devices: 23.5 us -> 25 us
  Pallas kernels: 15.8 us -> 14.4 us
    ppermute x14, waiting for transfers between devices: 14.2 us -> 15.3 us  [shifted(): lax.ppermute(value, axis, [(i, (i + step) % length) for i in range(length)])]
  transfers between devices with their start and end apart: 17 -> 17, of which waited for: 7 -> 7; matrix products, arithmetic and copies ran while one was open for 3% -> 3% of each run, Pallas kernels for 12% -> 11%
where the time goes in v13:
time: 103 us
  starting transfers between devices  41.8 us (41%)
  waiting for transfers between devices  25 us (24%)
  blocking collectives  15.9 us (15%)
  Pallas kernels  14.4 us (14%)
  local copies, waits for them, and re-layouts  4.73 us (5%)
    ppermute x14, starting transfers between devices, shifted(): lax.ppermute(value, axis, [(i, (i + step) % length) for i in range(length)])  21.5 us
    all_to_all x1, blocking collectives, body(): far_sums = lax.all_to_all(dense, ALONG, 0, 0, tiled=True)  15.9 us
    ppermute x14, waiting for transfers between devices, shifted(): lax.ppermute(value, axis, [(i, (i + step) % length) for i in range(length)])  15.3 us
    all_to_all x1, starting transfers between devices, body(): returned = lax.all_to_all(picked, CROSS, 0, 0, tiled=True)  8.91 us
    all_to_all x1, starting transfers between devices, body(): near_sums = lax.all_to_all(sums, CROSS, 0, 0, tiled=True)  7.95 us
    all_to_all x1, waiting for transfers between devices, body(): residuals = lax.all_to_all(copies, ALONG, 0, 0, tiled=True)  6.03 us
    pallas_call x1, Pallas kernels, body(): call(frame_gradients, (shape(2, 128, NZ),) + (shape(2, 128, NZ, dtype=bf1...  3.66 us
    all_to_all x1, waiting for transfers between devices, body(): returned = lax.all_to_all(picked, CROSS, 0, 0, tiled=True)  3.62 us
  transfers between devices with their start and end apart: 17, of which 7 were waited for; matrix products, arithmetic and copies ran while one was open for 3% of the time, Pallas kernels for 11%

profile of v13, /device:TPU:1, one launch (start us, length us, event | category | flops | bytes accessed | tf_op | source)
XLA Modules:
  0.0 102.8 jit_solution(12597169928825728923)
XLA Ops:
  0.6 7.8 %collective-permute-start = (f32[128,128]{1,0:T(8,128)}, f32[128,128]{1,0:T(8,128)S(1)}, u32[]{:S(2)}, u32[]{:S(2)}) collective-permute-start(f32[128,128]{1,0:T(8,128)} %bitcast.19), channel_id=1, source_target_pairs={{0,4},{4,0},{1,5},{5,1},{2,6},{6,2},{3,7},{7,3},{8,12},{12,8},{9,1... | collective-permute-start | bytes 196616 | tf_op jit(solution)/shard_map/ray_sums/ppermute | solution.py:333
  8.5 0.7 copy-done.14
  9.2 3.3 %ray_sums.1 = (bf16[32,4,16,256]{3,2,1,0:T(8,128)(2,1)}, f32[8,128]{1,0:T(8,128)}) custom-call(bf16[32,2,32,256]{3,2,1,0:T(8,128)(2,1)} %bitcast.25, f32[512,128]{1,0:T(8,128)} %bitcast.17, s32[1,32]{1,0:T(1,128)} %bitcast.29), custom_call_target="tpu_custom_call" | custom-call | flops 268435456 | bytes 1048576 | tf_op jit(solution)/shard_map/ray_sums/ray_sums/pallas_call | solution.py:356
  12.6 0.6 copy-done.9
  13.8 2.8 %collective-permute-start.3 = (f32[296,128]{1,0:T(8,128)S(1)}, f32[296,128]{1,0:T(8,128)S(1)}, u32[]{:S(2)}, u32[]{:S(2)}) collective-permute-start(f32[296,128]{1,0:T(8,128)S(1)} %get-tuple-element.38), channel_id=1, source_target_pairs={{0,3},{1,0},{2,1},{3,2},{4,7},{5,4},{6,5},{7,6},{8,11},{9,8},{10,9... | collective-permute-start | bytes 454664 | tf_op jit(solution)/shard_map/fields/ppermute | solution.py:333
  17.0 0.7 collective-permute-start.1
  17.7 7.9 %all-to-all-start = ((bf16[32,4,16,256]{3,2,1,0:T(8,128)(2,1)}), bf16[32,4,16,256]{3,2,1,0:T(8,128)(2,1)S(1)}, u32[]{:S(2)}, u32[]{:S(2)}) async-start(bf16[32,4,16,256]{3,2,1,0:T(8,128)(2,1)} %get-tuple-element.31), calls=%async_computation | async-start | bytes 2097152 | tf_op jit(solution)/shard_map/ray_sums/all_to_all | solution.py:371
  25.7 1.4 %collective-permute-done.1.field_1 = f32[296,128]{1,0:T(8,128)S(1)} collective-permute-done((f32[296,128]{1,0:T(8,128)S(1)}, f32[296,128]{1,0:T(8,128)S(1)}, u32[]{:S(2)}, u32[]{:S(2)}) %collective-permute-start.1) | collective-permute-done | bytes 151584 | tf_op jit(solution)/shard_map/fields/ppermute | solution.py:333
  27.1 3.7 %frame_gradients.1 = (f32[2,128,128]{2,1,0:T(8,128)S(1)}, bf16[2,128,128]{2,1,0:T(8,128)(2,1)S(1)}, bf16[2,128,128]{2,1,0:T(8,128)(2,1)S(1)}, bf16[2,128,128]{2,1,0:T(8,128)(2,1)S(1)}) custom-call(s32[11]{0:T(128)S(1)} %pad_add_fusion.place_ref, f32[296,128]{1,0:T(8,128)S(1)} %get-tuple-element.35.field_0, f32[296,128]{1,0:T(8,128)S(1)} %collective-permute-done.1.field_1, ...), custom_call_target="tpu_custom_call" | custom-call | flops 20000000000 | bytes 1048576 | tf_op jit(solution)/shard_map/frames/frame_gradients/pallas_call | solution.py:381
  30.8 2.4 %collective-permute-start.8 = (bf16[2,128,128]{2,1,0:T(8,128)(2,1)S(1)}, bf16[2,128,128]{2,1,0:T(8,128)(2,1)S(1)}, u32[]{:S(2)}, u32[]{:S(2)}) collective-permute-start(bf16[2,128,128]{2,1,0:T(8,128)(2,1)S(1)} %get-tuple-element.42), channel_id=1, source_target_pairs={{0,2},{1,3},{2,0},{3,1},{4,6},{5,7},{6,4},{7,5},{8,10},{9,11},{10,... | collective-permute-start | bytes 196616 | tf_op jit(solution)/shard_map/frames/ppermute | solution.py:333
  33.2 1.2 %collective-permute-start.9 = (bf16[2,128,128]{2,1,0:T(8,128)(2,1)S(1)}, bf16[2,128,128]{2,1,0:T(8,128)(2,1)S(1)}, u32[]{:S(2)}, u32[]{:S(2)}) collective-permute-start(bf16[2,128,128]{2,1,0:T(8,128)(2,1)S(1)} %get-tuple-element.43), channel_id=1, source_target_pairs={{0,3},{1,0},{2,1},{3,2},{4,7},{5,4},{6,5},{7,6},{8,11},{9,8},{10,9... | collective-permute-start | bytes 196616 | tf_op jit(solution)/shard_map/frames/ppermute | solution.py:333
  34.4 0.8 collective-permute-start.4
  35.2 1.2 %collective-permute-start.5 = (s32[4,32]{1,0:T(4,128)S(1)}, s32[4,32]{1,0:T(4,128)S(1)}, u32[]{:S(2)}, u32[]{:S(2)}) collective-permute-start(s32[4,32]{1,0:T(4,128)S(1)} %maximum_convert_fusion.table_0), channel_id=1, source_target_pairs={{0,128},{64,192},{128,0},{192,64},{1,129},{65,193},{129,1},{193,65... | collective-permute-start | bytes 1544 | tf_op jit(solution)/shard_map/targets/ppermute | solution.py:333
  36.4 2.6 %collective-permute-done.4.table_1 = s32[4,32]{1,0:T(4,128)S(1)} collective-permute-done((s32[4,32]{1,0:T(4,128)S(1)}, s32[4,32]{1,0:T(4,128)S(1)}, u32[]{:S(2)}, u32[]{:S(2)}) %collective-permute-start.4) | collective-permute-done | bytes 544 | tf_op jit(solution)/shard_map/targets/ppermute | solution.py:333
  39.1 2.7 %collective-permute-done.6.table_3 = s32[4,32]{1,0:T(4,128)S(1)} collective-permute-done((s32[4,32]{1,0:T(4,128)S(1)}, s32[4,32]{1,0:T(4,128)S(1)}, u32[]{:S(2)}, u32[]{:S(2)}) %collective-permute-start.6) | collective-permute-done | bytes 544 | tf_op jit(solution)/shard_map/targets/ppermute | solution.py:333
  41.8 2.0 %collective-permute-done.8.inter_2 = bf16[2,128,128]{2,1,0:T(8,128)(2,1)S(1)} collective-permute-done((bf16[2,128,128]{2,1,0:T(8,128)(2,1)S(1)}, bf16[2,128,128]{2,1,0:T(8,128)(2,1)S(1)}, u32[]{:S(2)}, u32[]{:S(2)}) %collective-permute-start.8) | collective-permute-done | bytes 65568 | tf_op jit(solution)/shard_map/frames/ppermute | solution.py:333
  43.8 1.1 %add_tiles.1 = (bf16[8,128,128]{2,1,0:T(8,128)(2,1)S(1)}, f32[2,128,128]{2,1,0:T(8,128)S(1)}) custom-call(s32[11]{0:T(128)S(1)} %pad_add_fusion.place_ref, s32[4,32]{1,0:T(4,128)S(1)} %maximum_convert_fusion.table_0, s32[4,32]{1,0:T(4,128)S(1)} %collective-permute-done.4.table_1, s32[4,32]{1,0:T(4,128)S(1)} %collective-permute-done.5.table_2, ...), custom_call_target="tpu_custom_call" | custom-call | flops 1000000 | bytes 1048576 | tf_op jit(solution)/shard_map/near_sum/add_tiles/pallas_call | solution.py:399
  44.9 15.9 %all_to_all.20.sums_ref = bf16[8,128,128]{2,1,0:T(8,128)(2,1)S(1)} all-to-all(bf16[8,128,128]{2,1,0:T(8,128)(2,1)S(1)} %get-tuple-element.44), channel_id=1, replica_groups=mesh['zl'=4,'x'=4,'c'=2,'zh'=2,'y'=4] {'zh','zl'}, dimensions={0} | all-to-all | bytes 524288 | tf_op jit(solution)/shard_map/near_sum/all_to_all | solution.py:407
  60.8 0.8 residual_part.1
  61.5 3.4 %all-to-all-start.2 = ((bf16[8,128,128]{2,1,0:T(8,128)(2,1)}), bf16[8,128,128]{2,1,0:T(8,128)(2,1)S(1)}, u32[]{:S(2)}, u32[]{:S(2)}) async-start(bf16[8,128,128]{2,1,0:T(8,128)(2,1)} %get-tuple-element.45), calls=%async_computation.2 | async-start | bytes 524288 | tf_op jit(solution)/shard_map/residual/all_to_all | solution.py:413
  66.1 2.2 %collective-permute-start.12 = (f32[2,3,16,128]{3,2,1,0:T(8,128)S(1)}, f32[2,3,16,128]{3,2,1,0:T(8,128)S(1)}, u32[]{:S(2)}, u32[]{:S(2)}) collective-permute-start(f32[2,3,16,128]{3,2,1,0:T(8,128)S(1)} %get-tuple-element.51), channel_id=1, source_target_pairs={{0,3},{1,0},{2,1},{3,2},{4,7},{5,4},{6,5},{7,6},{8,11},{9,8},{10,9... | collective-permute-start | bytes 147464 | tf_op jit(solution)/shard_map/residual/ppermute | solution.py:333
  68.3 6.0 %all-to-all-done.2.residual_ref = bf16[8,128,128]{2,1,0:T(8,128)(2,1)S(1)} async-done(((bf16[8,128,128]{2,1,0:T(8,128)(2,1)}), bf16[8,128,128]{2,1,0:T(8,128)(2,1)S(1)}, u32[]{:S(2)}, u32[]{:S(2)}) %all-to-all-start.2) | async-done | bytes 262176 | tf_op jit(solution)/shard_map/residual/all_to_all | solution.py:413
  74.3 2.0 %pick_tiles.1 = bf16[32,4,16,256]{3,2,1,0:T(8,128)(2,1)} custom-call(s32[11]{0:T(128)S(1)} %pad_add_fusion.place_ref, s32[4,32]{1,0:T(4,128)S(1)} %maximum_convert_fusion.table_0, s32[4,32]{1,0:T(4,128)S(1)} %collective-permute-done.4.table_1, s32[4,32]{1,0:T(4,128)S(1)} %collective-permute-done.5.table_2, s32[4,32]{1,0:T(4,128)S(1)} %collective-permute-done.6.table_3, ...), custom_call_target="tpu_custom_call" | custom-call | flops 1000000 | bytes 1048576 | tf_op jit(solution)/shard_map/pick/pick_tiles/pallas_call | solution.py:418
  76.4 8.9 %all-to-all-start.3 = ((bf16[32,4,16,256]{3,2,1,0:T(8,128)(2,1)}), bf16[32,4,16,256]{3,2,1,0:T(8,128)(2,1)S(1)}, u32[]{:S(2)}, u32[]{:S(2)}) async-start(bf16[32,4,16,256]{3,2,1,0:T(8,128)(2,1)} %pick_tiles.1), calls=%async_computation.3 | async-start | bytes 2097152 | tf_op jit(solution)/shard_map/pick/all_to_all | solution.py:427
  85.4 0.7 slice-done.2
  86.1 1.4 %collective-permute-start.13 = (f32[4,3,16,128]{3,2,1,0:T(8,128)S(1)}, f32[4,3,16,128]{3,2,1,0:T(8,128)S(1)}, u32[]{:S(2)}, u32[]{:S(2)}) collective-permute-start(f32[4,3,16,128]{3,2,1,0:T(8,128)S(1)} %pad_maximum_fusion), channel_id=1, source_target_pairs={{0,4},{4,0},{1,5},{5,1},{2,6},{6,2},{3,7},{7,3},{8,12},{12,8},{9,1... | collective-permute-start | bytes 294920 | tf_op jit(solution)/shard_map/updates/ppermute | solution.py:333
  87.6 1.1 %copy.14 = bf16[256,8,4,4,2,8]{0,5,4,3,2,1:T(8,128)(2,1)} copy(bf16[256,8,4,4,2,8]{0,5,2,4,1,3:T(8,128)(2,1)S(1)} %bitcast.26) | data formatting | bytes 2097152 | tf_op jit(solution)/shard_map/back_project/transpose | solution.py:436
  88.7 1.5 %copy.15.radon_ref = bf16[256,2048]{1,0:T(8,128)(2,1)S(1)} copy(bf16[256,2048]{0,1:T(8,128)(2,1)} %bitcast.27) | data formatting | bytes 2097152 | tf_op jit(solution)/shard_map/back_project/reshape | solution.py:436
  90.2 6.6 %collective-permute-done.13.theirs_ref = f32[4,3,16,128]{3,2,1,0:T(8,128)S(1)} collective-permute-done((f32[4,3,16,128]{3,2,1,0:T(8,128)S(1)}, f32[4,3,16,128]{3,2,1,0:T(8,128)S(1)}, u32[]{:S(2)}, u32[]{:S(2)}) %collective-permute-start.13) | collective-permute-done | bytes 98336 | tf_op jit(solution)/shard_map/updates/ppermute | solution.py:333
  96.8 1.2 %updates.1 = (f32[128,128]{1,0:T(8,128)}, f32[128,128]{1,0:T(8,128)}) custom-call(s32[11]{0:T(128)S(1)} %pad_add_fusion.place_ref, f32[2,3,16,128]{3,2,1,0:T(8,128)S(1)} %get-tuple-element.52.own_ref, f32[2,3,16,128]{3,2,1,0:T(8,128)S(1)} %copy-done.4, f32[2,3,16,128]{3,2,1,0:T(8,128)S(1)} %copy-done.6, f32[2,3,16,128]{3,2,1,0:T(8,128)S(1)} %copy-done.8, ...), custom_call_target="tpu_custom_call" | custom-call | flops 1000000 | bytes 1048576 | tf_op jit(solution)/shard_map/updates/updates/pallas_call | solution.py:431
  98.0 3.6 %all-to-all-done.3.picked_ref = bf16[32,4,16,256]{3,2,1,0:T(8,128)(2,1)S(1)} async-done(((bf16[32,4,16,256]{3,2,1,0:T(8,128)(2,1)}), bf16[32,4,16,256]{3,2,1,0:T(8,128)(2,1)S(1)}, u32[]{:S(2)}, u32[]{:S(2)}) %all-to-all-start.3) | async-done | bytes 1048608 | tf_op jit(solution)/shard_map/pick/all_to_all | solution.py:427
  101.6 1.1 %back_project.1 = f32[512,128]{1,0:T(8,128)} custom-call(bf16[256,2048]{1,0:T(8,128)(2,1)S(1)} %copy.15.radon_ref, bf16[32,4,16,256]{3,2,1,0:T(8,128)(2,1)S(1)} %all-to-all-done.3.picked_ref, f32[512,128]{1,0:T(8,128)S(1)} %bitcast.18), custom_call_target="tpu_custom_call" | custom-call | flops 268435456 | bytes 1048576 | tf_op jit(solution)/shard_map/back_project/back_project/pallas_call | solution.py:437
  (58 shorter events, 2.4 us)
Async XLA Ops:
  0.6 11.9 %collective-permute-start = (f32[128,128]{1,0:T(8,128)}, f32[128,128]{1,0:T(8,128)S(1)}, u32[]{:S(2)}, u32[]{:S(2)}) collective-permute-start(f32[128,128]{1,0:T(8,128)} %bitcast.19), channel_id=1, source_target_pairs={{0,4},{4,0},{1,5},{5,1},{2,6},{6,2},{3,7},{7,3},{8,12},{12,8},{9,1... | collective-permute-start | bytes 196616 | tf_op jit(solution)/shard_map/ray_sums/ppermute | solution.py:333
  9.2 3.4 %copy-start.1 = (f32[1,64,2,128]{3,2,1,0:T(2,128)S(1)}, f32[1,64,2,128]{3,2,1,0:T(2,128)}, u32[]{:S(2)}) copy-start(f32[1,64,2,128]{3,2,1,0:T(2,128)} %param.12) | copy-start | bytes 196612
  9.2 3.4 %copy-start.2 = (f32[1,64,2,128]{3,2,1,0:T(2,128)S(1)}, f32[1,64,2,128]{3,2,1,0:T(2,128)}, u32[]{:S(2)}) copy-start(f32[1,64,2,128]{3,2,1,0:T(2,128)} %param.13) | copy-start | bytes 196612
  13.8 11.8 %collective-permute-start.3 = (f32[296,128]{1,0:T(8,128)S(1)}, f32[296,128]{1,0:T(8,128)S(1)}, u32[]{:S(2)}, u32[]{:S(2)}) collective-permute-start(f32[296,128]{1,0:T(8,128)S(1)} %get-tuple-element.38), channel_id=1, source_target_pairs={{0,3},{1,0},{2,1},{3,2},{4,7},{5,4},{6,5},{7,6},{8,11},{9,8},{10,9... | collective-permute-start | bytes 454664 | tf_op jit(solution)/shard_map/fields/ppermute | solution.py:333
  16.6 9.0 %collective-permute-start.2 = (f32[296,128]{1,0:T(8,128)S(1)}, f32[296,128]{1,0:T(8,128)S(1)}, u32[]{:S(2)}, u32[]{:S(2)}) collective-permute-start(f32[296,128]{1,0:T(8,128)S(1)} %get-tuple-element.37), channel_id=1, source_target_pairs={{0,2},{1,3},{2,0},{3,1},{4,6},{5,7},{6,4},{7,5},{8,10},{9,11},{10,... | collective-permute-start | bytes 454664 | tf_op jit(solution)/shard_map/fields/ppermute | solution.py:333
  17.0 10.1 %copy-start.10 = (f32[1,8,128,128]{3,2,1,0:T(8,128)S(1)}, f32[1,8,128,128]{3,2,1,0:T(8,128)}, u32[]{:S(2)}) copy-start(f32[1,8,128,128]{3,2,1,0:T(8,128)} %param.9) | copy-start | bytes 1572868
  17.0 10.1 %copy-start.11 = (f32[2,128,128]{2,1,0:T(8,128)S(1)}, f32[2,128,128]{2,1,0:T(8,128)}, u32[]{:S(2)}) copy-start(f32[2,128,128]{2,1,0:T(8,128)} %probe_ref.1) | copy-start | bytes 393220
  17.0 10.1 %copy-start.12 = (bf16[4,128,128]{2,1,0:T(8,128)(2,1)S(1)}, bf16[4,128,128]{2,1,0:T(8,128)(2,1)}, u32[]{:S(2)}) copy-start(bf16[4,128,128]{2,1,0:T(8,128)(2,1)} %constant.15.clone.dft_ref) | copy-start | bytes 393220
  17.0 10.1 %collective-permute-start.1 = (f32[296,128]{1,0:T(8,128)S(1)}, f32[296,128]{1,0:T(8,128)S(1)}, u32[]{:S(2)}, u32[]{:S(2)}) collective-permute-start(f32[296,128]{1,0:T(8,128)S(1)} %get-tuple-element.36), channel_id=1, source_target_pairs={{0,1},{1,2},{2,3},{3,0},{4,5},{5,6},{6,7},{7,4},{8,9},{9,10},{10,1... | collective-permute-start | bytes 454664 | tf_op jit(solution)/shard_map/fields/ppermute | solution.py:333
  17.7 26.1 %all-to-all-start = ((bf16[32,4,16,256]{3,2,1,0:T(8,128)(2,1)}), bf16[32,4,16,256]{3,2,1,0:T(8,128)(2,1)S(1)}, u32[]{:S(2)}, u32[]{:S(2)}) async-start(bf16[32,4,16,256]{3,2,1,0:T(8,128)(2,1)} %get-tuple-element.31), calls=%async_computation | async-start | bytes 2097152 | tf_op jit(solution)/shard_map/ray_sums/all_to_all | solution.py:371
  30.7 11.0 %collective-permute-start.7 = (bf16[2,128,128]{2,1,0:T(8,128)(2,1)S(1)}, bf16[2,128,128]{2,1,0:T(8,128)(2,1)S(1)}, u32[]{:S(2)}, u32[]{:S(2)}) collective-permute-start(bf16[2,128,128]{2,1,0:T(8,128)(2,1)S(1)} %get-tuple-element.41), channel_id=1, source_target_pairs={{0,1},{1,2},{2,3},{3,0},{4,5},{5,6},{6,7},{7,4},{8,9},{9,10},{10,1... | collective-permute-start | bytes 196616 | tf_op jit(solution)/shard_map/frames/ppermute | solution.py:333
  30.8 13.0 %collective-permute-start.8 = (bf16[2,128,128]{2,1,0:T(8,128)(2,1)S(1)}, bf16[2,128,128]{2,1,0:T(8,128)(2,1)S(1)}, u32[]{:S(2)}, u32[]{:S(2)}) collective-permute-start(bf16[2,128,128]{2,1,0:T(8,128)(2,1)S(1)} %get-tuple-element.42), channel_id=1, source_target_pairs={{0,2},{1,3},{2,0},{3,1},{4,6},{5,7},{6,4},{7,5},{8,10},{9,11},{10,... | collective-permute-start | bytes 196616 | tf_op jit(solution)/shard_map/frames/ppermute | solution.py:333
  33.2 10.6 %collective-permute-start.9 = (bf16[2,128,128]{2,1,0:T(8,128)(2,1)S(1)}, bf16[2,128,128]{2,1,0:T(8,128)(2,1)S(1)}, u32[]{:S(2)}, u32[]{:S(2)}) collective-permute-start(bf16[2,128,128]{2,1,0:T(8,128)(2,1)S(1)} %get-tuple-element.43), channel_id=1, source_target_pairs={{0,3},{1,0},{2,1},{3,2},{4,7},{5,4},{6,5},{7,6},{8,11},{9,8},{10,9... | collective-permute-start | bytes 196616 | tf_op jit(solution)/shard_map/frames/ppermute | solution.py:333
  34.4 4.6 %collective-permute-start.4 = (s32[4,32]{1,0:T(4,128)S(1)}, s32[4,32]{1,0:T(4,128)S(1)}, u32[]{:S(2)}, u32[]{:S(2)}) collective-permute-start(s32[4,32]{1,0:T(4,128)S(1)} %maximum_convert_fusion.table_0), channel_id=1, source_target_pairs={{0,64},{64,128},{128,192},{192,0},{1,65},{65,129},{129,193},{193,1... | collective-permute-start | bytes 1544 | tf_op jit(solution)/shard_map/targets/ppermute | solution.py:333
  35.2 3.8 %collective-permute-start.5 = (s32[4,32]{1,0:T(4,128)S(1)}, s32[4,32]{1,0:T(4,128)S(1)}, u32[]{:S(2)}, u32[]{:S(2)}) collective-permute-start(s32[4,32]{1,0:T(4,128)S(1)} %maximum_convert_fusion.table_0), channel_id=1, source_target_pairs={{0,128},{64,192},{128,0},{192,64},{1,129},{65,193},{129,1},{193,65... | collective-permute-start | bytes 1544 | tf_op jit(solution)/shard_map/targets/ppermute | solution.py:333
  39.0 2.7 %collective-permute-start.6 = (s32[4,32]{1,0:T(4,128)S(1)}, s32[4,32]{1,0:T(4,128)S(1)}, u32[]{:S(2)}, u32[]{:S(2)}) collective-permute-start(s32[4,32]{1,0:T(4,128)S(1)} %maximum_convert_fusion.table_0), channel_id=1, source_target_pairs={{0,192},{64,0},{128,64},{192,128},{1,193},{65,1},{129,65},{193,129... | collective-permute-start | bytes 1544 | tf_op jit(solution)/shard_map/targets/ppermute | solution.py:333
  61.5 12.8 %all-to-all-start.2 = ((bf16[8,128,128]{2,1,0:T(8,128)(2,1)}), bf16[8,128,128]{2,1,0:T(8,128)(2,1)S(1)}, u32[]{:S(2)}, u32[]{:S(2)}) async-start(bf16[8,128,128]{2,1,0:T(8,128)(2,1)} %get-tuple-element.45), calls=%async_computation.2 | async-start | bytes 524288 | tf_op jit(solution)/shard_map/residual/all_to_all | solution.py:413
  65.5 10.8 %collective-permute-start.10 = (f32[2,3,16,128]{3,2,1,0:T(8,128)S(1)}, f32[2,3,16,128]{3,2,1,0:T(8,128)S(1)}, u32[]{:S(2)}, u32[]{:S(2)}) collective-permute-start(f32[2,3,16,128]{3,2,1,0:T(8,128)S(1)} %get-tuple-element.49), channel_id=1, source_target_pairs={{0,1},{1,2},{2,3},{3,0},{4,5},{5,6},{6,7},{7,4},{8,9},{9,10},{10,1... | collective-permute-start | bytes 147464 | tf_op jit(solution)/shard_map/residual/ppermute | solution.py:333
  65.6 10.7 %collective-permute-start.11 = (f32[2,3,16,128]{3,2,1,0:T(8,128)S(1)}, f32[2,3,16,128]{3,2,1,0:T(8,128)S(1)}, u32[]{:S(2)}, u32[]{:S(2)}) collective-permute-start(f32[2,3,16,128]{3,2,1,0:T(8,128)S(1)} %get-tuple-element.50), channel_id=1, source_target_pairs={{0,2},{1,3},{2,0},{3,1},{4,6},{5,7},{6,4},{7,5},{8,10},{9,11},{10,... | collective-permute-start | bytes 147464 | tf_op jit(solution)/shard_map/residual/ppermute | solution.py:333
  66.1 10.2 %collective-permute-start.12 = (f32[2,3,16,128]{3,2,1,0:T(8,128)S(1)}, f32[2,3,16,128]{3,2,1,0:T(8,128)S(1)}, u32[]{:S(2)}, u32[]{:S(2)}) collective-permute-start(f32[2,3,16,128]{3,2,1,0:T(8,128)S(1)} %get-tuple-element.51), channel_id=1, source_target_pairs={{0,3},{1,0},{2,1},{3,2},{4,7},{5,4},{6,5},{7,6},{8,11},{9,8},{10,9... | collective-permute-start | bytes 147464 | tf_op jit(solution)/shard_map/residual/ppermute | solution.py:333
  76.3 9.0 %copy-start.3 = (f32[2,3,16,128]{3,2,1,0:T(8,128)}, f32[2,3,16,128]{3,2,1,0:T(8,128)S(1)}, u32[]{:S(2)}) copy-start(f32[2,3,16,128]{3,2,1,0:T(8,128)S(1)} %collective-permute-done.10.one_ref) | copy-start | bytes 147460
  76.4 9.0 %copy-start.5 = (f32[2,3,16,128]{3,2,1,0:T(8,128)}, f32[2,3,16,128]{3,2,1,0:T(8,128)S(1)}, u32[]{:S(2)}) copy-start(f32[2,3,16,128]{3,2,1,0:T(8,128)S(1)} %collective-permute-done.11.two_ref) | copy-start | bytes 147460
  76.4 8.9 %copy-start.7 = (f32[2,3,16,128]{3,2,1,0:T(8,128)}, f32[2,3,16,128]{3,2,1,0:T(8,128)S(1)}, u32[]{:S(2)}) copy-start(f32[2,3,16,128]{3,2,1,0:T(8,128)S(1)} %collective-permute-done.12.three_ref) | copy-start | bytes 147460
  76.4 11.2 %copy-start.13 = (bf16[1,32,2,32,256]{4,3,2,1,0:T(8,128)(2,1)S(1)}, bf16[1,32,2,32,256]{4,3,2,1,0:T(8,128)(2,1)}, u32[]{:S(2)}) copy-start(bf16[1,32,2,32,256]{4,3,2,1,0:T(8,128)(2,1)} %param.15) | copy-start | bytes 3145732
  76.4 25.2 %all-to-all-start.3 = ((bf16[32,4,16,256]{3,2,1,0:T(8,128)(2,1)}), bf16[32,4,16,256]{3,2,1,0:T(8,128)(2,1)S(1)}, u32[]{:S(2)}, u32[]{:S(2)}) async-start(bf16[32,4,16,256]{3,2,1,0:T(8,128)(2,1)} %pick_tiles.1), calls=%async_computation.3 | async-start | bytes 2097152 | tf_op jit(solution)/shard_map/pick/all_to_all | solution.py:427
  85.4 0.7 slice-start
  85.4 0.8 slice-start.1
  86.1 10.6 %collective-permute-start.13 = (f32[4,3,16,128]{3,2,1,0:T(8,128)S(1)}, f32[4,3,16,128]{3,2,1,0:T(8,128)S(1)}, u32[]{:S(2)}, u32[]{:S(2)}) collective-permute-start(f32[4,3,16,128]{3,2,1,0:T(8,128)S(1)} %pad_maximum_fusion), channel_id=1, source_target_pairs={{0,4},{4,0},{1,5},{5,1},{2,6},{6,2},{3,7},{7,3},{8,12},{12,8},{9,1... | collective-permute-start | bytes 294920 | tf_op jit(solution)/shard_map/updates/ppermute | solution.py:333
  88.7 8.1 %copy-start.4 = (f32[2,3,16,128]{3,2,1,0:T(8,128)S(1)}, f32[2,3,16,128]{3,2,1,0:T(8,128)}, u32[]{:S(2)}) copy-start(f32[2,3,16,128]{3,2,1,0:T(8,128)} %copy-done.3) | copy-start | bytes 147460
  88.7 8.1 %copy-start.6 = (f32[2,3,16,128]{3,2,1,0:T(8,128)S(1)}, f32[2,3,16,128]{3,2,1,0:T(8,128)}, u32[]{:S(2)}) copy-start(f32[2,3,16,128]{3,2,1,0:T(8,128)} %copy-done.5) | copy-start | bytes 147460
  88.7 8.1 %copy-start.8 = (f32[2,3,16,128]{3,2,1,0:T(8,128)S(1)}, f32[2,3,16,128]{3,2,1,0:T(8,128)}, u32[]{:S(2)}) copy-start(f32[2,3,16,128]{3,2,1,0:T(8,128)} %copy-done.7) | copy-start | bytes 147460
  90.2 11.5 %copy-start = (f32[256,2,128]{2,1,0:T(2,128)S(1)}, f32[256,2,128]{2,1,0:T(2,128)}, u32[]{:S(2)}) copy-start(f32[256,2,128]{2,1,0:T(2,128)} %param.14) | copy-start | bytes 786436
  (3 other events, 2.1 us)

commit v14 on v13

--- a/solution.py
+++ b/solution.py
@@ -35,6 +35,7 @@
 share = object_step / keep
 f32 = jnp.float32
 bf16 = jnp.bfloat16
+f16 = jnp.float16
 
 VM = pl.BlockSpec(memory_space=pltpu.VMEM)
 SM = pl.BlockSpec(memory_space=pltpu.SMEM)
@@ -242,20 +243,19 @@
 
 FIELD_ROWS = 2 * 128
 DRIFT_ROWS = 4 * QR
-SENT_ROWS = FIELD_ROWS + DRIFT_ROWS + QR
-
-
-def pack(place_ref, object_ref, theirs_ref, dual_ref, target_ref, own_ref, one_ref, two_ref, three_ref, both):
+OWN_ROWS = 128 + DRIFT_ROWS + QR
+
+
+def pack(place_ref, object_ref, dual_ref, target_ref, own_ref, one_ref, two_ref, three_ref, both):
     y = place_ref[1]
     both[...] = object_ref[...] + dual_ref[...]
     for ahead, ref in enumerate((own_ref, one_ref, two_ref, three_ref)):
         ref[0:128, :] = object_ref[...]
-        ref[128:256, :] = theirs_ref[...]
-        ref[FIELD_ROWS + DRIFT_ROWS :, :] = target_ref[...]
+        ref[128 + DRIFT_ROWS :, :] = target_ref[...]
         for part in range(2):
             for tile in range(2):
                 start = (tile * RAYS + lax.rem(y + ahead, Y) * QR) * 2 + part
-                base = FIELD_ROWS + (part * 2 + tile) * QR
+                base = 128 + (part * 2 + tile) * QR
                 ref[base : base + QR, :] = both[pl.ds(start, QR, stride=2), :]
 
 
@@ -269,8 +269,8 @@
         for other in range(ZH):
             owner = lax.rem(zh + other, ZH) * Y + lax.rem(y + Y - back, Y)
             rows = pl.ds(pl.multiple_of(owner * 64, 64), 64)
-            field_re[rows, :] = field_ref[pl.ds(other * 128, 64, stride=2), :]
-            field_im[rows, :] = field_ref[pl.ds(other * 128 + 1, 64, stride=2), :]
+            field_re[rows, :] = field_ref[pl.ds((1 - other) * 128, 64, stride=2), :]
+            field_im[rows, :] = field_ref[pl.ds((1 - other) * 128 + 1, 64, stride=2), :]
     total_re[...] = jnp.zeros(total_re.shape, f32)
     total_im[...] = jnp.zeros(total_im.shape, f32)
     probe_re = probe_ref[0]
@@ -352,7 +352,7 @@
     dual_rows = dual_field.reshape(128, NZ)
 
     with jax.named_scope("ray_sums"):
-        object_theirs = across(object_rows)
+        object_theirs = across(object_rows.astype(f16))
         sums, targets = call(
             ray_sums,
             (shape(NEAR, ZL, HITS * QR, 2 * NZ, dtype=bf16), shape(QR, NZ)),
@@ -371,11 +371,13 @@
         near_sums = lax.all_to_all(sums, CROSS, 0, 0, tiled=True)
 
     with jax.named_scope("fields"):
-        object_theirs, sums, targets = lax.optimization_barrier((object_theirs, sums, targets))
         packed = call(
-            pack, (shape(SENT_ROWS, NZ),) * Y, 1, 4, scratch=[pltpu.VMEM((128, NZ), f32)], flops=1_000_000
-        )(place, object_rows, object_theirs, dual_rows, targets)
-        fields = round_y(packed)
+            pack, (shape(OWN_ROWS, NZ),) * Y, 1, 3, scratch=[pltpu.VMEM((128, NZ), f32)], flops=1_000_000
+        )(place, object_rows, dual_rows, targets)
+        packed = [piece.astype(f16) for piece in packed]
+        object_theirs, sums, packed = lax.optimization_barrier((object_theirs, sums, packed))
+        fields = round_y([jnp.concatenate([object_theirs, piece]) for piece in packed])
+        fields = [field.astype(f32) for field in fields]
 
     with jax.named_scope("frames"):
         inter_parts = call(

time: 103 us -> 102 us (level)
  waiting for transfers between devices: 25 us -> 21 us
  starting transfers between devices: 41.8 us -> 45.7 us
  blocking collectives: 15.9 us -> 12.4 us
    all_to_all x1, blocking collectives: 15.9 us -> 12.4 us  [body(): far_sums = lax.all_to_all(dense, ALONG, 0, 0, tiled=True)]
    ppermute x14, starting transfers between devices: 21.5 us -> 24.5 us  [shifted(): lax.ppermute(value, axis, [(i, (i + step) % length) for i in range(length)])]
    ppermute x14, waiting for transfers between devices: 15.3 us -> 12.5 us  [shifted(): lax.ppermute(value, axis, [(i, (i + step) % length) for i in range(length)])]
    all_to_all x1, waiting for transfers between devices: 6.03 us -> 4.96 us  [body(): residuals = lax.all_to_all(copies, ALONG, 0, 0, tiled=True)]
  transfers between devices with their start and end apart: 17 -> 17, of which waited for: 7 -> 6; matrix products, arithmetic and copies ran while one was open for 3% -> 3% of each run, Pallas kernels for 11% -> 11%
where the time goes in v14:
time: 102 us; the launch traced here: 101 us
  starting transfers between devices  45.7 us (45%)
  waiting for transfers between devices  21 us (21%)
  Pallas kernels  14.4 us (14%)
  blocking collectives  12.4 us (12%)
  local copies, waits for them, and re-layouts  5.72 us (6%)
  other arithmetic  1.08 us (1%)
    ppermute x14, starting transfers between devices, shifted(): lax.ppermute(value, axis, [(i, (i + step) % length) for i in range(length)])  24.5 us
    ppermute x14, waiting for transfers between devices, shifted(): lax.ppermute(value, axis, [(i, (i + step) % length) for i in range(length)])  12.5 us
    all_to_all x1, blocking collectives, body(): far_sums = lax.all_to_all(dense, ALONG, 0, 0, tiled=True)  12.4 us
    all_to_all x1, starting transfers between devices, body(): returned = lax.all_to_all(picked, CROSS, 0, 0, tiled=True)  9.7 us
    all_to_all x1, starting transfers between devices, body(): near_sums = lax.all_to_all(sums, CROSS, 0, 0, tiled=True)  8.08 us
    all_to_all x1, waiting for transfers between devices, body(): residuals = lax.all_to_all(copies, ALONG, 0, 0, tiled=True)  4.96 us
    pallas_call x1, Pallas kernels, body(): call(frame_gradients, (shape(2, 128, NZ),) + (shape(2, 128, NZ, dtype=bf1...  3.64 us
    all_to_all x1, waiting for transfers between devices, body(): returned = lax.all_to_all(picked, CROSS, 0, 0, tiled=True)  3.55 us
  transfers between devices with their start and end apart: 17, of which 6 were waited for; matrix products, arithmetic and copies ran while one was open for 3% of the time, Pallas kernels for 11%

profile of v14, /device:TPU:1, one launch (start us, length us, event | category | flops | bytes accessed | tf_op | source)
XLA Modules:
  0.0 101.3 jit_solution(11967095293354751213)
XLA Ops:
  0.6 0.8 convert_element_type.30
  1.5 7.7 %collective-permute-start = (f16[128,128]{1,0:T(8,128)(2,1)S(1)}, f16[128,128]{1,0:T(8,128)(2,1)S(1)}, u32[]{:S(2)}, u32[]{:S(2)}) collective-permute-start(f16[128,128]{1,0:T(8,128)(2,1)S(1)} %convert_element_type.30), channel_id=1, source_target_pairs={{0,4},{4,0},{1,5},{5,1},{2,6},{6,2},{3,7},{7,3},{8,12},{12,8},{9,1... | collective-permute-start | bytes 98312 | tf_op jit(solution)/shard_map/ray_sums/ppermute | solution.py:333
  10.0 3.3 %ray_sums.1 = (bf16[32,4,16,256]{3,2,1,0:T(8,128)(2,1)}, f32[8,128]{1,0:T(8,128)}) custom-call(bf16[32,2,32,256]{3,2,1,0:T(8,128)(2,1)} %bitcast.25, f32[512,128]{1,0:T(8,128)} %bitcast.17, s32[1,32]{1,0:T(1,128)} %bitcast.29), custom_call_target="tpu_custom_call" | custom-call | flops 268435456 | bytes 1048576 | tf_op jit(solution)/shard_map/ray_sums/ray_sums/pallas_call | solution.py:356
  14.7 2.8 %collective-permute-start.3 = (f16[296,128]{1,0:T(8,128)(2,1)S(1)}, f16[296,128]{1,0:T(8,128)(2,1)S(1)}, u32[]{:S(2)}, u32[]{:S(2)}) collective-permute-start(f16[296,128]{1,0:T(8,128)(2,1)S(1)} %get-tuple-element.68), channel_id=1, source_target_pairs={{0,3},{1,0},{2,1},{3,2},{4,7},{5,4},{6,5},{7,6},{8,11},{9,8},{10,9... | collective-permute-start | bytes 227336 | tf_op jit(solution)/shard_map/fields/ppermute | solution.py:333
  18.6 8.1 %all-to-all-start = ((bf16[32,4,16,256]{3,2,1,0:T(8,128)(2,1)}), bf16[32,4,16,256]{3,2,1,0:T(8,128)(2,1)S(1)}, u32[]{:S(2)}, u32[]{:S(2)}) async-start(bf16[32,4,16,256]{3,2,1,0:T(8,128)(2,1)} %get-tuple-element.34), calls=%async_computation | async-start | bytes 2097152 | tf_op jit(solution)/shard_map/ray_sums/all_to_all | solution.py:371
  26.8 0.9 copy-done.10
  27.8 3.6 %frame_gradients.1 = (f32[2,128,128]{2,1,0:T(8,128)S(1)}, bf16[2,128,128]{2,1,0:T(8,128)(2,1)S(1)}, bf16[2,128,128]{2,1,0:T(8,128)(2,1)S(1)}, bf16[2,128,128]{2,1,0:T(8,128)(2,1)S(1)}) custom-call(s32[11]{0:T(128)S(1)} %pad_add_fusion.place_ref, f32[296,128]{1,0:T(8,128)S(1)} %get-tuple-element.65.field_0, f32[296,128]{1,0:T(8,128)S(1)} %convert_element_type.36.field_1, ...), custom_call_target="tpu_custom_call" | custom-call | flops 20000000000 | bytes 1048576 | tf_op jit(solution)/shard_map/frames/frame_gradients/pallas_call | solution.py:383
  31.4 1.5 %collective-permute-start.7 = (bf16[2,128,128]{2,1,0:T(8,128)(2,1)S(1)}, bf16[2,128,128]{2,1,0:T(8,128)(2,1)S(1)}, u32[]{:S(2)}, u32[]{:S(2)}) collective-permute-start(bf16[2,128,128]{2,1,0:T(8,128)(2,1)S(1)} %get-tuple-element.47), channel_id=1, source_target_pairs={{0,1},{1,2},{2,3},{3,0},{4,5},{5,6},{6,7},{7,4},{8,9},{9,10},{10,1... | collective-permute-start | bytes 196616 | tf_op jit(solution)/shard_map/frames/ppermute | solution.py:333
  32.9 2.4 %collective-permute-start.8 = (bf16[2,128,128]{2,1,0:T(8,128)(2,1)S(1)}, bf16[2,128,128]{2,1,0:T(8,128)(2,1)S(1)}, u32[]{:S(2)}, u32[]{:S(2)}) collective-permute-start(bf16[2,128,128]{2,1,0:T(8,128)(2,1)S(1)} %get-tuple-element.48), channel_id=1, source_target_pairs={{0,2},{1,3},{2,0},{3,1},{4,6},{5,7},{6,4},{7,5},{8,10},{9,11},{10,... | collective-permute-start | bytes 196616 | tf_op jit(solution)/shard_map/frames/ppermute | solution.py:333
  35.3 1.2 %collective-permute-start.9 = (bf16[2,128,128]{2,1,0:T(8,128)(2,1)S(1)}, bf16[2,128,128]{2,1,0:T(8,128)(2,1)S(1)}, u32[]{:S(2)}, u32[]{:S(2)}) collective-permute-start(bf16[2,128,128]{2,1,0:T(8,128)(2,1)S(1)} %get-tuple-element.49), channel_id=1, source_target_pairs={{0,3},{1,0},{2,1},{3,2},{4,7},{5,4},{6,5},{7,6},{8,11},{9,8},{10,9... | collective-permute-start | bytes 196616 | tf_op jit(solution)/shard_map/frames/ppermute | solution.py:333
  36.5 0.8 collective-permute-start.4
  37.3 1.2 %collective-permute-start.5 = (s32[4,32]{1,0:T(4,128)S(1)}, s32[4,32]{1,0:T(4,128)S(1)}, u32[]{:S(2)}, u32[]{:S(2)}) collective-permute-start(s32[4,32]{1,0:T(4,128)S(1)} %maximum_convert_fusion.table_0), channel_id=1, source_target_pairs={{0,128},{64,192},{128,0},{192,64},{1,129},{65,193},{129,1},{193,65... | collective-permute-start | bytes 1544 | tf_op jit(solution)/shard_map/targets/ppermute | solution.py:333
  38.5 2.6 %collective-permute-done.4.table_1 = s32[4,32]{1,0:T(4,128)S(1)} collective-permute-done((s32[4,32]{1,0:T(4,128)S(1)}, s32[4,32]{1,0:T(4,128)S(1)}, u32[]{:S(2)}, u32[]{:S(2)}) %collective-permute-start.4) | collective-permute-done | bytes 544 | tf_op jit(solution)/shard_map/targets/ppermute | solution.py:333
  41.1 2.7 %collective-permute-done.6.table_3 = s32[4,32]{1,0:T(4,128)S(1)} collective-permute-done((s32[4,32]{1,0:T(4,128)S(1)}, s32[4,32]{1,0:T(4,128)S(1)}, u32[]{:S(2)}, u32[]{:S(2)}) %collective-permute-start.6) | collective-permute-done | bytes 544 | tf_op jit(solution)/shard_map/targets/ppermute | solution.py:333
  43.8 1.1 %collective-permute-done.8.inter_2 = bf16[2,128,128]{2,1,0:T(8,128)(2,1)S(1)} collective-permute-done((bf16[2,128,128]{2,1,0:T(8,128)(2,1)S(1)}, bf16[2,128,128]{2,1,0:T(8,128)(2,1)S(1)}, u32[]{:S(2)}, u32[]{:S(2)}) %collective-permute-start.8) | collective-permute-done | bytes 65568 | tf_op jit(solution)/shard_map/frames/ppermute | solution.py:333
  45.0 1.1 %add_tiles.1 = (bf16[8,128,128]{2,1,0:T(8,128)(2,1)S(1)}, f32[2,128,128]{2,1,0:T(8,128)S(1)}) custom-call(s32[11]{0:T(128)S(1)} %pad_add_fusion.place_ref, s32[4,32]{1,0:T(4,128)S(1)} %maximum_convert_fusion.table_0, s32[4,32]{1,0:T(4,128)S(1)} %collective-permute-done.4.table_1, s32[4,32]{1,0:T(4,128)S(1)} %collective-permute-done.5.table_2, ...), custom_call_target="tpu_custom_call" | custom-call | flops 1000000 | bytes 1048576 | tf_op jit(solution)/shard_map/near_sum/add_tiles/pallas_call | solution.py:401
  46.1 12.4 %all_to_all.20.sums_ref = bf16[8,128,128]{2,1,0:T(8,128)(2,1)S(1)} all-to-all(bf16[8,128,128]{2,1,0:T(8,128)(2,1)S(1)} %get-tuple-element.50), channel_id=1, replica_groups=mesh['zl'=4,'x'=4,'c'=2,'zh'=2,'y'=4] {'zh','zl'}, dimensions={0} | all-to-all | bytes 524288 | tf_op jit(solution)/shard_map/near_sum/all_to_all | solution.py:409
  58.5 0.8 residual_part.1
  59.2 3.4 %all-to-all-start.2 = ((bf16[8,128,128]{2,1,0:T(8,128)(2,1)}), bf16[8,128,128]{2,1,0:T(8,128)(2,1)S(1)}, u32[]{:S(2)}, u32[]{:S(2)}) async-start(bf16[8,128,128]{2,1,0:T(8,128)(2,1)} %get-tuple-element.51), calls=%async_computation.2 | async-start | bytes 524288 | tf_op jit(solution)/shard_map/residual/all_to_all | solution.py:415
  63.5 1.9 %collective-permute-start.11 = (f32[2,3,16,128]{3,2,1,0:T(8,128)S(1)}, f32[2,3,16,128]{3,2,1,0:T(8,128)S(1)}, u32[]{:S(2)}, u32[]{:S(2)}) collective-permute-start(f32[2,3,16,128]{3,2,1,0:T(8,128)S(1)} %get-tuple-element.56), channel_id=1, source_target_pairs={{0,2},{1,3},{2,0},{3,1},{4,6},{5,7},{6,4},{7,5},{8,10},{9,11},{10,... | collective-permute-start | bytes 147464 | tf_op jit(solution)/shard_map/residual/ppermute | solution.py:333
  65.4 1.6 %collective-permute-start.12 = (f32[2,3,16,128]{3,2,1,0:T(8,128)S(1)}, f32[2,3,16,128]{3,2,1,0:T(8,128)S(1)}, u32[]{:S(2)}, u32[]{:S(2)}) collective-permute-start(f32[2,3,16,128]{3,2,1,0:T(8,128)S(1)} %get-tuple-element.57), channel_id=1, source_target_pairs={{0,3},{1,0},{2,1},{3,2},{4,7},{5,4},{6,5},{7,6},{8,11},{9,8},{10,9... | collective-permute-start | bytes 147464 | tf_op jit(solution)/shard_map/residual/ppermute | solution.py:333
  67.1 5.0 %all-to-all-done.2.residual_ref = bf16[8,128,128]{2,1,0:T(8,128)(2,1)S(1)} async-done(((bf16[8,128,128]{2,1,0:T(8,128)(2,1)}), bf16[8,128,128]{2,1,0:T(8,128)(2,1)S(1)}, u32[]{:S(2)}, u32[]{:S(2)}) %all-to-all-start.2) | async-done | bytes 262176 | tf_op jit(solution)/shard_map/residual/all_to_all | solution.py:415
  72.0 2.0 %pick_tiles.1 = bf16[32,4,16,256]{3,2,1,0:T(8,128)(2,1)} custom-call(s32[11]{0:T(128)S(1)} %pad_add_fusion.place_ref, s32[4,32]{1,0:T(4,128)S(1)} %maximum_convert_fusion.table_0, s32[4,32]{1,0:T(4,128)S(1)} %collective-permute-done.4.table_1, s32[4,32]{1,0:T(4,128)S(1)} %collective-permute-done.5.table_2, s32[4,32]{1,0:T(4,128)S(1)} %collective-permute-done.6.table_3, ...), custom_call_target="tpu_custom_call" | custom-call | flops 1000000 | bytes 1048576 | tf_op jit(solution)/shard_map/pick/pick_tiles/pallas_call | solution.py:420
  74.1 9.7 %all-to-all-start.3 = ((bf16[32,4,16,256]{3,2,1,0:T(8,128)(2,1)}), bf16[32,4,16,256]{3,2,1,0:T(8,128)(2,1)S(1)}, u32[]{:S(2)}, u32[]{:S(2)}) async-start(bf16[32,4,16,256]{3,2,1,0:T(8,128)(2,1)} %pick_tiles.1), calls=%async_computation.3 | async-start | bytes 2097152 | tf_op jit(solution)/shard_map/pick/all_to_all | solution.py:429
  83.9 0.7 slice-done.2
  84.6 2.0 %collective-permute-start.13 = (f32[4,3,16,128]{3,2,1,0:T(8,128)S(1)}, f32[4,3,16,128]{3,2,1,0:T(8,128)S(1)}, u32[]{:S(2)}, u32[]{:S(2)}) collective-permute-start(f32[4,3,16,128]{3,2,1,0:T(8,128)S(1)} %pad_maximum_fusion.4), channel_id=1, source_target_pairs={{0,4},{4,0},{1,5},{5,1},{2,6},{6,2},{3,7},{7,3},{8,12},{12,8},{9,1... | collective-permute-start | bytes 294920 | tf_op jit(solution)/shard_map/updates/ppermute | solution.py:333
  86.7 1.1 %copy.14 = bf16[256,8,4,4,2,8]{0,5,4,3,2,1:T(8,128)(2,1)} copy(bf16[256,8,4,4,2,8]{0,5,2,4,1,3:T(8,128)(2,1)S(1)} %bitcast.26) | data formatting | bytes 2097152 | tf_op jit(solution)/shard_map/back_project/transpose | solution.py:438
  87.8 1.5 %copy.15.radon_ref = bf16[256,2048]{1,0:T(8,128)(2,1)S(1)} copy(bf16[256,2048]{0,1:T(8,128)(2,1)} %bitcast.27) | data formatting | bytes 2097152 | tf_op jit(solution)/shard_map/back_project/reshape | solution.py:438
  89.3 6.0 %collective-permute-done.13.theirs_ref = f32[4,3,16,128]{3,2,1,0:T(8,128)S(1)} collective-permute-done((f32[4,3,16,128]{3,2,1,0:T(8,128)S(1)}, f32[4,3,16,128]{3,2,1,0:T(8,128)S(1)}, u32[]{:S(2)}, u32[]{:S(2)}) %collective-permute-start.13) | collective-permute-done | bytes 98336 | tf_op jit(solution)/shard_map/updates/ppermute | solution.py:333
  95.4 1.2 %updates.1 = (f32[128,128]{1,0:T(8,128)}, f32[128,128]{1,0:T(8,128)}) custom-call(s32[11]{0:T(128)S(1)} %pad_add_fusion.place_ref, f32[2,3,16,128]{3,2,1,0:T(8,128)S(1)} %get-tuple-element.58.own_ref, f32[2,3,16,128]{3,2,1,0:T(8,128)S(1)} %copy-done.4, f32[2,3,16,128]{3,2,1,0:T(8,128)S(1)} %copy-done.6, f32[2,3,16,128]{3,2,1,0:T(8,128)S(1)} %copy-done.8, ...), custom_call_target="tpu_custom_call" | custom-call | flops 1000000 | bytes 1048576 | tf_op jit(solution)/shard_map/updates/updates/pallas_call | solution.py:433
  96.6 3.5 %all-to-all-done.3.picked_ref = bf16[32,4,16,256]{3,2,1,0:T(8,128)(2,1)S(1)} async-done(((bf16[32,4,16,256]{3,2,1,0:T(8,128)(2,1)}), bf16[32,4,16,256]{3,2,1,0:T(8,128)(2,1)S(1)}, u32[]{:S(2)}, u32[]{:S(2)}) %all-to-all-start.3) | async-done | bytes 1048608 | tf_op jit(solution)/shard_map/pick/all_to_all | solution.py:429
  100.2 1.1 %back_project.1 = f32[512,128]{1,0:T(8,128)} custom-call(bf16[256,2048]{1,0:T(8,128)(2,1)S(1)} %copy.15.radon_ref, bf16[32,4,16,256]{3,2,1,0:T(8,128)(2,1)S(1)} %all-to-all-done.3.picked_ref, f32[512,128]{1,0:T(8,128)S(1)} %bitcast.18), custom_call_target="tpu_custom_call" | custom-call | flops 268435456 | bytes 1048576 | tf_op jit(solution)/shard_map/back_project/back_project/pallas_call | solution.py:439
  (67 shorter events, 4.2 us)
Async XLA Ops:
  1.5 13.2 %collective-permute-start = (f16[128,128]{1,0:T(8,128)(2,1)S(1)}, f16[128,128]{1,0:T(8,128)(2,1)S(1)}, u32[]{:S(2)}, u32[]{:S(2)}) collective-permute-start(f16[128,128]{1,0:T(8,128)(2,1)S(1)} %convert_element_type.30), channel_id=1, source_target_pairs={{0,4},{4,0},{1,5},{5,1},{2,6},{6,2},{3,7},{7,3},{8,12},{12,8},{9,1... | collective-permute-start | bytes 98312 | tf_op jit(solution)/shard_map/ray_sums/ppermute | solution.py:333
  10.0 3.3 %copy-start.1 = (f32[1,64,2,128]{3,2,1,0:T(2,128)S(1)}, f32[1,64,2,128]{3,2,1,0:T(2,128)}, u32[]{:S(2)}) copy-start(f32[1,64,2,128]{3,2,1,0:T(2,128)} %param.12) | copy-start | bytes 196612
  10.0 3.4 %copy-start.2 = (f32[1,64,2,128]{3,2,1,0:T(2,128)S(1)}, f32[1,64,2,128]{3,2,1,0:T(2,128)}, u32[]{:S(2)}) copy-start(f32[1,64,2,128]{3,2,1,0:T(2,128)} %param.13) | copy-start | bytes 196612
  14.7 12.0 %collective-permute-start.3 = (f16[296,128]{1,0:T(8,128)(2,1)S(1)}, f16[296,128]{1,0:T(8,128)(2,1)S(1)}, u32[]{:S(2)}, u32[]{:S(2)}) collective-permute-start(f16[296,128]{1,0:T(8,128)(2,1)S(1)} %get-tuple-element.68), channel_id=1, source_target_pairs={{0,3},{1,0},{2,1},{3,2},{4,7},{5,4},{6,5},{7,6},{8,11},{9,8},{10,9... | collective-permute-start | bytes 227336 | tf_op jit(solution)/shard_map/fields/ppermute | solution.py:333
  17.5 9.2 %collective-permute-start.2 = (f16[296,128]{1,0:T(8,128)(2,1)S(1)}, f16[296,128]{1,0:T(8,128)(2,1)S(1)}, u32[]{:S(2)}, u32[]{:S(2)}) collective-permute-start(f16[296,128]{1,0:T(8,128)(2,1)S(1)} %get-tuple-element.67), channel_id=1, source_target_pairs={{0,2},{1,3},{2,0},{3,1},{4,6},{5,7},{6,4},{7,5},{8,10},{9,11},{10,... | collective-permute-start | bytes 227336 | tf_op jit(solution)/shard_map/fields/ppermute | solution.py:333
  17.9 8.9 %collective-permute-start.1 = (f16[296,128]{1,0:T(8,128)(2,1)S(1)}, f16[296,128]{1,0:T(8,128)(2,1)S(1)}, u32[]{:S(2)}, u32[]{:S(2)}) collective-permute-start(f16[296,128]{1,0:T(8,128)(2,1)S(1)} %get-tuple-element.66), channel_id=1, source_target_pairs={{0,1},{1,2},{2,3},{3,0},{4,5},{5,6},{6,7},{7,4},{8,9},{9,10},{10,1... | collective-permute-start | bytes 227336 | tf_op jit(solution)/shard_map/fields/ppermute | solution.py:333
  18.6 8.2 %copy-start.12 = (bf16[4,128,128]{2,1,0:T(8,128)(2,1)S(1)}, bf16[4,128,128]{2,1,0:T(8,128)(2,1)}, u32[]{:S(2)}) copy-start(bf16[4,128,128]{2,1,0:T(8,128)(2,1)} %constant.15.clone.dft_ref) | copy-start | bytes 393220
  18.6 26.4 %all-to-all-start = ((bf16[32,4,16,256]{3,2,1,0:T(8,128)(2,1)}), bf16[32,4,16,256]{3,2,1,0:T(8,128)(2,1)S(1)}, u32[]{:S(2)}, u32[]{:S(2)}) async-start(bf16[32,4,16,256]{3,2,1,0:T(8,128)(2,1)} %get-tuple-element.34), calls=%async_computation | async-start | bytes 2097152 | tf_op jit(solution)/shard_map/ray_sums/all_to_all | solution.py:371
  26.7 1.0 %copy-start.10 = (f32[1,8,128,128]{3,2,1,0:T(8,128)S(1)}, f32[1,8,128,128]{3,2,1,0:T(8,128)}, u32[]{:S(2)}) copy-start(f32[1,8,128,128]{3,2,1,0:T(8,128)} %param.9) | copy-start | bytes 1572868
  26.8 1.0 copy-start.11
  31.4 12.4 %collective-permute-start.7 = (bf16[2,128,128]{2,1,0:T(8,128)(2,1)S(1)}, bf16[2,128,128]{2,1,0:T(8,128)(2,1)S(1)}, u32[]{:S(2)}, u32[]{:S(2)}) collective-permute-start(bf16[2,128,128]{2,1,0:T(8,128)(2,1)S(1)} %get-tuple-element.47), channel_id=1, source_target_pairs={{0,1},{1,2},{2,3},{3,0},{4,5},{5,6},{6,7},{7,4},{8,9},{9,10},{10,1... | collective-permute-start | bytes 196616 | tf_op jit(solution)/shard_map/frames/ppermute | solution.py:333
  32.9 12.1 %collective-permute-start.8 = (bf16[2,128,128]{2,1,0:T(8,128)(2,1)S(1)}, bf16[2,128,128]{2,1,0:T(8,128)(2,1)S(1)}, u32[]{:S(2)}, u32[]{:S(2)}) collective-permute-start(bf16[2,128,128]{2,1,0:T(8,128)(2,1)S(1)} %get-tuple-element.48), channel_id=1, source_target_pairs={{0,2},{1,3},{2,0},{3,1},{4,6},{5,7},{6,4},{7,5},{8,10},{9,11},{10,... | collective-permute-start | bytes 196616 | tf_op jit(solution)/shard_map/frames/ppermute | solution.py:333
  35.3 9.7 %collective-permute-start.9 = (bf16[2,128,128]{2,1,0:T(8,128)(2,1)S(1)}, bf16[2,128,128]{2,1,0:T(8,128)(2,1)S(1)}, u32[]{:S(2)}, u32[]{:S(2)}) collective-permute-start(bf16[2,128,128]{2,1,0:T(8,128)(2,1)S(1)} %get-tuple-element.49), channel_id=1, source_target_pairs={{0,3},{1,0},{2,1},{3,2},{4,7},{5,4},{6,5},{7,6},{8,11},{9,8},{10,9... | collective-permute-start | bytes 196616 | tf_op jit(solution)/shard_map/frames/ppermute | solution.py:333
  36.5 4.6 %collective-permute-start.4 = (s32[4,32]{1,0:T(4,128)S(1)}, s32[4,32]{1,0:T(4,128)S(1)}, u32[]{:S(2)}, u32[]{:S(2)}) collective-permute-start(s32[4,32]{1,0:T(4,128)S(1)} %maximum_convert_fusion.table_0), channel_id=1, source_target_pairs={{0,64},{64,128},{128,192},{192,0},{1,65},{65,129},{129,193},{193,1... | collective-permute-start | bytes 1544 | tf_op jit(solution)/shard_map/targets/ppermute | solution.py:333
  37.3 3.8 %collective-permute-start.5 = (s32[4,32]{1,0:T(4,128)S(1)}, s32[4,32]{1,0:T(4,128)S(1)}, u32[]{:S(2)}, u32[]{:S(2)}) collective-permute-start(s32[4,32]{1,0:T(4,128)S(1)} %maximum_convert_fusion.table_0), channel_id=1, source_target_pairs={{0,128},{64,192},{128,0},{192,64},{1,129},{65,193},{129,1},{193,65... | collective-permute-start | bytes 1544 | tf_op jit(solution)/shard_map/targets/ppermute | solution.py:333
  41.1 2.7 %collective-permute-start.6 = (s32[4,32]{1,0:T(4,128)S(1)}, s32[4,32]{1,0:T(4,128)S(1)}, u32[]{:S(2)}, u32[]{:S(2)}) collective-permute-start(s32[4,32]{1,0:T(4,128)S(1)} %maximum_convert_fusion.table_0), channel_id=1, source_target_pairs={{0,192},{64,0},{128,64},{192,128},{1,193},{65,1},{129,65},{193,129... | collective-permute-start | bytes 1544 | tf_op jit(solution)/shard_map/targets/ppermute | solution.py:333
  59.2 12.8 %all-to-all-start.2 = ((bf16[8,128,128]{2,1,0:T(8,128)(2,1)}), bf16[8,128,128]{2,1,0:T(8,128)(2,1)S(1)}, u32[]{:S(2)}, u32[]{:S(2)}) async-start(bf16[8,128,128]{2,1,0:T(8,128)(2,1)} %get-tuple-element.51), calls=%async_computation.2 | async-start | bytes 524288 | tf_op jit(solution)/shard_map/residual/all_to_all | solution.py:415
  63.2 10.8 %collective-permute-start.10 = (f32[2,3,16,128]{3,2,1,0:T(8,128)S(1)}, f32[2,3,16,128]{3,2,1,0:T(8,128)S(1)}, u32[]{:S(2)}, u32[]{:S(2)}) collective-permute-start(f32[2,3,16,128]{3,2,1,0:T(8,128)S(1)} %get-tuple-element.55), channel_id=1, source_target_pairs={{0,1},{1,2},{2,3},{3,0},{4,5},{5,6},{6,7},{7,4},{8,9},{9,10},{10,1... | collective-permute-start | bytes 147464 | tf_op jit(solution)/shard_map/residual/ppermute | solution.py:333
  63.5 10.6 %collective-permute-start.11 = (f32[2,3,16,128]{3,2,1,0:T(8,128)S(1)}, f32[2,3,16,128]{3,2,1,0:T(8,128)S(1)}, u32[]{:S(2)}, u32[]{:S(2)}) collective-permute-start(f32[2,3,16,128]{3,2,1,0:T(8,128)S(1)} %get-tuple-element.56), channel_id=1, source_target_pairs={{0,2},{1,3},{2,0},{3,1},{4,6},{5,7},{6,4},{7,5},{8,10},{9,11},{10,... | collective-permute-start | bytes 147464 | tf_op jit(solution)/shard_map/residual/ppermute | solution.py:333
  65.4 8.7 %collective-permute-start.12 = (f32[2,3,16,128]{3,2,1,0:T(8,128)S(1)}, f32[2,3,16,128]{3,2,1,0:T(8,128)S(1)}, u32[]{:S(2)}, u32[]{:S(2)}) collective-permute-start(f32[2,3,16,128]{3,2,1,0:T(8,128)S(1)} %get-tuple-element.57), channel_id=1, source_target_pairs={{0,3},{1,0},{2,1},{3,2},{4,7},{5,4},{6,5},{7,6},{8,11},{9,8},{10,9... | collective-permute-start | bytes 147464 | tf_op jit(solution)/shard_map/residual/ppermute | solution.py:333
  74.1 9.8 %copy-start.3 = (f32[2,3,16,128]{3,2,1,0:T(8,128)}, f32[2,3,16,128]{3,2,1,0:T(8,128)S(1)}, u32[]{:S(2)}) copy-start(f32[2,3,16,128]{3,2,1,0:T(8,128)S(1)} %collective-permute-done.10.one_ref) | copy-start | bytes 147460
  74.1 9.8 %copy-start.5 = (f32[2,3,16,128]{3,2,1,0:T(8,128)}, f32[2,3,16,128]{3,2,1,0:T(8,128)S(1)}, u32[]{:S(2)}) copy-start(f32[2,3,16,128]{3,2,1,0:T(8,128)S(1)} %collective-permute-done.11.two_ref) | copy-start | bytes 147460
  74.1 9.7 %copy-start.7 = (f32[2,3,16,128]{3,2,1,0:T(8,128)}, f32[2,3,16,128]{3,2,1,0:T(8,128)S(1)}, u32[]{:S(2)}) copy-start(f32[2,3,16,128]{3,2,1,0:T(8,128)S(1)} %collective-permute-done.12.three_ref) | copy-start | bytes 147460
  74.1 12.5 %copy-start.13 = (bf16[1,32,2,32,256]{4,3,2,1,0:T(8,128)(2,1)S(1)}, bf16[1,32,2,32,256]{4,3,2,1,0:T(8,128)(2,1)}, u32[]{:S(2)}) copy-start(bf16[1,32,2,32,256]{4,3,2,1,0:T(8,128)(2,1)} %param.15) | copy-start | bytes 3145732
  74.1 26.0 %all-to-all-start.3 = ((bf16[32,4,16,256]{3,2,1,0:T(8,128)(2,1)}), bf16[32,4,16,256]{3,2,1,0:T(8,128)(2,1)S(1)}, u32[]{:S(2)}, u32[]{:S(2)}) async-start(bf16[32,4,16,256]{3,2,1,0:T(8,128)(2,1)} %pick_tiles.1), calls=%async_computation.3 | async-start | bytes 2097152 | tf_op jit(solution)/shard_map/pick/all_to_all | solution.py:429
  83.9 0.7 slice-start
  83.9 0.8 slice-start.1
  84.6 10.7 %collective-permute-start.13 = (f32[4,3,16,128]{3,2,1,0:T(8,128)S(1)}, f32[4,3,16,128]{3,2,1,0:T(8,128)S(1)}, u32[]{:S(2)}, u32[]{:S(2)}) collective-permute-start(f32[4,3,16,128]{3,2,1,0:T(8,128)S(1)} %pad_maximum_fusion.4), channel_id=1, source_target_pairs={{0,4},{4,0},{1,5},{5,1},{2,6},{6,2},{3,7},{7,3},{8,12},{12,8},{9,1... | collective-permute-start | bytes 294920 | tf_op jit(solution)/shard_map/updates/ppermute | solution.py:333
  87.8 7.6 %copy-start.4 = (f32[2,3,16,128]{3,2,1,0:T(8,128)S(1)}, f32[2,3,16,128]{3,2,1,0:T(8,128)}, u32[]{:S(2)}) copy-start(f32[2,3,16,128]{3,2,1,0:T(8,128)} %copy-done.3) | copy-start | bytes 147460
  87.8 7.6 %copy-start.6 = (f32[2,3,16,128]{3,2,1,0:T(8,128)S(1)}, f32[2,3,16,128]{3,2,1,0:T(8,128)}, u32[]{:S(2)}) copy-start(f32[2,3,16,128]{3,2,1,0:T(8,128)} %copy-done.5) | copy-start | bytes 147460
  87.8 7.6 %copy-start.8 = (f32[2,3,16,128]{3,2,1,0:T(8,128)S(1)}, f32[2,3,16,128]{3,2,1,0:T(8,128)}, u32[]{:S(2)}) copy-start(f32[2,3,16,128]{3,2,1,0:T(8,128)} %copy-done.7) | copy-start | bytes 147460
  89.3 10.9 %copy-start = (f32[256,2,128]{2,1,0:T(2,128)S(1)}, f32[256,2,128]{2,1,0:T(2,128)}, u32[]{:S(2)}) copy-start(f32[256,2,128]{2,1,0:T(2,128)} %param.14) | copy-start | bytes 786436
  (3 other events, 2.1 us)

commit v15 on v14

--- a/solution.py
+++ b/solution.py
@@ -260,7 +260,7 @@
 
 
 def frame_gradients(
-    place_ref, field_0, field_1, field_2, field_3, probe_ref, measured_ref, dft_ref, own_ref, sent_one, sent_two, sent_three,
+    place_ref, field_0, field_1, field_2, field_3, probe_ref, amplitude_ref, dft_ref, own_ref, sent_one, sent_two, sent_three,
     field_re, field_im, total_re, total_im,
 ):
     zh = place_ref[0]
@@ -299,8 +299,8 @@
     far_re = far[:, :NZ]
     far_im = far[:, NZ:]
     modulus = jnp.sqrt(far_re * far_re + far_im * far_im)
-    intensity = measured_ref[...].reshape(FR_DEV * PROBE, NZ)
-    shrink = 1.0 - jnp.sqrt(intensity) / jnp.maximum(modulus, 1.0)
+    amplitude = amplitude_ref[...].reshape(FR_DEV * PROBE, NZ)
+    shrink = 1.0 - amplitude / jnp.maximum(modulus, 1.0)
     half = from_right(jnp.concatenate([far_re * shrink, far_im * shrink], axis=1), ah, al)
     stacked = jnp.concatenate(
         [
@@ -375,7 +375,8 @@
             pack, (shape(OWN_ROWS, NZ),) * Y, 1, 3, scratch=[pltpu.VMEM((128, NZ), f32)], flops=1_000_000
         )(place, object_rows, dual_rows, targets)
         packed = [piece.astype(f16) for piece in packed]
-        object_theirs, sums, packed = lax.optimization_barrier((object_theirs, sums, packed))
+        amplitude = jnp.sqrt(measured[0])
+        object_theirs, sums, packed, amplitude = lax.optimization_barrier((object_theirs, sums, packed, amplitude))
         fields = round_y([jnp.concatenate([object_theirs, piece]) for piece in packed])
         fields = [field.astype(f32) for field in fields]
 
@@ -387,7 +388,7 @@
             7,
             scratch=[pltpu.VMEM((NDET, NZ), f32)] * 4,
             flops=FRAMES_COST,
-        )(place, *fields, probe_field, measured[0], dft_blocks())
+        )(place, *fields, probe_field, amplitude, dft_blocks())
         inter_own = inter_parts[0]
         inter_parts = round_y(inter_parts)
 

time: 102 us -> 103 us (level)
  local copies, waits for them, and re-layouts: 5.72 us -> 6.82 us
    sqrt x0 -> x1, local copies, waits for them, and re-layouts: none -> 1.16 us  [body(): amplitude = jnp.sqrt(measured[0])]
    unnamed x30 -> x28, local copies, waits for them, and re-layouts: 2.34 us -> 2.29 us
  transfers between devices with their start and end apart: 17 -> 17, of which waited for: 6 -> 6; matrix products, arithmetic and copies ran while one was open for 3% -> 4% of each run, Pallas kernels for 11% -> 11%
where the time goes in v15:
time: 103 us; the launch traced here: 102 us
  starting transfers between devices  45.3 us (44%)
  waiting for transfers between devices  21.4 us (21%)
  Pallas kernels  14.3 us (14%)
  blocking collectives  11.9 us (12%)
  local copies, waits for them, and re-layouts  6.82 us (7%)
  other arithmetic  1.08 us (1%)
    ppermute x14, starting transfers between devices, shifted(): lax.ppermute(value, axis, [(i, (i + step) % length) for i in range(length)])  24.3 us
    ppermute x14, waiting for transfers between devices, shifted(): lax.ppermute(value, axis, [(i, (i + step) % length) for i in range(length)])  12.7 us
    all_to_all x1, blocking collectives, body(): far_sums = lax.all_to_all(dense, ALONG, 0, 0, tiled=True)  11.9 us
    all_to_all x1, starting transfers between devices, body(): returned = lax.all_to_all(picked, CROSS, 0, 0, tiled=True)  9.68 us
    all_to_all x1, starting transfers between devices, body(): near_sums = lax.all_to_all(sums, CROSS, 0, 0, tiled=True)  7.95 us
    all_to_all x1, waiting for transfers between devices, body(): residuals = lax.all_to_all(copies, ALONG, 0, 0, tiled=True)  5.07 us
    all_to_all x1, waiting for transfers between devices, body(): returned = lax.all_to_all(picked, CROSS, 0, 0, tiled=True)  3.63 us
    pallas_call x1, Pallas kernels, body(): call(frame_gradients, (shape(2, 128, NZ),) + (shape(2, 128, NZ, dtype=bf1...  3.56 us
  transfers between devices with their start and end apart: 17, of which 6 were waited for; matrix products, arithmetic and copies ran while one was open for 4% of the time, Pallas kernels for 11%

profile of v15, /device:TPU:1, one launch (start us, length us, event | category | flops | bytes accessed | tf_op | source)
XLA Modules:
  0.0 101.9 jit_solution(6770322744303312218)
XLA Ops:
  0.6 0.8 convert_element_type.30
  1.5 7.7 %collective-permute-start = (f16[128,128]{1,0:T(8,128)(2,1)S(1)}, f16[128,128]{1,0:T(8,128)(2,1)S(1)}, u32[]{:S(2)}, u32[]{:S(2)}) collective-permute-start(f16[128,128]{1,0:T(8,128)(2,1)S(1)} %convert_element_type.30), channel_id=1, source_target_pairs={{0,4},{4,0},{1,5},{5,1},{2,6},{6,2},{3,7},{7,3},{8,12},{12,8},{9,1... | collective-permute-start | bytes 98312 | tf_op jit(solution)/shard_map/ray_sums/ppermute | solution.py:333
  9.2 1.2 %sqrt_bitcast_fusion.amplitude_ref = f32[8,128,128]{2,1,0:T(8,128)S(1)} fusion(f32[1,8,128,128]{3,2,1,0:T(8,128)} %param.9), kind=kLoop, calls=%fused_computation | loop fusion | bytes 1048576 | tf_op jit(solution)/shard_map/fields/sqrt | solution.py:378
  11.1 3.3 %ray_sums.1 = (bf16[32,4,16,256]{3,2,1,0:T(8,128)(2,1)}, f32[8,128]{1,0:T(8,128)}) custom-call(bf16[32,2,32,256]{3,2,1,0:T(8,128)(2,1)} %bitcast.25, f32[512,128]{1,0:T(8,128)} %bitcast.18, s32[1,32]{1,0:T(1,128)} %bitcast.29), custom_call_target="tpu_custom_call" | custom-call | flops 268435456 | bytes 1048576 | tf_op jit(solution)/shard_map/ray_sums/ray_sums/pallas_call | solution.py:356
  15.9 2.8 %collective-permute-start.3 = (f16[296,128]{1,0:T(8,128)(2,1)S(1)}, f16[296,128]{1,0:T(8,128)(2,1)S(1)}, u32[]{:S(2)}, u32[]{:S(2)}) collective-permute-start(f16[296,128]{1,0:T(8,128)(2,1)S(1)} %get-tuple-element.70), channel_id=1, source_target_pairs={{0,3},{1,0},{2,1},{3,2},{4,7},{5,4},{6,5},{7,6},{8,11},{9,8},{10,9... | collective-permute-start | bytes 227336 | tf_op jit(solution)/shard_map/fields/ppermute | solution.py:333
  19.8 8.0 %all-to-all-start = ((bf16[32,4,16,256]{3,2,1,0:T(8,128)(2,1)}), bf16[32,4,16,256]{3,2,1,0:T(8,128)(2,1)S(1)}, u32[]{:S(2)}, u32[]{:S(2)}) async-start(bf16[32,4,16,256]{3,2,1,0:T(8,128)(2,1)} %get-tuple-element.35), calls=%async_computation | async-start | bytes 2097152 | tf_op jit(solution)/shard_map/ray_sums/all_to_all | solution.py:371
  27.8 0.8 copy-done.11
  28.7 3.6 %frame_gradients.1 = (f32[2,128,128]{2,1,0:T(8,128)S(1)}, bf16[2,128,128]{2,1,0:T(8,128)(2,1)S(1)}, bf16[2,128,128]{2,1,0:T(8,128)(2,1)S(1)}, bf16[2,128,128]{2,1,0:T(8,128)(2,1)S(1)}) custom-call(s32[11]{0:T(128)S(1)} %pad_add_fusion.place_ref, f32[296,128]{1,0:T(8,128)S(1)} %get-tuple-element.67.field_0, f32[296,128]{1,0:T(8,128)S(1)} %convert_element_type.36.field_1, ...), custom_call_target="tpu_custom_call" | custom-call | flops 20000000000 | bytes 1048576 | tf_op jit(solution)/shard_map/frames/frame_gradients/pallas_call | solution.py:384
  32.3 1.5 %collective-permute-start.7 = (bf16[2,128,128]{2,1,0:T(8,128)(2,1)S(1)}, bf16[2,128,128]{2,1,0:T(8,128)(2,1)S(1)}, u32[]{:S(2)}, u32[]{:S(2)}) collective-permute-start(bf16[2,128,128]{2,1,0:T(8,128)(2,1)S(1)} %get-tuple-element.49), channel_id=1, source_target_pairs={{0,1},{1,2},{2,3},{3,0},{4,5},{5,6},{6,7},{7,4},{8,9},{9,10},{10,1... | collective-permute-start | bytes 196616 | tf_op jit(solution)/shard_map/frames/ppermute | solution.py:333
  33.8 2.4 %collective-permute-start.8 = (bf16[2,128,128]{2,1,0:T(8,128)(2,1)S(1)}, bf16[2,128,128]{2,1,0:T(8,128)(2,1)S(1)}, u32[]{:S(2)}, u32[]{:S(2)}) collective-permute-start(bf16[2,128,128]{2,1,0:T(8,128)(2,1)S(1)} %get-tuple-element.50), channel_id=1, source_target_pairs={{0,2},{1,3},{2,0},{3,1},{4,6},{5,7},{6,4},{7,5},{8,10},{9,11},{10,... | collective-permute-start | bytes 196616 | tf_op jit(solution)/shard_map/frames/ppermute | solution.py:333
  36.2 1.2 %collective-permute-start.9 = (bf16[2,128,128]{2,1,0:T(8,128)(2,1)S(1)}, bf16[2,128,128]{2,1,0:T(8,128)(2,1)S(1)}, u32[]{:S(2)}, u32[]{:S(2)}) collective-permute-start(bf16[2,128,128]{2,1,0:T(8,128)(2,1)S(1)} %get-tuple-element.51), channel_id=1, source_target_pairs={{0,3},{1,0},{2,1},{3,2},{4,7},{5,4},{6,5},{7,6},{8,11},{9,8},{10,9... | collective-permute-start | bytes 196616 | tf_op jit(solution)/shard_map/frames/ppermute | solution.py:333
  37.4 0.8 collective-permute-start.4
  38.2 1.2 %collective-permute-start.5 = (s32[4,32]{1,0:T(4,128)S(1)}, s32[4,32]{1,0:T(4,128)S(1)}, u32[]{:S(2)}, u32[]{:S(2)}) collective-permute-start(s32[4,32]{1,0:T(4,128)S(1)} %maximum_convert_fusion.table_0), channel_id=1, source_target_pairs={{0,128},{64,192},{128,0},{192,64},{1,129},{65,193},{129,1},{193,65... | collective-permute-start | bytes 1544 | tf_op jit(solution)/shard_map/targets/ppermute | solution.py:333
  39.4 2.6 %collective-permute-done.4.table_1 = s32[4,32]{1,0:T(4,128)S(1)} collective-permute-done((s32[4,32]{1,0:T(4,128)S(1)}, s32[4,32]{1,0:T(4,128)S(1)}, u32[]{:S(2)}, u32[]{:S(2)}) %collective-permute-start.4) | collective-permute-done | bytes 544 | tf_op jit(solution)/shard_map/targets/ppermute | solution.py:333
  42.0 2.7 %collective-permute-done.6.table_3 = s32[4,32]{1,0:T(4,128)S(1)} collective-permute-done((s32[4,32]{1,0:T(4,128)S(1)}, s32[4,32]{1,0:T(4,128)S(1)}, u32[]{:S(2)}, u32[]{:S(2)}) %collective-permute-start.6) | collective-permute-done | bytes 544 | tf_op jit(solution)/shard_map/targets/ppermute | solution.py:333
  44.7 1.3 %collective-permute-done.8.inter_2 = bf16[2,128,128]{2,1,0:T(8,128)(2,1)S(1)} collective-permute-done((bf16[2,128,128]{2,1,0:T(8,128)(2,1)S(1)}, bf16[2,128,128]{2,1,0:T(8,128)(2,1)S(1)}, u32[]{:S(2)}, u32[]{:S(2)}) %collective-permute-start.8) | collective-permute-done | bytes 65568 | tf_op jit(solution)/shard_map/frames/ppermute | solution.py:333
  46.0 1.1 %add_tiles.1 = (bf16[8,128,128]{2,1,0:T(8,128)(2,1)S(1)}, f32[2,128,128]{2,1,0:T(8,128)S(1)}) custom-call(s32[11]{0:T(128)S(1)} %pad_add_fusion.place_ref, s32[4,32]{1,0:T(4,128)S(1)} %maximum_convert_fusion.table_0, s32[4,32]{1,0:T(4,128)S(1)} %collective-permute-done.4.table_1, s32[4,32]{1,0:T(4,128)S(1)} %collective-permute-done.5.table_2, ...), custom_call_target="tpu_custom_call" | custom-call | flops 1000000 | bytes 1048576 | tf_op jit(solution)/shard_map/near_sum/add_tiles/pallas_call | solution.py:402
  47.2 11.9 %all_to_all.20.sums_ref = bf16[8,128,128]{2,1,0:T(8,128)(2,1)S(1)} all-to-all(bf16[8,128,128]{2,1,0:T(8,128)(2,1)S(1)} %get-tuple-element.52), channel_id=1, replica_groups=mesh['zl'=4,'x'=4,'c'=2,'zh'=2,'y'=4] {'zh','zl'}, dimensions={0} | all-to-all | bytes 524288 | tf_op jit(solution)/shard_map/near_sum/all_to_all | solution.py:410
  59.1 0.8 residual_part.1
  59.8 3.4 %all-to-all-start.2 = ((bf16[8,128,128]{2,1,0:T(8,128)(2,1)}), bf16[8,128,128]{2,1,0:T(8,128)(2,1)S(1)}, u32[]{:S(2)}, u32[]{:S(2)}) async-start(bf16[8,128,128]{2,1,0:T(8,128)(2,1)} %get-tuple-element.53), calls=%async_computation.2 | async-start | bytes 524288 | tf_op jit(solution)/shard_map/residual/all_to_all | solution.py:416
  64.1 1.5 %collective-permute-start.11 = (f32[2,3,16,128]{3,2,1,0:T(8,128)S(1)}, f32[2,3,16,128]{3,2,1,0:T(8,128)S(1)}, u32[]{:S(2)}, u32[]{:S(2)}) collective-permute-start(f32[2,3,16,128]{3,2,1,0:T(8,128)S(1)} %get-tuple-element.58), channel_id=1, source_target_pairs={{0,2},{1,3},{2,0},{3,1},{4,6},{5,7},{6,4},{7,5},{8,10},{9,11},{10,... | collective-permute-start | bytes 147464 | tf_op jit(solution)/shard_map/residual/ppermute | solution.py:333
  65.6 2.0 %collective-permute-start.12 = (f32[2,3,16,128]{3,2,1,0:T(8,128)S(1)}, f32[2,3,16,128]{3,2,1,0:T(8,128)S(1)}, u32[]{:S(2)}, u32[]{:S(2)}) collective-permute-start(f32[2,3,16,128]{3,2,1,0:T(8,128)S(1)} %get-tuple-element.59), channel_id=1, source_target_pairs={{0,3},{1,0},{2,1},{3,2},{4,7},{5,4},{6,5},{7,6},{8,11},{9,8},{10,9... | collective-permute-start | bytes 147464 | tf_op jit(solution)/shard_map/residual/ppermute | solution.py:333
  67.6 5.1 %all-to-all-done.2.residual_ref = bf16[8,128,128]{2,1,0:T(8,128)(2,1)S(1)} async-done(((bf16[8,128,128]{2,1,0:T(8,128)(2,1)}), bf16[8,128,128]{2,1,0:T(8,128)(2,1)S(1)}, u32[]{:S(2)}, u32[]{:S(2)}) %all-to-all-start.2) | async-done | bytes 262176 | tf_op jit(solution)/shard_map/residual/all_to_all | solution.py:416
  72.7 2.0 %pick_tiles.1 = bf16[32,4,16,256]{3,2,1,0:T(8,128)(2,1)} custom-call(s32[11]{0:T(128)S(1)} %pad_add_fusion.place_ref, s32[4,32]{1,0:T(4,128)S(1)} %maximum_convert_fusion.table_0, s32[4,32]{1,0:T(4,128)S(1)} %collective-permute-done.4.table_1, s32[4,32]{1,0:T(4,128)S(1)} %collective-permute-done.5.table_2, s32[4,32]{1,0:T(4,128)S(1)} %collective-permute-done.6.table_3, ...), custom_call_target="tpu_custom_call" | custom-call | flops 1000000 | bytes 1048576 | tf_op jit(solution)/shard_map/pick/pick_tiles/pallas_call | solution.py:421
  74.8 9.7 %all-to-all-start.3 = ((bf16[32,4,16,256]{3,2,1,0:T(8,128)(2,1)}), bf16[32,4,16,256]{3,2,1,0:T(8,128)(2,1)S(1)}, u32[]{:S(2)}, u32[]{:S(2)}) async-start(bf16[32,4,16,256]{3,2,1,0:T(8,128)(2,1)} %pick_tiles.1), calls=%async_computation.3 | async-start | bytes 2097152 | tf_op jit(solution)/shard_map/pick/all_to_all | solution.py:430
  85.3 1.9 %collective-permute-start.13 = (f32[4,3,16,128]{3,2,1,0:T(8,128)S(1)}, f32[4,3,16,128]{3,2,1,0:T(8,128)S(1)}, u32[]{:S(2)}, u32[]{:S(2)}) collective-permute-start(f32[4,3,16,128]{3,2,1,0:T(8,128)S(1)} %pad_maximum_fusion.4), channel_id=1, source_target_pairs={{0,4},{4,0},{1,5},{5,1},{2,6},{6,2},{3,7},{7,3},{8,12},{12,8},{9,1... | collective-permute-start | bytes 294920 | tf_op jit(solution)/shard_map/updates/ppermute | solution.py:333
  87.2 1.1 %copy.14 = bf16[256,8,4,4,2,8]{0,5,4,3,2,1:T(8,128)(2,1)} copy(bf16[256,8,4,4,2,8]{0,5,2,4,1,3:T(8,128)(2,1)S(1)} %bitcast.26) | data formatting | bytes 2097152 | tf_op jit(solution)/shard_map/back_project/transpose | solution.py:439
  88.3 1.5 %copy.15.radon_ref = bf16[256,2048]{1,0:T(8,128)(2,1)S(1)} copy(bf16[256,2048]{0,1:T(8,128)(2,1)} %bitcast.27) | data formatting | bytes 2097152 | tf_op jit(solution)/shard_map/back_project/reshape | solution.py:439
  89.8 6.1 %collective-permute-done.13.theirs_ref = f32[4,3,16,128]{3,2,1,0:T(8,128)S(1)} collective-permute-done((f32[4,3,16,128]{3,2,1,0:T(8,128)S(1)}, f32[4,3,16,128]{3,2,1,0:T(8,128)S(1)}, u32[]{:S(2)}, u32[]{:S(2)}) %collective-permute-start.13) | collective-permute-done | bytes 98336 | tf_op jit(solution)/shard_map/updates/ppermute | solution.py:333
  95.9 1.2 %updates.1 = (f32[128,128]{1,0:T(8,128)}, f32[128,128]{1,0:T(8,128)}) custom-call(s32[11]{0:T(128)S(1)} %pad_add_fusion.place_ref, f32[2,3,16,128]{3,2,1,0:T(8,128)S(1)} %get-tuple-element.60.own_ref, f32[2,3,16,128]{3,2,1,0:T(8,128)S(1)} %copy-done.4, f32[2,3,16,128]{3,2,1,0:T(8,128)S(1)} %copy-done.6, f32[2,3,16,128]{3,2,1,0:T(8,128)S(1)} %copy-done.8, ...), custom_call_target="tpu_custom_call" | custom-call | flops 1000000 | bytes 1048576 | tf_op jit(solution)/shard_map/updates/updates/pallas_call | solution.py:434
  97.1 3.6 %all-to-all-done.3.picked_ref = bf16[32,4,16,256]{3,2,1,0:T(8,128)(2,1)S(1)} async-done(((bf16[32,4,16,256]{3,2,1,0:T(8,128)(2,1)}), bf16[32,4,16,256]{3,2,1,0:T(8,128)(2,1)S(1)}, u32[]{:S(2)}, u32[]{:S(2)}) %all-to-all-start.3) | async-done | bytes 1048608 | tf_op jit(solution)/shard_map/pick/all_to_all | solution.py:430
  100.8 1.1 %back_project.1 = f32[512,128]{1,0:T(8,128)} custom-call(bf16[256,2048]{1,0:T(8,128)(2,1)S(1)} %copy.15.radon_ref, bf16[32,4,16,256]{3,2,1,0:T(8,128)(2,1)S(1)} %all-to-all-done.3.picked_ref, f32[512,128]{1,0:T(8,128)S(1)} %bitcast.19), custom_call_target="tpu_custom_call" | custom-call | flops 268435456 | bytes 1048576 | tf_op jit(solution)/shard_map/back_project/back_project/pallas_call | solution.py:440
  (66 shorter events, 4.9 us)
Async XLA Ops:
  1.5 14.4 %collective-permute-start = (f16[128,128]{1,0:T(8,128)(2,1)S(1)}, f16[128,128]{1,0:T(8,128)(2,1)S(1)}, u32[]{:S(2)}, u32[]{:S(2)}) collective-permute-start(f16[128,128]{1,0:T(8,128)(2,1)S(1)} %convert_element_type.30), channel_id=1, source_target_pairs={{0,4},{4,0},{1,5},{5,1},{2,6},{6,2},{3,7},{7,3},{8,12},{12,8},{9,1... | collective-permute-start | bytes 98312 | tf_op jit(solution)/shard_map/ray_sums/ppermute | solution.py:333
  11.1 3.3 %copy-start.1 = (f32[1,64,2,128]{3,2,1,0:T(2,128)S(1)}, f32[1,64,2,128]{3,2,1,0:T(2,128)}, u32[]{:S(2)}) copy-start(f32[1,64,2,128]{3,2,1,0:T(2,128)} %param.12) | copy-start | bytes 196612
  11.1 3.4 %copy-start.2 = (f32[1,64,2,128]{3,2,1,0:T(2,128)S(1)}, f32[1,64,2,128]{3,2,1,0:T(2,128)}, u32[]{:S(2)}) copy-start(f32[1,64,2,128]{3,2,1,0:T(2,128)} %param.13) | copy-start | bytes 196612
  15.9 11.8 %collective-permute-start.3 = (f16[296,128]{1,0:T(8,128)(2,1)S(1)}, f16[296,128]{1,0:T(8,128)(2,1)S(1)}, u32[]{:S(2)}, u32[]{:S(2)}) collective-permute-start(f16[296,128]{1,0:T(8,128)(2,1)S(1)} %get-tuple-element.70), channel_id=1, source_target_pairs={{0,3},{1,0},{2,1},{3,2},{4,7},{5,4},{6,5},{7,6},{8,11},{9,8},{10,9... | collective-permute-start | bytes 227336 | tf_op jit(solution)/shard_map/fields/ppermute | solution.py:333
  18.7 9.0 %collective-permute-start.2 = (f16[296,128]{1,0:T(8,128)(2,1)S(1)}, f16[296,128]{1,0:T(8,128)(2,1)S(1)}, u32[]{:S(2)}, u32[]{:S(2)}) collective-permute-start(f16[296,128]{1,0:T(8,128)(2,1)S(1)} %get-tuple-element.69), channel_id=1, source_target_pairs={{0,2},{1,3},{2,0},{3,1},{4,6},{5,7},{6,4},{7,5},{8,10},{9,11},{10,... | collective-permute-start | bytes 227336 | tf_op jit(solution)/shard_map/fields/ppermute | solution.py:333
  19.1 8.8 %collective-permute-start.1 = (f16[296,128]{1,0:T(8,128)(2,1)S(1)}, f16[296,128]{1,0:T(8,128)(2,1)S(1)}, u32[]{:S(2)}, u32[]{:S(2)}) collective-permute-start(f16[296,128]{1,0:T(8,128)(2,1)S(1)} %get-tuple-element.68), channel_id=1, source_target_pairs={{0,1},{1,2},{2,3},{3,0},{4,5},{5,6},{6,7},{7,4},{8,9},{9,10},{10,1... | collective-permute-start | bytes 227336 | tf_op jit(solution)/shard_map/fields/ppermute | solution.py:333
  19.8 26.3 %all-to-all-start = ((bf16[32,4,16,256]{3,2,1,0:T(8,128)(2,1)}), bf16[32,4,16,256]{3,2,1,0:T(8,128)(2,1)S(1)}, u32[]{:S(2)}, u32[]{:S(2)}) async-start(bf16[32,4,16,256]{3,2,1,0:T(8,128)(2,1)} %get-tuple-element.35), calls=%async_computation | async-start | bytes 2097152 | tf_op jit(solution)/shard_map/ray_sums/all_to_all | solution.py:371
  27.8 0.9 copy-start.11
  27.8 0.9 copy-start.10
  32.3 12.4 %collective-permute-start.7 = (bf16[2,128,128]{2,1,0:T(8,128)(2,1)S(1)}, bf16[2,128,128]{2,1,0:T(8,128)(2,1)S(1)}, u32[]{:S(2)}, u32[]{:S(2)}) collective-permute-start(bf16[2,128,128]{2,1,0:T(8,128)(2,1)S(1)} %get-tuple-element.49), channel_id=1, source_target_pairs={{0,1},{1,2},{2,3},{3,0},{4,5},{5,6},{6,7},{7,4},{8,9},{9,10},{10,1... | collective-permute-start | bytes 196616 | tf_op jit(solution)/shard_map/frames/ppermute | solution.py:333
  33.8 12.2 %collective-permute-start.8 = (bf16[2,128,128]{2,1,0:T(8,128)(2,1)S(1)}, bf16[2,128,128]{2,1,0:T(8,128)(2,1)S(1)}, u32[]{:S(2)}, u32[]{:S(2)}) collective-permute-start(bf16[2,128,128]{2,1,0:T(8,128)(2,1)S(1)} %get-tuple-element.50), channel_id=1, source_target_pairs={{0,2},{1,3},{2,0},{3,1},{4,6},{5,7},{6,4},{7,5},{8,10},{9,11},{10,... | collective-permute-start | bytes 196616 | tf_op jit(solution)/shard_map/frames/ppermute | solution.py:333
  36.2 9.8 %collective-permute-start.9 = (bf16[2,128,128]{2,1,0:T(8,128)(2,1)S(1)}, bf16[2,128,128]{2,1,0:T(8,128)(2,1)S(1)}, u32[]{:S(2)}, u32[]{:S(2)}) collective-permute-start(bf16[2,128,128]{2,1,0:T(8,128)(2,1)S(1)} %get-tuple-element.51), channel_id=1, source_target_pairs={{0,3},{1,0},{2,1},{3,2},{4,7},{5,4},{6,5},{7,6},{8,11},{9,8},{10,9... | collective-permute-start | bytes 196616 | tf_op jit(solution)/shard_map/frames/ppermute | solution.py:333
  37.4 4.6 %collective-permute-start.4 = (s32[4,32]{1,0:T(4,128)S(1)}, s32[4,32]{1,0:T(4,128)S(1)}, u32[]{:S(2)}, u32[]{:S(2)}) collective-permute-start(s32[4,32]{1,0:T(4,128)S(1)} %maximum_convert_fusion.table_0), channel_id=1, source_target_pairs={{0,64},{64,128},{128,192},{192,0},{1,65},{65,129},{129,193},{193,1... | collective-permute-start | bytes 1544 | tf_op jit(solution)/shard_map/targets/ppermute | solution.py:333
  38.2 3.8 %collective-permute-start.5 = (s32[4,32]{1,0:T(4,128)S(1)}, s32[4,32]{1,0:T(4,128)S(1)}, u32[]{:S(2)}, u32[]{:S(2)}) collective-permute-start(s32[4,32]{1,0:T(4,128)S(1)} %maximum_convert_fusion.table_0), channel_id=1, source_target_pairs={{0,128},{64,192},{128,0},{192,64},{1,129},{65,193},{129,1},{193,65... | collective-permute-start | bytes 1544 | tf_op jit(solution)/shard_map/targets/ppermute | solution.py:333
  42.0 2.7 %collective-permute-start.6 = (s32[4,32]{1,0:T(4,128)S(1)}, s32[4,32]{1,0:T(4,128)S(1)}, u32[]{:S(2)}, u32[]{:S(2)}) collective-permute-start(s32[4,32]{1,0:T(4,128)S(1)} %maximum_convert_fusion.table_0), channel_id=1, source_target_pairs={{0,192},{64,0},{128,64},{192,128},{1,193},{65,1},{129,65},{193,129... | collective-permute-start | bytes 1544 | tf_op jit(solution)/shard_map/targets/ppermute | solution.py:333
  59.8 12.8 %all-to-all-start.2 = ((bf16[8,128,128]{2,1,0:T(8,128)(2,1)}), bf16[8,128,128]{2,1,0:T(8,128)(2,1)S(1)}, u32[]{:S(2)}, u32[]{:S(2)}) async-start(bf16[8,128,128]{2,1,0:T(8,128)(2,1)} %get-tuple-element.53), calls=%async_computation.2 | async-start | bytes 524288 | tf_op jit(solution)/shard_map/residual/all_to_all | solution.py:416
  63.8 10.9 %collective-permute-start.10 = (f32[2,3,16,128]{3,2,1,0:T(8,128)S(1)}, f32[2,3,16,128]{3,2,1,0:T(8,128)S(1)}, u32[]{:S(2)}, u32[]{:S(2)}) collective-permute-start(f32[2,3,16,128]{3,2,1,0:T(8,128)S(1)} %get-tuple-element.57), channel_id=1, source_target_pairs={{0,1},{1,2},{2,3},{3,0},{4,5},{5,6},{6,7},{7,4},{8,9},{9,10},{10,1... | collective-permute-start | bytes 147464 | tf_op jit(solution)/shard_map/residual/ppermute | solution.py:333
  64.1 10.6 %collective-permute-start.11 = (f32[2,3,16,128]{3,2,1,0:T(8,128)S(1)}, f32[2,3,16,128]{3,2,1,0:T(8,128)S(1)}, u32[]{:S(2)}, u32[]{:S(2)}) collective-permute-start(f32[2,3,16,128]{3,2,1,0:T(8,128)S(1)} %get-tuple-element.58), channel_id=1, source_target_pairs={{0,2},{1,3},{2,0},{3,1},{4,6},{5,7},{6,4},{7,5},{8,10},{9,11},{10,... | collective-permute-start | bytes 147464 | tf_op jit(solution)/shard_map/residual/ppermute | solution.py:333
  65.6 9.1 %collective-permute-start.12 = (f32[2,3,16,128]{3,2,1,0:T(8,128)S(1)}, f32[2,3,16,128]{3,2,1,0:T(8,128)S(1)}, u32[]{:S(2)}, u32[]{:S(2)}) collective-permute-start(f32[2,3,16,128]{3,2,1,0:T(8,128)S(1)} %get-tuple-element.59), channel_id=1, source_target_pairs={{0,3},{1,0},{2,1},{3,2},{4,7},{5,4},{6,5},{7,6},{8,11},{9,8},{10,9... | collective-permute-start | bytes 147464 | tf_op jit(solution)/shard_map/residual/ppermute | solution.py:333
  74.7 9.8 %copy-start.3 = (f32[2,3,16,128]{3,2,1,0:T(8,128)}, f32[2,3,16,128]{3,2,1,0:T(8,128)S(1)}, u32[]{:S(2)}) copy-start(f32[2,3,16,128]{3,2,1,0:T(8,128)S(1)} %collective-permute-done.10.one_ref) | copy-start | bytes 147460
  74.7 9.7 %copy-start.5 = (f32[2,3,16,128]{3,2,1,0:T(8,128)}, f32[2,3,16,128]{3,2,1,0:T(8,128)S(1)}, u32[]{:S(2)}) copy-start(f32[2,3,16,128]{3,2,1,0:T(8,128)S(1)} %collective-permute-done.11.two_ref) | copy-start | bytes 147460
  74.7 9.7 %copy-start.7 = (f32[2,3,16,128]{3,2,1,0:T(8,128)}, f32[2,3,16,128]{3,2,1,0:T(8,128)S(1)}, u32[]{:S(2)}) copy-start(f32[2,3,16,128]{3,2,1,0:T(8,128)S(1)} %collective-permute-done.12.three_ref) | copy-start | bytes 147460
  74.7 12.4 %copy-start.12 = (bf16[1,32,2,32,256]{4,3,2,1,0:T(8,128)(2,1)S(1)}, bf16[1,32,2,32,256]{4,3,2,1,0:T(8,128)(2,1)}, u32[]{:S(2)}) copy-start(bf16[1,32,2,32,256]{4,3,2,1,0:T(8,128)(2,1)} %param.15) | copy-start | bytes 3145732
  74.8 26.0 %all-to-all-start.3 = ((bf16[32,4,16,256]{3,2,1,0:T(8,128)(2,1)}), bf16[32,4,16,256]{3,2,1,0:T(8,128)(2,1)S(1)}, u32[]{:S(2)}, u32[]{:S(2)}) async-start(bf16[32,4,16,256]{3,2,1,0:T(8,128)(2,1)} %pick_tiles.1), calls=%async_computation.3 | async-start | bytes 2097152 | tf_op jit(solution)/shard_map/pick/all_to_all | solution.py:430
  84.5 0.7 slice-start.2
  84.5 0.7 slice-start
  84.5 0.8 slice-start.1
  85.3 10.6 %collective-permute-start.13 = (f32[4,3,16,128]{3,2,1,0:T(8,128)S(1)}, f32[4,3,16,128]{3,2,1,0:T(8,128)S(1)}, u32[]{:S(2)}, u32[]{:S(2)}) collective-permute-start(f32[4,3,16,128]{3,2,1,0:T(8,128)S(1)} %pad_maximum_fusion.4), channel_id=1, source_target_pairs={{0,4},{4,0},{1,5},{5,1},{2,6},{6,2},{3,7},{7,3},{8,12},{12,8},{9,1... | collective-permute-start | bytes 294920 | tf_op jit(solution)/shard_map/updates/ppermute | solution.py:333
  88.3 7.6 %copy-start.4 = (f32[2,3,16,128]{3,2,1,0:T(8,128)S(1)}, f32[2,3,16,128]{3,2,1,0:T(8,128)}, u32[]{:S(2)}) copy-start(f32[2,3,16,128]{3,2,1,0:T(8,128)} %copy-done.3) | copy-start | bytes 147460
  88.3 7.6 %copy-start.6 = (f32[2,3,16,128]{3,2,1,0:T(8,128)S(1)}, f32[2,3,16,128]{3,2,1,0:T(8,128)}, u32[]{:S(2)}) copy-start(f32[2,3,16,128]{3,2,1,0:T(8,128)} %copy-done.5) | copy-start | bytes 147460
  88.3 7.6 %copy-start.8 = (f32[2,3,16,128]{3,2,1,0:T(8,128)S(1)}, f32[2,3,16,128]{3,2,1,0:T(8,128)}, u32[]{:S(2)}) copy-start(f32[2,3,16,128]{3,2,1,0:T(8,128)} %copy-done.7) | copy-start | bytes 147460
  89.8 11.0 %copy-start = (f32[256,2,128]{2,1,0:T(2,128)S(1)}, f32[256,2,128]{2,1,0:T(2,128)}, u32[]{:S(2)}) copy-start(f32[256,2,128]{2,1,0:T(2,128)} %param.14) | copy-start | bytes 786436
  (2 other events, 1.3 us)
